TPU v7x, 256 devices: a whole 4x4x8 slice. The times are simulated.
256 devices in a mesh: sta: 64 (over z, x_lo, y), freq: 4 (over x_hi, core).
Axes of the slice: x: 4 (x_hi: 2, x_lo: 2; x = x_hi * 2 + x_lo), y: 4, z: 8, core: 2. Of those that a mesh axis runs over, the one named last changes fastest.
Arguments:
- spectra: bfloat16 [4, 2, 4096], P('freq', None, 'sta'), may hold values from -6 to 6
- green: bfloat16 [4, 2, 4096, 1024], P('freq', None, 'sta'), may hold values from -1.0546875 to 1.0546875
- source: float32 [4, 1024], P('freq'), may hold values from 0.25 to 4
- pair_mask: int32 [4096, 4096], P('sta'), may hold values 0 or 1
Outputs:
- new_source: float32 [4, 1024], P('freq')
- misfit: float32 [4], P('freq')
All inputs are finite; a program needn't handle non-finite values. No bound on the sum of `pair_mask` on one device may be relied on, other than what follows from the above.
Results may differ from a plain program's by a relative error of at most 0.0003.
Values may be sent and summed in bfloat16 or wider, within the bound.
No kernel may reach another device: no remote copies, remote signals or barrier semaphores. Data moves between devices by JAX's collectives and lax.ppermute only.
A program may use at most 64 MiB of HBM per device.

v0:
```python
import jax
import jax.numpy as jnp
from jax import lax
from jax.sharding import PartitionSpec as P


def copy_for_each(array, axis):
    peers = lax.axis_size(axis)
    return lax.all_to_all(
        jnp.broadcast_to(array[None], (peers, *array.shape)), axis, 0, 0, tiled=True
    )


def taken_together(array, axis):
    return copy_for_each(array, axis).sum(axis=0)


def in_one(arrays, axis):
    ends = [0]
    for a in arrays:
        ends.append(ends[-1] + a.size)
    total = taken_together(jnp.concatenate([a.ravel() for a in arrays]), axis)
    return tuple((total[b:e].reshape(a.shape) for a, b, e in zip(arrays, ends, ends[1:])))


def contract(a, b):
    return jnp.einsum("fix,fjx->fij", a, b, preferred_element_type=jnp.float32)


def spread(a, b):
    return jnp.einsum("fij,fjx->fix", a, b, preferred_element_type=jnp.float32)


def absorb(block_green, block_spec, weighted, spec_own, pair_mask):
    window = pair_mask.astype(jnp.float32)
    model_re = contract(weighted[:, 0], block_green[:, 0]) + contract(
        weighted[:, 1], block_green[:, 1]
    )
    model_im = contract(weighted[:, 1], block_green[:, 0]) - contract(
        weighted[:, 0], block_green[:, 1]
    )
    other = block_spec.astype(jnp.float32)
    data_re = (
        spec_own[:, 0, :, None] * other[:, 0, None, :]
        + spec_own[:, 1, :, None] * other[:, 1, None, :]
    )
    data_im = (
        spec_own[:, 1, :, None] * other[:, 0, None, :]
        - spec_own[:, 0, :, None] * other[:, 1, None, :]
    )
    resid_re = window[None] * (data_re - model_re)
    resid_im = window[None] * (data_im - model_im)
    mis = 0.5 * jnp.sum(resid_re * resid_re + resid_im * resid_im, axis=(1, 2))
    round_re = resid_re.astype(jnp.bfloat16)
    round_im = resid_im.astype(jnp.bfloat16)
    delta_re = spread(round_re, block_green[:, 0]) - spread(round_im, block_green[:, 1])
    delta_im = spread(round_re, block_green[:, 1]) + spread(round_im, block_green[:, 0])
    accum = jnp.stack([delta_re, delta_im], axis=1)
    return (accum, mis)


def local(spectra, green, source, pair_mask):
    count = lax.axis_size("sta")
    rows = green.shape[2]
    weighted = (source[:, None, None, :] * green).astype(jnp.bfloat16)
    spec_own = spectra.astype(jnp.float32)
    every_green, every_spec = (
        lax.all_gather(green, "sta", axis=2, tiled=True),
        lax.all_gather(spectra, "sta", axis=2, tiled=True),
    )
    state = absorb(every_green, every_spec, weighted, spec_own, pair_mask)
    accum, mis = state
    part = -jnp.sum(green * accum, axis=(1, 2))
    total_entries = green.shape[0] * lax.axis_size("freq") * green.shape[3]
    stations = rows * count
    grad, misfit = in_one((part, mis), "sta")
    squares = taken_together(jnp.sum(grad * grad), "freq")
    rms = jnp.sqrt(squares / total_entries + 1e-06)
    new_source = source * jnp.exp(-0.5 * grad / rms)
    return (new_source, misfit / (stations * stations))


def solution(mesh):
    placed = (P("freq", None, "sta"), P("freq", None, "sta", None), P("freq", None), P("sta", None))
    return jax.shard_map(
        local, mesh=mesh, in_specs=placed, out_specs=(P("freq", None), P("freq")), check_vma=False
    )
```

profile of v0, /device:TPU:1, one launch (start us, length us, event | category | flops | bytes accessed | tf_op | source)
XLA Modules:
  0.0 413.4 jit_solution(2978690009812199864)
XLA Ops:
  7.2 0.0 all-gather.2.cloned.1.call-start
  7.2 0.7 all-gather.2.cloned.1.call-update
  7.9 0.8 copy.9
  8.7 0.7 convert_element_type.26
  9.3 156.1 %all_gather.6 = bf16[1,2,4096]{1,0,2:T(2,128)(2,1)S(1)} all-gather(bf16[1,2,64]{1,0,2:T(2,128)(2,1)S(1)} %copy.9), channel_id=1, replica_groups=mesh['sta'=64,'freq'=4] {'sta'}, dimensions={2}, use_global_device_ids=true | all-gather | bytes 16640 | tf_op jit(solution)/shard_map/all_gather | solution.py:69
  165.4 2.2 convert_element_type.27
  167.6 1.0 fusion.18
  168.6 66.1 %slice_reduce_fusion.1 = (f32[4096]{0:T(1024)S(1)}, f32[4096]{0:T(1024)S(1)}) fusion(f32[1,2,4096]{1,0,2:T(1,128)S(1)} %convert_element_type.27), kind=kLoop, calls=%fused_computation.17 | loop fusion | bytes 65536 | tf_op jit(solution)/shard_map/slice | solution.py:44
  234.8 0.0 copy-start.2
  234.8 81.2 %all-gather.2.cloned.1.call-done = bf16[1,2,4096,1024]{3,2,1,0:T(8,128)(2,1)} async-done(((bf16[1,2,64,1024]{3,2,1,0:T(8,128)(2,1)}), bf16[1,2,4096,1024]{3,2,1,0:T(8,128)(2,1)}) %all-gather.2.cloned.1.call-update) | async-done | bytes 16777232 | tf_op jit(solution)/shard_map/all_gather | solution.py:68
  316.0 0.0 copy-start
  316.0 6.2 %fusion.3 = f32[64,4096]{1,0:T(8,128)S(1)} fusion(bf16[1,2,4096,1024]{3,2,1,0:T(8,128)(2,1)} %all-gather.2.cloned.1.call-done, bf16[1,2,64,1024]{3,2,1,0:T(8,128)(2,1)S(1)} %fusion.18), kind=kOutput, calls=%fused_computation.5 | convolution fusion | flops 536870912 | bytes 9568256 | tf_op jit(solution)/shard_map/fix,fjx->fij/dot_general | solution.py:27
  322.2 6.8 %fusion.1 = f32[64,4096]{1,0:T(8,128)S(1)} fusion(bf16[1,2,4096,1024]{3,2,1,0:T(8,128)(2,1)} %all-gather.2.cloned.1.call-done, bf16[1,2,64,1024]{3,2,1,0:T(8,128)(2,1)S(1)} %fusion.18), kind=kOutput, calls=%fused_computation.3 | convolution fusion | flops 536870912 | bytes 9568256 | tf_op jit(solution)/shard_map/fix,fjx->fij/dot_general | solution.py:27
  329.0 0.0 copy-done.2
  329.0 0.0 copy-done
  329.0 2.7 fusion.10
  331.7 1.6 fusion.2
  333.3 3.8 add_reduce_fusion
  337.0 1.6 fusion
  338.6 0.0 copy-start.1
  338.6 1.6 fusion.15
  340.2 0.0 copy-start.3
  340.2 1.6 fusion.17
  341.8 0.0 copy-done.1
  341.8 0.1 fusion.19
  342.6 0.2 broadcast_in_dim.4
  342.7 16.6 %all_to_all.12 = f32[64,1,1025]{2,1,0:T(1,128)S(1)} all-to-all(f32[64,1,1025]{2,1,0:T(1,128)S(1)} %broadcast_in_dim.4), channel_id=1, replica_groups=mesh['sta'=64,'freq'=4] {'sta'}, dimensions={0} | all-to-all | bytes 524800 | tf_op jit(solution)/shard_map/all_to_all | solution.py:9
  359.3 0.2 reduce_sum.47
  359.5 0.6 multiply_reduce_fusion
  360.1 0.6 slice.59
  360.7 1.2 broadcast_in_dim.5
  362.0 37.0 %all-to-all-start.1 = ((f32[4,1,1]{2,1,0:T(1,128)}), f32[4,1,1]{2,1,0:T(1,128)S(1)}, u32[]{:S(2)}, u32[]{:S(2)}) async-start(f32[4,1,1]{2,1,0:T(1,128)} %broadcast_in_dim.5), calls=%async_computation.1 | async-start | bytes 4096 | tf_op jit(solution)/shard_map/all_to_all | solution.py:9
  399.7 3.8 all-to-all-done.1
  403.5 0.6 reduce_sum.49
  404.8 0.0 copy-done.3
  404.8 0.6 mul.130
  (4 shorter events, 0.0 us)
Async XLA Ops:
  7.2 308.8 %all-gather.2.cloned.1.call-start = ((), (), s32[]{:S(2)}) async-start(), calls=%async_computation.2 | async-start | bytes 17039360 | tf_op jit(solution)/shard_map/all_gather | solution.py:68
  234.8 94.2 %copy-start.2 = (s32[64,4096]{1,0:T(8,128)S(1)}, s32[64,4096]{1,0:T(8,128)}, u32[]{:S(2)}) copy-start(s32[64,4096]{1,0:T(8,128)} %param.7) | copy-start | bytes 3145732
  316.0 13.0 %copy-start = (bf16[1,2,4096,1024]{3,2,1,0:T(8,128)(2,1)S(1)}, bf16[1,2,4096,1024]{3,2,1,0:T(8,128)(2,1)}, u32[]{:S(2)}) copy-start(bf16[1,2,4096,1024]{3,2,1,0:T(8,128)(2,1)} %all-gather.2.cloned.1.call-done) | copy-start | bytes 50331652
  338.6 3.2 copy-start.1
  340.2 64.6 %copy-start.3 = (f32[1,1024]{1,0:T(1,128)S(1)}, f32[1,1024]{1,0:T(1,128)}, u32[]{:S(2)}) copy-start(f32[1,1024]{1,0:T(1,128)} %param.6) | copy-start | bytes 12292
  362.0 41.5 %all-to-all-start.1 = ((f32[4,1,1]{2,1,0:T(1,128)}), f32[4,1,1]{2,1,0:T(1,128)S(1)}, u32[]{:S(2)}, u32[]{:S(2)}) async-start(f32[4,1,1]{2,1,0:T(1,128)} %broadcast_in_dim.5), calls=%async_computation.1 | async-start | bytes 4096 | tf_op jit(solution)/shard_map/all_to_all | solution.py:9
Sparse Core Ops, SparseCore 0:
  9.8 306.1 all-gather.1
where the time goes:
time: 414 us; the launch traced here: 413 us
  blocking collectives  173 us (42%)
  waiting for transfers between devices  85.7 us (21%)
  local copies, waits for them, and re-layouts  68.9 us (17%)
  starting transfers between devices  37.1 us (9%)
  matrix products  25.7 us (6%)
  between operations  17.4 us (4%)
  other arithmetic  5.96 us (1%)
    all_gather x1, blocking collectives, local(): lax.all_gather(spectra, 'sta', axis=2, tiled=True)  156 us
    all_gather x1, waiting for transfers between devices, local(): lax.all_gather(green, 'sta', axis=2, tiled=True)  81.2 us
    slice x1, local copies, waits for them, and re-layouts, absorb(): other[:, 0, None, :]  66.1 us
    all_to_all x1, starting transfers between devices, copy_for_each(): lax.all_to_all(jnp.broadcast_to(array[None], (peers, *array.shape)), axis...  37 us
    dot_general x4, matrix products, contract(): return jnp.einsum('fix,fjx->fij', a, b, preferred_element_type=jnp.float32)  19.4 us
    all_to_all x1, blocking collectives, copy_for_each(): lax.all_to_all(jnp.broadcast_to(array[None], (peers, *array.shape)), axis...  16.6 us
  transfers between devices with their start and end apart: 2, of which 2 were waited for; matrix products, arithmetic and copies ran while one was open for 17% of the time, Pallas kernels for 0%

commit v1 on v0

v1 whole, which is shorter than its diff:
```python
import jax
import jax.numpy as jnp
from jax import lax
from jax.experimental import pallas as pl
from jax.experimental.pallas import tpu as pltpu
from jax.sharding import PartitionSpec as P

NZ, NX, NY = 8, 2, 4
NQ = NX * NY
ROWS = 64
CELLS = 1024
WIDE = NQ * ROWS
BOTH = (1, 2, -3)
OFFSETS = (1, 2, -3, 4)


def z_shift(u):
    return [
        (z * NQ + q, ((z - u) % NZ) * NQ + q) for z in range(NZ) for q in range(NQ)
    ]


def q_minus(q, a):
    return ((q // NY) ^ (a // NY)) * NY + (q % NY - a % NY) % NY


def q_shift(a):
    return [(z * NQ + q, z * NQ + q_minus(q, a)) for z in range(NZ) for q in range(NQ)]


def nt(a, b):
    return lax.dot_general(
        a, b, (((1,), (1,)), ((), ())), preferred_element_type=jnp.float32
    )


def nn(a, b):
    return lax.dot_general(
        a, b, (((1,), (0,)), ((), ())), preferred_element_type=jnp.float32
    )


def pack(place, green, mask, spec_col, *outs):
    line = outs[: len(OFFSETS)]
    plane = outs[len(OFFSETS) : len(OFFSETS) + NQ - 1]
    own_mask, own_back = outs[-2:]
    z, q = place[0], place[1]
    x, y = q // NY, q % NY

    def window(at):
        start = pl.multiple_of(lax.rem(at + NZ, NZ) * WIDE, WIDE)
        return mask[:, pl.ds(start, WIDE)].astype(jnp.float32).astype(jnp.bfloat16)

    def other(col, sign):
        a = col // ROWS
        ax, ay = a // NY, a % NY
        return (
            ((x + ax) % NX * NY + (y + sign * ay + NY) % NY) * ROWS + col % ROWS
        )

    down = lax.broadcasted_iota(jnp.int32, (WIDE, WIDE), 0)
    across = lax.broadcasted_iota(jnp.int32, (WIDE, WIDE), 1)
    order = (down == other(across, 1)).astype(jnp.float32).astype(jnp.bfloat16)
    ahead = jnp.concatenate([window(z)] + [window(z - u) for u in OFFSETS], axis=0)
    ahead = nn(ahead, order).astype(jnp.bfloat16)
    order = (across == other(down, -1)).astype(jnp.float32).astype(jnp.bfloat16)
    col = lax.broadcasted_iota(jnp.int32, (ROWS, WIDE), 1) % ROWS
    spectra = jnp.where(
        col == 0, spec_col[:, 0:1], jnp.where(col == 1, spec_col[:, 1:2], 0.0)
    )
    back = jnp.concatenate(
        [window(z + u) for u in BOTH] + [spectra.astype(jnp.bfloat16)], axis=0
    )
    back = nt(order, back).astype(jnp.bfloat16)

    own_mask[...] = ahead[:ROWS]
    own_back[...] = back[:ROWS]
    lane = lax.broadcasted_iota(jnp.int32, (ROWS, 128), 1)
    column = jnp.where(
        lane == 0, spec_col[:, 0:1], jnp.where(lane == 1, spec_col[:, 1:2], 0.0)
    ).astype(jnp.bfloat16)
    for k, ref in enumerate(line):
        ref[0:64, :] = green[0]
        ref[64:128, :] = green[1]
        part = ahead[ROWS * (k + 1) : ROWS * (k + 2)]
        ref[128:160, 0:512] = part[0:32]
        ref[128:160, 512:1024] = part[32:64]
        for g in range(8):
            ref[160:168, 128 * g : 128 * (g + 1)] = column[8 * g : 8 * (g + 1)]
    for k, ref in enumerate(plane):
        ref[0:64, :] = green[0]
        ref[64:128, :] = green[1]
        part = back[ROWS * (k + 1) : ROWS * (k + 2)]
        for g in range(4):
            ref[128:144, 256 * g : 256 * (g + 1)] = part[16 * g : 16 * (g + 1)]


def absorb(source, green, spec_col, own_mask, own_back, *rest):
    line = rest[: len(OFFSETS)]
    plane = rest[len(OFFSETS) : len(OFFSETS) + NQ - 1]
    out, far_re, far_im, far_spec, back, near_re, near_im, wt_re, wt_im = rest[
        len(OFFSETS) + NQ - 1 :
    ]
    f32, bf16 = jnp.float32, jnp.bfloat16
    scale = source[...]
    for a in range(NQ):
        rows = slice(ROWS * a, ROWS * (a + 1))
        if a == 0:
            far_re[rows, :] = green[0]
            far_im[rows, :] = green[1]
            piece = own_back[...].astype(f32)
        else:
            ref = plane[a - 1]
            far_re[rows, :] = ref[0:64, :]
            far_im[rows, :] = ref[64:128, :]
            piece = jnp.concatenate(
                [ref[128:144, 256 * g : 256 * (g + 1)].astype(f32) for g in range(4)],
                axis=0,
            )
        for k in range(len(BOTH)):
            back[ROWS * k : ROWS * (k + 1), rows] = piece[:, ROWS * k : ROWS * (k + 1)]
        far_spec[0:2, rows] = piece[0:2, 3 * ROWS : 4 * ROWS]
    us, masks = [], []
    for k in range(1 + len(OFFSETS)):
        rows = slice(ROWS * k, ROWS * (k + 1))
        if k == 0:
            re, im = green[0], green[1]
            us.append(spec_col[...])
            masks.append(own_mask[...].astype(f32))
        else:
            ref = line[k - 1]
            re, im = ref[0:64, :], ref[64:128, :]
            us.append(
                jnp.concatenate(
                    [ref[160:168, 128 * g : 128 * (g + 1)].astype(f32) for g in range(8)],
                    axis=0,
                )
            )
            masks.append(
                jnp.concatenate(
                    [ref[128:160, 0:512], ref[128:160, 512:1024]], axis=0
                ).astype(f32)
            )
        near_re[rows, :] = re
        near_im[rows, :] = im
        wt_re[rows, :] = (scale * re.astype(f32)).astype(bf16)
        wt_im[rows, :] = (scale * im.astype(f32)).astype(bf16)
    for k in range(len(BOTH)):
        masks[k + 1] = masks[k + 1] + back[ROWS * k : ROWS * (k + 1), :]
    weight = jnp.concatenate(masks, axis=0)
    u_re = jnp.concatenate([u[:, 0:1] for u in us], axis=0)
    u_im = jnp.concatenate([u[:, 1:2] for u in us], axis=0)
    v_re, v_im = far_spec[0:1, :], far_spec[1:2, :]
    g_re, g_im = far_re[...], far_im[...]
    model_re = nt(wt_re[...], g_re) + nt(wt_im[...], g_im)
    model_im = nt(wt_im[...], g_re) - nt(wt_re[...], g_im)
    x_re = (u_re * v_re + u_im * v_im) - model_re
    x_im = (u_im * v_re - u_re * v_im) - model_im
    mis = 0.5 * jnp.sum(weight * (x_re * x_re + x_im * x_im), keepdims=True)
    r_re = (weight * x_re.astype(bf16).astype(f32)).astype(bf16)
    r_im = (weight * x_im.astype(bf16).astype(f32)).astype(bf16)
    y_re = nn(r_re, g_re) - nn(r_im, g_im)
    y_im = nn(r_re, g_im) + nn(r_im, g_re)
    total = jnp.sum(
        near_re[...].astype(f32) * y_re + near_im[...].astype(f32) * y_im,
        axis=0,
        keepdims=True,
    )
    out[0:1, 0:CELLS] = -total
    out[0:1, CELLS : CELLS + 128] = jnp.broadcast_to(mis, (1, 128))


def copy_for_each(array, axis):
    peers = lax.axis_size(axis)
    return lax.all_to_all(
        jnp.broadcast_to(array[None], (peers, *array.shape)), axis, 0, 0, tiled=True
    )


def taken_together(array, axis):
    return copy_for_each(array, axis).sum(axis=0)


def local(spectra, green, source, pair_mask):
    g = green[0]
    here = lax.axis_index("sta")
    place = jnp.stack([here // NQ, here % NQ]).astype(jnp.int32)
    spec_col = spectra[0].astype(jnp.float32).T
    vmem = pl.BlockSpec(memory_space=pltpu.VMEM)
    sent = pl.pallas_call(
        pack,
        out_shape=[jax.ShapeDtypeStruct((168, CELLS), jnp.bfloat16)] * len(OFFSETS)
        + [jax.ShapeDtypeStruct((144, CELLS), jnp.bfloat16)] * (NQ - 1)
        + [
            jax.ShapeDtypeStruct((ROWS, WIDE), jnp.bfloat16),
            jax.ShapeDtypeStruct((ROWS, 4 * ROWS), jnp.bfloat16),
        ],
        in_specs=[pl.BlockSpec(memory_space=pltpu.SMEM), vmem, vmem, vmem],
        out_specs=[vmem] * (len(OFFSETS) + NQ + 1),
        name="pack",
    )(place, g, pair_mask, spec_col)
    line = [
        lax.ppermute(s, "sta", z_shift(u)) for s, u in zip(sent[: len(OFFSETS)], OFFSETS)
    ]
    plane = [
        lax.ppermute(s, "sta", q_shift(a + 1))
        for a, s in enumerate(sent[len(OFFSETS) : len(OFFSETS) + NQ - 1])
    ]
    own_mask, own_back = sent[-2:]
    tall = ROWS * (1 + len(OFFSETS))
    part = pl.pallas_call(
        absorb,
        out_shape=jax.ShapeDtypeStruct((1, CELLS + 128), jnp.float32),
        in_specs=[vmem] * (5 + len(OFFSETS) + NQ - 1),
        out_specs=vmem,
        scratch_shapes=[
            pltpu.VMEM((WIDE, CELLS), jnp.bfloat16),
            pltpu.VMEM((WIDE, CELLS), jnp.bfloat16),
            pltpu.VMEM((8, WIDE), jnp.float32),
            pltpu.VMEM((ROWS * len(BOTH), WIDE), jnp.float32),
            pltpu.VMEM((tall, CELLS), jnp.bfloat16),
            pltpu.VMEM((tall, CELLS), jnp.bfloat16),
            pltpu.VMEM((tall, CELLS), jnp.bfloat16),
            pltpu.VMEM((tall, CELLS), jnp.bfloat16),
        ],
        name="absorb",
    )(source, g, spec_col, own_mask, own_back, *line, *plane)
    total = taken_together(part[0], "sta")
    grad, misfit = total[None, :CELLS], total[CELLS : CELLS + 1]
    total_entries = lax.axis_size("freq") * CELLS
    stations = NZ * NQ * ROWS
    squares = taken_together(jnp.sum(grad * grad), "freq")
    rms = jnp.sqrt(squares / total_entries + 1e-06)
    new_source = source * jnp.exp(-0.5 * grad / rms)
    return (new_source, misfit / (stations * stations))


def solution(mesh):
    placed = (P("freq", None, "sta"), P("freq", None, "sta", None), P("freq", None), P("sta", None))
    return jax.shard_map(
        local, mesh=mesh, in_specs=placed, out_specs=(P("freq", None), P("freq")), check_vma=False
    )
```

time: 414 us -> 120 us (0.29)
  blocking collectives: 173 us -> 24.5 us
  local copies, waits for them, and re-layouts: 68.9 us -> 4.64 us
  waiting for transfers between devices: 85.7 us -> 43.1 us
  matrix products: 25.7 us -> 0 us
  between operations: 17.4 us -> 3.25 us
  Pallas kernels: 0 us -> 9.49 us
  starting transfers between devices: 37.1 us -> 31.1 us
    all_gather x1 -> x0, blocking collectives: 156 us -> none  [local(): lax.all_gather(spectra, 'sta', axis=2, tiled=True)]
    all_gather x1 -> x0, waiting for transfers between devices: 81.2 us -> none  [local(): lax.all_gather(green, 'sta', axis=2, tiled=True)]
    slice x2 -> x1, local copies, waits for them, and re-layouts: 66.7 us -> 0.57 us  [local(): grad, misfit = (total[None, :CELLS], total[CELLS:CELLS + 1])]
    ppermute x0 -> x11, waiting for transfers between devices: none -> 39.2 us  [the longest x4 21.7 us: local(): lax.ppermute(s, 'sta', z_shift(u))]
    all_to_all x1, starting transfers between devices: 37 us -> 8.13 us  [copy_for_each(): lax.all_to_all(jnp.broadcast_to(array[None], (peers, *array.shape)), axis...]
    dot_general x8 -> x0, matrix products: 25.7 us -> none  [the longest x4 19.4 us: contract(): return jnp.einsum('fix,fjx->fij', a, b, preferred_element_type=jnp.float32)]
    ppermute x0 -> x11, starting transfers between devices: none -> 23 us  [the longest x7 13.2 us: local(): lax.ppermute(s, 'sta', q_shift(a + 1))]
    pallas_call x0 -> x2, Pallas kernels: none -> 9.49 us  [the longest x1 5.76 us: local(): pl.pallas_call(absorb, out_shape=jax.ShapeDtypeStruct((1, CELLS + 128), j...]
  transfers between devices with their start and end apart: 2 -> 12, of which waited for: 2 -> 6; matrix products, arithmetic and copies ran while one was open for 17% -> 0% of each run, Pallas kernels for 0% -> 0%
where the time goes in v1:
time: 120 us
  waiting for transfers between devices  43.1 us (36%)
  starting transfers between devices  31.1 us (26%)
  blocking collectives  24.5 us (20%)
  Pallas kernels  9.49 us (8%)
  local copies, waits for them, and re-layouts  4.64 us (4%)
  other arithmetic  3.38 us (3%)
  between operations  3.25 us (3%)
    all_to_all x1, blocking collectives, copy_for_each(): lax.all_to_all(jnp.broadcast_to(array[None], (peers, *array.shape)), axis...  24.5 us
    ppermute x4, waiting for transfers between devices, local(): lax.ppermute(s, 'sta', z_shift(u))  21.7 us
    ppermute x7, waiting for transfers between devices, local(): lax.ppermute(s, 'sta', q_shift(a + 1))  17.6 us
    ppermute x7, starting transfers between devices, local(): lax.ppermute(s, 'sta', q_shift(a + 1))  13.2 us
    ppermute x4, starting transfers between devices, local(): lax.ppermute(s, 'sta', z_shift(u))  9.79 us
    all_to_all x1, starting transfers between devices, copy_for_each(): lax.all_to_all(jnp.broadcast_to(array[None], (peers, *array.shape)), axis...  8.13 us
    pallas_call x1, Pallas kernels, local(): pl.pallas_call(absorb, out_shape=jax.ShapeDtypeStruct((1, CELLS + 128), j...  5.76 us
    all_to_all x1, waiting for transfers between devices, copy_for_each(): lax.all_to_all(jnp.broadcast_to(array[None], (peers, *array.shape)), axis...  3.86 us
  transfers between devices with their start and end apart: 12, of which 6 were waited for; matrix products, arithmetic and copies ran while one was open for 0% of the time, Pallas kernels for 0%

profile of v1, /device:TPU:1, one launch (start us, length us, event | category | flops | bytes accessed | tf_op | source)
XLA Modules:
  0.0 119.5 jit_solution(15711552729182530526)
XLA Ops:
  0.6 0.0 copy-start.12
  0.7 0.6 copy-done.12
  1.3 0.7 copy.8
  2.0 0.7 pad_add_fusion.place
  2.7 3.7 %pack.1 = (bf16[168,1024]{1,0:T(8,128)(2,1)}, bf16[168,1024]{1,0:T(8,128)(2,1)}, bf16[168,1024]{1,0:T(8,128)(2,1)}, bf16[168,1024]{1,0:T(8,128)(2,1)}, bf16[144,...) custom-call(s32[2]{0:T(128)} %pad_add_fusion.place, ...), custom_call_target="tpu_custom_call" | custom-call | tf_op jit(solution)/shard_map/pack/pallas_call | solution.py:190
  6.4 3.6 %collective-permute-start.4 = (bf16[144,1024]{1,0:T(8,128)(2,1)}, bf16[144,1024]{1,0:T(8,128)(2,1)S(1)}, u32[]{:S(2)}, u32[]{:S(2)}) collective-permute-start(bf16[144,1024]{1,0:T(8,128)(2,1)} %get-tuple-element.21), channel_id=1, source_target_pairs={{0,12},{4,0},{8,4},{12,8},{16,28},{20,16},{24,20},{28,24},{32,44},... | collective-permute-start | bytes 884744 | tf_op jit(solution)/shard_map/ppermute | solution.py:206
  10.0 0.3 collective-permute-start.5
  10.3 0.7 collective-permute-start.6
  11.0 1.2 %collective-permute-start.7 = (bf16[144,1024]{1,0:T(8,128)(2,1)}, bf16[144,1024]{1,0:T(8,128)(2,1)S(1)}, u32[]{:S(2)}, u32[]{:S(2)}) collective-permute-start(bf16[144,1024]{1,0:T(8,128)(2,1)} %get-tuple-element.24), channel_id=1, source_target_pairs={{0,16},{4,20},{8,24},{12,28},{16,0},{20,4},{24,8},{28,12},{32,48},... | collective-permute-start | bytes 884744 | tf_op jit(solution)/shard_map/ppermute | solution.py:206
  12.2 2.0 %collective-permute-start.8 = (bf16[144,1024]{1,0:T(8,128)(2,1)}, bf16[144,1024]{1,0:T(8,128)(2,1)S(1)}, u32[]{:S(2)}, u32[]{:S(2)}) collective-permute-start(bf16[144,1024]{1,0:T(8,128)(2,1)} %get-tuple-element.25), channel_id=1, source_target_pairs={{0,28},{4,16},{8,20},{12,24},{16,12},{20,0},{24,4},{28,8},{32,60},... | collective-permute-start | bytes 884744 | tf_op jit(solution)/shard_map/ppermute | solution.py:206
  14.2 12.1 %collective-permute-done.4.rest_4_ = bf16[144,1024]{1,0:T(8,128)(2,1)S(1)} collective-permute-done((bf16[144,1024]{1,0:T(8,128)(2,1)}, bf16[144,1024]{1,0:T(8,128)(2,1)S(1)}, u32[]{:S(2)}, u32[]{:S(2)}) %collective-permute-start.4) | collective-permute-done | bytes 294944 | tf_op jit(solution)/shard_map/ppermute | solution.py:206
  26.2 0.0 copy-start.4
  26.2 0.0 collective-permute-start.9
  26.2 0.0 collective-permute-done.5.rest_5_
  26.2 0.0 copy-start.5
  26.2 0.1 collective-permute-start
  26.3 0.6 collective-permute-done.6.rest_6_
  26.9 0.0 copy-start.6
  26.9 6.0 %collective-permute-start.1 = (bf16[168,1024]{1,0:T(8,128)(2,1)}, bf16[168,1024]{1,0:T(8,128)(2,1)S(1)}, u32[]{:S(2)}, u32[]{:S(2)}) collective-permute-start(bf16[168,1024]{1,0:T(8,128)(2,1)} %get-tuple-element.18), channel_id=1, source_target_pairs={{0,192},{4,196},{8,200},{12,204},{16,208},{20,212},{24,216},{28,22... | collective-permute-start | bytes 1032200 | tf_op jit(solution)/shard_map/ppermute | solution.py:203
  32.9 0.0 collective-permute-done.7.rest_7_
  32.9 0.0 copy-start.7
  33.0 0.0 collective-permute-start.2
  33.0 0.0 collective-permute-done.8.rest_8_
  33.0 0.0 copy-start.8
  33.0 3.7 %collective-permute-start.3 = (bf16[168,1024]{1,0:T(8,128)(2,1)}, bf16[168,1024]{1,0:T(8,128)(2,1)S(1)}, u32[]{:S(2)}, u32[]{:S(2)}) collective-permute-start(bf16[168,1024]{1,0:T(8,128)(2,1)} %get-tuple-element.20), channel_id=1, source_target_pairs={{0,128},{4,132},{8,136},{12,140},{16,144},{20,148},{24,152},{28,15... | collective-permute-start | bytes 1032200 | tf_op jit(solution)/shard_map/ppermute | solution.py:203
  36.7 0.0 collective-permute-done.9.rest_9_
  36.7 0.0 copy-start.9
  36.7 5.4 %collective-permute-start.10 = (bf16[144,1024]{1,0:T(8,128)(2,1)}, bf16[144,1024]{1,0:T(8,128)(2,1)S(1)}, u32[]{:S(2)}, u32[]{:S(2)}) collective-permute-start(bf16[144,1024]{1,0:T(8,128)(2,1)} %get-tuple-element.27), channel_id=1, source_target_pairs={{0,20},{4,24},{8,28},{12,16},{16,4},{20,8},{24,12},{28,0},{32,52},... | collective-permute-start | bytes 884744 | tf_op jit(solution)/shard_map/ppermute | solution.py:206
  42.1 4.9 %collective-permute-done.10.rest_10_ = bf16[144,1024]{1,0:T(8,128)(2,1)S(1)} collective-permute-done((bf16[144,1024]{1,0:T(8,128)(2,1)}, bf16[144,1024]{1,0:T(8,128)(2,1)S(1)}, u32[]{:S(2)}, u32[]{:S(2)}) %collective-permute-start.10) | collective-permute-done | bytes 294944 | tf_op jit(solution)/shard_map/ppermute | solution.py:206
  47.0 0.0 copy-start.10
  47.0 0.0 collective-permute-done.rest_0_
  47.0 0.0 copy-start
  47.0 0.0 collective-permute-done.1.rest_1_
  47.0 0.0 copy-start.1
  47.0 5.7 %collective-permute-done.2.rest_2_ = bf16[168,1024]{1,0:T(8,128)(2,1)S(1)} collective-permute-done((bf16[168,1024]{1,0:T(8,128)(2,1)}, bf16[168,1024]{1,0:T(8,128)(2,1)S(1)}, u32[]{:S(2)}, u32[]{:S(2)}) %collective-permute-start.2) | collective-permute-done | bytes 344096 | tf_op jit(solution)/shard_map/ppermute | solution.py:203
  52.7 0.0 copy-start.2
  52.7 16.0 %collective-permute-done.3.rest_3_ = bf16[168,1024]{1,0:T(8,128)(2,1)S(1)} collective-permute-done((bf16[168,1024]{1,0:T(8,128)(2,1)}, bf16[168,1024]{1,0:T(8,128)(2,1)S(1)}, u32[]{:S(2)}, u32[]{:S(2)}) %collective-permute-start.3) | collective-permute-done | bytes 344096 | tf_op jit(solution)/shard_map/ppermute | solution.py:203
  68.7 0.0 copy-start.3
  68.7 0.0 copy-done.4
  68.7 0.0 copy-done.5
  68.7 0.0 copy-done.6
  68.7 0.0 copy-done.7
  68.7 0.0 copy-done.8
  68.7 0.0 copy-done.9
  68.7 0.0 copy-done.10
  68.7 0.0 copy-done
  68.7 0.0 copy-done.1
  68.8 0.0 copy-done.2
  68.8 0.6 copy-done.3
  69.4 5.8 %absorb.1 = f32[1,1152]{1,0:T(1,128)} custom-call(f32[1,1024]{1,0:T(1,128)} %source.1, bf16[2,64,1024]{2,1,0:T(8,128)(2,1)} %bitcast.9, f32[64,2]{1,0:T(8,128)} %bitcast.11, bf16[64,512]{1,0:T(8,128)(2,1)} %get-tuple-element.15.own_mask, bf16[64,256]{1,0:T(8,128)(2,1)} %get-tuple-element.16.own_back, bf16[168,1024]{1,0:T(8,128)(2,1)} %copy-done, ...), custom_call_target="tpu_custom_call" | custom-call | tf_op jit(solution)/shard_map/absorb/pallas_call | solution.py:211
  75.2 0.7 reduce.4
  75.9 0.2 broadcast_in_dim.4
  76.0 24.5 %all_to_all.12 = f32[64,1,1152]{2,1,0:T(1,128)S(1)} all-to-all(f32[64,1,1152]{2,1,0:T(1,128)S(1)} %broadcast_in_dim.4), channel_id=1, replica_groups=mesh['sta'=64,'freq'=4] {'sta'}, dimensions={0} | all-to-all | bytes 589824 | tf_op jit(solution)/shard_map/all_to_all | solution.py:175
  100.6 0.2 reduce_sum.27
  100.8 0.6 multiply_reduce_fusion
  101.4 0.6 slice.9
  102.0 1.2 %broadcast_in_dim.5 = f32[4,1,1]{2,1,0:T(1,128)} broadcast(f32[]{:T(128)} %multiply_reduce_fusion), dimensions={} | broadcast | bytes 20 | tf_op jit(solution)/shard_map/broadcast_in_dim | solution.py:176
  103.2 8.1 %all-to-all-start.1 = ((f32[4,1,1]{2,1,0:T(1,128)}), f32[4,1,1]{2,1,0:T(1,128)S(1)}, u32[]{:S(2)}, u32[]{:S(2)}) async-start(f32[4,1,1]{2,1,0:T(1,128)} %broadcast_in_dim.5), calls=%async_computation.1 | async-start | bytes 4096 | tf_op jit(solution)/shard_map/all_to_all | solution.py:175
  111.9 3.9 %all-to-all-done.1 = f32[4,1,1]{2,1,0:T(1,128)S(1)} async-done(((f32[4,1,1]{2,1,0:T(1,128)}), f32[4,1,1]{2,1,0:T(1,128)S(1)}, u32[]{:S(2)}, u32[]{:S(2)}) %all-to-all-start.1) | async-done | bytes 48 | tf_op jit(solution)/shard_map/all_to_all | solution.py:175
  115.8 0.6 reduce_sum.29
  117.1 0.0 copy-start.11
  117.1 0.7 copy-done.11
  117.8 0.6 mul.17
  (2 shorter events, 0.0 us)
Async XLA Ops:
  0.6 0.7 copy-start.12
  6.4 19.8 %collective-permute-start.4 = (bf16[144,1024]{1,0:T(8,128)(2,1)}, bf16[144,1024]{1,0:T(8,128)(2,1)S(1)}, u32[]{:S(2)}, u32[]{:S(2)}) collective-permute-start(bf16[144,1024]{1,0:T(8,128)(2,1)} %get-tuple-element.21), channel_id=1, source_target_pairs={{0,12},{4,0},{8,4},{12,8},{16,28},{20,16},{24,20},{28,24},{32,44},... | collective-permute-start | bytes 884744 | tf_op jit(solution)/shard_map/ppermute | solution.py:206
  10.0 16.3 %collective-permute-start.5 = (bf16[144,1024]{1,0:T(8,128)(2,1)}, bf16[144,1024]{1,0:T(8,128)(2,1)S(1)}, u32[]{:S(2)}, u32[]{:S(2)}) collective-permute-start(bf16[144,1024]{1,0:T(8,128)(2,1)} %get-tuple-element.22), channel_id=1, source_target_pairs={{0,8},{4,12},{8,0},{12,4},{16,24},{20,28},{24,16},{28,20},{32,40},... | collective-permute-start | bytes 884744 | tf_op jit(solution)/shard_map/ppermute | solution.py:206
  10.3 16.6 %collective-permute-start.6 = (bf16[144,1024]{1,0:T(8,128)(2,1)}, bf16[144,1024]{1,0:T(8,128)(2,1)S(1)}, u32[]{:S(2)}, u32[]{:S(2)}) collective-permute-start(bf16[144,1024]{1,0:T(8,128)(2,1)} %get-tuple-element.23), channel_id=1, source_target_pairs={{0,4},{4,8},{8,12},{12,0},{16,20},{20,24},{24,28},{28,16},{32,36},... | collective-permute-start | bytes 884744 | tf_op jit(solution)/shard_map/ppermute | solution.py:206
  11.0 21.9 %collective-permute-start.7 = (bf16[144,1024]{1,0:T(8,128)(2,1)}, bf16[144,1024]{1,0:T(8,128)(2,1)S(1)}, u32[]{:S(2)}, u32[]{:S(2)}) collective-permute-start(bf16[144,1024]{1,0:T(8,128)(2,1)} %get-tuple-element.24), channel_id=1, source_target_pairs={{0,16},{4,20},{8,24},{12,28},{16,0},{20,4},{24,8},{28,12},{32,48},... | collective-permute-start | bytes 884744 | tf_op jit(solution)/shard_map/ppermute | solution.py:206
  12.2 20.7 %collective-permute-start.8 = (bf16[144,1024]{1,0:T(8,128)(2,1)}, bf16[144,1024]{1,0:T(8,128)(2,1)S(1)}, u32[]{:S(2)}, u32[]{:S(2)}) collective-permute-start(bf16[144,1024]{1,0:T(8,128)(2,1)} %get-tuple-element.25), channel_id=1, source_target_pairs={{0,28},{4,16},{8,20},{12,24},{16,12},{20,0},{24,4},{28,8},{32,60},... | collective-permute-start | bytes 884744 | tf_op jit(solution)/shard_map/ppermute | solution.py:206
  26.2 42.5 %copy-start.4 = (bf16[144,1024]{1,0:T(8,128)(2,1)}, bf16[144,1024]{1,0:T(8,128)(2,1)S(1)}, u32[]{:S(2)}) copy-start(bf16[144,1024]{1,0:T(8,128)(2,1)S(1)} %collective-permute-done.4.rest_4_) | copy-start | bytes 884740
  26.2 10.4 %collective-permute-start.9 = (bf16[144,1024]{1,0:T(8,128)(2,1)}, bf16[144,1024]{1,0:T(8,128)(2,1)S(1)}, u32[]{:S(2)}, u32[]{:S(2)}) collective-permute-start(bf16[144,1024]{1,0:T(8,128)(2,1)} %get-tuple-element.26), channel_id=1, source_target_pairs={{0,24},{4,28},{8,16},{12,20},{16,8},{20,12},{24,0},{28,4},{32,56},... | collective-permute-start | bytes 884744 | tf_op jit(solution)/shard_map/ppermute | solution.py:206
  26.2 42.5 %copy-start.5 = (bf16[144,1024]{1,0:T(8,128)(2,1)}, bf16[144,1024]{1,0:T(8,128)(2,1)S(1)}, u32[]{:S(2)}) copy-start(bf16[144,1024]{1,0:T(8,128)(2,1)S(1)} %collective-permute-done.5.rest_5_) | copy-start | bytes 884740
  26.2 20.8 %collective-permute-start = (bf16[168,1024]{1,0:T(8,128)(2,1)}, bf16[168,1024]{1,0:T(8,128)(2,1)S(1)}, u32[]{:S(2)}, u32[]{:S(2)}) collective-permute-start(bf16[168,1024]{1,0:T(8,128)(2,1)} %get-tuple-element.17), channel_id=1, source_target_pairs={{0,224},{4,228},{8,232},{12,236},{16,240},{20,244},{24,248},{28,25... | collective-permute-start | bytes 1032200 | tf_op jit(solution)/shard_map/ppermute | solution.py:203
  26.9 41.8 %copy-start.6 = (bf16[144,1024]{1,0:T(8,128)(2,1)}, bf16[144,1024]{1,0:T(8,128)(2,1)S(1)}, u32[]{:S(2)}) copy-start(bf16[144,1024]{1,0:T(8,128)(2,1)S(1)} %collective-permute-done.6.rest_6_) | copy-start | bytes 884740
  26.9 20.1 %collective-permute-start.1 = (bf16[168,1024]{1,0:T(8,128)(2,1)}, bf16[168,1024]{1,0:T(8,128)(2,1)S(1)}, u32[]{:S(2)}, u32[]{:S(2)}) collective-permute-start(bf16[168,1024]{1,0:T(8,128)(2,1)} %get-tuple-element.18), channel_id=1, source_target_pairs={{0,192},{4,196},{8,200},{12,204},{16,208},{20,212},{24,216},{28,22... | collective-permute-start | bytes 1032200 | tf_op jit(solution)/shard_map/ppermute | solution.py:203
  32.9 35.8 %copy-start.7 = (bf16[144,1024]{1,0:T(8,128)(2,1)}, bf16[144,1024]{1,0:T(8,128)(2,1)S(1)}, u32[]{:S(2)}) copy-start(bf16[144,1024]{1,0:T(8,128)(2,1)S(1)} %collective-permute-done.7.rest_7_) | copy-start | bytes 884740
  33.0 19.8 %collective-permute-start.2 = (bf16[168,1024]{1,0:T(8,128)(2,1)}, bf16[168,1024]{1,0:T(8,128)(2,1)S(1)}, u32[]{:S(2)}, u32[]{:S(2)}) collective-permute-start(bf16[168,1024]{1,0:T(8,128)(2,1)} %get-tuple-element.19), channel_id=1, source_target_pairs={{0,96},{4,100},{8,104},{12,108},{16,112},{20,116},{24,120},{28,124... | collective-permute-start | bytes 1032200 | tf_op jit(solution)/shard_map/ppermute | solution.py:203
  33.0 35.7 %copy-start.8 = (bf16[144,1024]{1,0:T(8,128)(2,1)}, bf16[144,1024]{1,0:T(8,128)(2,1)S(1)}, u32[]{:S(2)}) copy-start(bf16[144,1024]{1,0:T(8,128)(2,1)S(1)} %collective-permute-done.8.rest_8_) | copy-start | bytes 884740
  33.0 35.7 %collective-permute-start.3 = (bf16[168,1024]{1,0:T(8,128)(2,1)}, bf16[168,1024]{1,0:T(8,128)(2,1)S(1)}, u32[]{:S(2)}, u32[]{:S(2)}) collective-permute-start(bf16[168,1024]{1,0:T(8,128)(2,1)} %get-tuple-element.20), channel_id=1, source_target_pairs={{0,128},{4,132},{8,136},{12,140},{16,144},{20,148},{24,152},{28,15... | collective-permute-start | bytes 1032200 | tf_op jit(solution)/shard_map/ppermute | solution.py:203
  36.7 32.1 %copy-start.9 = (bf16[144,1024]{1,0:T(8,128)(2,1)}, bf16[144,1024]{1,0:T(8,128)(2,1)S(1)}, u32[]{:S(2)}) copy-start(bf16[144,1024]{1,0:T(8,128)(2,1)S(1)} %collective-permute-done.9.rest_9_) | copy-start | bytes 884740
  36.7 10.3 %collective-permute-start.10 = (bf16[144,1024]{1,0:T(8,128)(2,1)}, bf16[144,1024]{1,0:T(8,128)(2,1)S(1)}, u32[]{:S(2)}, u32[]{:S(2)}) collective-permute-start(bf16[144,1024]{1,0:T(8,128)(2,1)} %get-tuple-element.27), channel_id=1, source_target_pairs={{0,20},{4,24},{8,28},{12,16},{16,4},{20,8},{24,12},{28,0},{32,52},... | collective-permute-start | bytes 884744 | tf_op jit(solution)/shard_map/ppermute | solution.py:206
  47.0 21.7 %copy-start.10 = (bf16[144,1024]{1,0:T(8,128)(2,1)}, bf16[144,1024]{1,0:T(8,128)(2,1)S(1)}, u32[]{:S(2)}) copy-start(bf16[144,1024]{1,0:T(8,128)(2,1)S(1)} %collective-permute-done.10.rest_10_) | copy-start | bytes 884740
  47.0 21.7 %copy-start = (bf16[168,1024]{1,0:T(8,128)(2,1)}, bf16[168,1024]{1,0:T(8,128)(2,1)S(1)}, u32[]{:S(2)}) copy-start(bf16[168,1024]{1,0:T(8,128)(2,1)S(1)} %collective-permute-done.rest_0_) | copy-start | bytes 1032196
  47.0 21.7 %copy-start.1 = (bf16[168,1024]{1,0:T(8,128)(2,1)}, bf16[168,1024]{1,0:T(8,128)(2,1)S(1)}, u32[]{:S(2)}) copy-start(bf16[168,1024]{1,0:T(8,128)(2,1)S(1)} %collective-permute-done.1.rest_1_) | copy-start | bytes 1032196
  52.7 16.0 %copy-start.2 = (bf16[168,1024]{1,0:T(8,128)(2,1)}, bf16[168,1024]{1,0:T(8,128)(2,1)S(1)}, u32[]{:S(2)}) copy-start(bf16[168,1024]{1,0:T(8,128)(2,1)S(1)} %collective-permute-done.2.rest_2_) | copy-start | bytes 1032196
  68.7 0.7 copy-start.3
  103.2 12.6 %all-to-all-start.1 = ((f32[4,1,1]{2,1,0:T(1,128)}), f32[4,1,1]{2,1,0:T(1,128)S(1)}, u32[]{:S(2)}, u32[]{:S(2)}) async-start(f32[4,1,1]{2,1,0:T(1,128)} %broadcast_in_dim.5), calls=%async_computation.1 | async-start | bytes 4096 | tf_op jit(solution)/shard_map/all_to_all | solution.py:175
  117.1 0.7 copy-start.11

commit v2 on v1

v2 whole, which is shorter than its diff:
```python
import jax
import jax.numpy as jnp
from jax import lax
from jax.experimental import pallas as pl
from jax.experimental.pallas import tpu as pltpu
from jax.sharding import Mesh, PartitionSpec as P

NZ, NX, NY = 8, 2, 4
NQ = NX * NY
NF = 4
ROWS = 64
CELLS = 1024
WIDE = NQ * ROWS
PLANE = ("xl", "y")
FREQ = ("xh", "core")
STA = ("z",) + PLANE
BOTH = (1, 2, -3)
OFFSETS = (1, 2, -3, 4)
MASKED, PLAIN, SHARED = 168, 136, 152
LONG = CELLS + 128
f32, bf16 = jnp.float32, jnp.bfloat16


def nt(a, b):
    return lax.dot_general(
        a, b, (((1,), (1,)), ((), ())), preferred_element_type=f32
    )


def nn(a, b):
    return lax.dot_general(
        a, b, (((1,), (0,)), ((), ())), preferred_element_type=f32
    )


def identity(n):
    down = lax.broadcasted_iota(jnp.int32, (n, n), 0)
    across = lax.broadcasted_iota(jnp.int32, (n, n), 1)
    return (down == across).astype(f32).astype(bf16)


def pack(green, mask, spec_row, *outs):
    line = outs[: len(OFFSETS)]
    shared, own_mask, own_spec = outs[len(OFFSETS) :]
    z = lax.axis_index("z")

    def window(at):
        start = pl.multiple_of(lax.rem(at + NZ, NZ) * WIDE, WIDE)
        return mask[:, pl.ds(start, WIDE)].astype(f32)

    row = spec_row[...]
    col = nt(identity(ROWS), row)
    lane = lax.broadcasted_iota(jnp.int32, (ROWS, 128), 1)
    own_spec[...] = jnp.where(
        lane == 0, col[:, 0:1], jnp.where(lane == 1, col[:, 1:2], 0.0)
    )
    own_spec[0:2, 64:128] = row.astype(f32)
    spectra = own_spec[...].astype(bf16)

    def put(ref, at):
        for g in range(8):
            ref[at : at + 8, 128 * g : 128 * (g + 1)] = spectra[8 * g : 8 * (g + 1)]

    own_mask[...] = window(z).astype(bf16)
    for k, (u, ref) in enumerate(zip(OFFSETS, line)):
        ref[0:64, :] = green[0]
        ref[64:128, :] = green[1]
        if u in BOTH:
            part = window(z - u).astype(bf16)
            ref[128:160, 0:512] = part[0:32]
            ref[128:160, 512:1024] = part[32:64]
            put(ref, 160)
        else:
            put(ref, 128)
    wide = [window(z + u) for u in OFFSETS]
    for q in range(NQ):
        ref = shared.at[q]
        ref[0:64, :] = green[0]
        ref[64:128, :] = green[1]
        part = jnp.concatenate(
            [w[:, ROWS * q : ROWS * (q + 1)] for w in wide], axis=1
        ).astype(bf16)
        for g in range(4):
            ref[128:144, 256 * g : 256 * (g + 1)] = part[16 * g : 16 * (g + 1)]
        put(ref, 144)


def absorb(source, green, own_mask, own_spec, shared, *rest):
    line = rest[: len(OFFSETS)]
    out, far_re, far_im, far_spec, back, near_re, near_im, wt_re, wt_im = rest[
        len(OFFSETS) :
    ]
    scale = source[...]
    for q in range(NQ):
        rows = slice(ROWS * q, ROWS * (q + 1))
        ref = shared.at[q]
        far_re[rows, :] = ref[0:64, :]
        far_im[rows, :] = ref[64:128, :]
        for g in range(4):
            back[ROWS * q + 16 * g : ROWS * q + 16 * (g + 1), :] = ref[
                128:144, 256 * g : 256 * (g + 1)
            ]
        far_spec[0:2, rows] = ref[144:152, 0:128].astype(f32)[0:2, 64:128]
    behind = nt(identity(4 * ROWS), back[...])
    us, masks = [], []
    for k in range(1 + len(OFFSETS)):
        rows = slice(ROWS * k, ROWS * (k + 1))
        opposite = behind[ROWS * (k - 1) : ROWS * k] if k else None
        if k == 0:
            re, im = green[0], green[1]
            us.append(own_spec[...])
            masks.append(own_mask[...].astype(f32))
        else:
            ref = line[k - 1]
            re, im = ref[0:64, :], ref[64:128, :]
            at = 128
            if OFFSETS[k - 1] in BOTH:
                at = 160
                opposite = opposite + jnp.concatenate(
                    [ref[128:160, 0:512], ref[128:160, 512:1024]], axis=0
                ).astype(f32)
            us.append(
                jnp.concatenate(
                    [
                        ref[at : at + 8, 128 * g : 128 * (g + 1)].astype(f32)
                        for g in range(8)
                    ],
                    axis=0,
                )
            )
            masks.append(opposite)
        near_re[rows, :] = re
        near_im[rows, :] = im
        wt_re[rows, :] = (scale * re.astype(f32)).astype(bf16)
        wt_im[rows, :] = (scale * im.astype(f32)).astype(bf16)
    weight = jnp.concatenate(masks, axis=0)
    u_re = jnp.concatenate([u[:, 0:1] for u in us], axis=0)
    u_im = jnp.concatenate([u[:, 1:2] for u in us], axis=0)
    v_re, v_im = far_spec[0:1, :], far_spec[1:2, :]
    g_re, g_im = far_re[...], far_im[...]
    model_re = nt(wt_re[...], g_re) + nt(wt_im[...], g_im)
    model_im = nt(wt_im[...], g_re) - nt(wt_re[...], g_im)
    x_re = (u_re * v_re + u_im * v_im) - model_re
    x_im = (u_im * v_re - u_re * v_im) - model_im
    mis = 0.5 * jnp.sum(weight * (x_re * x_re + x_im * x_im), keepdims=True)
    r_re = (weight * x_re.astype(bf16).astype(f32)).astype(bf16)
    r_im = (weight * x_im.astype(bf16).astype(f32)).astype(bf16)
    y_re = nn(r_re, g_re) - nn(r_im, g_im)
    y_im = nn(r_re, g_im) + nn(r_im, g_re)
    total = jnp.sum(
        near_re[...].astype(f32) * y_re + near_im[...].astype(f32) * y_im,
        axis=0,
        keepdims=True,
    )
    out[:, 0:CELLS] = jnp.broadcast_to(-total, (NZ, CELLS))
    out[:, CELLS:LONG] = jnp.broadcast_to(mis, (NZ, 128))


def gather_z(parts, out):
    out[...] = jnp.broadcast_to(
        jnp.sum(parts[...], axis=0, keepdims=True), out.shape
    )


def finish(parts, source, new_source, misfit):
    mine = lax.axis_index("xh") * 2 + lax.axis_index("core")
    by_freq = jnp.sum(parts[...].reshape(NQ, NF, LONG), axis=0)
    grads = by_freq[:, 0:CELLS]
    rms = jnp.sqrt(jnp.sum(grads * grads, keepdims=True) / (NF * CELLS) + 1e-06)
    rows = lax.broadcasted_iota(jnp.int32, (NF, LONG), 0)
    own = jnp.sum(jnp.where(rows == mine, by_freq, 0.0), axis=0, keepdims=True)
    new_source[...] = source[...] * jnp.exp(-0.5 * own[:, 0:CELLS] / rms)
    stations = NZ * NQ * ROWS
    misfit[0] = jnp.max(own[:, CELLS:LONG]) / (stations * stations)


def local(spectra, green, source, pair_mask):
    g = green[0]
    vmem = pl.BlockSpec(memory_space=pltpu.VMEM)
    tall = ROWS * (1 + len(OFFSETS))
    *sent, shared, own_mask, own_spec = pl.pallas_call(
        pack,
        out_shape=[
            jax.ShapeDtypeStruct((MASKED if u in BOTH else PLAIN, CELLS), bf16)
            for u in OFFSETS
        ]
        + [
            jax.ShapeDtypeStruct((NQ, SHARED, CELLS), bf16),
            jax.ShapeDtypeStruct((ROWS, WIDE), bf16),
            jax.ShapeDtypeStruct((ROWS, 128), f32),
        ],
        in_specs=[vmem] * 3,
        out_specs=[vmem] * (len(OFFSETS) + 3),
        name="pack",
    )(g, pair_mask, spectra[0])
    line = [
        lax.ppermute(s, "z", [(z, (z - u) % NZ) for z in range(NZ)])
        for s, u in zip(sent, OFFSETS)
    ]
    shared = lax.all_to_all(shared, PLANE, 0, 0, tiled=True)
    part = pl.pallas_call(
        absorb,
        out_shape=jax.ShapeDtypeStruct((NZ, LONG), f32),
        in_specs=[vmem] * (5 + len(OFFSETS)),
        out_specs=vmem,
        scratch_shapes=[
            pltpu.VMEM((WIDE, CELLS), bf16),
            pltpu.VMEM((WIDE, CELLS), bf16),
            pltpu.VMEM((8, WIDE), f32),
            pltpu.VMEM((WIDE, 4 * ROWS), bf16),
            pltpu.VMEM((tall, CELLS), bf16),
            pltpu.VMEM((tall, CELLS), bf16),
            pltpu.VMEM((tall, CELLS), bf16),
            pltpu.VMEM((tall, CELLS), bf16),
        ],
        name="absorb",
    )(source, g, own_mask, own_spec, shared, *line)
    part = lax.all_to_all(part, "z", 0, 0, tiled=True)
    part = pl.pallas_call(
        gather_z,
        out_shape=jax.ShapeDtypeStruct((NQ * NF, LONG), f32),
        in_specs=[vmem],
        out_specs=vmem,
        name="gather_z",
    )(part)
    part = lax.all_to_all(part, PLANE + FREQ, 0, 0, tiled=True)
    return pl.pallas_call(
        finish,
        out_shape=(
            jax.ShapeDtypeStruct((1, CELLS), f32),
            jax.ShapeDtypeStruct((1,), f32),
        ),
        in_specs=[vmem, vmem],
        out_specs=(vmem, pl.BlockSpec(memory_space=pltpu.SMEM)),
        name="finish",
    )(part, source)


def solution(mesh):
    fine = Mesh(mesh.devices.reshape(NZ, NX, NY, 2, 2), STA + FREQ)
    placed = (P(FREQ, None, STA), P(FREQ, None, STA, None), P(FREQ, None), P(STA, None))
    return jax.shard_map(
        local, mesh=fine, in_specs=placed, out_specs=(P(FREQ, None), P(FREQ)), check_vma=False
    )
```

time: 120 us -> 97.3 us (0.81)
  starting transfers between devices: 31.1 us -> 16.4 us
  waiting for transfers between devices: 43.1 us -> 28.5 us
  blocking collectives: 24.5 us -> 33.4 us
  other arithmetic: 3.38 us -> 0 us
  Pallas kernels: 9.49 us -> 12.7 us
  between operations: 3.25 us -> 0.66 us
    ppermute x11 -> x4, starting transfers between devices: 23 us -> 10.5 us  [local(): lax.ppermute(s, 'z', [(z, (z - u) % NZ) for z in range(NZ)])]
    ppermute x11 -> x4, waiting for transfers between devices: 39.2 us -> 28.5 us  [local(): lax.ppermute(s, 'z', [(z, (z - u) % NZ) for z in range(NZ)])]
    all_to_all x1 -> x2, blocking collectives: 24.5 us -> 33.4 us  [the longest x1 16.9 us: local(): part = lax.all_to_all(part, PLANE + FREQ, 0, 0, tiled=True)]
    all_to_all x1, waiting for transfers between devices: 3.86 us -> 0.01 us  [local(): shared = lax.all_to_all(shared, PLANE, 0, 0, tiled=True)]
    pallas_call x2 -> x4, Pallas kernels: 9.49 us -> 12.7 us  [the longest x1 6.02 us: local(): pl.pallas_call(absorb, out_shape=jax.ShapeDtypeStruct((NZ, LONG), f32), i...]
    all_to_all x1, starting transfers between devices: 8.13 us -> 5.95 us  [local(): shared = lax.all_to_all(shared, PLANE, 0, 0, tiled=True)]
    all_to_all x0 -> x2, local copies, waits for them, and re-layouts: none -> 1.87 us  [the longest x1 1.06 us: local(): part = lax.all_to_all(part, PLANE + FREQ, 0, 0, tiled=True)]
    reduce_sum x3 -> x0, other arithmetic: 1.4 us -> none  [the longest x2 0.8 us: taken_together(): return copy_for_each(array, axis).sum(axis=0)]
  transfers between devices with their start and end apart: 12 -> 5, of which waited for: 6 -> 2; matrix products, arithmetic and copies ran while one was open for 0% -> 0% of each run, Pallas kernels for 0% -> 0%
where the time goes in v2:
time: 97.3 us; the launch traced here: 96.9 us
  blocking collectives  33.4 us (34%)
  waiting for transfers between devices  28.5 us (29%)
  starting transfers between devices  16.4 us (17%)
  Pallas kernels  12.7 us (13%)
  local copies, waits for them, and re-layouts  5.27 us (5%)
    ppermute x4, waiting for transfers between devices, local(): lax.ppermute(s, 'z', [(z, (z - u) % NZ) for z in range(NZ)])  28.5 us
    all_to_all x1, blocking collectives, local(): part = lax.all_to_all(part, PLANE + FREQ, 0, 0, tiled=True)  16.9 us
    all_to_all x1, blocking collectives, local(): part = lax.all_to_all(part, 'z', 0, 0, tiled=True)  16.5 us
    ppermute x4, starting transfers between devices, local(): lax.ppermute(s, 'z', [(z, (z - u) % NZ) for z in range(NZ)])  10.5 us
    pallas_call x1, Pallas kernels, local(): pl.pallas_call(absorb, out_shape=jax.ShapeDtypeStruct((NZ, LONG), f32), i...  6.02 us
    all_to_all x1, starting transfers between devices, local(): shared = lax.all_to_all(shared, PLANE, 0, 0, tiled=True)  5.95 us
    pallas_call x1, Pallas kernels, local(): pl.pallas_call(pack, out_shape=[jax.ShapeDtypeStruct((MASKED if u in BOTH...  3.51 us
    unnamed x12, local copies, waits for them, and re-layouts  3.4 us
  transfers between devices with their start and end apart: 5, of which 2 were waited for; matrix products, arithmetic and copies ran while one was open for 0% of the time, Pallas kernels for 0%

profile of v2, /device:TPU:1, one launch (start us, length us, event | category | flops | bytes accessed | tf_op | source)
XLA Modules:
  0.0 96.9 jit_solution(9760156775214932745)
XLA Ops:
  0.6 3.5 %pack.1 = (bf16[168,1024]{1,0:T(8,128)(2,1)}, bf16[168,1024]{1,0:T(8,128)(2,1)}, bf16[168,1024]{1,0:T(8,128)(2,1)}, bf16[136,1024]{1,0:T(8,128)(2,1)}, bf16[8,15...) custom-call(bf16[2,64,1024]{2,1,0:T(8,128)(2,1)} %bitcast.10, s32[64,4096]{1,0:T(8,128)} %mask.1, ...), custom_call_target="tpu_custom_call" | custom-call | tf_op jit(solution)/shard_map/pack/pallas_call | solution.py:181
  4.1 5.9 %all-to-all-start = ((bf16[8,152,1024]{2,1,0:T(8,128)(2,1)}), bf16[8,152,1024]{2,1,0:T(8,128)(2,1)S(1)}, u32[]{:S(2)}, u32[]{:S(2)}) async-start(bf16[8,152,1024]{2,1,0:T(8,128)(2,1)} %get-tuple-element.11), calls=%async_computation | async-start | bytes 4980736 | tf_op jit(solution)/shard_map/all_to_all | solution.py:200
  10.1 5.6 %collective-permute-start = (bf16[168,1024]{1,0:T(8,128)(2,1)}, bf16[168,1024]{1,0:T(8,128)(2,1)S(1)}, u32[]{:S(2)}, u32[]{:S(2)}) collective-permute-start(bf16[168,1024]{1,0:T(8,128)(2,1)} %get-tuple-element.12), channel_id=1, source_target_pairs={{0,224},{32,0},{64,32},{96,64},{128,96},{160,128},{192,160},{224,1... | collective-permute-start | bytes 1032200 | tf_op jit(solution)/shard_map/ppermute | solution.py:197
  15.7 1.2 %collective-permute-start.1 = (bf16[168,1024]{1,0:T(8,128)(2,1)}, bf16[168,1024]{1,0:T(8,128)(2,1)S(1)}, u32[]{:S(2)}, u32[]{:S(2)}) collective-permute-start(bf16[168,1024]{1,0:T(8,128)(2,1)} %get-tuple-element.13), channel_id=1, source_target_pairs={{0,192},{32,224},{64,0},{96,32},{128,64},{160,96},{192,128},{224,1... | collective-permute-start | bytes 1032200 | tf_op jit(solution)/shard_map/ppermute | solution.py:197
  16.8 0.0 collective-permute-start.2
  16.8 3.7 %collective-permute-start.3 = (bf16[136,1024]{1,0:T(8,128)(2,1)}, bf16[136,1024]{1,0:T(8,128)(2,1)S(1)}, u32[]{:S(2)}, u32[]{:S(2)}) collective-permute-start(bf16[136,1024]{1,0:T(8,128)(2,1)} %get-tuple-element.15), channel_id=1, source_target_pairs={{0,128},{32,160},{64,192},{96,224},{128,0},{160,32},{192,64},{224,... | collective-permute-start | bytes 835592 | tf_op jit(solution)/shard_map/ppermute | solution.py:197
  20.5 28.3 %collective-permute-done.3.rest_3_ = bf16[136,1024]{1,0:T(8,128)(2,1)S(1)} collective-permute-done((bf16[136,1024]{1,0:T(8,128)(2,1)}, bf16[136,1024]{1,0:T(8,128)(2,1)S(1)}, u32[]{:S(2)}, u32[]{:S(2)}) %collective-permute-start.3) | collective-permute-done | bytes 278560 | tf_op jit(solution)/shard_map/ppermute | solution.py:197
  48.8 0.0 copy-start.4
  48.8 0.0 collective-permute-done.rest_0_
  48.9 0.0 copy-start.1
  48.9 0.2 collective-permute-done.1.rest_1_
  49.1 0.5 copy-done.4
  49.6 0.0 copy-start.2
  49.6 0.0 collective-permute-done.2.rest_2_
  49.6 0.0 copy-start.3
  49.6 0.0 all-to-all-done.shared
  49.6 0.0 copy-start
  49.6 0.1 copy-done.1
  49.7 0.6 copy-done.2
  50.3 0.1 copy-done.3
  50.4 0.8 copy-done
  51.2 6.0 %absorb.1 = f32[8,1152]{1,0:T(8,128)} custom-call(f32[1,1024]{1,0:T(1,128)} %source.3, bf16[2,64,1024]{2,1,0:T(8,128)(2,1)} %bitcast.11, bf16[64,512]{1,0:T(8,128)(2,1)} %get-tuple-element.9.own_mask, f32[64,128]{1,0:T(8,128)} %get-tuple-element.10.own_spec, bf16[8,152,1024]{2,1,0:T(8,128)(2,1)} %copy-done, bf16[168,1024]{1,0:T(8,128)(2,1)} %copy-done.1, ...), custom_call_target="tpu_custom_call" | custom-call | tf_op jit(solution)/shard_map/absorb/pallas_call | solution.py:201
  57.2 0.8 copy.6
  58.1 16.5 %all_to_all.27 = f32[8,1,1152]{2,1,0:T(1,128)S(1)} all-to-all(f32[8,1,1152]{2,1,0:T(1,128)S(1)} %copy.6), channel_id=1, replica_groups=mesh['z'=8,'xl'=2,'y'=4,'xh'=2,'core'=2] {'z'}, dimensions={0} | all-to-all | bytes 73728 | tf_op jit(solution)/shard_map/all_to_all | solution.py:218
  74.6 0.6 copy.13
  75.2 1.4 %gather_z.1 = f32[32,1152]{1,0:T(8,128)} custom-call(f32[8,1152]{1,0:T(8,128)} %bitcast.14), custom_call_target="tpu_custom_call" | custom-call | tf_op jit(solution)/shard_map/gather_z/pallas_call | solution.py:219
  76.6 1.1 %copy.7 = f32[32,1,1152]{2,1,0:T(1,128)S(1)} copy(f32[32,1,1152]{2,0,1:T(8,128)} %bitcast.13) | data formatting | bytes 294912 | tf_op jit(solution)/shard_map/all_to_all | solution.py:226
  77.7 16.9 %all_to_all.28 = f32[32,1,1152]{2,1,0:T(1,128)S(1)} all-to-all(f32[32,1,1152]{2,1,0:T(1,128)S(1)} %copy.7), channel_id=1, replica_groups=mesh['z'=8,'xl'=2,'y'=4,'xh'=2,'core'=2] {'xl','y','xh','core'}, dimensions={0} | all-to-all | bytes 294912 | tf_op jit(solution)/shard_map/all_to_all | solution.py:226
  94.6 0.7 copy.12
  95.2 1.7 %finish.1 = (f32[1,1024]{1,0:T(1,128)}, f32[1]{0:T(128)}) custom-call(f32[32,1152]{1,0:T(8,128)} %bitcast.12, f32[1,1024]{1,0:T(1,128)} %source.3), custom_call_target="tpu_custom_call" | custom-call | tf_op jit(solution)/shard_map/finish/pallas_call | solution.py:227
Async XLA Ops:
  4.1 45.4 %all-to-all-start = ((bf16[8,152,1024]{2,1,0:T(8,128)(2,1)}), bf16[8,152,1024]{2,1,0:T(8,128)(2,1)S(1)}, u32[]{:S(2)}, u32[]{:S(2)}) async-start(bf16[8,152,1024]{2,1,0:T(8,128)(2,1)} %get-tuple-element.11), calls=%async_computation | async-start | bytes 4980736 | tf_op jit(solution)/shard_map/all_to_all | solution.py:200
  10.1 38.8 %collective-permute-start = (bf16[168,1024]{1,0:T(8,128)(2,1)}, bf16[168,1024]{1,0:T(8,128)(2,1)S(1)}, u32[]{:S(2)}, u32[]{:S(2)}) collective-permute-start(bf16[168,1024]{1,0:T(8,128)(2,1)} %get-tuple-element.12), channel_id=1, source_target_pairs={{0,224},{32,0},{64,32},{96,64},{128,96},{160,128},{192,160},{224,1... | collective-permute-start | bytes 1032200 | tf_op jit(solution)/shard_map/ppermute | solution.py:197
  15.7 33.4 %collective-permute-start.1 = (bf16[168,1024]{1,0:T(8,128)(2,1)}, bf16[168,1024]{1,0:T(8,128)(2,1)S(1)}, u32[]{:S(2)}, u32[]{:S(2)}) collective-permute-start(bf16[168,1024]{1,0:T(8,128)(2,1)} %get-tuple-element.13), channel_id=1, source_target_pairs={{0,192},{32,224},{64,0},{96,32},{128,64},{160,96},{192,128},{224,1... | collective-permute-start | bytes 1032200 | tf_op jit(solution)/shard_map/ppermute | solution.py:197
  16.8 32.7 %collective-permute-start.2 = (bf16[168,1024]{1,0:T(8,128)(2,1)}, bf16[168,1024]{1,0:T(8,128)(2,1)S(1)}, u32[]{:S(2)}, u32[]{:S(2)}) collective-permute-start(bf16[168,1024]{1,0:T(8,128)(2,1)} %get-tuple-element.14), channel_id=1, source_target_pairs={{0,96},{32,128},{64,160},{96,192},{128,224},{160,0},{192,32},{224,... | collective-permute-start | bytes 1032200 | tf_op jit(solution)/shard_map/ppermute | solution.py:197
  16.8 32.0 %collective-permute-start.3 = (bf16[136,1024]{1,0:T(8,128)(2,1)}, bf16[136,1024]{1,0:T(8,128)(2,1)S(1)}, u32[]{:S(2)}, u32[]{:S(2)}) collective-permute-start(bf16[136,1024]{1,0:T(8,128)(2,1)} %get-tuple-element.15), channel_id=1, source_target_pairs={{0,128},{32,160},{64,192},{96,224},{128,0},{160,32},{192,64},{224,... | collective-permute-start | bytes 835592 | tf_op jit(solution)/shard_map/ppermute | solution.py:197
  48.8 0.7 copy-start.4
  48.9 0.8 copy-start.1
  49.6 0.7 copy-start.2
  49.6 0.8 copy-start.3
  49.6 1.7 %copy-start = (bf16[8,152,1024]{2,1,0:T(8,128)(2,1)}, bf16[8,152,1024]{2,1,0:T(8,128)(2,1)S(1)}, u32[]{:S(2)}) copy-start(bf16[8,152,1024]{2,1,0:T(8,128)(2,1)S(1)} %all-to-all-done.shared) | copy-start | bytes 7471108

commit v3 on v2

v3 whole, which is shorter than its diff:
```python
import jax
import jax.numpy as jnp
from jax import lax
from jax.experimental import pallas as pl
from jax.experimental.pallas import tpu as pltpu
from jax.sharding import Mesh, PartitionSpec as P

NZ, NX, NY = 8, 2, 4
NQ = NX * NY
NF = 4
ROWS = 64
CELLS = 1024
WIDE = NQ * ROWS
PLANE = ("xl", "y")
FREQ = ("xh", "core")
STA = ("z",) + PLANE
OFFSETS = (1, 2, -3, 4)
SHARED = 152
TILES = CELLS // 128
f32, bf16 = jnp.float32, jnp.bfloat16


def nt(a, b):
    return lax.dot_general(
        a, b, (((1,), (1,)), ((), ())), preferred_element_type=f32
    )


def nn(a, b):
    return lax.dot_general(
        a, b, (((1,), (0,)), ((), ())), preferred_element_type=f32
    )


def identity(n):
    down = lax.broadcasted_iota(jnp.int32, (n, n), 0)
    across = lax.broadcasted_iota(jnp.int32, (n, n), 1)
    return (down == across).astype(f32).astype(bf16)


SPEC, IMAG, REAL, MASK, MASKED = 0, 8, 72, 136, 168


def window(mask, at):
    start = pl.multiple_of(lax.rem(at + NZ, NZ) * WIDE, WIDE)
    return mask[:, pl.ds(start, WIDE)].astype(f32)


def put_mask(ref, at, part):
    ref[at : at + 32, 0:512] = part[0:32]
    ref[at : at + 32, 512:1024] = part[32:64]


def take_mask(ref, at):
    return jnp.concatenate(
        [ref[at : at + 32, 0:512], ref[at : at + 32, 512:1024]], axis=0
    ).astype(f32)


def put_spectra(ref, at, spectra):
    for g in range(8):
        ref[at : at + 8, 128 * g : 128 * (g + 1)] = spectra[8 * g : 8 * (g + 1)]


def take_spectra(ref, at):
    return jnp.concatenate(
        [ref[at : at + 8, 128 * g : 128 * (g + 1)].astype(f32) for g in range(8)],
        axis=0,
    )


def pack_line(green, mask, spec_row, near, far, two, own_mask, own_spec):
    z = lax.axis_index("z")
    row = spec_row[...]
    col = nt(identity(ROWS), row)
    lane = lax.broadcasted_iota(jnp.int32, (ROWS, 128), 1)
    own_spec[...] = jnp.where(
        lane == 0, col[:, 0:1], jnp.where(lane == 1, col[:, 1:2], 0.0)
    )
    own_spec[0:2, 64:128] = row.astype(f32)
    spectra = own_spec[...].astype(bf16)
    for ref, u in ((near, 1), (far, -3)):
        put_spectra(ref, SPEC, spectra)
        ref[IMAG : IMAG + ROWS, :] = green[1]
        ref[REAL : REAL + ROWS, :] = green[0]
        put_mask(ref, MASK, window(mask, z - u).astype(bf16))
    put_mask(two, 0, window(mask, z - 2).astype(bf16))
    own_mask[...] = window(mask, z).astype(bf16)


def pack_plane(green, mask, own_spec, shared):
    z = lax.axis_index("z")
    spectra = own_spec[...].astype(bf16)
    wide = [window(mask, z + u) for u in OFFSETS]
    for q in range(NQ):
        ref = shared.at[q]
        ref[0:64, :] = green[0]
        ref[64:128, :] = green[1]
        part = jnp.concatenate(
            [w[:, ROWS * q : ROWS * (q + 1)] for w in wide], axis=1
        ).astype(bf16)
        for g in range(4):
            ref[128:144, 256 * g : 256 * (g + 1)] = part[16 * g : 16 * (g + 1)]
        put_spectra(ref, 144, spectra)


def absorb(
    source, green, own_mask, own_spec, shared, one, two, two_mask, three, four_re, four_im,
    out, far_re, far_im, far_spec, back, near_re, near_im, wt_re, wt_im
):
    scale = source[...]
    for q in range(NQ):
        rows = slice(ROWS * q, ROWS * (q + 1))
        ref = shared.at[q]
        far_re[rows, :] = ref[0:64, :]
        far_im[rows, :] = ref[64:128, :]
        for g in range(4):
            back[ROWS * q + 16 * g : ROWS * q + 16 * (g + 1), :] = ref[
                128:144, 256 * g : 256 * (g + 1)
            ]
        far_spec[0:2, rows] = ref[144:152, 0:128].astype(f32)[0:2, 64:128]
    behind = nt(identity(4 * ROWS), back[...])
    us = [
        own_spec[...],
        take_spectra(one, SPEC),
        take_spectra(two, SPEC),
        take_spectra(three, SPEC),
        take_spectra(four_im, SPEC),
    ]
    weight = jnp.concatenate(
        [
            own_mask[...].astype(f32),
            take_mask(one, MASK) + behind[0:ROWS],
            take_mask(two_mask, 0) + behind[ROWS : 2 * ROWS],
            take_mask(three, MASK) + behind[2 * ROWS : 3 * ROWS],
            behind[3 * ROWS : 4 * ROWS],
        ],
        axis=0,
    )
    real, imag = slice(REAL, REAL + ROWS), slice(IMAG, IMAG + ROWS)
    held = [
        (green[0], green[1]),
        (one[real, :], one[imag, :]),
        (two[real, :], two[imag, :]),
        (three[real, :], three[imag, :]),
        (four_re[...], four_im[imag, :]),
    ]
    for k, (re, im) in enumerate(held):
        rows = slice(ROWS * k, ROWS * (k + 1))
        near_re[rows, :] = re
        near_im[rows, :] = im
        wt_re[rows, :] = (scale * re.astype(f32)).astype(bf16)
        wt_im[rows, :] = (scale * im.astype(f32)).astype(bf16)
    u_re = jnp.concatenate([u[:, 0:1] for u in us], axis=0)
    u_im = jnp.concatenate([u[:, 1:2] for u in us], axis=0)
    v_re, v_im = far_spec[0:1, :], far_spec[1:2, :]
    g_re, g_im = far_re[...], far_im[...]
    model_re = nt(wt_re[...], g_re) + nt(wt_im[...], g_im)
    model_im = nt(wt_im[...], g_re) - nt(wt_re[...], g_im)
    x_re = (u_re * v_re + u_im * v_im) - model_re
    x_im = (u_im * v_re - u_re * v_im) - model_im
    mis = 0.5 * jnp.sum(weight * (x_re * x_re + x_im * x_im), keepdims=True)
    r_re = (weight * x_re.astype(bf16).astype(f32)).astype(bf16)
    r_im = (weight * x_im.astype(bf16).astype(f32)).astype(bf16)
    y_re = nn(r_re, g_re) - nn(r_im, g_im)
    y_im = nn(r_re, g_im) + nn(r_im, g_re)
    total = -jnp.sum(
        near_re[...].astype(f32) * y_re + near_im[...].astype(f32) * y_im,
        axis=0,
        keepdims=True,
    )
    tiles = jnp.concatenate(
        [total[:, 128 * i : 128 * (i + 1)] for i in range(TILES)], axis=0
    )
    out[:, 0:TILES] = jnp.broadcast_to(tiles[None], (NZ, TILES, 128))
    out[:, TILES : 2 * TILES] = jnp.broadcast_to(mis[None], (NZ, TILES, 128))


def gather_z(parts, out):
    out[...] = jnp.broadcast_to(
        jnp.sum(parts[...], axis=0, keepdims=True), out.shape
    )


def finish(parts, source, new_source, misfit):
    mine = lax.axis_index("xh") * 2 + lax.axis_index("core")
    squares = jnp.zeros((TILES, 128), f32)
    own = jnp.zeros((2 * TILES, 128), f32)
    for f in range(NF):
        here = jnp.sum(
            jnp.concatenate([parts[q * NF + f][None] for q in range(NQ)], axis=0), axis=0
        )
        squares = squares + here[0:TILES] * here[0:TILES]
        own = jnp.where(mine == f, here, own)
    rms = jnp.sqrt(jnp.sum(squares, keepdims=True) / (NF * CELLS) + 1e-06)
    step = jnp.exp(-0.5 * own[0:TILES] / rms)
    step = jnp.concatenate([step[i : i + 1] for i in range(TILES)], axis=1)
    new_source[...] = source[...] * step
    stations = NZ * NQ * ROWS
    misfit[0] = jnp.max(own[TILES : TILES + 1]) / (stations * stations)


def shape(dtype, *dims):
    return jax.ShapeDtypeStruct(dims, dtype)


def from_z(array, u):
    return lax.ppermute(array, "z", [(z, (z - u) % NZ) for z in range(NZ)])


def local(spectra, green, source, pair_mask):
    g = green[0]
    vmem = pl.BlockSpec(memory_space=pltpu.VMEM)
    tall = ROWS * (1 + len(OFFSETS))
    near, far, two_mask, own_mask, own_spec = pl.pallas_call(
        pack_line,
        out_shape=[
            shape(bf16, MASKED, CELLS),
            shape(bf16, MASKED, CELLS),
            shape(bf16, 32, CELLS),
            shape(bf16, ROWS, WIDE),
            shape(f32, ROWS, 128),
        ],
        in_specs=[vmem] * 3,
        out_specs=[vmem] * 5,
        name="pack_line",
    )(g, pair_mask, spectra[0])
    two_mask = from_z(two_mask, 2)
    one = from_z(near, 1)
    three = from_z(far, -3)
    shared = pl.pallas_call(
        pack_plane,
        out_shape=shape(bf16, NQ, SHARED, CELLS),
        in_specs=[vmem] * 3,
        out_specs=vmem,
        name="pack_plane",
    )(g, pair_mask, own_spec)
    shared = lax.all_to_all(shared, PLANE, 0, 0, tiled=True)
    two = from_z(one[:MASK], 1)
    four_re = from_z(two[REAL:MASK], 2)
    four_im = from_z(three[:REAL], -1)
    part = pl.pallas_call(
        absorb,
        out_shape=shape(f32, NZ, 2 * TILES, 128),
        in_specs=[vmem] * 11,
        out_specs=vmem,
        scratch_shapes=[
            pltpu.VMEM((WIDE, CELLS), bf16),
            pltpu.VMEM((WIDE, CELLS), bf16),
            pltpu.VMEM((8, WIDE), f32),
            pltpu.VMEM((WIDE, 4 * ROWS), bf16),
            pltpu.VMEM((tall, CELLS), bf16),
            pltpu.VMEM((tall, CELLS), bf16),
            pltpu.VMEM((tall, CELLS), bf16),
            pltpu.VMEM((tall, CELLS), bf16),
        ],
        name="absorb",
    )(source, g, own_mask, own_spec, shared, one, two, two_mask, three, four_re, four_im)
    part = lax.all_to_all(part, "z", 0, 0, tiled=True)
    part = pl.pallas_call(
        gather_z,
        out_shape=shape(f32, NQ * NF, 2 * TILES, 128),
        in_specs=[vmem],
        out_specs=vmem,
        name="gather_z",
    )(part)
    part = lax.all_to_all(part, PLANE + FREQ, 0, 0, tiled=True)
    return pl.pallas_call(
        finish,
        out_shape=(shape(f32, 1, CELLS), shape(f32, 1)),
        in_specs=[vmem, vmem],
        out_specs=(vmem, pl.BlockSpec(memory_space=pltpu.SMEM)),
        name="finish",
    )(part, source)


def solution(mesh):
    fine = Mesh(mesh.devices.reshape(NZ, NX, NY, 2, 2), STA + FREQ)
    placed = (P(FREQ, None, STA), P(FREQ, None, STA, None), P(FREQ, None), P(STA, None))
    return jax.shard_map(
        local, mesh=fine, in_specs=placed, out_specs=(P(FREQ, None), P(FREQ)), check_vma=False
    )
```

time: 97.3 us -> 97.7 us (level)
  local copies, waits for them, and re-layouts: 5.27 us -> 2.18 us
  starting transfers between devices: 16.4 us -> 18.8 us
  Pallas kernels: 12.7 us -> 14.6 us
    ppermute x4 -> x6, starting transfers between devices: 10.5 us -> 12.7 us  [from_z(): return lax.ppermute(array, 'z', [(z, (z - u) % NZ) for z in range(NZ)])]
    pallas_call x4 -> x5, Pallas kernels: 12.7 us -> 14.6 us  [the longest x1 5.99 us: local(): pl.pallas_call(absorb, out_shape=shape(f32, NZ, 2 * TILES, 128), in_specs...]
    all_to_all x2 -> x0, local copies, waits for them, and re-layouts: 1.87 us -> none  [the longest x1 1.06 us: local(): part = lax.all_to_all(part, PLANE + FREQ, 0, 0, tiled=True)]
    all_to_all x1, blocking collectives: 16.5 us -> 14.7 us  [local(): part = lax.all_to_all(part, 'z', 0, 0, tiled=True)]
    all_to_all x1, blocking collectives: 16.9 us -> 18.3 us  [local(): part = lax.all_to_all(part, PLANE + FREQ, 0, 0, tiled=True)]
    unnamed x12 -> x14, local copies, waits for them, and re-layouts: 3.4 us -> 2.14 us
    ppermute x4 -> x6, waiting for transfers between devices: 28.5 us -> 28 us  [from_z(): return lax.ppermute(array, 'z', [(z, (z - u) % NZ) for z in range(NZ)])]
  transfers between devices with their start and end apart: 5 -> 7, of which waited for: 2 -> 3; matrix products, arithmetic and copies ran while one was open for 0% -> 0% of each run, Pallas kernels for 0% -> 0%
where the time goes in v3:
time: 97.7 us; the launch traced here: 97.3 us
  blocking collectives  33 us (34%)
  waiting for transfers between devices  28 us (29%)
  starting transfers between devices  18.8 us (19%)
  Pallas kernels  14.6 us (15%)
  local copies, waits for them, and re-layouts  2.18 us (2%)
    ppermute x6, waiting for transfers between devices, from_z(): return lax.ppermute(array, 'z', [(z, (z - u) % NZ) for z in range(NZ)])  28 us
    all_to_all x1, blocking collectives, local(): part = lax.all_to_all(part, PLANE + FREQ, 0, 0, tiled=True)  18.3 us
    all_to_all x1, blocking collectives, local(): part = lax.all_to_all(part, 'z', 0, 0, tiled=True)  14.7 us
    ppermute x6, starting transfers between devices, from_z(): return lax.ppermute(array, 'z', [(z, (z - u) % NZ) for z in range(NZ)])  12.7 us
    all_to_all x1, starting transfers between devices, local(): shared = lax.all_to_all(shared, PLANE, 0, 0, tiled=True)  6.08 us
    pallas_call x1, Pallas kernels, local(): pl.pallas_call(absorb, out_shape=shape(f32, NZ, 2 * TILES, 128), in_specs...  5.99 us
    pallas_call x1, Pallas kernels, local(): pl.pallas_call(pack_plane, out_shape=shape(bf16, NQ, SHARED, CELLS), in_s...  2.99 us
    pallas_call x1, Pallas kernels, local(): pl.pallas_call(pack_line, out_shape=[shape(bf16, MASKED, CELLS), shape(bf...  2.36 us
  transfers between devices with their start and end apart: 7, of which 3 were waited for; matrix products, arithmetic and copies ran while one was open for 0% of the time, Pallas kernels for 0%

profile of v3, /device:TPU:1, one launch (start us, length us, event | category | flops | bytes accessed | tf_op | source)
XLA Modules:
  0.0 97.3 jit_solution(2268107813193343287)
XLA Ops:
  0.6 2.4 %pack_line.1 = (bf16[168,1024]{1,0:T(8,128)(2,1)}, bf16[168,1024]{1,0:T(8,128)(2,1)}, bf16[32,1024]{1,0:T(8,128)(2,1)}, bf16[64,512]{1,0:T(8,128)(2,1)}, f32[64,128]{1,0:T(8,128)}) custom-call(bf16[2,64,1024]{2,1,0:T(8,128)(2,1)} %bitcast.2, s32[64,4096]{1,0:T(8,128)} %mask.3, bf16[2,64]{1,0:T(2,128)(2,1)} %bitcast.5), custom_call_target="tpu_custom_call" | custom-call | tf_op jit(solution)/shard_map/pack_line/pallas_call | solution.py:215
  3.0 3.0 %pack_plane.1 = bf16[8,152,1024]{2,1,0:T(8,128)(2,1)} custom-call(bf16[2,64,1024]{2,1,0:T(8,128)(2,1)} %bitcast.3, s32[64,4096]{1,0:T(8,128)} %mask.3, f32[64,128]{1,0:T(8,128)} %get-tuple-element.8.own_spec), custom_call_target="tpu_custom_call" | custom-call | tf_op jit(solution)/shard_map/pack_plane/pallas_call | solution.py:231
  6.0 0.0 copy-start.6
  6.0 6.1 %all-to-all-start = ((bf16[8,152,1024]{2,1,0:T(8,128)(2,1)}), bf16[8,152,1024]{2,1,0:T(8,128)(2,1)S(1)}, u32[]{:S(2)}, u32[]{:S(2)}) async-start(bf16[8,152,1024]{2,1,0:T(8,128)(2,1)} %pack_plane.1), calls=%async_computation | async-start | bytes 4980736 | tf_op jit(solution)/shard_map/all_to_all | solution.py:238
  12.1 0.0 copy-done.6
  12.1 5.7 %collective-permute-start = (bf16[168,1024]{1,0:T(8,128)(2,1)S(1)}, bf16[168,1024]{1,0:T(8,128)(2,1)S(1)}, u32[]{:S(2)}, u32[]{:S(2)}) collective-permute-start(bf16[168,1024]{1,0:T(8,128)(2,1)S(1)} %copy-done.6), channel_id=1, source_target_pairs={{0,224},{32,0},{64,32},{96,64},{128,96},{160,128},{192,160},{224,1... | collective-permute-start | bytes 1032200 | tf_op jit(solution)/shard_map/ppermute | solution.py:208
  17.7 0.0 collective-permute-start.3
  17.7 6.4 %collective-permute-done.one = bf16[168,1024]{1,0:T(8,128)(2,1)S(1)} collective-permute-done((bf16[168,1024]{1,0:T(8,128)(2,1)S(1)}, bf16[168,1024]{1,0:T(8,128)(2,1)S(1)}, u32[]{:S(2)}, u32[]{:S(2)}) %collective-permute-start) | collective-permute-done | bytes 344096 | tf_op jit(solution)/shard_map/ppermute | solution.py:208
  24.1 0.0 copy-start.1
  24.2 3.5 %collective-permute-start.1 = (bf16[136,1024]{1,0:T(8,128)(2,1)S(1)}, bf16[136,1024]{1,0:T(8,128)(2,1)S(1)}, u32[]{:S(2)}, u32[]{:S(2)}) collective-permute-start(bf16[136,1024]{1,0:T(8,128)(2,1)S(1)} %slice.12), channel_id=1, source_target_pairs={{0,224},{32,0},{64,32},{96,64},{128,96},{160,128},{192,160},{224,1... | collective-permute-start | bytes 835592 | tf_op jit(solution)/shard_map/ppermute | solution.py:208
  27.6 15.4 %collective-permute-done.3.three = bf16[168,1024]{1,0:T(8,128)(2,1)S(1)} collective-permute-done((bf16[168,1024]{1,0:T(8,128)(2,1)}, bf16[168,1024]{1,0:T(8,128)(2,1)S(1)}, u32[]{:S(2)}, u32[]{:S(2)}) %collective-permute-start.3) | collective-permute-done | bytes 344096 | tf_op jit(solution)/shard_map/ppermute | solution.py:208
  43.0 0.0 copy-start.2
  43.1 0.1 collective-permute-start.5
  43.1 0.0 collective-permute-done.1.two
  43.2 0.0 copy-start.3
  43.2 3.4 %collective-permute-start.4 = (bf16[64,1024]{1,0:T(8,128)(2,1)S(1)}, bf16[64,1024]{1,0:T(8,128)(2,1)}, u32[]{:S(2)}, u32[]{:S(2)}) collective-permute-start(bf16[64,1024]{1,0:T(8,128)(2,1)S(1)} %slice.13), channel_id=1, source_target_pairs={{0,192},{32,224},{64,0},{96,32},{128,64},{160,96},{192,128},{224,1... | collective-permute-start | bytes 393224 | tf_op jit(solution)/shard_map/ppermute | solution.py:208
  46.6 0.1 collective-permute-start.2
  46.7 6.2 %collective-permute-done.2.two_mask = bf16[32,1024]{1,0:T(8,128)(2,1)S(1)} collective-permute-done((bf16[32,1024]{1,0:T(8,128)(2,1)}, bf16[32,1024]{1,0:T(8,128)(2,1)S(1)}, u32[]{:S(2)}, u32[]{:S(2)}) %collective-permute-start.2) | collective-permute-done | bytes 65568 | tf_op jit(solution)/shard_map/ppermute | solution.py:208
  52.8 0.0 copy-start.5
  52.8 0.0 collective-permute-done.5.four_im
  52.8 0.0 copy-start.4
  52.8 0.7 copy-done.4
  53.5 0.0 collective-permute-done.4.four_re
  53.5 0.0 all-to-all-done.shared
  53.5 0.0 copy-start
  53.5 0.0 copy-done.1
  53.5 0.0 copy-done.2
  53.5 0.0 copy-done.3
  53.6 0.0 copy-done.5
  53.6 1.4 %copy-done = bf16[8,152,1024]{2,1,0:T(8,128)(2,1)} copy-done((bf16[8,152,1024]{2,1,0:T(8,128)(2,1)}, bf16[8,152,1024]{2,1,0:T(8,128)(2,1)S(1)}, u32[]{:S(2)}) %copy-start) | copy-done | bytes 2490392
  55.0 6.0 %absorb.1 = f32[8,16,128]{2,1,0:T(8,128)} custom-call(f32[1,1024]{1,0:T(1,128)} %source.3, bf16[2,64,1024]{2,1,0:T(8,128)(2,1)} %bitcast.4, bf16[64,512]{1,0:T(8,128)(2,1)} %get-tuple-element.7.own_mask, f32[64,128]{1,0:T(8,128)} %get-tuple-element.8.own_spec, bf16[8,152,1024]{2,1,0:T(8,128)(2,1)} %copy-done, bf16[168,1024]{1,0:T(8,128)(2,1)} %copy-done.1, ...), custom_call_target="tpu_custom_call" | custom-call | tf_op jit(solution)/shard_map/absorb/pallas_call | solution.py:242
  61.0 14.7 %all_to_all.15.parts = f32[8,16,128]{2,1,0:T(8,128)} all-to-all(f32[8,16,128]{2,1,0:T(8,128)} %absorb.1), channel_id=1, replica_groups=mesh['z'=8,'xl'=2,'y'=4,'xh'=2,'core'=2] {'z'}, dimensions={0} | all-to-all | bytes 131072 | tf_op jit(solution)/shard_map/all_to_all | solution.py:259
  75.7 1.6 %gather_z.1 = f32[32,16,128]{2,1,0:T(8,128)} custom-call(f32[8,16,128]{2,1,0:T(8,128)} %all_to_all.15.parts), custom_call_target="tpu_custom_call" | custom-call | tf_op jit(solution)/shard_map/gather_z/pallas_call | solution.py:260
  77.2 18.3 %all_to_all.16.parts = f32[32,16,128]{2,1,0:T(8,128)} all-to-all(f32[32,16,128]{2,1,0:T(8,128)} %gather_z.1), channel_id=1, replica_groups=mesh['z'=8,'xl'=2,'y'=4,'xh'=2,'core'=2] {'xl','y','xh','core'}, dimensions={0} | all-to-all | bytes 524288 | tf_op jit(solution)/shard_map/all_to_all | solution.py:267
  95.5 1.7 %finish.1 = (f32[1,1024]{1,0:T(1,128)}, f32[1]{0:T(128)}) custom-call(f32[32,16,128]{2,1,0:T(8,128)} %all_to_all.16.parts, f32[1,1024]{1,0:T(1,128)} %source.3), custom_call_target="tpu_custom_call" | custom-call | tf_op jit(solution)/shard_map/finish/pallas_call | solution.py:268
  (3 shorter events, 0.0 us)
Async XLA Ops:
  6.0 6.1 %copy-start.6 = (bf16[168,1024]{1,0:T(8,128)(2,1)S(1)}, bf16[168,1024]{1,0:T(8,128)(2,1)}, u32[]{:S(2)}) copy-start(bf16[168,1024]{1,0:T(8,128)(2,1)} %get-tuple-element.9) | copy-start | bytes 1032196
  6.0 47.5 %all-to-all-start = ((bf16[8,152,1024]{2,1,0:T(8,128)(2,1)}), bf16[8,152,1024]{2,1,0:T(8,128)(2,1)S(1)}, u32[]{:S(2)}, u32[]{:S(2)}) async-start(bf16[8,152,1024]{2,1,0:T(8,128)(2,1)} %pack_plane.1), calls=%async_computation | async-start | bytes 4980736 | tf_op jit(solution)/shard_map/all_to_all | solution.py:238
  12.1 12.1 %collective-permute-start = (bf16[168,1024]{1,0:T(8,128)(2,1)S(1)}, bf16[168,1024]{1,0:T(8,128)(2,1)S(1)}, u32[]{:S(2)}, u32[]{:S(2)}) collective-permute-start(bf16[168,1024]{1,0:T(8,128)(2,1)S(1)} %copy-done.6), channel_id=1, source_target_pairs={{0,224},{32,0},{64,32},{96,64},{128,96},{160,128},{192,160},{224,1... | collective-permute-start | bytes 1032200 | tf_op jit(solution)/shard_map/ppermute | solution.py:208
  17.7 25.3 %collective-permute-start.3 = (bf16[168,1024]{1,0:T(8,128)(2,1)}, bf16[168,1024]{1,0:T(8,128)(2,1)S(1)}, u32[]{:S(2)}, u32[]{:S(2)}) collective-permute-start(bf16[168,1024]{1,0:T(8,128)(2,1)} %get-tuple-element.11), channel_id=1, source_target_pairs={{0,96},{32,128},{64,160},{96,192},{128,224},{160,0},{192,32},{224,... | collective-permute-start | bytes 1032200 | tf_op jit(solution)/shard_map/ppermute | solution.py:208
  24.1 29.4 %copy-start.1 = (bf16[168,1024]{1,0:T(8,128)(2,1)}, bf16[168,1024]{1,0:T(8,128)(2,1)S(1)}, u32[]{:S(2)}) copy-start(bf16[168,1024]{1,0:T(8,128)(2,1)S(1)} %collective-permute-done.one) | copy-start | bytes 1032196
  24.2 19.0 %collective-permute-start.1 = (bf16[136,1024]{1,0:T(8,128)(2,1)S(1)}, bf16[136,1024]{1,0:T(8,128)(2,1)S(1)}, u32[]{:S(2)}, u32[]{:S(2)}) collective-permute-start(bf16[136,1024]{1,0:T(8,128)(2,1)S(1)} %slice.12), channel_id=1, source_target_pairs={{0,224},{32,0},{64,32},{96,64},{128,96},{160,128},{192,160},{224,1... | collective-permute-start | bytes 835592 | tf_op jit(solution)/shard_map/ppermute | solution.py:208
  43.0 10.5 %copy-start.2 = (bf16[168,1024]{1,0:T(8,128)(2,1)}, bf16[168,1024]{1,0:T(8,128)(2,1)S(1)}, u32[]{:S(2)}) copy-start(bf16[168,1024]{1,0:T(8,128)(2,1)S(1)} %collective-permute-done.3.three) | copy-start | bytes 1032196
  43.1 9.8 %collective-permute-start.5 = (bf16[72,1024]{1,0:T(8,128)(2,1)S(1)}, bf16[72,1024]{1,0:T(8,128)(2,1)S(1)}, u32[]{:S(2)}, u32[]{:S(2)}) collective-permute-start(bf16[72,1024]{1,0:T(8,128)(2,1)S(1)} %slice.14), channel_id=1, source_target_pairs={{0,32},{32,64},{64,96},{96,128},{128,160},{160,192},{192,224},{224... | collective-permute-start | bytes 442376 | tf_op jit(solution)/shard_map/ppermute | solution.py:208
  43.2 10.4 %copy-start.3 = (bf16[136,1024]{1,0:T(8,128)(2,1)}, bf16[136,1024]{1,0:T(8,128)(2,1)S(1)}, u32[]{:S(2)}) copy-start(bf16[136,1024]{1,0:T(8,128)(2,1)S(1)} %collective-permute-done.1.two) | copy-start | bytes 835588
  43.2 10.3 %collective-permute-start.4 = (bf16[64,1024]{1,0:T(8,128)(2,1)S(1)}, bf16[64,1024]{1,0:T(8,128)(2,1)}, u32[]{:S(2)}, u32[]{:S(2)}) collective-permute-start(bf16[64,1024]{1,0:T(8,128)(2,1)S(1)} %slice.13), channel_id=1, source_target_pairs={{0,192},{32,224},{64,0},{96,32},{128,64},{160,96},{192,128},{224,1... | collective-permute-start | bytes 393224 | tf_op jit(solution)/shard_map/ppermute | solution.py:208
  46.6 6.3 %collective-permute-start.2 = (bf16[32,1024]{1,0:T(8,128)(2,1)}, bf16[32,1024]{1,0:T(8,128)(2,1)S(1)}, u32[]{:S(2)}, u32[]{:S(2)}) collective-permute-start(bf16[32,1024]{1,0:T(8,128)(2,1)} %get-tuple-element.10), channel_id=1, source_target_pairs={{0,192},{32,224},{64,0},{96,32},{128,64},{160,96},{192,128},{224,1... | collective-permute-start | bytes 196616 | tf_op jit(solution)/shard_map/ppermute | solution.py:208
  52.8 0.7 copy-start.5
  52.8 0.7 copy-start.4
  53.5 1.5 %copy-start = (bf16[8,152,1024]{2,1,0:T(8,128)(2,1)}, bf16[8,152,1024]{2,1,0:T(8,128)(2,1)S(1)}, u32[]{:S(2)}) copy-start(bf16[8,152,1024]{2,1,0:T(8,128)(2,1)S(1)} %all-to-all-done.shared) | copy-start | bytes 7471108

commit v4 on v3

--- a/solution.py
+++ b/solution.py
@@ -16,7 +16,7 @@
 STA = ("z",) + PLANE
 OFFSETS = (1, 2, -3, 4)
 SHARED = 152
-TILES = CELLS // 128
+LONG = CELLS + 128
 f32, bf16 = jnp.float32, jnp.bfloat16
 
 
@@ -39,6 +39,7 @@
 
 
 SPEC, IMAG, REAL, MASK, MASKED = 0, 8, 72, 136, 168
+PREPARE = 14_500_000_000
 
 
 def window(mask, at):
@@ -104,11 +105,39 @@
         put_spectra(ref, 144, spectra)
 
 
-def absorb(
-    source, green, own_mask, own_spec, shared, one, two, two_mask, three, four_re, four_im,
-    out, far_re, far_im, far_spec, back, near_re, near_im, wt_re, wt_im
+def prepare(
+    source, green, own_mask, own_spec, one, two, two_mask, three, four,
+    near_re, near_im, wt_re, wt_im, weight, spec_re, spec_im
 ):
     scale = source[...]
+    real, imag = slice(REAL, REAL + ROWS), slice(IMAG, IMAG + ROWS)
+    us = [own_spec[...]]
+    held = [(green[0], green[1])]
+    for ref in (one, two, three, four):
+        us.append(take_spectra(ref, SPEC))
+        held.append((ref[real, :], ref[imag, :]))
+    masks = [
+        own_mask[...].astype(f32),
+        take_mask(one, MASK),
+        take_mask(two_mask, 0),
+        take_mask(three, MASK),
+        jnp.zeros((ROWS, WIDE), f32),
+    ]
+    for k, (re, im) in enumerate(held):
+        rows = slice(ROWS * k, ROWS * (k + 1))
+        near_re[rows, :] = re
+        near_im[rows, :] = im
+        wt_re[rows, :] = (scale * re.astype(f32)).astype(bf16)
+        wt_im[rows, :] = (scale * im.astype(f32)).astype(bf16)
+        weight[rows, :] = masks[k]
+        spec_re[rows, :] = jnp.broadcast_to(us[k][:, 0:1], (ROWS, 128))
+        spec_im[rows, :] = jnp.broadcast_to(us[k][:, 1:2], (ROWS, 128))
+
+
+def absorb(
+    shared, near_re, near_im, wt_re, wt_im, weight, spec_re, spec_im,
+    out, far_re, far_im, far_spec, back
+):
     for q in range(NQ):
         rows = slice(ROWS * q, ROWS * (q + 1))
         ref = shared.at[q]
@@ -120,48 +149,19 @@
             ]
         far_spec[0:2, rows] = ref[144:152, 0:128].astype(f32)[0:2, 64:128]
     behind = nt(identity(4 * ROWS), back[...])
-    us = [
-        own_spec[...],
-        take_spectra(one, SPEC),
-        take_spectra(two, SPEC),
-        take_spectra(three, SPEC),
-        take_spectra(four_im, SPEC),
-    ]
-    weight = jnp.concatenate(
-        [
-            own_mask[...].astype(f32),
-            take_mask(one, MASK) + behind[0:ROWS],
-            take_mask(two_mask, 0) + behind[ROWS : 2 * ROWS],
-            take_mask(three, MASK) + behind[2 * ROWS : 3 * ROWS],
-            behind[3 * ROWS : 4 * ROWS],
-        ],
-        axis=0,
-    )
-    real, imag = slice(REAL, REAL + ROWS), slice(IMAG, IMAG + ROWS)
-    held = [
-        (green[0], green[1]),
-        (one[real, :], one[imag, :]),
-        (two[real, :], two[imag, :]),
-        (three[real, :], three[imag, :]),
-        (four_re[...], four_im[imag, :]),
-    ]
-    for k, (re, im) in enumerate(held):
-        rows = slice(ROWS * k, ROWS * (k + 1))
-        near_re[rows, :] = re
-        near_im[rows, :] = im
-        wt_re[rows, :] = (scale * re.astype(f32)).astype(bf16)
-        wt_im[rows, :] = (scale * im.astype(f32)).astype(bf16)
-    u_re = jnp.concatenate([u[:, 0:1] for u in us], axis=0)
-    u_im = jnp.concatenate([u[:, 1:2] for u in us], axis=0)
+    counts = weight[...] + jnp.concatenate(
+        [jnp.zeros((ROWS, WIDE), f32), behind], axis=0
+    )
+    u_re, u_im = spec_re[:, 0:1], spec_im[:, 0:1]
     v_re, v_im = far_spec[0:1, :], far_spec[1:2, :]
     g_re, g_im = far_re[...], far_im[...]
     model_re = nt(wt_re[...], g_re) + nt(wt_im[...], g_im)
     model_im = nt(wt_im[...], g_re) - nt(wt_re[...], g_im)
     x_re = (u_re * v_re + u_im * v_im) - model_re
     x_im = (u_im * v_re - u_re * v_im) - model_im
-    mis = 0.5 * jnp.sum(weight * (x_re * x_re + x_im * x_im), keepdims=True)
-    r_re = (weight * x_re.astype(bf16).astype(f32)).astype(bf16)
-    r_im = (weight * x_im.astype(bf16).astype(f32)).astype(bf16)
+    mis = 0.5 * jnp.sum(counts * (x_re * x_re + x_im * x_im), keepdims=True)
+    r_re = (counts * x_re.astype(bf16).astype(f32)).astype(bf16)
+    r_im = (counts * x_im.astype(bf16).astype(f32)).astype(bf16)
     y_re = nn(r_re, g_re) - nn(r_im, g_im)
     y_im = nn(r_re, g_im) + nn(r_im, g_re)
     total = -jnp.sum(
@@ -169,11 +169,8 @@
         axis=0,
         keepdims=True,
     )
-    tiles = jnp.concatenate(
-        [total[:, 128 * i : 128 * (i + 1)] for i in range(TILES)], axis=0
-    )
-    out[:, 0:TILES] = jnp.broadcast_to(tiles[None], (NZ, TILES, 128))
-    out[:, TILES : 2 * TILES] = jnp.broadcast_to(mis[None], (NZ, TILES, 128))
+    out[:, :, 0:CELLS] = jnp.broadcast_to(total[None], (NZ, 1, CELLS))
+    out[:, :, CELLS:LONG] = jnp.broadcast_to(mis[None], (NZ, 1, 128))
 
 
 def gather_z(parts, out):
@@ -184,20 +181,18 @@
 
 def finish(parts, source, new_source, misfit):
     mine = lax.axis_index("xh") * 2 + lax.axis_index("core")
-    squares = jnp.zeros((TILES, 128), f32)
-    own = jnp.zeros((2 * TILES, 128), f32)
+    squares = jnp.zeros((1, CELLS), f32)
+    own = jnp.zeros((1, LONG), f32)
     for f in range(NF):
-        here = jnp.sum(
-            jnp.concatenate([parts[q * NF + f][None] for q in range(NQ)], axis=0), axis=0
-        )
-        squares = squares + here[0:TILES] * here[0:TILES]
+        here = parts[f]
+        for q in range(1, NQ):
+            here = here + parts[q * NF + f]
+        squares = squares + here[:, 0:CELLS] * here[:, 0:CELLS]
         own = jnp.where(mine == f, here, own)
     rms = jnp.sqrt(jnp.sum(squares, keepdims=True) / (NF * CELLS) + 1e-06)
-    step = jnp.exp(-0.5 * own[0:TILES] / rms)
-    step = jnp.concatenate([step[i : i + 1] for i in range(TILES)], axis=1)
-    new_source[...] = source[...] * step
+    new_source[...] = source[...] * jnp.exp(-0.5 * own[:, 0:CELLS] / rms)
     stations = NZ * NQ * ROWS
-    misfit[0] = jnp.max(own[TILES : TILES + 1]) / (stations * stations)
+    misfit[0] = jnp.max(own[:, CELLS:LONG]) / (stations * stations)
 
 
 def shape(dtype, *dims):
@@ -225,9 +220,9 @@
         out_specs=[vmem] * 5,
         name="pack_line",
     )(g, pair_mask, spectra[0])
+    three = from_z(from_z(from_z(far, -1), -1), -1)
+    one = from_z(near, 1)
     two_mask = from_z(two_mask, 2)
-    one = from_z(near, 1)
-    three = from_z(far, -3)
     shared = pl.pallas_call(
         pack_plane,
         out_shape=shape(bf16, NQ, SHARED, CELLS),
@@ -237,29 +232,36 @@
     )(g, pair_mask, own_spec)
     shared = lax.all_to_all(shared, PLANE, 0, 0, tiled=True)
     two = from_z(one[:MASK], 1)
-    four_re = from_z(two[REAL:MASK], 2)
-    four_im = from_z(three[:REAL], -1)
+    four = from_z(two, 2)
+    ready = pl.pallas_call(
+        prepare,
+        out_shape=[shape(bf16, tall, CELLS)] * 4
+        + [shape(f32, tall, WIDE)]
+        + [shape(f32, tall, 128)] * 2,
+        in_specs=[vmem] * 9,
+        out_specs=[vmem] * 7,
+        cost_estimate=pl.CostEstimate(
+            flops=PREPARE, transcendentals=0, bytes_accessed=0
+        ),
+        name="prepare",
+    )(source, g, own_mask, own_spec, one, two, two_mask, three, four)
     part = pl.pallas_call(
         absorb,
-        out_shape=shape(f32, NZ, 2 * TILES, 128),
-        in_specs=[vmem] * 11,
+        out_shape=shape(f32, NZ, 1, LONG),
+        in_specs=[vmem] * 8,
         out_specs=vmem,
         scratch_shapes=[
             pltpu.VMEM((WIDE, CELLS), bf16),
             pltpu.VMEM((WIDE, CELLS), bf16),
             pltpu.VMEM((8, WIDE), f32),
             pltpu.VMEM((WIDE, 4 * ROWS), bf16),
-            pltpu.VMEM((tall, CELLS), bf16),
-            pltpu.VMEM((tall, CELLS), bf16),
-            pltpu.VMEM((tall, CELLS), bf16),
-            pltpu.VMEM((tall, CELLS), bf16),
         ],
         name="absorb",
-    )(source, g, own_mask, own_spec, shared, one, two, two_mask, three, four_re, four_im)
+    )(shared, *ready)
     part = lax.all_to_all(part, "z", 0, 0, tiled=True)
     part = pl.pallas_call(
         gather_z,
-        out_shape=shape(f32, NQ * NF, 2 * TILES, 128),
+        out_shape=shape(f32, NQ * NF, 1, LONG),
         in_specs=[vmem],
         out_specs=vmem,
         name="gather_z",

time: 97.7 us -> 90.7 us (0.928)
  waiting for transfers between devices: 28 us -> 18.6 us
  Pallas kernels: 14.6 us -> 18.4 us
  blocking collectives: 33 us -> 31 us
    ppermute x6 -> x7, waiting for transfers between devices: 28 us -> 11.6 us  [from_z(): return lax.ppermute(array, 'z', [(z, (z - u) % NZ) for z in range(NZ)])]
    all_to_all x1, waiting for transfers between devices: 0.01 us -> 7.06 us  [local(): shared = lax.all_to_all(shared, PLANE, 0, 0, tiled=True)]
    pallas_call x2 -> x3, Pallas kernels: 7.55 us -> 11.3 us  [the longest x1 6.56 us: local(): pl.pallas_call(absorb, out_shape=shape(f32, NZ, 1, LONG), in_specs=[vmem]...]
    all_to_all x1, blocking collectives: 18.3 us -> 16.3 us  [local(): part = lax.all_to_all(part, PLANE + FREQ, 0, 0, tiled=True)]
    ppermute x6 -> x7, starting transfers between devices: 12.7 us -> 13.3 us  [from_z(): return lax.ppermute(array, 'z', [(z, (z - u) % NZ) for z in range(NZ)])]
  transfers between devices with their start and end apart: 7 -> 8, of which waited for: 3 -> 3; matrix products, arithmetic and copies ran while one was open for 0% -> 0% of each run, Pallas kernels for 0% -> 7%
where the time goes in v4:
time: 90.7 us; the launch traced here: 90.2 us
  blocking collectives  31 us (34%)
  starting transfers between devices  18.6 us (21%)
  waiting for transfers between devices  18.6 us (21%)
  Pallas kernels  18.4 us (20%)
  local copies, waits for them, and re-layouts  2.95 us (3%)
    all_to_all x1, blocking collectives, local(): part = lax.all_to_all(part, PLANE + FREQ, 0, 0, tiled=True)  16.3 us
    all_to_all x1, blocking collectives, local(): part = lax.all_to_all(part, 'z', 0, 0, tiled=True)  14.7 us
    ppermute x7, starting transfers between devices, from_z(): return lax.ppermute(array, 'z', [(z, (z - u) % NZ) for z in range(NZ)])  13.3 us
    ppermute x7, waiting for transfers between devices, from_z(): return lax.ppermute(array, 'z', [(z, (z - u) % NZ) for z in range(NZ)])  11.6 us
    all_to_all x1, waiting for transfers between devices, local(): shared = lax.all_to_all(shared, PLANE, 0, 0, tiled=True)  7.06 us
    pallas_call x1, Pallas kernels, local(): pl.pallas_call(absorb, out_shape=shape(f32, NZ, 1, LONG), in_specs=[vmem]...  6.56 us
    all_to_all x1, starting transfers between devices, local(): shared = lax.all_to_all(shared, PLANE, 0, 0, tiled=True)  5.25 us
    pallas_call x1, Pallas kernels, local(): pl.pallas_call(prepare, out_shape=[shape(bf16, tall, CELLS)] * 4 + [shape...  3.3 us
  transfers between devices with their start and end apart: 8, of which 3 were waited for; matrix products, arithmetic and copies ran while one was open for 0% of the time, Pallas kernels for 7%

profile of v4, /device:TPU:1, one launch (start us, length us, event | category | flops | bytes accessed | tf_op | source)
XLA Modules:
  0.0 90.2 jit_solution(17552596220051417508)
XLA Ops:
  0.6 2.4 %pack_line.1 = (bf16[168,1024]{1,0:T(8,128)(2,1)}, bf16[168,1024]{1,0:T(8,128)(2,1)}, bf16[32,1024]{1,0:T(8,128)(2,1)}, bf16[64,512]{1,0:T(8,128)(2,1)}, f32[64,128]{1,0:T(8,128)}) custom-call(bf16[2,64,1024]{2,1,0:T(8,128)(2,1)} %bitcast.2, s32[64,4096]{1,0:T(8,128)} %mask.3, bf16[2,64]{1,0:T(2,128)(2,1)} %bitcast.5), custom_call_target="tpu_custom_call" | custom-call | tf_op jit(solution)/shard_map/pack_line/pallas_call | solution.py:210
  3.0 2.5 %collective-permute-start.3 = (bf16[168,1024]{1,0:T(8,128)(2,1)}, bf16[168,1024]{1,0:T(8,128)(2,1)S(1)}, u32[]{:S(2)}, u32[]{:S(2)}) collective-permute-start(bf16[168,1024]{1,0:T(8,128)(2,1)} %get-tuple-element.18), channel_id=1, source_target_pairs={{0,32},{32,64},{64,96},{96,128},{128,160},{160,192},{192,224},{224... | collective-permute-start | bytes 1032200 | tf_op jit(solution)/shard_map/ppermute | solution.py:203
  5.5 3.9 %collective-permute-start = (bf16[168,1024]{1,0:T(8,128)(2,1)}, bf16[168,1024]{1,0:T(8,128)(2,1)S(1)}, u32[]{:S(2)}, u32[]{:S(2)}) collective-permute-start(bf16[168,1024]{1,0:T(8,128)(2,1)} %get-tuple-element.16), channel_id=1, source_target_pairs={{0,224},{32,0},{64,32},{96,64},{128,96},{160,128},{192,160},{224,1... | collective-permute-start | bytes 1032200 | tf_op jit(solution)/shard_map/ppermute | solution.py:203
  9.4 3.0 %pack_plane.1 = bf16[8,152,1024]{2,1,0:T(8,128)(2,1)} custom-call(bf16[2,64,1024]{2,1,0:T(8,128)(2,1)} %bitcast.3, s32[64,4096]{1,0:T(8,128)} %mask.3, f32[64,128]{1,0:T(8,128)} %get-tuple-element.14.own_spec), custom_call_target="tpu_custom_call" | custom-call | tf_op jit(solution)/shard_map/pack_plane/pallas_call | solution.py:226
  12.4 0.0 copy-start.5
  12.4 5.2 %all-to-all-start = ((bf16[8,152,1024]{2,1,0:T(8,128)(2,1)}), bf16[8,152,1024]{2,1,0:T(8,128)(2,1)S(1)}, u32[]{:S(2)}, u32[]{:S(2)}) async-start(bf16[8,152,1024]{2,1,0:T(8,128)(2,1)} %pack_plane.1), calls=%async_computation | async-start | bytes 4980736 | tf_op jit(solution)/shard_map/all_to_all | solution.py:233
  17.6 0.0 collective-permute-done.3
  17.6 0.1 collective-permute-start.4
  17.7 0.0 collective-permute-done.one
  17.7 0.0 copy-start.1
  17.8 2.7 %collective-permute-start.1 = (bf16[136,1024]{1,0:T(8,128)(2,1)S(1)}, bf16[136,1024]{1,0:T(8,128)(2,1)S(1)}, u32[]{:S(2)}, u32[]{:S(2)}) collective-permute-start(bf16[136,1024]{1,0:T(8,128)(2,1)S(1)} %slice.4), channel_id=1, source_target_pairs={{0,224},{32,0},{64,32},{96,64},{128,96},{160,128},{192,160},{224,1... | collective-permute-start | bytes 835592 | tf_op jit(solution)/shard_map/ppermute | solution.py:203
  20.5 6.7 %collective-permute-done.4 = bf16[168,1024]{1,0:T(8,128)(2,1)S(1)} collective-permute-done((bf16[168,1024]{1,0:T(8,128)(2,1)S(1)}, bf16[168,1024]{1,0:T(8,128)(2,1)S(1)}, u32[]{:S(2)}, u32[]{:S(2)}) %collective-permute-start.4) | collective-permute-done | bytes 344096 | tf_op jit(solution)/shard_map/ppermute | solution.py:203
  27.2 0.0 collective-permute-start.5
  27.3 0.0 collective-permute-done.1.two
  27.3 0.0 copy-start.3
  27.3 1.1 %collective-permute-start.6 = (bf16[136,1024]{1,0:T(8,128)(2,1)S(1)}, bf16[136,1024]{1,0:T(8,128)(2,1)S(1)}, u32[]{:S(2)}, u32[]{:S(2)}) collective-permute-start(bf16[136,1024]{1,0:T(8,128)(2,1)S(1)} %collective-permute-done.1.two), channel_id=1, source_target_pairs={{0,192},{32,224},{64,0},{96,32},{128,64},{160,96},{192,128},{224,1... | collective-permute-start | bytes 835592 | tf_op jit(solution)/shard_map/ppermute | solution.py:203
  28.4 0.0 copy-done.5
  28.4 2.9 %collective-permute-start.2 = (bf16[32,1024]{1,0:T(8,128)(2,1)S(1)}, bf16[32,1024]{1,0:T(8,128)(2,1)S(1)}, u32[]{:S(2)}, u32[]{:S(2)}) collective-permute-start(bf16[32,1024]{1,0:T(8,128)(2,1)S(1)} %copy-done.5), channel_id=1, source_target_pairs={{0,192},{32,224},{64,0},{96,32},{128,64},{160,96},{192,128},{224,1... | collective-permute-start | bytes 196616 | tf_op jit(solution)/shard_map/ppermute | solution.py:203
  31.4 4.8 %collective-permute-done.2.two_mask = bf16[32,1024]{1,0:T(8,128)(2,1)S(1)} collective-permute-done((bf16[32,1024]{1,0:T(8,128)(2,1)S(1)}, bf16[32,1024]{1,0:T(8,128)(2,1)S(1)}, u32[]{:S(2)}, u32[]{:S(2)}) %collective-permute-start.2) | collective-permute-done | bytes 65568 | tf_op jit(solution)/shard_map/ppermute | solution.py:203
  36.2 0.0 copy-start.6
  36.2 0.0 collective-permute-done.6.four
  36.2 0.0 copy-start.4
  36.2 0.0 collective-permute-done.5.three
  36.2 0.6 copy-done.6
  36.8 0.1 copy-done.4
  36.9 0.0 copy-start.2
  36.9 0.0 copy-done.1
  36.9 0.0 copy-done.3
  36.9 0.7 copy-done.2
  37.6 3.3 %prepare.1 = (bf16[320,1024]{1,0:T(8,128)(2,1)}, bf16[320,1024]{1,0:T(8,128)(2,1)}, bf16[320,1024]{1,0:T(8,128)(2,1)}, bf16[320,1024]{1,0:T(8,128)(2,1)}, f32[32...) custom-call(f32[1,1024]{1,0:T(1,128)} %source.3, bf16[2,64,1024]{2,1,0:T(8,128)(2,1)} %bitcast.4, ...), custom_call_target="tpu_custom_call" | custom-call | flops 14499999744 | tf_op jit(solution)/shard_map/prepare/pallas_call | solution.py:236
  40.9 7.1 %all-to-all-done.shared = bf16[8,152,1024]{2,1,0:T(8,128)(2,1)S(1)} async-done(((bf16[8,152,1024]{2,1,0:T(8,128)(2,1)}), bf16[8,152,1024]{2,1,0:T(8,128)(2,1)S(1)}, u32[]{:S(2)}, u32[]{:S(2)}) %all-to-all-start) | async-done | bytes 2490400 | tf_op jit(solution)/shard_map/all_to_all | solution.py:233
  48.0 0.0 copy-start
  48.0 1.5 %copy-done = bf16[8,152,1024]{2,1,0:T(8,128)(2,1)} copy-done((bf16[8,152,1024]{2,1,0:T(8,128)(2,1)}, bf16[8,152,1024]{2,1,0:T(8,128)(2,1)S(1)}, u32[]{:S(2)}) %copy-start) | copy-done | bytes 2490392
  49.5 6.6 %absorb.1 = f32[8,1,1152]{2,1,0:T(1,128)} custom-call(bf16[8,152,1024]{2,1,0:T(8,128)(2,1)} %copy-done, bf16[320,1024]{1,0:T(8,128)(2,1)} %get-tuple-element.19.near_re, bf16[320,1024]{1,0:T(8,128)(2,1)} %get-tuple-element.20.near_im, bf16[320,1024]{1,0:T(8,128)(2,1)} %get-tuple-element.21.wt_re, bf16[320,1024]{1,0:T(8,128)(2,1)} %get-tuple-element.22.wt_im, ...), custom_call_target="tpu_custom_call" | custom-call | tf_op jit(solution)/shard_map/absorb/pallas_call | solution.py:248
  56.0 14.7 %all_to_all.15.parts = f32[8,1,1152]{2,1,0:T(1,128)} all-to-all(f32[8,1,1152]{2,1,0:T(1,128)} %absorb.1), channel_id=1, replica_groups=mesh['z'=8,'xl'=2,'y'=4,'xh'=2,'core'=2] {'z'}, dimensions={0} | all-to-all | bytes 73728 | tf_op jit(solution)/shard_map/all_to_all | solution.py:261
  70.7 1.5 %gather_z.1 = f32[32,1,1152]{2,1,0:T(1,128)} custom-call(f32[8,1,1152]{2,1,0:T(1,128)} %all_to_all.15.parts), custom_call_target="tpu_custom_call" | custom-call | tf_op jit(solution)/shard_map/gather_z/pallas_call | solution.py:262
  72.2 16.3 %all_to_all.16.parts = f32[32,1,1152]{2,1,0:T(1,128)} all-to-all(f32[32,1,1152]{2,1,0:T(1,128)} %gather_z.1), channel_id=1, replica_groups=mesh['z'=8,'xl'=2,'y'=4,'xh'=2,'core'=2] {'xl','y','xh','core'}, dimensions={0} | all-to-all | bytes 294912 | tf_op jit(solution)/shard_map/all_to_all | solution.py:269
  88.5 1.7 %finish.1 = (f32[1,1024]{1,0:T(1,128)}, f32[1]{0:T(128)}) custom-call(f32[32,1,1152]{2,1,0:T(1,128)} %all_to_all.16.parts, f32[1,1024]{1,0:T(1,128)} %source.3), custom_call_target="tpu_custom_call" | custom-call | tf_op jit(solution)/shard_map/finish/pallas_call | solution.py:270
  (1 shorter events, 0.0 us)
Async XLA Ops:
  3.0 14.6 %collective-permute-start.3 = (bf16[168,1024]{1,0:T(8,128)(2,1)}, bf16[168,1024]{1,0:T(8,128)(2,1)S(1)}, u32[]{:S(2)}, u32[]{:S(2)}) collective-permute-start(bf16[168,1024]{1,0:T(8,128)(2,1)} %get-tuple-element.18), channel_id=1, source_target_pairs={{0,32},{32,64},{64,96},{96,128},{128,160},{160,192},{192,224},{224... | collective-permute-start | bytes 1032200 | tf_op jit(solution)/shard_map/ppermute | solution.py:203
  5.5 12.3 %collective-permute-start = (bf16[168,1024]{1,0:T(8,128)(2,1)}, bf16[168,1024]{1,0:T(8,128)(2,1)S(1)}, u32[]{:S(2)}, u32[]{:S(2)}) collective-permute-start(bf16[168,1024]{1,0:T(8,128)(2,1)} %get-tuple-element.16), channel_id=1, source_target_pairs={{0,224},{32,0},{64,32},{96,64},{128,96},{160,128},{192,160},{224,1... | collective-permute-start | bytes 1032200 | tf_op jit(solution)/shard_map/ppermute | solution.py:203
  12.4 16.0 %copy-start.5 = (bf16[32,1024]{1,0:T(8,128)(2,1)S(1)}, bf16[32,1024]{1,0:T(8,128)(2,1)}, u32[]{:S(2)}) copy-start(bf16[32,1024]{1,0:T(8,128)(2,1)} %get-tuple-element.17) | copy-start | bytes 196612
  12.4 35.6 %all-to-all-start = ((bf16[8,152,1024]{2,1,0:T(8,128)(2,1)}), bf16[8,152,1024]{2,1,0:T(8,128)(2,1)S(1)}, u32[]{:S(2)}, u32[]{:S(2)}) async-start(bf16[8,152,1024]{2,1,0:T(8,128)(2,1)} %pack_plane.1), calls=%async_computation | async-start | bytes 4980736 | tf_op jit(solution)/shard_map/all_to_all | solution.py:233
  17.6 9.6 %collective-permute-start.4 = (bf16[168,1024]{1,0:T(8,128)(2,1)S(1)}, bf16[168,1024]{1,0:T(8,128)(2,1)S(1)}, u32[]{:S(2)}, u32[]{:S(2)}) collective-permute-start(bf16[168,1024]{1,0:T(8,128)(2,1)S(1)} %collective-permute-done.3), channel_id=1, source_target_pairs={{0,32},{32,64},{64,96},{96,128},{128,160},{160,192},{192,224},{224... | collective-permute-start | bytes 1032200 | tf_op jit(solution)/shard_map/ppermute | solution.py:203
  17.7 19.2 %copy-start.1 = (bf16[168,1024]{1,0:T(8,128)(2,1)}, bf16[168,1024]{1,0:T(8,128)(2,1)S(1)}, u32[]{:S(2)}) copy-start(bf16[168,1024]{1,0:T(8,128)(2,1)S(1)} %collective-permute-done.one) | copy-start | bytes 1032196
  17.8 9.5 %collective-permute-start.1 = (bf16[136,1024]{1,0:T(8,128)(2,1)S(1)}, bf16[136,1024]{1,0:T(8,128)(2,1)S(1)}, u32[]{:S(2)}, u32[]{:S(2)}) collective-permute-start(bf16[136,1024]{1,0:T(8,128)(2,1)S(1)} %slice.4), channel_id=1, source_target_pairs={{0,224},{32,0},{64,32},{96,64},{128,96},{160,128},{192,160},{224,1... | collective-permute-start | bytes 835592 | tf_op jit(solution)/shard_map/ppermute | solution.py:203
  27.2 8.9 %collective-permute-start.5 = (bf16[168,1024]{1,0:T(8,128)(2,1)S(1)}, bf16[168,1024]{1,0:T(8,128)(2,1)S(1)}, u32[]{:S(2)}, u32[]{:S(2)}) collective-permute-start(bf16[168,1024]{1,0:T(8,128)(2,1)S(1)} %collective-permute-done.4), channel_id=1, source_target_pairs={{0,32},{32,64},{64,96},{96,128},{128,160},{160,192},{192,224},{224... | collective-permute-start | bytes 1032200 | tf_op jit(solution)/shard_map/ppermute | solution.py:203
  27.3 9.7 %copy-start.3 = (bf16[136,1024]{1,0:T(8,128)(2,1)}, bf16[136,1024]{1,0:T(8,128)(2,1)S(1)}, u32[]{:S(2)}) copy-start(bf16[136,1024]{1,0:T(8,128)(2,1)S(1)} %collective-permute-done.1.two) | copy-start | bytes 835588
  27.3 8.9 %collective-permute-start.6 = (bf16[136,1024]{1,0:T(8,128)(2,1)S(1)}, bf16[136,1024]{1,0:T(8,128)(2,1)S(1)}, u32[]{:S(2)}, u32[]{:S(2)}) collective-permute-start(bf16[136,1024]{1,0:T(8,128)(2,1)S(1)} %collective-permute-done.1.two), channel_id=1, source_target_pairs={{0,192},{32,224},{64,0},{96,32},{128,64},{160,96},{192,128},{224,1... | collective-permute-start | bytes 835592 | tf_op jit(solution)/shard_map/ppermute | solution.py:203
  28.4 7.7 %collective-permute-start.2 = (bf16[32,1024]{1,0:T(8,128)(2,1)S(1)}, bf16[32,1024]{1,0:T(8,128)(2,1)S(1)}, u32[]{:S(2)}, u32[]{:S(2)}) collective-permute-start(bf16[32,1024]{1,0:T(8,128)(2,1)S(1)} %copy-done.5), channel_id=1, source_target_pairs={{0,192},{32,224},{64,0},{96,32},{128,64},{160,96},{192,128},{224,1... | collective-permute-start | bytes 196616 | tf_op jit(solution)/shard_map/ppermute | solution.py:203
  36.2 0.6 copy-start.6
  36.2 0.7 copy-start.4
  36.9 0.7 copy-start.2
  48.0 1.5 %copy-start = (bf16[8,152,1024]{2,1,0:T(8,128)(2,1)}, bf16[8,152,1024]{2,1,0:T(8,128)(2,1)S(1)}, u32[]{:S(2)}) copy-start(bf16[8,152,1024]{2,1,0:T(8,128)(2,1)S(1)} %all-to-all-done.shared) | copy-start | bytes 7471108

commit v5 on v4

--- a/solution.py
+++ b/solution.py
@@ -39,7 +39,7 @@
 
 
 SPEC, IMAG, REAL, MASK, MASKED = 0, 8, 72, 136, 168
-PREPARE = 14_500_000_000
+PREPARE = 16_500_000_000
 
 
 def window(mask, at):
@@ -47,9 +47,9 @@
     return mask[:, pl.ds(start, WIDE)].astype(f32)
 
 
-def put_mask(ref, at, part):
-    ref[at : at + 32, 0:512] = part[0:32]
-    ref[at : at + 32, 512:1024] = part[32:64]
+def put_mask(ref, part):
+    ref[:, 0:512] = part[0:32]
+    ref[:, 512:1024] = part[32:64]
 
 
 def take_mask(ref, at):
@@ -58,11 +58,6 @@
     ).astype(f32)
 
 
-def put_spectra(ref, at, spectra):
-    for g in range(8):
-        ref[at : at + 8, 128 * g : 128 * (g + 1)] = spectra[8 * g : 8 * (g + 1)]
-
-
 def take_spectra(ref, at):
     return jnp.concatenate(
         [ref[at : at + 8, 128 * g : 128 * (g + 1)].astype(f32) for g in range(8)],
@@ -70,8 +65,26 @@
     )
 
 
-def pack_line(green, mask, spec_row, near, far, two, own_mask, own_spec):
+def pack(
+    green, mask_hbm, spec_row, near, far, two, shared, own_mask, own_spec,
+    mask, masks, spec8, extra, sems
+):
     z = lax.axis_index("z")
+    used = []
+
+    def copy(src, dst):
+        done = pltpu.make_async_copy(src, dst, sems.at[len(used)])
+        done.start()
+        used.append(done)
+        return done
+
+    loaded = copy(mask_hbm, mask)
+    for ref in (near, far):
+        copy(green.at[1], ref.at[IMAG : IMAG + ROWS])
+        copy(green.at[0], ref.at[REAL : REAL + ROWS])
+    for q in range(NQ):
+        copy(green.at[0], shared.at[q, 0:64])
+        copy(green.at[1], shared.at[q, 64:128])
     row = spec_row[...]
     col = nt(identity(ROWS), row)
     lane = lax.broadcasted_iota(jnp.int32, (ROWS, 128), 1)
@@ -80,34 +93,32 @@
     )
     own_spec[0:2, 64:128] = row.astype(f32)
     spectra = own_spec[...].astype(bf16)
-    for ref, u in ((near, 1), (far, -3)):
-        put_spectra(ref, SPEC, spectra)
-        ref[IMAG : IMAG + ROWS, :] = green[1]
-        ref[REAL : REAL + ROWS, :] = green[0]
-        put_mask(ref, MASK, window(mask, z - u).astype(bf16))
-    put_mask(two, 0, window(mask, z - 2).astype(bf16))
-    own_mask[...] = window(mask, z).astype(bf16)
-
-
-def pack_plane(green, mask, own_spec, shared):
-    z = lax.axis_index("z")
-    spectra = own_spec[...].astype(bf16)
+    for g in range(8):
+        spec8[:, 128 * g : 128 * (g + 1)] = spectra[8 * g : 8 * (g + 1)]
+    copy(spec8, near.at[SPEC : SPEC + 8])
+    copy(spec8, far.at[SPEC : SPEC + 8])
+    loaded.wait()
+    for k, (u, ref) in enumerate(((1, near), (-3, far), (2, two))):
+        put_mask(masks.at[k], window(mask, z - u).astype(bf16))
+        copy(masks.at[k], two if ref is two else ref.at[MASK : MASK + 32])
     wide = [window(mask, z + u) for u in OFFSETS]
     for q in range(NQ):
-        ref = shared.at[q]
-        ref[0:64, :] = green[0]
-        ref[64:128, :] = green[1]
         part = jnp.concatenate(
             [w[:, ROWS * q : ROWS * (q + 1)] for w in wide], axis=1
         ).astype(bf16)
         for g in range(4):
-            ref[128:144, 256 * g : 256 * (g + 1)] = part[16 * g : 16 * (g + 1)]
-        put_spectra(ref, 144, spectra)
+            extra[q, 0:16, 256 * g : 256 * (g + 1)] = part[16 * g : 16 * (g + 1)]
+        for g in range(8):
+            extra[q, 16:24, 128 * g : 128 * (g + 1)] = spectra[8 * g : 8 * (g + 1)]
+        copy(extra.at[q], shared.at[q, 128:152])
+    own_mask[...] = window(mask, z).astype(bf16)
+    for done in used[1:]:
+        done.wait()
 
 
 def prepare(
     source, green, own_mask, own_spec, one, two, two_mask, three, four,
-    near_re, near_im, wt_re, wt_im, weight, spec_re, spec_im
+    wt_re, wt_im, weight, spec_re, spec_im
 ):
     scale = source[...]
     real, imag = slice(REAL, REAL + ROWS), slice(IMAG, IMAG + ROWS)
@@ -125,8 +136,6 @@
     ]
     for k, (re, im) in enumerate(held):
         rows = slice(ROWS * k, ROWS * (k + 1))
-        near_re[rows, :] = re
-        near_im[rows, :] = im
         wt_re[rows, :] = (scale * re.astype(f32)).astype(bf16)
         wt_im[rows, :] = (scale * im.astype(f32)).astype(bf16)
         weight[rows, :] = masks[k]
@@ -135,19 +144,30 @@
 
 
 def absorb(
-    shared, near_re, near_im, wt_re, wt_im, weight, spec_re, spec_im,
-    out, far_re, far_im, far_spec, back
+    shared, green, one, two, three, four, wt_re, wt_im, weight, spec_re, spec_im,
+    out, far_re, far_im, extra, far_spec, back, sems
 ):
+    copies = []
     for q in range(NQ):
         rows = slice(ROWS * q, ROWS * (q + 1))
-        ref = shared.at[q]
-        far_re[rows, :] = ref[0:64, :]
-        far_im[rows, :] = ref[64:128, :]
+        for i, (src, dst) in enumerate(
+            (
+                (shared.at[q, 0:64], far_re.at[rows]),
+                (shared.at[q, 64:128], far_im.at[rows]),
+                (shared.at[q, 128:152], extra.at[q]),
+            )
+        ):
+            copies.append(pltpu.make_async_copy(src, dst, sems.at[3 * q + i]))
+            copies[-1].start()
+    for done in copies:
+        done.wait()
+    for q in range(NQ):
+        rows = slice(ROWS * q, ROWS * (q + 1))
         for g in range(4):
-            back[ROWS * q + 16 * g : ROWS * q + 16 * (g + 1), :] = ref[
-                128:144, 256 * g : 256 * (g + 1)
+            back[ROWS * q + 16 * g : ROWS * q + 16 * (g + 1), :] = extra[
+                q, 0:16, 256 * g : 256 * (g + 1)
             ]
-        far_spec[0:2, rows] = ref[144:152, 0:128].astype(f32)[0:2, 64:128]
+        far_spec[0:2, rows] = extra[q, 16:24, 0:128].astype(f32)[0:2, 64:128]
     behind = nt(identity(4 * ROWS), back[...])
     counts = weight[...] + jnp.concatenate(
         [jnp.zeros((ROWS, WIDE), f32), behind], axis=0
@@ -164,11 +184,15 @@
     r_im = (counts * x_im.astype(bf16).astype(f32)).astype(bf16)
     y_re = nn(r_re, g_re) - nn(r_im, g_im)
     y_im = nn(r_re, g_im) + nn(r_im, g_re)
-    total = -jnp.sum(
-        near_re[...].astype(f32) * y_re + near_im[...].astype(f32) * y_im,
-        axis=0,
-        keepdims=True,
-    )
+    real, imag = slice(REAL, REAL + ROWS), slice(IMAG, IMAG + ROWS)
+    held = [(green[0], green[1])]
+    for ref in (one, two, three, four):
+        held.append((ref[real, :], ref[imag, :]))
+    total = jnp.zeros((ROWS, CELLS), f32)
+    for k, (re, im) in enumerate(held):
+        rows = slice(ROWS * k, ROWS * (k + 1))
+        total = total + (re.astype(f32) * y_re[rows] + im.astype(f32) * y_im[rows])
+    total = -jnp.sum(total, axis=0, keepdims=True)
     out[:, :, 0:CELLS] = jnp.broadcast_to(total[None], (NZ, 1, CELLS))
     out[:, :, CELLS:LONG] = jnp.broadcast_to(mis[None], (NZ, 1, 128))
 
@@ -207,39 +231,41 @@
     g = green[0]
     vmem = pl.BlockSpec(memory_space=pltpu.VMEM)
     tall = ROWS * (1 + len(OFFSETS))
-    near, far, two_mask, own_mask, own_spec = pl.pallas_call(
-        pack_line,
+    hbm = pl.BlockSpec(memory_space=pl.ANY)
+    near, far, two_mask, shared, own_mask, own_spec = pl.pallas_call(
+        pack,
         out_shape=[
             shape(bf16, MASKED, CELLS),
             shape(bf16, MASKED, CELLS),
             shape(bf16, 32, CELLS),
+            shape(bf16, NQ, SHARED, CELLS),
             shape(bf16, ROWS, WIDE),
             shape(f32, ROWS, 128),
         ],
-        in_specs=[vmem] * 3,
-        out_specs=[vmem] * 5,
-        name="pack_line",
+        in_specs=[hbm, hbm, vmem],
+        out_specs=[hbm] * 4 + [vmem] * 2,
+        scratch_shapes=[
+            pltpu.VMEM((ROWS, NZ * WIDE), jnp.int32),
+            pltpu.VMEM((3, 32, CELLS), bf16),
+            pltpu.VMEM((8, CELLS), bf16),
+            pltpu.VMEM((NQ, 24, CELLS), bf16),
+            pltpu.SemaphoreType.DMA((34,)),
+        ],
+        name="pack",
     )(g, pair_mask, spectra[0])
-    three = from_z(from_z(from_z(far, -1), -1), -1)
+    three = from_z(from_z(far, -2), -1)
     one = from_z(near, 1)
     two_mask = from_z(two_mask, 2)
-    shared = pl.pallas_call(
-        pack_plane,
-        out_shape=shape(bf16, NQ, SHARED, CELLS),
-        in_specs=[vmem] * 3,
-        out_specs=vmem,
-        name="pack_plane",
-    )(g, pair_mask, own_spec)
     shared = lax.all_to_all(shared, PLANE, 0, 0, tiled=True)
     two = from_z(one[:MASK], 1)
     four = from_z(two, 2)
     ready = pl.pallas_call(
         prepare,
-        out_shape=[shape(bf16, tall, CELLS)] * 4
+        out_shape=[shape(bf16, tall, CELLS)] * 2
         + [shape(f32, tall, WIDE)]
         + [shape(f32, tall, 128)] * 2,
         in_specs=[vmem] * 9,
-        out_specs=[vmem] * 7,
+        out_specs=[vmem] * 5,
         cost_estimate=pl.CostEstimate(
             flops=PREPARE, transcendentals=0, bytes_accessed=0
         ),
@@ -248,16 +274,18 @@
     part = pl.pallas_call(
         absorb,
         out_shape=shape(f32, NZ, 1, LONG),
-        in_specs=[vmem] * 8,
+        in_specs=[hbm] + [vmem] * 10,
         out_specs=vmem,
         scratch_shapes=[
             pltpu.VMEM((WIDE, CELLS), bf16),
             pltpu.VMEM((WIDE, CELLS), bf16),
+            pltpu.VMEM((NQ, 24, CELLS), bf16),
             pltpu.VMEM((8, WIDE), f32),
             pltpu.VMEM((WIDE, 4 * ROWS), bf16),
+            pltpu.SemaphoreType.DMA((3 * NQ,)),
         ],
         name="absorb",
-    )(shared, *ready)
+    )(shared, g, one, two, three, four, *ready)
     part = lax.all_to_all(part, "z", 0, 0, tiled=True)
     part = pl.pallas_call(
         gather_z,

time: 90.7 us -> 171 us (1.89)
  Pallas kernels: 18.4 us -> 96.1 us
  waiting for transfers between devices: 18.6 us -> 20.6 us
  starting transfers between devices: 18.6 us -> 20.5 us
    pallas_call x4 -> x3, Pallas kernels: 15.2 us -> 92.9 us  [the longest x1 82.1 us: local(): pl.pallas_call(pack, out_shape=[shape(bf16, MASKED, CELLS), shape(bf16, M...]
    ppermute x7 -> x6, waiting for transfers between devices: 11.6 us -> 20.6 us  [from_z(): return lax.ppermute(array, 'z', [(z, (z - u) % NZ) for z in range(NZ)])]
    all_to_all x1, waiting for transfers between devices: 7.06 us -> 0.01 us  [local(): shared = lax.all_to_all(shared, PLANE, 0, 0, tiled=True)]
    ppermute x7 -> x6, starting transfers between devices: 13.3 us -> 15.3 us  [from_z(): return lax.ppermute(array, 'z', [(z, (z - u) % NZ) for z in range(NZ)])]
  transfers between devices with their start and end apart: 8 -> 7, of which waited for: 3 -> 3; matrix products, arithmetic and copies ran while one was open for 0% -> 0% of each run, Pallas kernels for 7% -> 2%
where the time goes in v5:
time: 171 us; the launch traced here: 170 us
  Pallas kernels  96.1 us (56%)
  blocking collectives  30.3 us (18%)
  waiting for transfers between devices  20.6 us (12%)
  starting transfers between devices  20.5 us (12%)
  local copies, waits for them, and re-layouts  2.33 us (1%)
    pallas_call x1, Pallas kernels, local(): pl.pallas_call(pack, out_shape=[shape(bf16, MASKED, CELLS), shape(bf16, M...  82.1 us
    ppermute x6, waiting for transfers between devices, from_z(): return lax.ppermute(array, 'z', [(z, (z - u) % NZ) for z in range(NZ)])  20.6 us
    all_to_all x1, blocking collectives, local(): part = lax.all_to_all(part, PLANE + FREQ, 0, 0, tiled=True)  17.2 us
    ppermute x6, starting transfers between devices, from_z(): return lax.ppermute(array, 'z', [(z, (z - u) % NZ) for z in range(NZ)])  15.3 us
    all_to_all x1, blocking collectives, local(): part = lax.all_to_all(part, 'z', 0, 0, tiled=True)  13.1 us
    pallas_call x1, Pallas kernels, local(): pl.pallas_call(absorb, out_shape=shape(f32, NZ, 1, LONG), in_specs=[hbm]...  7.83 us
    all_to_all x1, starting transfers between devices, local(): shared = lax.all_to_all(shared, PLANE, 0, 0, tiled=True)  5.25 us
  transfers between devices with their start and end apart: 7, of which 3 were waited for; matrix products, arithmetic and copies ran while one was open for 0% of the time, Pallas kernels for 2%

profile of v5, /device:TPU:1, one launch (start us, length us, event | category | flops | bytes accessed | tf_op | source)
XLA Modules:
  0.0 170.5 jit_solution(8106656694950226488)
XLA Ops:
  0.6 82.1 %pack.1 = (bf16[168,1024]{1,0:T(8,128)(2,1)}, bf16[168,1024]{1,0:T(8,128)(2,1)}, bf16[32,1024]{1,0:T(8,128)(2,1)}, bf16[8,152,1024]{2,1,0:T(8,128)(2,1)}, bf16[64,512]{1,0:T(8,128)(2,1)}, /*index=5*/f32[64,128]{1,0:T(8,128)}) custom-call(bf16[2,64,1024]{2,1,0:T(8,128)(2,1)} %bitcast.2, s32[64,4096]{1,0:T(8,128)} %mask_hbm.1, bf16[2,64]{1,0:T(2,128)(2,1)} %bitcast.5), custom_call_target="tpu_custom_call" | custom-call | tf_op jit(solution)/shard_map/pack/pallas_call | solution.py:235
  82.8 6.5 %collective-permute-start = (bf16[168,1024]{1,0:T(8,128)(2,1)}, bf16[168,1024]{1,0:T(8,128)(2,1)S(1)}, u32[]{:S(2)}, u32[]{:S(2)}) collective-permute-start(bf16[168,1024]{1,0:T(8,128)(2,1)} %get-tuple-element.14), channel_id=1, source_target_pairs={{0,224},{32,0},{64,32},{96,64},{128,96},{160,128},{192,160},{224,1... | collective-permute-start | bytes 1032200 | tf_op jit(solution)/shard_map/ppermute | solution.py:227
  89.3 0.0 collective-permute-start.2
  89.3 0.0 copy-start.5
  89.3 5.2 %all-to-all-start = ((bf16[8,152,1024]{2,1,0:T(8,128)(2,1)}), bf16[8,152,1024]{2,1,0:T(8,128)(2,1)S(1)}, u32[]{:S(2)}, u32[]{:S(2)}) async-start(bf16[8,152,1024]{2,1,0:T(8,128)(2,1)} %get-tuple-element.13), calls=%async_computation | async-start | bytes 4980736 | tf_op jit(solution)/shard_map/all_to_all | solution.py:259
  94.5 1.8 %collective-permute-done.one = bf16[168,1024]{1,0:T(8,128)(2,1)S(1)} collective-permute-done((bf16[168,1024]{1,0:T(8,128)(2,1)}, bf16[168,1024]{1,0:T(8,128)(2,1)S(1)}, u32[]{:S(2)}, u32[]{:S(2)}) %collective-permute-start) | collective-permute-done | bytes 344096 | tf_op jit(solution)/shard_map/ppermute | solution.py:227
  96.3 0.0 copy-start.1
  96.3 3.4 %collective-permute-start.1 = (bf16[136,1024]{1,0:T(8,128)(2,1)S(1)}, bf16[136,1024]{1,0:T(8,128)(2,1)S(1)}, u32[]{:S(2)}, u32[]{:S(2)}) collective-permute-start(bf16[136,1024]{1,0:T(8,128)(2,1)S(1)} %slice.4), channel_id=1, source_target_pairs={{0,224},{32,0},{64,32},{96,64},{128,96},{160,128},{192,160},{224,1... | collective-permute-start | bytes 835592 | tf_op jit(solution)/shard_map/ppermute | solution.py:227
  99.7 6.3 %collective-permute-done.2 = bf16[168,1024]{1,0:T(8,128)(2,1)} collective-permute-done((bf16[168,1024]{1,0:T(8,128)(2,1)}, bf16[168,1024]{1,0:T(8,128)(2,1)}, u32[]{:S(2)}, u32[]{:S(2)}) %collective-permute-start.2) | collective-permute-done | bytes 344096 | tf_op jit(solution)/shard_map/ppermute | solution.py:227
  106.0 0.0 collective-permute-start.3
  106.0 0.0 collective-permute-done.1.two
  106.0 0.0 copy-start.3
  106.0 3.2 %collective-permute-start.4 = (bf16[136,1024]{1,0:T(8,128)(2,1)S(1)}, bf16[136,1024]{1,0:T(8,128)(2,1)S(1)}, u32[]{:S(2)}, u32[]{:S(2)}) collective-permute-start(bf16[136,1024]{1,0:T(8,128)(2,1)S(1)} %collective-permute-done.1.two), channel_id=1, source_target_pairs={{0,192},{32,224},{64,0},{96,32},{128,64},{160,96},{192,128},{224,1... | collective-permute-start | bytes 835592 | tf_op jit(solution)/shard_map/ppermute | solution.py:227
  109.2 0.0 copy-done.5
  109.2 2.2 %collective-permute-start.5 = (bf16[32,1024]{1,0:T(8,128)(2,1)S(1)}, bf16[32,1024]{1,0:T(8,128)(2,1)S(1)}, u32[]{:S(2)}, u32[]{:S(2)}) collective-permute-start(bf16[32,1024]{1,0:T(8,128)(2,1)S(1)} %copy-done.5), channel_id=1, source_target_pairs={{0,192},{32,224},{64,0},{96,32},{128,64},{160,96},{192,128},{224,1... | collective-permute-start | bytes 196616 | tf_op jit(solution)/shard_map/ppermute | solution.py:227
  111.4 12.6 %collective-permute-done.5.two_mask = bf16[32,1024]{1,0:T(8,128)(2,1)S(1)} collective-permute-done((bf16[32,1024]{1,0:T(8,128)(2,1)S(1)}, bf16[32,1024]{1,0:T(8,128)(2,1)S(1)}, u32[]{:S(2)}, u32[]{:S(2)}) %collective-permute-start.5) | collective-permute-done | bytes 65568 | tf_op jit(solution)/shard_map/ppermute | solution.py:227
  124.0 0.0 copy-start.6
  124.0 0.0 collective-permute-done.3.three
  124.0 0.0 copy-start.2
  124.0 0.0 collective-permute-done.4.four
  124.0 0.0 copy-start.4
  124.0 0.8 copy-done.4
  124.7 0.0 copy-done.6
  124.7 0.0 copy-done.1
  124.8 0.0 copy-done.3
  124.8 0.1 copy-done.2
  124.8 2.9 %prepare.1 = (bf16[320,1024]{1,0:T(8,128)(2,1)}, bf16[320,1024]{1,0:T(8,128)(2,1)}, f32[320,512]{1,0:T(8,128)}, f32[320,128]{1,0:T(8,128)}, f32[320,128]{1,0:T(8,128)}) custom-call(f32[1,1024]{1,0:T(1,128)} %source.3, bf16[2,64,1024]{2,1,0:T(8,128)(2,1)} %bitcast.3, bf16[64,512]{1,0:T(8,128)(2,1)} %get-tuple-element.16.own_mask, ...), custom_call_target="tpu_custom_call" | custom-call | flops 16499999744 | tf_op jit(solution)/shard_map/prepare/pallas_call | solution.py:262
  127.8 0.0 all-to-all-done.shared
  127.8 0.0 copy-start
  127.8 1.5 copy-done
  129.2 7.8 %absorb.1 = f32[8,1,1152]{2,1,0:T(1,128)} custom-call(bf16[8,152,1024]{2,1,0:T(8,128)(2,1)} %copy-done, bf16[2,64,1024]{2,1,0:T(8,128)(2,1)} %bitcast.4, bf16[168,1024]{1,0:T(8,128)(2,1)} %copy-done.1, bf16[136,1024]{1,0:T(8,128)(2,1)} %copy-done.3, bf16[168,1024]{1,0:T(8,128)(2,1)} %copy-done.2, bf16[136,1024]{1,0:T(8,128)(2,1)} %copy-done.4, ...), custom_call_target="tpu_custom_call" | custom-call | tf_op jit(solution)/shard_map/absorb/pallas_call | solution.py:274
  137.1 13.1 %all_to_all.15.parts = f32[8,1,1152]{2,1,0:T(1,128)} all-to-all(f32[8,1,1152]{2,1,0:T(1,128)} %absorb.1), channel_id=1, replica_groups=mesh['z'=8,'xl'=2,'y'=4,'xh'=2,'core'=2] {'z'}, dimensions={0} | all-to-all | bytes 73728 | tf_op jit(solution)/shard_map/all_to_all | solution.py:289
  150.2 1.5 gather_z.1
  151.6 17.2 %all_to_all.16.parts = f32[32,1,1152]{2,1,0:T(1,128)} all-to-all(f32[32,1,1152]{2,1,0:T(1,128)} %gather_z.1), channel_id=1, replica_groups=mesh['z'=8,'xl'=2,'y'=4,'xh'=2,'core'=2] {'xl','y','xh','core'}, dimensions={0} | all-to-all | bytes 294912 | tf_op jit(solution)/shard_map/all_to_all | solution.py:297
  168.8 1.7 finish.1
  (1 shorter events, 0.0 us)
Async XLA Ops:
  82.8 13.5 %collective-permute-start = (bf16[168,1024]{1,0:T(8,128)(2,1)}, bf16[168,1024]{1,0:T(8,128)(2,1)S(1)}, u32[]{:S(2)}, u32[]{:S(2)}) collective-permute-start(bf16[168,1024]{1,0:T(8,128)(2,1)} %get-tuple-element.14), channel_id=1, source_target_pairs={{0,224},{32,0},{64,32},{96,64},{128,96},{160,128},{192,160},{224,1... | collective-permute-start | bytes 1032200 | tf_op jit(solution)/shard_map/ppermute | solution.py:227
  89.3 16.7 %collective-permute-start.2 = (bf16[168,1024]{1,0:T(8,128)(2,1)}, bf16[168,1024]{1,0:T(8,128)(2,1)}, u32[]{:S(2)}, u32[]{:S(2)}) collective-permute-start(bf16[168,1024]{1,0:T(8,128)(2,1)} %get-tuple-element.15), channel_id=1, source_target_pairs={{0,64},{32,96},{64,128},{96,160},{128,192},{160,224},{192,0},{224,... | collective-permute-start | bytes 1032200 | tf_op jit(solution)/shard_map/ppermute | solution.py:227
  89.3 20.0 %copy-start.5 = (bf16[32,1024]{1,0:T(8,128)(2,1)S(1)}, bf16[32,1024]{1,0:T(8,128)(2,1)}, u32[]{:S(2)}) copy-start(bf16[32,1024]{1,0:T(8,128)(2,1)} %get-tuple-element.18) | copy-start | bytes 196612
  89.3 38.5 %all-to-all-start = ((bf16[8,152,1024]{2,1,0:T(8,128)(2,1)}), bf16[8,152,1024]{2,1,0:T(8,128)(2,1)S(1)}, u32[]{:S(2)}, u32[]{:S(2)}) async-start(bf16[8,152,1024]{2,1,0:T(8,128)(2,1)} %get-tuple-element.13), calls=%async_computation | async-start | bytes 4980736 | tf_op jit(solution)/shard_map/all_to_all | solution.py:259
  96.3 28.4 %copy-start.1 = (bf16[168,1024]{1,0:T(8,128)(2,1)}, bf16[168,1024]{1,0:T(8,128)(2,1)S(1)}, u32[]{:S(2)}) copy-start(bf16[168,1024]{1,0:T(8,128)(2,1)S(1)} %collective-permute-done.one) | copy-start | bytes 1032196
  96.3 9.7 %collective-permute-start.1 = (bf16[136,1024]{1,0:T(8,128)(2,1)S(1)}, bf16[136,1024]{1,0:T(8,128)(2,1)S(1)}, u32[]{:S(2)}, u32[]{:S(2)}) collective-permute-start(bf16[136,1024]{1,0:T(8,128)(2,1)S(1)} %slice.4), channel_id=1, source_target_pairs={{0,224},{32,0},{64,32},{96,64},{128,96},{160,128},{192,160},{224,1... | collective-permute-start | bytes 835592 | tf_op jit(solution)/shard_map/ppermute | solution.py:227
  106.0 18.0 %collective-permute-start.3 = (bf16[168,1024]{1,0:T(8,128)(2,1)}, bf16[168,1024]{1,0:T(8,128)(2,1)S(1)}, u32[]{:S(2)}, u32[]{:S(2)}) collective-permute-start(bf16[168,1024]{1,0:T(8,128)(2,1)} %collective-permute-done.2), channel_id=1, source_target_pairs={{0,32},{32,64},{64,96},{96,128},{128,160},{160,192},{192,224},{224... | collective-permute-start | bytes 1032200 | tf_op jit(solution)/shard_map/ppermute | solution.py:227
  106.0 18.7 %copy-start.3 = (bf16[136,1024]{1,0:T(8,128)(2,1)}, bf16[136,1024]{1,0:T(8,128)(2,1)S(1)}, u32[]{:S(2)}) copy-start(bf16[136,1024]{1,0:T(8,128)(2,1)S(1)} %collective-permute-done.1.two) | copy-start | bytes 835588
  106.0 18.0 %collective-permute-start.4 = (bf16[136,1024]{1,0:T(8,128)(2,1)S(1)}, bf16[136,1024]{1,0:T(8,128)(2,1)S(1)}, u32[]{:S(2)}, u32[]{:S(2)}) collective-permute-start(bf16[136,1024]{1,0:T(8,128)(2,1)S(1)} %collective-permute-done.1.two), channel_id=1, source_target_pairs={{0,192},{32,224},{64,0},{96,32},{128,64},{160,96},{192,128},{224,1... | collective-permute-start | bytes 835592 | tf_op jit(solution)/shard_map/ppermute | solution.py:227
  109.2 14.7 %collective-permute-start.5 = (bf16[32,1024]{1,0:T(8,128)(2,1)S(1)}, bf16[32,1024]{1,0:T(8,128)(2,1)S(1)}, u32[]{:S(2)}, u32[]{:S(2)}) collective-permute-start(bf16[32,1024]{1,0:T(8,128)(2,1)S(1)} %copy-done.5), channel_id=1, source_target_pairs={{0,192},{32,224},{64,0},{96,32},{128,64},{160,96},{192,128},{224,1... | collective-permute-start | bytes 196616 | tf_op jit(solution)/shard_map/ppermute | solution.py:227
  124.0 0.8 copy-start.6
  124.0 0.8 copy-start.2
  124.0 0.8 copy-start.4
  127.8 1.5 copy-start

commit v6 on v5

--- a/solution.py
+++ b/solution.py
@@ -38,7 +38,7 @@
     return (down == across).astype(f32).astype(bf16)
 
 
-SPEC, IMAG, REAL, MASK, MASKED = 0, 8, 72, 136, 168
+SPEC, IMAG, REAL, MASK, NEXT, FULL = 0, 8, 72, 136, 168, 200
 PREPARE = 16_500_000_000
 
 
@@ -66,8 +66,8 @@
 
 
 def pack(
-    green, mask_hbm, spec_row, near, far, two, shared, own_mask, own_spec,
-    mask, masks, spec8, extra, sems
+    green_hbm, mask_hbm, spec_row, near, far, shared, own_mask, own_spec,
+    green, mask, masks, spec8, extra, sems
 ):
     z = lax.axis_index("z")
     used = []
@@ -78,7 +78,9 @@
         used.append(done)
         return done
 
+    held = copy(green_hbm, green)
     loaded = copy(mask_hbm, mask)
+    held.wait()
     for ref in (near, far):
         copy(green.at[1], ref.at[IMAG : IMAG + ROWS])
         copy(green.at[0], ref.at[REAL : REAL + ROWS])
@@ -98,9 +100,9 @@
     copy(spec8, near.at[SPEC : SPEC + 8])
     copy(spec8, far.at[SPEC : SPEC + 8])
     loaded.wait()
-    for k, (u, ref) in enumerate(((1, near), (-3, far), (2, two))):
+    for k, (u, ref, at) in enumerate(((1, near, NEXT), (2, near, MASK), (-3, far, MASK))):
         put_mask(masks.at[k], window(mask, z - u).astype(bf16))
-        copy(masks.at[k], two if ref is two else ref.at[MASK : MASK + 32])
+        copy(masks.at[k], ref.at[at : at + 32])
     wide = [window(mask, z + u) for u in OFFSETS]
     for q in range(NQ):
         part = jnp.concatenate(
@@ -112,27 +114,26 @@
             extra[q, 16:24, 128 * g : 128 * (g + 1)] = spectra[8 * g : 8 * (g + 1)]
         copy(extra.at[q], shared.at[q, 128:152])
     own_mask[...] = window(mask, z).astype(bf16)
-    for done in used[1:]:
+    for done in used[2:]:
         done.wait()
 
 
 def prepare(
-    source, green, own_mask, own_spec, one, two, two_mask, three, four,
+    source, green, own_mask, own_spec, one, two, three,
     wt_re, wt_im, weight, spec_re, spec_im
 ):
     scale = source[...]
     real, imag = slice(REAL, REAL + ROWS), slice(IMAG, IMAG + ROWS)
     us = [own_spec[...]]
     held = [(green[0], green[1])]
-    for ref in (one, two, three, four):
+    for ref in (one, two, three):
         us.append(take_spectra(ref, SPEC))
         held.append((ref[real, :], ref[imag, :]))
     masks = [
         own_mask[...].astype(f32),
-        take_mask(one, MASK),
-        take_mask(two_mask, 0),
+        take_mask(one, NEXT),
+        take_mask(two, MASK),
         take_mask(three, MASK),
-        jnp.zeros((ROWS, WIDE), f32),
     ]
     for k, (re, im) in enumerate(held):
         rows = slice(ROWS * k, ROWS * (k + 1))
@@ -144,8 +145,9 @@
 
 
 def absorb(
-    shared, green, one, two, three, four, wt_re, wt_im, weight, spec_re, spec_im,
-    out, far_re, far_im, extra, far_spec, back, sems
+    shared, source, green, one, two, three, four,
+    near_re, near_im, weight, spec_re, spec_im,
+    out, far_re, far_im, extra, far_spec, back, wt_re, wt_im, sems
 ):
     copies = []
     for q in range(NQ):
@@ -159,6 +161,16 @@
         ):
             copies.append(pltpu.make_async_copy(src, dst, sems.at[3 * q + i]))
             copies[-1].start()
+    real, imag = slice(REAL, REAL + ROWS), slice(IMAG, IMAG + ROWS)
+    first, last = slice(0, 4 * ROWS), slice(4 * ROWS, 5 * ROWS)
+    scale = source[...]
+    wt_re[first, :] = near_re[...]
+    wt_im[first, :] = near_im[...]
+    wt_re[last, :] = (scale * four[real, :].astype(f32)).astype(bf16)
+    wt_im[last, :] = (scale * four[imag, :].astype(f32)).astype(bf16)
+    spec = take_spectra(four, SPEC)
+    u_re = jnp.concatenate([spec_re[:, 0:1], spec[:, 0:1]], axis=0)
+    u_im = jnp.concatenate([spec_im[:, 0:1], spec[:, 1:2]], axis=0)
     for done in copies:
         done.wait()
     for q in range(NQ):
@@ -169,10 +181,14 @@
             ]
         far_spec[0:2, rows] = extra[q, 16:24, 0:128].astype(f32)[0:2, 64:128]
     behind = nt(identity(4 * ROWS), back[...])
-    counts = weight[...] + jnp.concatenate(
-        [jnp.zeros((ROWS, WIDE), f32), behind], axis=0
-    )
-    u_re, u_im = spec_re[:, 0:1], spec_im[:, 0:1]
+    counts = jnp.concatenate(
+        [
+            weight[0:ROWS, :],
+            weight[ROWS : 4 * ROWS, :] + behind[0 : 3 * ROWS],
+            behind[3 * ROWS : 4 * ROWS],
+        ],
+        axis=0,
+    )
     v_re, v_im = far_spec[0:1, :], far_spec[1:2, :]
     g_re, g_im = far_re[...], far_im[...]
     model_re = nt(wt_re[...], g_re) + nt(wt_im[...], g_im)
@@ -184,7 +200,6 @@
     r_im = (counts * x_im.astype(bf16).astype(f32)).astype(bf16)
     y_re = nn(r_re, g_re) - nn(r_im, g_im)
     y_im = nn(r_re, g_im) + nn(r_im, g_re)
-    real, imag = slice(REAL, REAL + ROWS), slice(IMAG, IMAG + ROWS)
     held = [(green[0], green[1])]
     for ref in (one, two, three, four):
         held.append((ref[real, :], ref[imag, :]))
@@ -230,51 +245,50 @@
 def local(spectra, green, source, pair_mask):
     g = green[0]
     vmem = pl.BlockSpec(memory_space=pltpu.VMEM)
-    tall = ROWS * (1 + len(OFFSETS))
-    hbm = pl.BlockSpec(memory_space=pl.ANY)
-    near, far, two_mask, shared, own_mask, own_spec = pl.pallas_call(
+    hbm = pl.BlockSpec(memory_space=pltpu.HBM)
+    near, far, shared, own_mask, own_spec = pl.pallas_call(
         pack,
         out_shape=[
-            shape(bf16, MASKED, CELLS),
-            shape(bf16, MASKED, CELLS),
-            shape(bf16, 32, CELLS),
+            shape(bf16, FULL, CELLS),
+            shape(bf16, NEXT, CELLS),
             shape(bf16, NQ, SHARED, CELLS),
             shape(bf16, ROWS, WIDE),
             shape(f32, ROWS, 128),
         ],
         in_specs=[hbm, hbm, vmem],
-        out_specs=[hbm] * 4 + [vmem] * 2,
+        out_specs=[hbm] * 3 + [vmem] * 2,
         scratch_shapes=[
+            pltpu.VMEM((2, ROWS, CELLS), bf16),
             pltpu.VMEM((ROWS, NZ * WIDE), jnp.int32),
             pltpu.VMEM((3, 32, CELLS), bf16),
             pltpu.VMEM((8, CELLS), bf16),
             pltpu.VMEM((NQ, 24, CELLS), bf16),
-            pltpu.SemaphoreType.DMA((34,)),
+            pltpu.SemaphoreType.DMA((35,)),
         ],
         name="pack",
     )(g, pair_mask, spectra[0])
     three = from_z(from_z(far, -2), -1)
     one = from_z(near, 1)
-    two_mask = from_z(two_mask, 2)
     shared = lax.all_to_all(shared, PLANE, 0, 0, tiled=True)
-    two = from_z(one[:MASK], 1)
-    four = from_z(two, 2)
+    two = from_z(one[:NEXT], 1)
+    four = from_z(two[:MASK], 2)
+    most = 4 * ROWS
     ready = pl.pallas_call(
         prepare,
-        out_shape=[shape(bf16, tall, CELLS)] * 2
-        + [shape(f32, tall, WIDE)]
-        + [shape(f32, tall, 128)] * 2,
-        in_specs=[vmem] * 9,
+        out_shape=[shape(bf16, most, CELLS)] * 2
+        + [shape(f32, most, WIDE)]
+        + [shape(f32, most, 128)] * 2,
+        in_specs=[vmem] * 7,
         out_specs=[vmem] * 5,
         cost_estimate=pl.CostEstimate(
             flops=PREPARE, transcendentals=0, bytes_accessed=0
         ),
         name="prepare",
-    )(source, g, own_mask, own_spec, one, two, two_mask, three, four)
+    )(source, g, own_mask, own_spec, one, two, three)
     part = pl.pallas_call(
         absorb,
         out_shape=shape(f32, NZ, 1, LONG),
-        in_specs=[hbm] + [vmem] * 10,
+        in_specs=[hbm] + [vmem] * 11,
         out_specs=vmem,
         scratch_shapes=[
             pltpu.VMEM((WIDE, CELLS), bf16),
@@ -282,10 +296,12 @@
             pltpu.VMEM((NQ, 24, CELLS), bf16),
             pltpu.VMEM((8, WIDE), f32),
             pltpu.VMEM((WIDE, 4 * ROWS), bf16),
+            pltpu.VMEM((5 * ROWS, CELLS), bf16),
+            pltpu.VMEM((5 * ROWS, CELLS), bf16),
             pltpu.SemaphoreType.DMA((3 * NQ,)),
         ],
         name="absorb",
-    )(shared, g, one, two, three, four, *ready)
+    )(shared, source, g, one, two, three, four, *ready)
     part = lax.all_to_all(part, "z", 0, 0, tiled=True)
     part = pl.pallas_call(
         gather_z,

time: 171 us -> 87.5 us (0.51)
  Pallas kernels: 96.1 us -> 17.9 us
  starting transfers between devices: 20.5 us -> 17.3 us
  blocking collectives: 30.3 us -> 27.8 us
    pallas_call x2, Pallas kernels: 85.1 us -> 6.99 us  [the longest x1 4.25 us: local(): pl.pallas_call(pack, out_shape=[shape(bf16, FULL, CELLS), shape(bf16, NEX...]
    all_to_all x1, waiting for transfers between devices: 0.01 us -> 5.94 us  [local(): shared = lax.all_to_all(shared, PLANE, 0, 0, tiled=True)]
    ppermute x6 -> x5, waiting for transfers between devices: 20.6 us -> 15.1 us  [from_z(): return lax.ppermute(array, 'z', [(z, (z - u) % NZ) for z in range(NZ)])]
    ppermute x6 -> x5, starting transfers between devices: 15.3 us -> 12.2 us  [from_z(): return lax.ppermute(array, 'z', [(z, (z - u) % NZ) for z in range(NZ)])]
  transfers between devices with their start and end apart: 7 -> 6, of which waited for: 3 -> 6; matrix products, arithmetic and copies ran while one was open for 0% -> 1% of each run, Pallas kernels for 2% -> 3%
where the time goes in v6:
time: 87.5 us; the launch traced here: 87 us
  blocking collectives  27.8 us (32%)
  waiting for transfers between devices  21.1 us (24%)
  Pallas kernels  17.9 us (20%)
  starting transfers between devices  17.3 us (20%)
  local copies, waits for them, and re-layouts  2.27 us (3%)
    all_to_all x1, blocking collectives, local(): part = lax.all_to_all(part, PLANE + FREQ, 0, 0, tiled=True)  15.9 us
    ppermute x5, waiting for transfers between devices, from_z(): return lax.ppermute(array, 'z', [(z, (z - u) % NZ) for z in range(NZ)])  15.1 us
    ppermute x5, starting transfers between devices, from_z(): return lax.ppermute(array, 'z', [(z, (z - u) % NZ) for z in range(NZ)])  12.2 us
    all_to_all x1, blocking collectives, local(): part = lax.all_to_all(part, 'z', 0, 0, tiled=True)  11.9 us
    pallas_call x1, Pallas kernels, local(): pl.pallas_call(absorb, out_shape=shape(f32, NZ, 1, LONG), in_specs=[hbm]...  7.79 us
    all_to_all x1, waiting for transfers between devices, local(): shared = lax.all_to_all(shared, PLANE, 0, 0, tiled=True)  5.94 us
    all_to_all x1, starting transfers between devices, local(): shared = lax.all_to_all(shared, PLANE, 0, 0, tiled=True)  5.12 us
    pallas_call x1, Pallas kernels, local(): pl.pallas_call(pack, out_shape=[shape(bf16, FULL, CELLS), shape(bf16, NEX...  4.25 us
  transfers between devices with their start and end apart: 6, of which 6 were waited for; matrix products, arithmetic and copies ran while one was open for 1% of the time, Pallas kernels for 3%

profile of v6, /device:TPU:1, one launch (start us, length us, event | category | flops | bytes accessed | tf_op | source)
XLA Modules:
  0.0 87.0 jit_solution(5454169899886131903)
XLA Ops:
  0.6 4.3 %pack.1 = (bf16[200,1024]{1,0:T(8,128)(2,1)}, bf16[168,1024]{1,0:T(8,128)(2,1)}, bf16[8,152,1024]{2,1,0:T(8,128)(2,1)}, bf16[64,512]{1,0:T(8,128)(2,1)}, f32[64,128]{1,0:T(8,128)}) custom-call(bf16[2,64,1024]{2,1,0:T(8,128)(2,1)} %bitcast.2, s32[64,4096]{1,0:T(8,128)} %mask_hbm.1, bf16[2,64]{1,0:T(2,128)(2,1)} %bitcast.5), custom_call_target="tpu_custom_call" | custom-call | tf_op jit(solution)/shard_map/pack/pallas_call | solution.py:249
  4.9 6.5 %collective-permute-start = (bf16[200,1024]{1,0:T(8,128)(2,1)}, bf16[200,1024]{1,0:T(8,128)(2,1)S(1)}, u32[]{:S(2)}, u32[]{:S(2)}) collective-permute-start(bf16[200,1024]{1,0:T(8,128)(2,1)} %get-tuple-element.13), channel_id=1, source_target_pairs={{0,224},{32,0},{64,32},{96,64},{128,96},{160,128},{192,160},{224,1... | collective-permute-start | bytes 1228808 | tf_op jit(solution)/shard_map/ppermute | solution.py:242
  11.4 0.0 collective-permute-start.2
  11.4 5.1 %all-to-all-start = ((bf16[8,152,1024]{2,1,0:T(8,128)(2,1)}), bf16[8,152,1024]{2,1,0:T(8,128)(2,1)S(1)}, u32[]{:S(2)}, u32[]{:S(2)}) async-start(bf16[8,152,1024]{2,1,0:T(8,128)(2,1)} %get-tuple-element.12), calls=%async_computation | async-start | bytes 4980736 | tf_op jit(solution)/shard_map/all_to_all | solution.py:272
  16.5 3.3 %collective-permute-done.one = bf16[200,1024]{1,0:T(8,128)(2,1)S(1)} collective-permute-done((bf16[200,1024]{1,0:T(8,128)(2,1)}, bf16[200,1024]{1,0:T(8,128)(2,1)S(1)}, u32[]{:S(2)}, u32[]{:S(2)}) %collective-permute-start) | collective-permute-done | bytes 409632 | tf_op jit(solution)/shard_map/ppermute | solution.py:242
  19.8 0.0 copy-start.1
  19.8 3.4 %collective-permute-start.1 = (bf16[168,1024]{1,0:T(8,128)(2,1)S(1)}, bf16[168,1024]{1,0:T(8,128)(2,1)S(1)}, u32[]{:S(2)}, u32[]{:S(2)}) collective-permute-start(bf16[168,1024]{1,0:T(8,128)(2,1)S(1)} %slice.8), channel_id=1, source_target_pairs={{0,224},{32,0},{64,32},{96,64},{128,96},{160,128},{192,160},{224,1... | collective-permute-start | bytes 1032200 | tf_op jit(solution)/shard_map/ppermute | solution.py:242
  23.2 4.9 %collective-permute-done.2 = bf16[168,1024]{1,0:T(8,128)(2,1)} collective-permute-done((bf16[168,1024]{1,0:T(8,128)(2,1)}, bf16[168,1024]{1,0:T(8,128)(2,1)}, u32[]{:S(2)}, u32[]{:S(2)}) %collective-permute-start.2) | collective-permute-done | bytes 344096 | tf_op jit(solution)/shard_map/ppermute | solution.py:242
  28.1 0.0 collective-permute-start.3
  28.1 0.9 %collective-permute-done.1.two = bf16[168,1024]{1,0:T(8,128)(2,1)S(1)} collective-permute-done((bf16[168,1024]{1,0:T(8,128)(2,1)S(1)}, bf16[168,1024]{1,0:T(8,128)(2,1)S(1)}, u32[]{:S(2)}, u32[]{:S(2)}) %collective-permute-start.1) | collective-permute-done | bytes 344096 | tf_op jit(solution)/shard_map/ppermute | solution.py:242
  29.0 0.0 copy-start.2
  29.0 0.8 slice.9
  29.8 2.3 %collective-permute-start.4 = (bf16[136,1024]{1,0:T(8,128)(2,1)}, bf16[136,1024]{1,0:T(8,128)(2,1)S(1)}, u32[]{:S(2)}, u32[]{:S(2)}) collective-permute-start(bf16[136,1024]{1,0:T(8,128)(2,1)} %slice.9), channel_id=1, source_target_pairs={{0,192},{32,224},{64,0},{96,32},{128,64},{160,96},{192,128},{224,1... | collective-permute-start | bytes 835592 | tf_op jit(solution)/shard_map/ppermute | solution.py:242
  32.1 4.0 %collective-permute-done.3.three = bf16[168,1024]{1,0:T(8,128)(2,1)} collective-permute-done((bf16[168,1024]{1,0:T(8,128)(2,1)}, bf16[168,1024]{1,0:T(8,128)(2,1)}, u32[]{:S(2)}, u32[]{:S(2)}) %collective-permute-start.3) | collective-permute-done | bytes 344096 | tf_op jit(solution)/shard_map/ppermute | solution.py:242
  36.2 0.0 copy-done.1
  36.2 0.0 copy-done.2
  36.2 2.7 %prepare.1 = (bf16[256,1024]{1,0:T(8,128)(2,1)}, bf16[256,1024]{1,0:T(8,128)(2,1)}, f32[256,512]{1,0:T(8,128)}, f32[256,128]{1,0:T(8,128)}, f32[256,128]{1,0:T(8,128)}) custom-call(f32[1,1024]{1,0:T(1,128)} %source.5, bf16[2,64,1024]{2,1,0:T(8,128)(2,1)} %bitcast.3, bf16[64,512]{1,0:T(8,128)(2,1)} %get-tuple-element.15.own_mask, ...), custom_call_target="tpu_custom_call" | custom-call | flops 16499999744 | tf_op jit(solution)/shard_map/prepare/pallas_call | solution.py:276
  38.9 2.0 %collective-permute-done.4.four = bf16[136,1024]{1,0:T(8,128)(2,1)S(1)} collective-permute-done((bf16[136,1024]{1,0:T(8,128)(2,1)}, bf16[136,1024]{1,0:T(8,128)(2,1)S(1)}, u32[]{:S(2)}, u32[]{:S(2)}) %collective-permute-start.4) | collective-permute-done | bytes 278560 | tf_op jit(solution)/shard_map/ppermute | solution.py:242
  40.9 0.0 copy-start.3
  40.9 5.9 %all-to-all-done.shared = bf16[8,152,1024]{2,1,0:T(8,128)(2,1)S(1)} async-done(((bf16[8,152,1024]{2,1,0:T(8,128)(2,1)}), bf16[8,152,1024]{2,1,0:T(8,128)(2,1)S(1)}, u32[]{:S(2)}, u32[]{:S(2)}) %all-to-all-start) | async-done | bytes 2490400 | tf_op jit(solution)/shard_map/all_to_all | solution.py:272
  46.8 0.0 copy-start
  46.8 0.0 copy-done.3
  46.8 1.5 %copy-done = bf16[8,152,1024]{2,1,0:T(8,128)(2,1)} copy-done((bf16[8,152,1024]{2,1,0:T(8,128)(2,1)}, bf16[8,152,1024]{2,1,0:T(8,128)(2,1)S(1)}, u32[]{:S(2)}) %copy-start) | copy-done | bytes 2490392
  48.3 7.8 %absorb.1 = f32[8,1,1152]{2,1,0:T(1,128)} custom-call(bf16[8,152,1024]{2,1,0:T(8,128)(2,1)} %copy-done, f32[1,1024]{1,0:T(1,128)} %source.5, bf16[2,64,1024]{2,1,0:T(8,128)(2,1)} %bitcast.4, bf16[200,1024]{1,0:T(8,128)(2,1)} %copy-done.1, bf16[168,1024]{1,0:T(8,128)(2,1)} %copy-done.2, bf16[168,1024]{1,0:T(8,128)(2,1)} %collective-permute-done.3.three, ...), custom_call_target="tpu_custom_call" | custom-call | tf_op jit(solution)/shard_map/absorb/pallas_call | solution.py:288
  56.1 11.9 %all_to_all.15.parts = f32[8,1,1152]{2,1,0:T(1,128)} all-to-all(f32[8,1,1152]{2,1,0:T(1,128)} %absorb.1), channel_id=1, replica_groups=mesh['z'=8,'xl'=2,'y'=4,'xh'=2,'core'=2] {'z'}, dimensions={0} | all-to-all | bytes 73728 | tf_op jit(solution)/shard_map/all_to_all | solution.py:305
  68.0 1.5 %gather_z.1 = f32[32,1,1152]{2,1,0:T(1,128)} custom-call(f32[8,1,1152]{2,1,0:T(1,128)} %all_to_all.15.parts), custom_call_target="tpu_custom_call" | custom-call | tf_op jit(solution)/shard_map/gather_z/pallas_call | solution.py:306
  69.4 15.9 %all_to_all.16.parts = f32[32,1,1152]{2,1,0:T(1,128)} all-to-all(f32[32,1,1152]{2,1,0:T(1,128)} %gather_z.1), channel_id=1, replica_groups=mesh['z'=8,'xl'=2,'y'=4,'xh'=2,'core'=2] {'xl','y','xh','core'}, dimensions={0} | all-to-all | bytes 294912 | tf_op jit(solution)/shard_map/all_to_all | solution.py:313
  85.4 1.7 %finish.1 = (f32[1,1024]{1,0:T(1,128)}, f32[1]{0:T(128)}) custom-call(f32[32,1,1152]{2,1,0:T(1,128)} %all_to_all.16.parts, f32[1,1024]{1,0:T(1,128)} %source.5), custom_call_target="tpu_custom_call" | custom-call | tf_op jit(solution)/shard_map/finish/pallas_call | solution.py:314
  (1 shorter events, 0.0 us)
Async XLA Ops:
  4.9 14.9 %collective-permute-start = (bf16[200,1024]{1,0:T(8,128)(2,1)}, bf16[200,1024]{1,0:T(8,128)(2,1)S(1)}, u32[]{:S(2)}, u32[]{:S(2)}) collective-permute-start(bf16[200,1024]{1,0:T(8,128)(2,1)} %get-tuple-element.13), channel_id=1, source_target_pairs={{0,224},{32,0},{64,32},{96,64},{128,96},{160,128},{192,160},{224,1... | collective-permute-start | bytes 1228808 | tf_op jit(solution)/shard_map/ppermute | solution.py:242
  11.4 16.7 %collective-permute-start.2 = (bf16[168,1024]{1,0:T(8,128)(2,1)}, bf16[168,1024]{1,0:T(8,128)(2,1)}, u32[]{:S(2)}, u32[]{:S(2)}) collective-permute-start(bf16[168,1024]{1,0:T(8,128)(2,1)} %get-tuple-element.14), channel_id=1, source_target_pairs={{0,64},{32,96},{64,128},{96,160},{128,192},{160,224},{192,0},{224,... | collective-permute-start | bytes 1032200 | tf_op jit(solution)/shard_map/ppermute | solution.py:242
  11.4 35.5 %all-to-all-start = ((bf16[8,152,1024]{2,1,0:T(8,128)(2,1)}), bf16[8,152,1024]{2,1,0:T(8,128)(2,1)S(1)}, u32[]{:S(2)}, u32[]{:S(2)}) async-start(bf16[8,152,1024]{2,1,0:T(8,128)(2,1)} %get-tuple-element.12), calls=%async_computation | async-start | bytes 4980736 | tf_op jit(solution)/shard_map/all_to_all | solution.py:272
  19.8 16.3 %copy-start.1 = (bf16[200,1024]{1,0:T(8,128)(2,1)}, bf16[200,1024]{1,0:T(8,128)(2,1)S(1)}, u32[]{:S(2)}) copy-start(bf16[200,1024]{1,0:T(8,128)(2,1)S(1)} %collective-permute-done.one) | copy-start | bytes 1228804
  19.8 9.2 %collective-permute-start.1 = (bf16[168,1024]{1,0:T(8,128)(2,1)S(1)}, bf16[168,1024]{1,0:T(8,128)(2,1)S(1)}, u32[]{:S(2)}, u32[]{:S(2)}) collective-permute-start(bf16[168,1024]{1,0:T(8,128)(2,1)S(1)} %slice.8), channel_id=1, source_target_pairs={{0,224},{32,0},{64,32},{96,64},{128,96},{160,128},{192,160},{224,1... | collective-permute-start | bytes 1032200 | tf_op jit(solution)/shard_map/ppermute | solution.py:242
  28.1 8.0 %collective-permute-start.3 = (bf16[168,1024]{1,0:T(8,128)(2,1)}, bf16[168,1024]{1,0:T(8,128)(2,1)}, u32[]{:S(2)}, u32[]{:S(2)}) collective-permute-start(bf16[168,1024]{1,0:T(8,128)(2,1)} %collective-permute-done.2), channel_id=1, source_target_pairs={{0,32},{32,64},{64,96},{96,128},{128,160},{160,192},{192,224},{224... | collective-permute-start | bytes 1032200 | tf_op jit(solution)/shard_map/ppermute | solution.py:242
  29.0 7.1 %copy-start.2 = (bf16[168,1024]{1,0:T(8,128)(2,1)}, bf16[168,1024]{1,0:T(8,128)(2,1)S(1)}, u32[]{:S(2)}) copy-start(bf16[168,1024]{1,0:T(8,128)(2,1)S(1)} %collective-permute-done.1.two) | copy-start | bytes 1032196
  29.8 11.1 %collective-permute-start.4 = (bf16[136,1024]{1,0:T(8,128)(2,1)}, bf16[136,1024]{1,0:T(8,128)(2,1)S(1)}, u32[]{:S(2)}, u32[]{:S(2)}) collective-permute-start(bf16[136,1024]{1,0:T(8,128)(2,1)} %slice.9), channel_id=1, source_target_pairs={{0,192},{32,224},{64,0},{96,32},{128,64},{160,96},{192,128},{224,1... | collective-permute-start | bytes 835592 | tf_op jit(solution)/shard_map/ppermute | solution.py:242
  40.9 5.9 %copy-start.3 = (bf16[136,1024]{1,0:T(8,128)(2,1)}, bf16[136,1024]{1,0:T(8,128)(2,1)S(1)}, u32[]{:S(2)}) copy-start(bf16[136,1024]{1,0:T(8,128)(2,1)S(1)} %collective-permute-done.4.four) | copy-start | bytes 835588
  46.8 1.5 %copy-start = (bf16[8,152,1024]{2,1,0:T(8,128)(2,1)}, bf16[8,152,1024]{2,1,0:T(8,128)(2,1)S(1)}, u32[]{:S(2)}) copy-start(bf16[8,152,1024]{2,1,0:T(8,128)(2,1)S(1)} %all-to-all-done.shared) | copy-start | bytes 7471108

commit v7 on v6

--- a/solution.py
+++ b/solution.py
@@ -66,27 +66,11 @@
 
 
 def pack(
-    green_hbm, mask_hbm, spec_row, near, far, shared, own_mask, own_spec,
-    green, mask, masks, spec8, extra, sems
+    green, mask_hbm, spec_row, near, far, shared, own_mask, own_spec, mask, sem
 ):
+    loading = pltpu.make_async_copy(mask_hbm, mask, sem)
+    loading.start()
     z = lax.axis_index("z")
-    used = []
-
-    def copy(src, dst):
-        done = pltpu.make_async_copy(src, dst, sems.at[len(used)])
-        done.start()
-        used.append(done)
-        return done
-
-    held = copy(green_hbm, green)
-    loaded = copy(mask_hbm, mask)
-    held.wait()
-    for ref in (near, far):
-        copy(green.at[1], ref.at[IMAG : IMAG + ROWS])
-        copy(green.at[0], ref.at[REAL : REAL + ROWS])
-    for q in range(NQ):
-        copy(green.at[0], shared.at[q, 0:64])
-        copy(green.at[1], shared.at[q, 64:128])
     row = spec_row[...]
     col = nt(identity(ROWS), row)
     lane = lax.broadcasted_iota(jnp.int32, (ROWS, 128), 1)
@@ -95,27 +79,24 @@
     )
     own_spec[0:2, 64:128] = row.astype(f32)
     spectra = own_spec[...].astype(bf16)
-    for g in range(8):
-        spec8[:, 128 * g : 128 * (g + 1)] = spectra[8 * g : 8 * (g + 1)]
-    copy(spec8, near.at[SPEC : SPEC + 8])
-    copy(spec8, far.at[SPEC : SPEC + 8])
-    loaded.wait()
-    for k, (u, ref, at) in enumerate(((1, near, NEXT), (2, near, MASK), (-3, far, MASK))):
-        put_mask(masks.at[k], window(mask, z - u).astype(bf16))
-        copy(masks.at[k], ref.at[at : at + 32])
+    places = [(near, IMAG, REAL, SPEC), (far, IMAG, REAL, SPEC)]
+    places += [(shared.at[q], 64, 0, 144) for q in range(NQ)]
+    for ref, imag, real, spec in places:
+        ref[imag : imag + ROWS, :] = green[1]
+        ref[real : real + ROWS, :] = green[0]
+        for g in range(8):
+            ref[spec : spec + 8, 128 * g : 128 * (g + 1)] = spectra[8 * g : 8 * (g + 1)]
+    loading.wait()
+    for u, ref, at in ((1, near, NEXT), (2, near, MASK), (-3, far, MASK)):
+        put_mask(ref.at[at : at + 32], window(mask, z - u).astype(bf16))
+    own_mask[...] = window(mask, z).astype(bf16)
     wide = [window(mask, z + u) for u in OFFSETS]
     for q in range(NQ):
         part = jnp.concatenate(
             [w[:, ROWS * q : ROWS * (q + 1)] for w in wide], axis=1
         ).astype(bf16)
         for g in range(4):
-            extra[q, 0:16, 256 * g : 256 * (g + 1)] = part[16 * g : 16 * (g + 1)]
-        for g in range(8):
-            extra[q, 16:24, 128 * g : 128 * (g + 1)] = spectra[8 * g : 8 * (g + 1)]
-        copy(extra.at[q], shared.at[q, 128:152])
-    own_mask[...] = window(mask, z).astype(bf16)
-    for done in used[2:]:
-        done.wait()
+            shared[q, 128:144, 256 * g : 256 * (g + 1)] = part[16 * g : 16 * (g + 1)]
 
 
 def prepare(
@@ -147,39 +128,29 @@
 def absorb(
     shared, source, green, one, two, three, four,
     near_re, near_im, weight, spec_re, spec_im,
-    out, far_re, far_im, extra, far_spec, back, wt_re, wt_im, sems
+    out, far_re, far_im, far_spec, back, wt
 ):
-    copies = []
-    for q in range(NQ):
-        rows = slice(ROWS * q, ROWS * (q + 1))
-        for i, (src, dst) in enumerate(
-            (
-                (shared.at[q, 0:64], far_re.at[rows]),
-                (shared.at[q, 64:128], far_im.at[rows]),
-                (shared.at[q, 128:152], extra.at[q]),
-            )
-        ):
-            copies.append(pltpu.make_async_copy(src, dst, sems.at[3 * q + i]))
-            copies[-1].start()
     real, imag = slice(REAL, REAL + ROWS), slice(IMAG, IMAG + ROWS)
-    first, last = slice(0, 4 * ROWS), slice(4 * ROWS, 5 * ROWS)
+    tall = 5 * ROWS
     scale = source[...]
-    wt_re[first, :] = near_re[...]
-    wt_im[first, :] = near_im[...]
-    wt_re[last, :] = (scale * four[real, :].astype(f32)).astype(bf16)
-    wt_im[last, :] = (scale * four[imag, :].astype(f32)).astype(bf16)
+    for at, near, part in ((0, near_re, real), (tall, near_im, imag)):
+        wt[at : at + 4 * ROWS, :] = near[...]
+        wt[at + 4 * ROWS : at + tall, :] = (scale * four[part, :].astype(f32)).astype(
+            bf16
+        )
     spec = take_spectra(four, SPEC)
     u_re = jnp.concatenate([spec_re[:, 0:1], spec[:, 0:1]], axis=0)
     u_im = jnp.concatenate([spec_im[:, 0:1], spec[:, 1:2]], axis=0)
-    for done in copies:
-        done.wait()
     for q in range(NQ):
         rows = slice(ROWS * q, ROWS * (q + 1))
+        ref = shared.at[q]
+        far_re[rows, :] = ref[0:64, :]
+        far_im[rows, :] = ref[64:128, :]
         for g in range(4):
-            back[ROWS * q + 16 * g : ROWS * q + 16 * (g + 1), :] = extra[
-                q, 0:16, 256 * g : 256 * (g + 1)
+            back[ROWS * q + 16 * g : ROWS * q + 16 * (g + 1), :] = ref[
+                128:144, 256 * g : 256 * (g + 1)
             ]
-        far_spec[0:2, rows] = extra[q, 16:24, 0:128].astype(f32)[0:2, 64:128]
+        far_spec[0:2, rows] = ref[144:152, 0:128].astype(f32)[0:2, 64:128]
     behind = nt(identity(4 * ROWS), back[...])
     counts = jnp.concatenate(
         [
@@ -191,22 +162,31 @@
     )
     v_re, v_im = far_spec[0:1, :], far_spec[1:2, :]
     g_re, g_im = far_re[...], far_im[...]
-    model_re = nt(wt_re[...], g_re) + nt(wt_im[...], g_im)
-    model_im = nt(wt_im[...], g_re) - nt(wt_re[...], g_im)
-    x_re = (u_re * v_re + u_im * v_im) - model_re
-    x_im = (u_im * v_re - u_re * v_im) - model_im
+    by_re = nt(wt[...], g_re)
+    by_im = nt(wt[...], g_im)
+    x_re = (u_re * v_re + u_im * v_im) - (by_re[:tall] + by_im[tall:])
+    x_im = (u_im * v_re - u_re * v_im) - (by_re[tall:] - by_im[:tall])
     mis = 0.5 * jnp.sum(counts * (x_re * x_re + x_im * x_im), keepdims=True)
-    r_re = (counts * x_re.astype(bf16).astype(f32)).astype(bf16)
-    r_im = (counts * x_im.astype(bf16).astype(f32)).astype(bf16)
-    y_re = nn(r_re, g_re) - nn(r_im, g_im)
-    y_im = nn(r_re, g_im) + nn(r_im, g_re)
+    resid = jnp.concatenate(
+        [
+            (counts * x_re.astype(bf16).astype(f32)).astype(bf16),
+            (counts * x_im.astype(bf16).astype(f32)).astype(bf16),
+        ],
+        axis=0,
+    )
+    by_re = nn(resid, g_re)
+    by_im = nn(resid, g_im)
     held = [(green[0], green[1])]
     for ref in (one, two, three, four):
         held.append((ref[real, :], ref[imag, :]))
     total = jnp.zeros((ROWS, CELLS), f32)
     for k, (re, im) in enumerate(held):
         rows = slice(ROWS * k, ROWS * (k + 1))
-        total = total + (re.astype(f32) * y_re[rows] + im.astype(f32) * y_im[rows])
+        more = slice(tall + ROWS * k, tall + ROWS * (k + 1))
+        total = total + (
+            re.astype(f32) * (by_re[rows] - by_im[more])
+            + im.astype(f32) * (by_im[rows] + by_re[more])
+        )
     total = -jnp.sum(total, axis=0, keepdims=True)
     out[:, :, 0:CELLS] = jnp.broadcast_to(total[None], (NZ, 1, CELLS))
     out[:, :, CELLS:LONG] = jnp.broadcast_to(mis[None], (NZ, 1, 128))
@@ -245,7 +225,6 @@
 def local(spectra, green, source, pair_mask):
     g = green[0]
     vmem = pl.BlockSpec(memory_space=pltpu.VMEM)
-    hbm = pl.BlockSpec(memory_space=pltpu.HBM)
     near, far, shared, own_mask, own_spec = pl.pallas_call(
         pack,
         out_shape=[
@@ -255,15 +234,11 @@
             shape(bf16, ROWS, WIDE),
             shape(f32, ROWS, 128),
         ],
-        in_specs=[hbm, hbm, vmem],
-        out_specs=[hbm] * 3 + [vmem] * 2,
+        in_specs=[vmem, pl.BlockSpec(memory_space=pl.ANY), vmem],
+        out_specs=[vmem] * 5,
         scratch_shapes=[
-            pltpu.VMEM((2, ROWS, CELLS), bf16),
             pltpu.VMEM((ROWS, NZ * WIDE), jnp.int32),
-            pltpu.VMEM((3, 32, CELLS), bf16),
-            pltpu.VMEM((8, CELLS), bf16),
-            pltpu.VMEM((NQ, 24, CELLS), bf16),
-            pltpu.SemaphoreType.DMA((35,)),
+            pltpu.SemaphoreType.DMA,
         ],
         name="pack",
     )(g, pair_mask, spectra[0])
@@ -288,17 +263,14 @@
     part = pl.pallas_call(
         absorb,
         out_shape=shape(f32, NZ, 1, LONG),
-        in_specs=[hbm] + [vmem] * 11,
+        in_specs=[vmem] * 12,
         out_specs=vmem,
         scratch_shapes=[
             pltpu.VMEM((WIDE, CELLS), bf16),
             pltpu.VMEM((WIDE, CELLS), bf16),
-            pltpu.VMEM((NQ, 24, CELLS), bf16),
             pltpu.VMEM((8, WIDE), f32),
             pltpu.VMEM((WIDE, 4 * ROWS), bf16),
-            pltpu.VMEM((5 * ROWS, CELLS), bf16),
-            pltpu.VMEM((5 * ROWS, CELLS), bf16),
-            pltpu.SemaphoreType.DMA((3 * NQ,)),
+            pltpu.VMEM((10 * ROWS, CELLS), bf16),
         ],
         name="absorb",
     )(shared, source, g, one, two, three, four, *ready)

time: 87.5 us -> 86.2 us (0.985)
  Pallas kernels: 17.9 us -> 16.7 us
    pallas_call x1, Pallas kernels: 7.79 us -> 6.79 us  [local(): pl.pallas_call(absorb, out_shape=shape(f32, NZ, 1, LONG), in_specs=[vmem]...]
where the time goes in v7:
time: 86.2 us; the launch traced here: 85.8 us
  blocking collectives  27.8 us (32%)
  waiting for transfers between devices  21.1 us (24%)
  starting transfers between devices  17.3 us (20%)
  Pallas kernels  16.7 us (19%)
  local copies, waits for them, and re-layouts  2.27 us (3%)
    all_to_all x1, blocking collectives, local(): part = lax.all_to_all(part, PLANE + FREQ, 0, 0, tiled=True)  15.9 us
    ppermute x5, waiting for transfers between devices, from_z(): return lax.ppermute(array, 'z', [(z, (z - u) % NZ) for z in range(NZ)])  15.1 us
    ppermute x5, starting transfers between devices, from_z(): return lax.ppermute(array, 'z', [(z, (z - u) % NZ) for z in range(NZ)])  12.2 us
    all_to_all x1, blocking collectives, local(): part = lax.all_to_all(part, 'z', 0, 0, tiled=True)  11.9 us
    pallas_call x1, Pallas kernels, local(): pl.pallas_call(absorb, out_shape=shape(f32, NZ, 1, LONG), in_specs=[vmem]...  6.79 us
    all_to_all x1, waiting for transfers between devices, local(): shared = lax.all_to_all(shared, PLANE, 0, 0, tiled=True)  5.94 us
    all_to_all x1, starting transfers between devices, local(): shared = lax.all_to_all(shared, PLANE, 0, 0, tiled=True)  5.12 us
    pallas_call x1, Pallas kernels, local(): pl.pallas_call(pack, out_shape=[shape(bf16, FULL, CELLS), shape(bf16, NEX...  4 us
  transfers between devices with their start and end apart: 6, of which 6 were waited for; matrix products, arithmetic and copies ran while one was open for 1% of the time, Pallas kernels for 3%

profile of v7, /device:TPU:1, one launch (start us, length us, event | category | flops | bytes accessed | tf_op | source)
XLA Modules:
  0.0 85.8 jit_solution(17569868677056898942)
XLA Ops:
  0.6 4.0 %pack.1 = (bf16[200,1024]{1,0:T(8,128)(2,1)}, bf16[168,1024]{1,0:T(8,128)(2,1)}, bf16[8,152,1024]{2,1,0:T(8,128)(2,1)}, bf16[64,512]{1,0:T(8,128)(2,1)}, f32[64,128]{1,0:T(8,128)}) custom-call(bf16[2,64,1024]{2,1,0:T(8,128)(2,1)} %bitcast.2, s32[64,4096]{1,0:T(8,128)} %mask_hbm.1, bf16[2,64]{1,0:T(2,128)(2,1)} %bitcast.5), custom_call_target="tpu_custom_call" | custom-call | tf_op jit(solution)/shard_map/pack/pallas_call | solution.py:228
  4.6 6.5 %collective-permute-start = (bf16[200,1024]{1,0:T(8,128)(2,1)}, bf16[200,1024]{1,0:T(8,128)(2,1)S(1)}, u32[]{:S(2)}, u32[]{:S(2)}) collective-permute-start(bf16[200,1024]{1,0:T(8,128)(2,1)} %get-tuple-element.13), channel_id=1, source_target_pairs={{0,224},{32,0},{64,32},{96,64},{128,96},{160,128},{192,160},{224,1... | collective-permute-start | bytes 1228808 | tf_op jit(solution)/shard_map/ppermute | solution.py:222
  11.1 0.0 collective-permute-start.2
  11.1 5.1 %all-to-all-start = ((bf16[8,152,1024]{2,1,0:T(8,128)(2,1)}), bf16[8,152,1024]{2,1,0:T(8,128)(2,1)S(1)}, u32[]{:S(2)}, u32[]{:S(2)}) async-start(bf16[8,152,1024]{2,1,0:T(8,128)(2,1)} %get-tuple-element.12), calls=%async_computation | async-start | bytes 4980736 | tf_op jit(solution)/shard_map/all_to_all | solution.py:247
  16.2 3.3 %collective-permute-done.one = bf16[200,1024]{1,0:T(8,128)(2,1)S(1)} collective-permute-done((bf16[200,1024]{1,0:T(8,128)(2,1)}, bf16[200,1024]{1,0:T(8,128)(2,1)S(1)}, u32[]{:S(2)}, u32[]{:S(2)}) %collective-permute-start) | collective-permute-done | bytes 409632 | tf_op jit(solution)/shard_map/ppermute | solution.py:222
  19.6 0.0 copy-start.1
  19.6 3.4 %collective-permute-start.1 = (bf16[168,1024]{1,0:T(8,128)(2,1)S(1)}, bf16[168,1024]{1,0:T(8,128)(2,1)S(1)}, u32[]{:S(2)}, u32[]{:S(2)}) collective-permute-start(bf16[168,1024]{1,0:T(8,128)(2,1)S(1)} %slice.8), channel_id=1, source_target_pairs={{0,224},{32,0},{64,32},{96,64},{128,96},{160,128},{192,160},{224,1... | collective-permute-start | bytes 1032200 | tf_op jit(solution)/shard_map/ppermute | solution.py:222
  23.0 4.9 %collective-permute-done.2 = bf16[168,1024]{1,0:T(8,128)(2,1)} collective-permute-done((bf16[168,1024]{1,0:T(8,128)(2,1)}, bf16[168,1024]{1,0:T(8,128)(2,1)}, u32[]{:S(2)}, u32[]{:S(2)}) %collective-permute-start.2) | collective-permute-done | bytes 344096 | tf_op jit(solution)/shard_map/ppermute | solution.py:222
  27.9 0.0 collective-permute-start.3
  27.9 0.9 %collective-permute-done.1.two = bf16[168,1024]{1,0:T(8,128)(2,1)S(1)} collective-permute-done((bf16[168,1024]{1,0:T(8,128)(2,1)S(1)}, bf16[168,1024]{1,0:T(8,128)(2,1)S(1)}, u32[]{:S(2)}, u32[]{:S(2)}) %collective-permute-start.1) | collective-permute-done | bytes 344096 | tf_op jit(solution)/shard_map/ppermute | solution.py:222
  28.8 0.0 copy-start.2
  28.8 0.8 slice.9
  29.6 2.3 %collective-permute-start.4 = (bf16[136,1024]{1,0:T(8,128)(2,1)}, bf16[136,1024]{1,0:T(8,128)(2,1)S(1)}, u32[]{:S(2)}, u32[]{:S(2)}) collective-permute-start(bf16[136,1024]{1,0:T(8,128)(2,1)} %slice.9), channel_id=1, source_target_pairs={{0,192},{32,224},{64,0},{96,32},{128,64},{160,96},{192,128},{224,1... | collective-permute-start | bytes 835592 | tf_op jit(solution)/shard_map/ppermute | solution.py:222
  31.9 4.0 %collective-permute-done.3.three = bf16[168,1024]{1,0:T(8,128)(2,1)} collective-permute-done((bf16[168,1024]{1,0:T(8,128)(2,1)}, bf16[168,1024]{1,0:T(8,128)(2,1)}, u32[]{:S(2)}, u32[]{:S(2)}) %collective-permute-start.3) | collective-permute-done | bytes 344096 | tf_op jit(solution)/shard_map/ppermute | solution.py:222
  35.9 0.0 copy-done.1
  35.9 0.0 copy-done.2
  35.9 2.7 %prepare.1 = (bf16[256,1024]{1,0:T(8,128)(2,1)}, bf16[256,1024]{1,0:T(8,128)(2,1)}, f32[256,512]{1,0:T(8,128)}, f32[256,128]{1,0:T(8,128)}, f32[256,128]{1,0:T(8,128)}) custom-call(f32[1,1024]{1,0:T(1,128)} %source.5, bf16[2,64,1024]{2,1,0:T(8,128)(2,1)} %bitcast.3, bf16[64,512]{1,0:T(8,128)(2,1)} %get-tuple-element.15.own_mask, ...), custom_call_target="tpu_custom_call" | custom-call | flops 16499999744 | tf_op jit(solution)/shard_map/prepare/pallas_call | solution.py:251
  38.6 2.0 %collective-permute-done.4.four = bf16[136,1024]{1,0:T(8,128)(2,1)S(1)} collective-permute-done((bf16[136,1024]{1,0:T(8,128)(2,1)}, bf16[136,1024]{1,0:T(8,128)(2,1)S(1)}, u32[]{:S(2)}, u32[]{:S(2)}) %collective-permute-start.4) | collective-permute-done | bytes 278560 | tf_op jit(solution)/shard_map/ppermute | solution.py:222
  40.6 0.0 copy-start.3
  40.6 5.9 %all-to-all-done.shared = bf16[8,152,1024]{2,1,0:T(8,128)(2,1)S(1)} async-done(((bf16[8,152,1024]{2,1,0:T(8,128)(2,1)}), bf16[8,152,1024]{2,1,0:T(8,128)(2,1)S(1)}, u32[]{:S(2)}, u32[]{:S(2)}) %all-to-all-start) | async-done | bytes 2490400 | tf_op jit(solution)/shard_map/all_to_all | solution.py:247
  46.6 0.0 copy-start
  46.6 0.0 copy-done.3
  46.6 1.5 %copy-done = bf16[8,152,1024]{2,1,0:T(8,128)(2,1)} copy-done((bf16[8,152,1024]{2,1,0:T(8,128)(2,1)}, bf16[8,152,1024]{2,1,0:T(8,128)(2,1)S(1)}, u32[]{:S(2)}) %copy-start) | copy-done | bytes 2490392
  48.0 6.8 %absorb.1 = f32[8,1,1152]{2,1,0:T(1,128)} custom-call(bf16[8,152,1024]{2,1,0:T(8,128)(2,1)} %copy-done, f32[1,1024]{1,0:T(1,128)} %source.5, bf16[2,64,1024]{2,1,0:T(8,128)(2,1)} %bitcast.4, bf16[200,1024]{1,0:T(8,128)(2,1)} %copy-done.1, bf16[168,1024]{1,0:T(8,128)(2,1)} %copy-done.2, bf16[168,1024]{1,0:T(8,128)(2,1)} %collective-permute-done.3.three, ...), custom_call_target="tpu_custom_call" | custom-call | tf_op jit(solution)/shard_map/absorb/pallas_call | solution.py:263
  54.8 11.9 %all_to_all.15.parts = f32[8,1,1152]{2,1,0:T(1,128)} all-to-all(f32[8,1,1152]{2,1,0:T(1,128)} %absorb.1), channel_id=1, replica_groups=mesh['z'=8,'xl'=2,'y'=4,'xh'=2,'core'=2] {'z'}, dimensions={0} | all-to-all | bytes 73728 | tf_op jit(solution)/shard_map/all_to_all | solution.py:277
  66.7 1.5 %gather_z.1 = f32[32,1,1152]{2,1,0:T(1,128)} custom-call(f32[8,1,1152]{2,1,0:T(1,128)} %all_to_all.15.parts), custom_call_target="tpu_custom_call" | custom-call | tf_op jit(solution)/shard_map/gather_z/pallas_call | solution.py:278
  68.2 15.9 %all_to_all.16.parts = f32[32,1,1152]{2,1,0:T(1,128)} all-to-all(f32[32,1,1152]{2,1,0:T(1,128)} %gather_z.1), channel_id=1, replica_groups=mesh['z'=8,'xl'=2,'y'=4,'xh'=2,'core'=2] {'xl','y','xh','core'}, dimensions={0} | all-to-all | bytes 294912 | tf_op jit(solution)/shard_map/all_to_all | solution.py:285
  84.1 1.7 %finish.1 = (f32[1,1024]{1,0:T(1,128)}, f32[1]{0:T(128)}) custom-call(f32[32,1,1152]{2,1,0:T(1,128)} %all_to_all.16.parts, f32[1,1024]{1,0:T(1,128)} %source.5), custom_call_target="tpu_custom_call" | custom-call | tf_op jit(solution)/shard_map/finish/pallas_call | solution.py:286
  (1 shorter events, 0.0 us)
Async XLA Ops:
  4.6 14.9 %collective-permute-start = (bf16[200,1024]{1,0:T(8,128)(2,1)}, bf16[200,1024]{1,0:T(8,128)(2,1)S(1)}, u32[]{:S(2)}, u32[]{:S(2)}) collective-permute-start(bf16[200,1024]{1,0:T(8,128)(2,1)} %get-tuple-element.13), channel_id=1, source_target_pairs={{0,224},{32,0},{64,32},{96,64},{128,96},{160,128},{192,160},{224,1... | collective-permute-start | bytes 1228808 | tf_op jit(solution)/shard_map/ppermute | solution.py:222
  11.1 16.7 %collective-permute-start.2 = (bf16[168,1024]{1,0:T(8,128)(2,1)}, bf16[168,1024]{1,0:T(8,128)(2,1)}, u32[]{:S(2)}, u32[]{:S(2)}) collective-permute-start(bf16[168,1024]{1,0:T(8,128)(2,1)} %get-tuple-element.14), channel_id=1, source_target_pairs={{0,64},{32,96},{64,128},{96,160},{128,192},{160,224},{192,0},{224,... | collective-permute-start | bytes 1032200 | tf_op jit(solution)/shard_map/ppermute | solution.py:222
  11.1 35.5 %all-to-all-start = ((bf16[8,152,1024]{2,1,0:T(8,128)(2,1)}), bf16[8,152,1024]{2,1,0:T(8,128)(2,1)S(1)}, u32[]{:S(2)}, u32[]{:S(2)}) async-start(bf16[8,152,1024]{2,1,0:T(8,128)(2,1)} %get-tuple-element.12), calls=%async_computation | async-start | bytes 4980736 | tf_op jit(solution)/shard_map/all_to_all | solution.py:247
  19.6 16.3 %copy-start.1 = (bf16[200,1024]{1,0:T(8,128)(2,1)}, bf16[200,1024]{1,0:T(8,128)(2,1)S(1)}, u32[]{:S(2)}) copy-start(bf16[200,1024]{1,0:T(8,128)(2,1)S(1)} %collective-permute-done.one) | copy-start | bytes 1228804
  19.6 9.2 %collective-permute-start.1 = (bf16[168,1024]{1,0:T(8,128)(2,1)S(1)}, bf16[168,1024]{1,0:T(8,128)(2,1)S(1)}, u32[]{:S(2)}, u32[]{:S(2)}) collective-permute-start(bf16[168,1024]{1,0:T(8,128)(2,1)S(1)} %slice.8), channel_id=1, source_target_pairs={{0,224},{32,0},{64,32},{96,64},{128,96},{160,128},{192,160},{224,1... | collective-permute-start | bytes 1032200 | tf_op jit(solution)/shard_map/ppermute | solution.py:222
  27.9 8.0 %collective-permute-start.3 = (bf16[168,1024]{1,0:T(8,128)(2,1)}, bf16[168,1024]{1,0:T(8,128)(2,1)}, u32[]{:S(2)}, u32[]{:S(2)}) collective-permute-start(bf16[168,1024]{1,0:T(8,128)(2,1)} %collective-permute-done.2), channel_id=1, source_target_pairs={{0,32},{32,64},{64,96},{96,128},{128,160},{160,192},{192,224},{224... | collective-permute-start | bytes 1032200 | tf_op jit(solution)/shard_map/ppermute | solution.py:222
  28.8 7.1 %copy-start.2 = (bf16[168,1024]{1,0:T(8,128)(2,1)}, bf16[168,1024]{1,0:T(8,128)(2,1)S(1)}, u32[]{:S(2)}) copy-start(bf16[168,1024]{1,0:T(8,128)(2,1)S(1)} %collective-permute-done.1.two) | copy-start | bytes 1032196
  29.6 11.1 %collective-permute-start.4 = (bf16[136,1024]{1,0:T(8,128)(2,1)}, bf16[136,1024]{1,0:T(8,128)(2,1)S(1)}, u32[]{:S(2)}, u32[]{:S(2)}) collective-permute-start(bf16[136,1024]{1,0:T(8,128)(2,1)} %slice.9), channel_id=1, source_target_pairs={{0,192},{32,224},{64,0},{96,32},{128,64},{160,96},{192,128},{224,1... | collective-permute-start | bytes 835592 | tf_op jit(solution)/shard_map/ppermute | solution.py:222
  40.6 5.9 %copy-start.3 = (bf16[136,1024]{1,0:T(8,128)(2,1)}, bf16[136,1024]{1,0:T(8,128)(2,1)S(1)}, u32[]{:S(2)}) copy-start(bf16[136,1024]{1,0:T(8,128)(2,1)S(1)} %collective-permute-done.4.four) | copy-start | bytes 835588
  46.6 1.5 %copy-start = (bf16[8,152,1024]{2,1,0:T(8,128)(2,1)}, bf16[8,152,1024]{2,1,0:T(8,128)(2,1)S(1)}, u32[]{:S(2)}) copy-start(bf16[8,152,1024]{2,1,0:T(8,128)(2,1)S(1)} %all-to-all-done.shared) | copy-start | bytes 7471108

commit v8 on v7

--- a/solution.py
+++ b/solution.py
@@ -42,14 +42,28 @@
 PREPARE = 16_500_000_000
 
 
-def window(mask, at):
-    start = pl.multiple_of(lax.rem(at + NZ, NZ) * WIDE, WIDE)
-    return mask[:, pl.ds(start, WIDE)].astype(f32)
+def start_windows(mask_hbm, windows, sems, offsets):
+    z = lax.axis_index("z")
+    copies = []
+    for k, u in enumerate(offsets):
+        start = pl.multiple_of(lax.rem(z + (u + NZ), NZ) * WIDE, WIDE)
+        copies.append(
+            pltpu.make_async_copy(
+                mask_hbm.at[:, pl.ds(start, WIDE)], windows.at[k], sems.at[k]
+            )
+        )
+        copies[-1].start()
+    return copies
 
 
 def put_mask(ref, part):
     ref[:, 0:512] = part[0:32]
     ref[:, 512:1024] = part[32:64]
+
+
+def put_spectra(ref, spectra):
+    for g in range(8):
+        ref[:, 128 * g : 128 * (g + 1)] = spectra[8 * g : 8 * (g + 1)]
 
 
 def take_mask(ref, at):
@@ -65,12 +79,10 @@
     )
 
 
-def pack(
-    green, mask_hbm, spec_row, near, far, shared, own_mask, own_spec, mask, sem
+def pack_line(
+    green, mask_hbm, spec_row, near, far, own_mask, own_spec, windows, sems
 ):
-    loading = pltpu.make_async_copy(mask_hbm, mask, sem)
-    loading.start()
-    z = lax.axis_index("z")
+    loading = start_windows(mask_hbm, windows, sems, (-1, -2, 3, 0))
     row = spec_row[...]
     col = nt(identity(ROWS), row)
     lane = lax.broadcasted_iota(jnp.int32, (ROWS, 128), 1)
@@ -79,18 +91,27 @@
     )
     own_spec[0:2, 64:128] = row.astype(f32)
     spectra = own_spec[...].astype(bf16)
-    places = [(near, IMAG, REAL, SPEC), (far, IMAG, REAL, SPEC)]
-    places += [(shared.at[q], 64, 0, 144) for q in range(NQ)]
-    for ref, imag, real, spec in places:
-        ref[imag : imag + ROWS, :] = green[1]
-        ref[real : real + ROWS, :] = green[0]
-        for g in range(8):
-            ref[spec : spec + 8, 128 * g : 128 * (g + 1)] = spectra[8 * g : 8 * (g + 1)]
-    loading.wait()
-    for u, ref, at in ((1, near, NEXT), (2, near, MASK), (-3, far, MASK)):
-        put_mask(ref.at[at : at + 32], window(mask, z - u).astype(bf16))
-    own_mask[...] = window(mask, z).astype(bf16)
-    wide = [window(mask, z + u) for u in OFFSETS]
+    for ref in (near, far):
+        ref[IMAG : IMAG + ROWS, :] = green[1]
+        ref[REAL : REAL + ROWS, :] = green[0]
+        put_spectra(ref.at[SPEC : SPEC + 8], spectra)
+    for k, (ref, at) in enumerate(((near, NEXT), (near, MASK), (far, MASK))):
+        loading[k].wait()
+        put_mask(ref.at[at : at + 32], windows[k].astype(f32).astype(bf16))
+    loading[3].wait()
+    own_mask[...] = windows[3].astype(f32).astype(bf16)
+
+
+def pack_plane(green, mask_hbm, own_spec, shared, windows, sems):
+    loading = start_windows(mask_hbm, windows, sems, OFFSETS)
+    spectra = own_spec[...].astype(bf16)
+    for q in range(NQ):
+        shared[q, 0:64, :] = green[0]
+        shared[q, 64:128, :] = green[1]
+        put_spectra(shared.at[q, 144:152], spectra)
+    for copy in loading:
+        copy.wait()
+    wide = [windows[k].astype(f32) for k in range(len(OFFSETS))]
     for q in range(NQ):
         part = jnp.concatenate(
             [w[:, ROWS * q : ROWS * (q + 1)] for w in wide], axis=1
@@ -126,21 +147,27 @@
 
 
 def absorb(
-    shared, source, green, one, two, three, four,
-    near_re, near_im, weight, spec_re, spec_im,
-    out, far_re, far_im, far_spec, back, wt
+    shared, source, green_hbm, one_hbm, two_hbm, three_hbm, four_hbm,
+    near_re, near_im, weight_hbm, spec_re_hbm, spec_im_hbm,
+    out, far_re, far_im, far_spec, back, wt, green, blocks, weight, spec_re, spec_im, sems
 ):
     real, imag = slice(REAL, REAL + ROWS), slice(IMAG, IMAG + ROWS)
-    tall = 5 * ROWS
-    scale = source[...]
-    for at, near, part in ((0, near_re, real), (tall, near_im, imag)):
-        wt[at : at + 4 * ROWS, :] = near[...]
-        wt[at + 4 * ROWS : at + tall, :] = (scale * four[part, :].astype(f32)).astype(
-            bf16
-        )
-    spec = take_spectra(four, SPEC)
-    u_re = jnp.concatenate([spec_re[:, 0:1], spec[:, 0:1]], axis=0)
-    u_im = jnp.concatenate([spec_im[:, 0:1], spec[:, 1:2]], axis=0)
+    tall, most = 5 * ROWS, 4 * ROWS
+    copies = []
+    for src, dst in (
+        (four_hbm, blocks.at[3]),
+        (weight_hbm, weight),
+        (spec_re_hbm, spec_re),
+        (spec_im_hbm, spec_im),
+        (near_re, wt.at[0:most]),
+        (near_im, wt.at[tall : tall + most]),
+        (green_hbm, green),
+        (one_hbm.at[0:MASK], blocks.at[0]),
+        (two_hbm.at[0:MASK], blocks.at[1]),
+        (three_hbm.at[0:MASK], blocks.at[2]),
+    ):
+        copies.append(pltpu.make_async_copy(src, dst, sems.at[len(copies)]))
+        copies[-1].start()
     for q in range(NQ):
         rows = slice(ROWS * q, ROWS * (q + 1))
         ref = shared.at[q]
@@ -152,6 +179,15 @@
             ]
         far_spec[0:2, rows] = ref[144:152, 0:128].astype(f32)[0:2, 64:128]
     behind = nt(identity(4 * ROWS), back[...])
+    for copy in copies:
+        copy.wait()
+    four = blocks.at[3]
+    scale = source[...]
+    wt[most:tall, :] = (scale * four[real, :].astype(f32)).astype(bf16)
+    wt[tall + most : 2 * tall, :] = (scale * four[imag, :].astype(f32)).astype(bf16)
+    spec = take_spectra(four, SPEC)
+    u_re = jnp.concatenate([spec_re[:, 0:1], spec[:, 0:1]], axis=0)
+    u_im = jnp.concatenate([spec_im[:, 0:1], spec[:, 1:2]], axis=0)
     counts = jnp.concatenate(
         [
             weight[0:ROWS, :],
@@ -177,8 +213,8 @@
     by_re = nn(resid, g_re)
     by_im = nn(resid, g_im)
     held = [(green[0], green[1])]
-    for ref in (one, two, three, four):
-        held.append((ref[real, :], ref[imag, :]))
+    for k in range(4):
+        held.append((blocks[k, real, :], blocks[k, imag, :]))
     total = jnp.zeros((ROWS, CELLS), f32)
     for k, (re, im) in enumerate(held):
         rows = slice(ROWS * k, ROWS * (k + 1))
@@ -225,23 +261,32 @@
 def local(spectra, green, source, pair_mask):
     g = green[0]
     vmem = pl.BlockSpec(memory_space=pltpu.VMEM)
-    near, far, shared, own_mask, own_spec = pl.pallas_call(
-        pack,
+    hbm = pl.BlockSpec(memory_space=pltpu.HBM)
+    windows = [
+        pltpu.VMEM((4, ROWS, WIDE), jnp.int32),
+        pltpu.SemaphoreType.DMA((4,)),
+    ]
+    near, far, own_mask, own_spec = pl.pallas_call(
+        pack_line,
         out_shape=[
             shape(bf16, FULL, CELLS),
             shape(bf16, NEXT, CELLS),
-            shape(bf16, NQ, SHARED, CELLS),
             shape(bf16, ROWS, WIDE),
             shape(f32, ROWS, 128),
         ],
-        in_specs=[vmem, pl.BlockSpec(memory_space=pl.ANY), vmem],
-        out_specs=[vmem] * 5,
-        scratch_shapes=[
-            pltpu.VMEM((ROWS, NZ * WIDE), jnp.int32),
-            pltpu.SemaphoreType.DMA,
-        ],
-        name="pack",
+        in_specs=[vmem, hbm, vmem],
+        out_specs=[vmem] * 4,
+        scratch_shapes=windows,
+        name="pack_line",
     )(g, pair_mask, spectra[0])
+    shared = pl.pallas_call(
+        pack_plane,
+        out_shape=shape(bf16, NQ, SHARED, CELLS),
+        in_specs=[vmem, hbm, vmem],
+        out_specs=vmem,
+        scratch_shapes=windows,
+        name="pack_plane",
+    )(g, pair_mask, own_spec)
     three = from_z(from_z(far, -2), -1)
     one = from_z(near, 1)
     shared = lax.all_to_all(shared, PLANE, 0, 0, tiled=True)
@@ -263,7 +308,7 @@
     part = pl.pallas_call(
         absorb,
         out_shape=shape(f32, NZ, 1, LONG),
-        in_specs=[vmem] * 12,
+        in_specs=[vmem] * 2 + [hbm] * 10,
         out_specs=vmem,
         scratch_shapes=[
             pltpu.VMEM((WIDE, CELLS), bf16),
@@ -271,6 +316,12 @@
             pltpu.VMEM((8, WIDE), f32),
             pltpu.VMEM((WIDE, 4 * ROWS), bf16),
             pltpu.VMEM((10 * ROWS, CELLS), bf16),
+            pltpu.VMEM((2, ROWS, CELLS), bf16),
+            pltpu.VMEM((4, MASK, CELLS), bf16),
+            pltpu.VMEM((most, WIDE), f32),
+            pltpu.VMEM((most, 128), f32),
+            pltpu.VMEM((most, 128), f32),
+            pltpu.SemaphoreType.DMA((10,)),
         ],
         name="absorb",
     )(shared, source, g, one, two, three, four, *ready)

time: 86.2 us -> 89.7 us (1.041)
  Pallas kernels: 16.7 us -> 20.4 us
    ppermute x5, waiting for transfers between devices: 15.1 us -> 11.2 us  [from_z(): return lax.ppermute(array, 'z', [(z, (z - u) % NZ) for z in range(NZ)])]
    all_to_all x1, waiting for transfers between devices: 5.94 us -> 9.69 us  [local(): shared = lax.all_to_all(shared, PLANE, 0, 0, tiled=True)]
    pallas_call x1 -> x2, Pallas kernels: 4 us -> 6.79 us  [the longest x1 3.69 us: local(): pl.pallas_call(pack_plane, out_shape=shape(bf16, NQ, SHARED, CELLS), in_s...]
    pallas_call x1, Pallas kernels: 6.79 us -> 7.7 us  [local(): pl.pallas_call(absorb, out_shape=shape(f32, NZ, 1, LONG), in_specs=[vmem]...]
  transfers between devices with their start and end apart: 6 -> 6, of which waited for: 6 -> 5; matrix products, arithmetic and copies ran while one was open for 1% -> 1% of each run, Pallas kernels for 3% -> 7%
where the time goes in v8:
time: 89.7 us; the launch traced here: 89.1 us
  blocking collectives  27.4 us (31%)
  waiting for transfers between devices  20.9 us (23%)
  Pallas kernels  20.4 us (23%)
  starting transfers between devices  17.5 us (20%)
  local copies, waits for them, and re-layouts  2.28 us (3%)
    all_to_all x1, blocking collectives, local(): part = lax.all_to_all(part, PLANE + FREQ, 0, 0, tiled=True)  15.5 us
    ppermute x5, starting transfers between devices, from_z(): return lax.ppermute(array, 'z', [(z, (z - u) % NZ) for z in range(NZ)])  12.4 us
    all_to_all x1, blocking collectives, local(): part = lax.all_to_all(part, 'z', 0, 0, tiled=True)  11.9 us
    ppermute x5, waiting for transfers between devices, from_z(): return lax.ppermute(array, 'z', [(z, (z - u) % NZ) for z in range(NZ)])  11.2 us
    all_to_all x1, waiting for transfers between devices, local(): shared = lax.all_to_all(shared, PLANE, 0, 0, tiled=True)  9.69 us
    pallas_call x1, Pallas kernels, local(): pl.pallas_call(absorb, out_shape=shape(f32, NZ, 1, LONG), in_specs=[vmem]...  7.7 us
    all_to_all x1, starting transfers between devices, local(): shared = lax.all_to_all(shared, PLANE, 0, 0, tiled=True)  5.13 us
    pallas_call x1, Pallas kernels, local(): pl.pallas_call(pack_plane, out_shape=shape(bf16, NQ, SHARED, CELLS), in_s...  3.69 us
  transfers between devices with their start and end apart: 6, of which 5 were waited for; matrix products, arithmetic and copies ran while one was open for 1% of the time, Pallas kernels for 7%

profile of v8, /device:TPU:1, one launch (start us, length us, event | category | flops | bytes accessed | tf_op | source)
XLA Modules:
  0.0 89.1 jit_solution(5879426068126437047)
XLA Ops:
  0.6 3.1 %pack_line.1 = (bf16[200,1024]{1,0:T(8,128)(2,1)}, bf16[168,1024]{1,0:T(8,128)(2,1)}, bf16[64,512]{1,0:T(8,128)(2,1)}, f32[64,128]{1,0:T(8,128)}) custom-call(bf16[2,64,1024]{2,1,0:T(8,128)(2,1)} %bitcast.2, s32[64,4096]{1,0:T(8,128)} %mask_hbm.3, bf16[2,64]{1,0:T(2,128)(2,1)} %bitcast.6), custom_call_target="tpu_custom_call" | custom-call | tf_op jit(solution)/shard_map/pack_line/pallas_call | solution.py:269
  3.7 6.5 %collective-permute-start = (bf16[200,1024]{1,0:T(8,128)(2,1)}, bf16[200,1024]{1,0:T(8,128)(2,1)S(1)}, u32[]{:S(2)}, u32[]{:S(2)}) collective-permute-start(bf16[200,1024]{1,0:T(8,128)(2,1)} %get-tuple-element.12), channel_id=1, source_target_pairs={{0,224},{32,0},{64,32},{96,64},{128,96},{160,128},{192,160},{224,1... | collective-permute-start | bytes 1228808 | tf_op jit(solution)/shard_map/ppermute | solution.py:258
  10.2 0.0 collective-permute-start.2
  10.2 3.7 %pack_plane.1 = bf16[8,152,1024]{2,1,0:T(8,128)(2,1)} custom-call(bf16[2,64,1024]{2,1,0:T(8,128)(2,1)} %bitcast.3, s32[64,4096]{1,0:T(8,128)} %mask_hbm.3, f32[64,128]{1,0:T(8,128)} %get-tuple-element.11.own_spec), custom_call_target="tpu_custom_call" | custom-call | tf_op jit(solution)/shard_map/pack_plane/pallas_call | solution.py:282
  13.9 5.1 %all-to-all-start = ((bf16[8,152,1024]{2,1,0:T(8,128)(2,1)}), bf16[8,152,1024]{2,1,0:T(8,128)(2,1)S(1)}, u32[]{:S(2)}, u32[]{:S(2)}) async-start(bf16[8,152,1024]{2,1,0:T(8,128)(2,1)} %pack_plane.1), calls=%async_computation | async-start | bytes 4980736 | tf_op jit(solution)/shard_map/all_to_all | solution.py:292
  19.1 0.0 collective-permute-done.one.one_hbm
  19.1 0.0 copy-start.1
  19.1 3.0 %collective-permute-start.1 = (bf16[168,1024]{1,0:T(8,128)(2,1)S(1)}, bf16[168,1024]{1,0:T(8,128)(2,1)S(1)}, u32[]{:S(2)}, u32[]{:S(2)}) collective-permute-start(bf16[168,1024]{1,0:T(8,128)(2,1)S(1)} %slice.8), channel_id=1, source_target_pairs={{0,224},{32,0},{64,32},{96,64},{128,96},{160,128},{192,160},{224,1... | collective-permute-start | bytes 1032200 | tf_op jit(solution)/shard_map/ppermute | solution.py:258
  22.1 4.9 %collective-permute-done.2 = bf16[168,1024]{1,0:T(8,128)(2,1)} collective-permute-done((bf16[168,1024]{1,0:T(8,128)(2,1)}, bf16[168,1024]{1,0:T(8,128)(2,1)}, u32[]{:S(2)}, u32[]{:S(2)}) %collective-permute-start.2) | collective-permute-done | bytes 344096 | tf_op jit(solution)/shard_map/ppermute | solution.py:258
  27.0 0.0 collective-permute-start.3
  27.0 0.9 %collective-permute-done.1.two.two_hbm = bf16[168,1024]{1,0:T(8,128)(2,1)S(1)} collective-permute-done((bf16[168,1024]{1,0:T(8,128)(2,1)S(1)}, bf16[168,1024]{1,0:T(8,128)(2,1)S(1)}, u32[]{:S(2)}, u32[]{:S(2)}) %collective-permute-start.1) | collective-permute-done | bytes 344096 | tf_op jit(solution)/shard_map/ppermute | solution.py:258
  27.9 0.0 copy-start.2
  27.9 0.8 slice.9
  28.7 2.9 %collective-permute-start.4 = (bf16[136,1024]{1,0:T(8,128)(2,1)}, bf16[136,1024]{1,0:T(8,128)(2,1)S(1)}, u32[]{:S(2)}, u32[]{:S(2)}) collective-permute-start(bf16[136,1024]{1,0:T(8,128)(2,1)} %slice.9), channel_id=1, source_target_pairs={{0,192},{32,224},{64,0},{96,32},{128,64},{160,96},{192,128},{224,1... | collective-permute-start | bytes 835592 | tf_op jit(solution)/shard_map/ppermute | solution.py:258
  31.6 3.4 %collective-permute-done.3.three.three_hbm = bf16[168,1024]{1,0:T(8,128)(2,1)} collective-permute-done((bf16[168,1024]{1,0:T(8,128)(2,1)}, bf16[168,1024]{1,0:T(8,128)(2,1)}, u32[]{:S(2)}, u32[]{:S(2)}) %collective-permute-start.3) | collective-permute-done | bytes 344096 | tf_op jit(solution)/shard_map/ppermute | solution.py:258
  35.0 0.0 copy-done.1
  35.0 0.0 copy-done.2
  35.0 2.7 %prepare.1 = (bf16[256,1024]{1,0:T(8,128)(2,1)}, bf16[256,1024]{1,0:T(8,128)(2,1)}, f32[256,512]{1,0:T(8,128)}, f32[256,128]{1,0:T(8,128)}, f32[256,128]{1,0:T(8,128)}) custom-call(f32[1,1024]{1,0:T(1,128)} %source.5, bf16[2,64,1024]{2,1,0:T(8,128)(2,1)} %bitcast.4, bf16[64,512]{1,0:T(8,128)(2,1)} %get-tuple-element.14.own_mask, ...), custom_call_target="tpu_custom_call" | custom-call | flops 16499999744 | tf_op jit(solution)/shard_map/prepare/pallas_call | solution.py:296
  37.8 2.0 %collective-permute-done.4.four_hbm = bf16[136,1024]{1,0:T(8,128)(2,1)S(1)} collective-permute-done((bf16[136,1024]{1,0:T(8,128)(2,1)}, bf16[136,1024]{1,0:T(8,128)(2,1)S(1)}, u32[]{:S(2)}, u32[]{:S(2)}) %collective-permute-start.4) | collective-permute-done | bytes 278560 | tf_op jit(solution)/shard_map/ppermute | solution.py:258
  39.7 0.0 copy-start.3
  39.7 9.7 %all-to-all-done.shared = bf16[8,152,1024]{2,1,0:T(8,128)(2,1)S(1)} async-done(((bf16[8,152,1024]{2,1,0:T(8,128)(2,1)}), bf16[8,152,1024]{2,1,0:T(8,128)(2,1)S(1)}, u32[]{:S(2)}, u32[]{:S(2)}) %all-to-all-start) | async-done | bytes 2490400 | tf_op jit(solution)/shard_map/all_to_all | solution.py:292
  49.4 0.0 copy-start
  49.4 0.0 copy-done.3
  49.4 1.5 %copy-done = bf16[8,152,1024]{2,1,0:T(8,128)(2,1)} copy-done((bf16[8,152,1024]{2,1,0:T(8,128)(2,1)}, bf16[8,152,1024]{2,1,0:T(8,128)(2,1)S(1)}, u32[]{:S(2)}) %copy-start) | copy-done | bytes 2490392
  50.9 7.7 %absorb.1 = f32[8,1,1152]{2,1,0:T(1,128)} custom-call(bf16[8,152,1024]{2,1,0:T(8,128)(2,1)} %copy-done, f32[1,1024]{1,0:T(1,128)} %source.5, bf16[2,64,1024]{2,1,0:T(8,128)(2,1)} %bitcast.5, bf16[200,1024]{1,0:T(8,128)(2,1)} %copy-done.1, bf16[168,1024]{1,0:T(8,128)(2,1)} %copy-done.2, bf16[168,1024]{1,0:T(8,128)(2,1)} %collective-permute-done.3.three.three_hbm, ...), custom_call_target="tpu_custom_call" | custom-call | tf_op jit(solution)/shard_map/absorb/pallas_call | solution.py:308
  58.6 11.9 %all_to_all.15.parts = f32[8,1,1152]{2,1,0:T(1,128)} all-to-all(f32[8,1,1152]{2,1,0:T(1,128)} %absorb.1), channel_id=1, replica_groups=mesh['z'=8,'xl'=2,'y'=4,'xh'=2,'core'=2] {'z'}, dimensions={0} | all-to-all | bytes 73728 | tf_op jit(solution)/shard_map/all_to_all | solution.py:328
  70.4 1.5 %gather_z.1 = f32[32,1,1152]{2,1,0:T(1,128)} custom-call(f32[8,1,1152]{2,1,0:T(1,128)} %all_to_all.15.parts), custom_call_target="tpu_custom_call" | custom-call | tf_op jit(solution)/shard_map/gather_z/pallas_call | solution.py:329
  71.9 15.5 %all_to_all.16.parts = f32[32,1,1152]{2,1,0:T(1,128)} all-to-all(f32[32,1,1152]{2,1,0:T(1,128)} %gather_z.1), channel_id=1, replica_groups=mesh['z'=8,'xl'=2,'y'=4,'xh'=2,'core'=2] {'xl','y','xh','core'}, dimensions={0} | all-to-all | bytes 294912 | tf_op jit(solution)/shard_map/all_to_all | solution.py:336
  87.4 1.7 %finish.1 = (f32[1,1024]{1,0:T(1,128)}, f32[1]{0:T(128)}) custom-call(f32[32,1,1152]{2,1,0:T(1,128)} %all_to_all.16.parts, f32[1,1024]{1,0:T(1,128)} %source.5), custom_call_target="tpu_custom_call" | custom-call | tf_op jit(solution)/shard_map/finish/pallas_call | solution.py:337
  (1 shorter events, 0.0 us)
Async XLA Ops:
  3.7 15.3 %collective-permute-start = (bf16[200,1024]{1,0:T(8,128)(2,1)}, bf16[200,1024]{1,0:T(8,128)(2,1)S(1)}, u32[]{:S(2)}, u32[]{:S(2)}) collective-permute-start(bf16[200,1024]{1,0:T(8,128)(2,1)} %get-tuple-element.12), channel_id=1, source_target_pairs={{0,224},{32,0},{64,32},{96,64},{128,96},{160,128},{192,160},{224,1... | collective-permute-start | bytes 1228808 | tf_op jit(solution)/shard_map/ppermute | solution.py:258
  10.2 16.7 %collective-permute-start.2 = (bf16[168,1024]{1,0:T(8,128)(2,1)}, bf16[168,1024]{1,0:T(8,128)(2,1)}, u32[]{:S(2)}, u32[]{:S(2)}) collective-permute-start(bf16[168,1024]{1,0:T(8,128)(2,1)} %get-tuple-element.13), channel_id=1, source_target_pairs={{0,64},{32,96},{64,128},{96,160},{128,192},{160,224},{192,0},{224,... | collective-permute-start | bytes 1032200 | tf_op jit(solution)/shard_map/ppermute | solution.py:258
  13.9 35.5 %all-to-all-start = ((bf16[8,152,1024]{2,1,0:T(8,128)(2,1)}), bf16[8,152,1024]{2,1,0:T(8,128)(2,1)S(1)}, u32[]{:S(2)}, u32[]{:S(2)}) async-start(bf16[8,152,1024]{2,1,0:T(8,128)(2,1)} %pack_plane.1), calls=%async_computation | async-start | bytes 4980736 | tf_op jit(solution)/shard_map/all_to_all | solution.py:292
  19.1 16.0 %copy-start.1 = (bf16[200,1024]{1,0:T(8,128)(2,1)}, bf16[200,1024]{1,0:T(8,128)(2,1)S(1)}, u32[]{:S(2)}) copy-start(bf16[200,1024]{1,0:T(8,128)(2,1)S(1)} %collective-permute-done.one.one_hbm) | copy-start | bytes 1228804
  19.1 8.8 %collective-permute-start.1 = (bf16[168,1024]{1,0:T(8,128)(2,1)S(1)}, bf16[168,1024]{1,0:T(8,128)(2,1)S(1)}, u32[]{:S(2)}, u32[]{:S(2)}) collective-permute-start(bf16[168,1024]{1,0:T(8,128)(2,1)S(1)} %slice.8), channel_id=1, source_target_pairs={{0,224},{32,0},{64,32},{96,64},{128,96},{160,128},{192,160},{224,1... | collective-permute-start | bytes 1032200 | tf_op jit(solution)/shard_map/ppermute | solution.py:258
  27.0 8.0 %collective-permute-start.3 = (bf16[168,1024]{1,0:T(8,128)(2,1)}, bf16[168,1024]{1,0:T(8,128)(2,1)}, u32[]{:S(2)}, u32[]{:S(2)}) collective-permute-start(bf16[168,1024]{1,0:T(8,128)(2,1)} %collective-permute-done.2), channel_id=1, source_target_pairs={{0,32},{32,64},{64,96},{96,128},{128,160},{160,192},{192,224},{224... | collective-permute-start | bytes 1032200 | tf_op jit(solution)/shard_map/ppermute | solution.py:258
  27.9 7.1 %copy-start.2 = (bf16[168,1024]{1,0:T(8,128)(2,1)}, bf16[168,1024]{1,0:T(8,128)(2,1)S(1)}, u32[]{:S(2)}) copy-start(bf16[168,1024]{1,0:T(8,128)(2,1)S(1)} %collective-permute-done.1.two.two_hbm) | copy-start | bytes 1032196
  28.7 11.0 %collective-permute-start.4 = (bf16[136,1024]{1,0:T(8,128)(2,1)}, bf16[136,1024]{1,0:T(8,128)(2,1)S(1)}, u32[]{:S(2)}, u32[]{:S(2)}) collective-permute-start(bf16[136,1024]{1,0:T(8,128)(2,1)} %slice.9), channel_id=1, source_target_pairs={{0,192},{32,224},{64,0},{96,32},{128,64},{160,96},{192,128},{224,1... | collective-permute-start | bytes 835592 | tf_op jit(solution)/shard_map/ppermute | solution.py:258
  39.7 9.7 %copy-start.3 = (bf16[136,1024]{1,0:T(8,128)(2,1)}, bf16[136,1024]{1,0:T(8,128)(2,1)S(1)}, u32[]{:S(2)}) copy-start(bf16[136,1024]{1,0:T(8,128)(2,1)S(1)} %collective-permute-done.4.four_hbm) | copy-start | bytes 835588
  49.4 1.5 %copy-start = (bf16[8,152,1024]{2,1,0:T(8,128)(2,1)}, bf16[8,152,1024]{2,1,0:T(8,128)(2,1)S(1)}, u32[]{:S(2)}) copy-start(bf16[8,152,1024]{2,1,0:T(8,128)(2,1)S(1)} %all-to-all-done.shared) | copy-start | bytes 7471108

commit v9 on v7

--- a/solution.py
+++ b/solution.py
@@ -65,11 +65,12 @@
     )
 
 
-def pack(
-    green, mask_hbm, spec_row, near, far, shared, own_mask, own_spec, mask, sem
-):
-    loading = pltpu.make_async_copy(mask_hbm, mask, sem)
-    loading.start()
+def put_spectra(ref, spectra):
+    for g in range(8):
+        ref[:, 128 * g : 128 * (g + 1)] = spectra[8 * g : 8 * (g + 1)]
+
+
+def pack_line(green, mask, spec_row, near, far, own_mask, own_spec):
     z = lax.axis_index("z")
     row = spec_row[...]
     col = nt(identity(ROWS), row)
@@ -79,19 +80,23 @@
     )
     own_spec[0:2, 64:128] = row.astype(f32)
     spectra = own_spec[...].astype(bf16)
-    places = [(near, IMAG, REAL, SPEC), (far, IMAG, REAL, SPEC)]
-    places += [(shared.at[q], 64, 0, 144) for q in range(NQ)]
-    for ref, imag, real, spec in places:
-        ref[imag : imag + ROWS, :] = green[1]
-        ref[real : real + ROWS, :] = green[0]
-        for g in range(8):
-            ref[spec : spec + 8, 128 * g : 128 * (g + 1)] = spectra[8 * g : 8 * (g + 1)]
-    loading.wait()
+    for ref in (near, far):
+        ref[IMAG : IMAG + ROWS, :] = green[1]
+        ref[REAL : REAL + ROWS, :] = green[0]
+        put_spectra(ref.at[SPEC : SPEC + 8], spectra)
     for u, ref, at in ((1, near, NEXT), (2, near, MASK), (-3, far, MASK)):
         put_mask(ref.at[at : at + 32], window(mask, z - u).astype(bf16))
     own_mask[...] = window(mask, z).astype(bf16)
+
+
+def pack_plane(green, mask, own_spec, shared):
+    z = lax.axis_index("z")
+    spectra = own_spec[...].astype(bf16)
     wide = [window(mask, z + u) for u in OFFSETS]
     for q in range(NQ):
+        shared[q, 0:64, :] = green[0]
+        shared[q, 64:128, :] = green[1]
+        put_spectra(shared.at[q, 144:152], spectra)
         part = jnp.concatenate(
             [w[:, ROWS * q : ROWS * (q + 1)] for w in wide], axis=1
         ).astype(bf16)
@@ -99,10 +104,13 @@
             shared[q, 128:144, 256 * g : 256 * (g + 1)] = part[16 * g : 16 * (g + 1)]
 
 
-def prepare(
-    source, green, own_mask, own_spec, one, two, three,
-    wt_re, wt_im, weight, spec_re, spec_im
-):
+MOST = 4 * ROWS
+WT_RE, WT_IM, NEAR_RE, NEAR_IM, COUNT = (MOST * i for i in range(5))
+SPECTRA = COUNT + MOST // 2
+BUNDLE = SPECTRA + MOST // 8
+
+
+def prepare(source, green, own_mask, own_spec, one, two, three, bundle):
     scale = source[...]
     real, imag = slice(REAL, REAL + ROWS), slice(IMAG, IMAG + ROWS)
     us = [own_spec[...]]
@@ -117,30 +125,46 @@
         take_mask(three, MASK),
     ]
     for k, (re, im) in enumerate(held):
-        rows = slice(ROWS * k, ROWS * (k + 1))
-        wt_re[rows, :] = (scale * re.astype(f32)).astype(bf16)
-        wt_im[rows, :] = (scale * im.astype(f32)).astype(bf16)
-        weight[rows, :] = masks[k]
-        spec_re[rows, :] = jnp.broadcast_to(us[k][:, 0:1], (ROWS, 128))
-        spec_im[rows, :] = jnp.broadcast_to(us[k][:, 1:2], (ROWS, 128))
-
-
-def absorb(
-    shared, source, green, one, two, three, four,
-    near_re, near_im, weight, spec_re, spec_im,
-    out, far_re, far_im, far_spec, back, wt
-):
+        at = ROWS * k
+        bundle[NEAR_RE + at : NEAR_RE + at + ROWS, :] = re
+        bundle[NEAR_IM + at : NEAR_IM + at + ROWS, :] = im
+        bundle[WT_RE + at : WT_RE + at + ROWS, :] = (scale * re.astype(f32)).astype(bf16)
+        bundle[WT_IM + at : WT_IM + at + ROWS, :] = (scale * im.astype(f32)).astype(bf16)
+    counts = jnp.concatenate(masks, axis=0).astype(bf16)
+    for h in range(2):
+        bundle[COUNT : COUNT + MOST // 2, WIDE * h : WIDE * (h + 1)] = counts[
+            MOST // 2 * h : MOST // 2 * (h + 1)
+        ]
+    spectra = jnp.concatenate(us, axis=0).astype(bf16)
+    for h in range(8):
+        bundle[SPECTRA : SPECTRA + MOST // 8, 128 * h : 128 * (h + 1)] = spectra[
+            MOST // 8 * h : MOST // 8 * (h + 1)
+        ]
+
+
+def absorb(shared, source, four, bundle, out, far_re, far_im, far_spec, back, wt):
     real, imag = slice(REAL, REAL + ROWS), slice(IMAG, IMAG + ROWS)
     tall = 5 * ROWS
     scale = source[...]
-    for at, near, part in ((0, near_re, real), (tall, near_im, imag)):
-        wt[at : at + 4 * ROWS, :] = near[...]
-        wt[at + 4 * ROWS : at + tall, :] = (scale * four[part, :].astype(f32)).astype(
-            bf16
-        )
-    spec = take_spectra(four, SPEC)
-    u_re = jnp.concatenate([spec_re[:, 0:1], spec[:, 0:1]], axis=0)
-    u_im = jnp.concatenate([spec_im[:, 0:1], spec[:, 1:2]], axis=0)
+    for at, near, part in ((0, WT_RE, real), (tall, WT_IM, imag)):
+        wt[at : at + MOST, :] = bundle[near : near + MOST, :]
+        wt[at + MOST : at + tall, :] = (scale * four[part, :].astype(f32)).astype(bf16)
+    spec = jnp.concatenate(
+        [
+            bundle[SPECTRA : SPECTRA + MOST // 8, 128 * h : 128 * (h + 1)].astype(f32)
+            for h in range(8)
+        ]
+        + [take_spectra(four, SPEC)],
+        axis=0,
+    )
+    u_re, u_im = spec[:, 0:1], spec[:, 1:2]
+    weight = jnp.concatenate(
+        [
+            bundle[COUNT : COUNT + MOST // 2, WIDE * h : WIDE * (h + 1)].astype(f32)
+            for h in range(2)
+        ],
+        axis=0,
+    )
     for q in range(NQ):
         rows = slice(ROWS * q, ROWS * (q + 1))
         ref = shared.at[q]
@@ -154,8 +178,8 @@
     behind = nt(identity(4 * ROWS), back[...])
     counts = jnp.concatenate(
         [
-            weight[0:ROWS, :],
-            weight[ROWS : 4 * ROWS, :] + behind[0 : 3 * ROWS],
+            weight[0:ROWS],
+            weight[ROWS : 4 * ROWS] + behind[0 : 3 * ROWS],
             behind[3 * ROWS : 4 * ROWS],
         ],
         axis=0,
@@ -176,9 +200,16 @@
     )
     by_re = nn(resid, g_re)
     by_im = nn(resid, g_im)
-    held = [(green[0], green[1])]
-    for ref in (one, two, three, four):
-        held.append((ref[real, :], ref[imag, :]))
+    held = []
+    for k in range(4):
+        at = ROWS * k
+        held.append(
+            (
+                bundle[NEAR_RE + at : NEAR_RE + at + ROWS, :],
+                bundle[NEAR_IM + at : NEAR_IM + at + ROWS, :],
+            )
+        )
+    held.append((four[real, :], four[imag, :]))
     total = jnp.zeros((ROWS, CELLS), f32)
     for k, (re, im) in enumerate(held):
         rows = slice(ROWS * k, ROWS * (k + 1))
@@ -225,36 +256,35 @@
 def local(spectra, green, source, pair_mask):
     g = green[0]
     vmem = pl.BlockSpec(memory_space=pltpu.VMEM)
-    near, far, shared, own_mask, own_spec = pl.pallas_call(
-        pack,
+    near, far, own_mask, own_spec = pl.pallas_call(
+        pack_line,
         out_shape=[
             shape(bf16, FULL, CELLS),
             shape(bf16, NEXT, CELLS),
-            shape(bf16, NQ, SHARED, CELLS),
             shape(bf16, ROWS, WIDE),
             shape(f32, ROWS, 128),
         ],
-        in_specs=[vmem, pl.BlockSpec(memory_space=pl.ANY), vmem],
-        out_specs=[vmem] * 5,
-        scratch_shapes=[
-            pltpu.VMEM((ROWS, NZ * WIDE), jnp.int32),
-            pltpu.SemaphoreType.DMA,
-        ],
-        name="pack",
+        in_specs=[vmem] * 3,
+        out_specs=[vmem] * 4,
+        name="pack_line",
     )(g, pair_mask, spectra[0])
+    shared = pl.pallas_call(
+        pack_plane,
+        out_shape=shape(bf16, NQ, SHARED, CELLS),
+        in_specs=[vmem] * 3,
+        out_specs=vmem,
+        name="pack_plane",
+    )(g, pair_mask, own_spec)
     three = from_z(from_z(far, -2), -1)
     one = from_z(near, 1)
     shared = lax.all_to_all(shared, PLANE, 0, 0, tiled=True)
     two = from_z(one[:NEXT], 1)
     four = from_z(two[:MASK], 2)
-    most = 4 * ROWS
     ready = pl.pallas_call(
         prepare,
-        out_shape=[shape(bf16, most, CELLS)] * 2
-        + [shape(f32, most, WIDE)]
-        + [shape(f32, most, 128)] * 2,
+        out_shape=shape(bf16, BUNDLE, CELLS),
         in_specs=[vmem] * 7,
-        out_specs=[vmem] * 5,
+        out_specs=vmem,
         cost_estimate=pl.CostEstimate(
             flops=PREPARE, transcendentals=0, bytes_accessed=0
         ),
@@ -263,7 +293,7 @@
     part = pl.pallas_call(
         absorb,
         out_shape=shape(f32, NZ, 1, LONG),
-        in_specs=[vmem] * 12,
+        in_specs=[vmem] * 4,
         out_specs=vmem,
         scratch_shapes=[
             pltpu.VMEM((WIDE, CELLS), bf16),
@@ -273,7 +303,8 @@
             pltpu.VMEM((10 * ROWS, CELLS), bf16),
         ],
         name="absorb",
-    )(shared, source, g, one, two, three, four, *ready)
+        compiler_params=pltpu.CompilerParams(vmem_limit_bytes=40 << 20),
+    )(shared, source, four, ready)
     part = lax.all_to_all(part, "z", 0, 0, tiled=True)
     part = pl.pallas_call(
         gather_z,
@@ -281,6 +312,7 @@
         in_specs=[vmem],
         out_specs=vmem,
         name="gather_z",
+        compiler_params=pltpu.CompilerParams(vmem_limit_bytes=8 << 20),
     )(part)
     part = lax.all_to_all(part, PLANE + FREQ, 0, 0, tiled=True)
     return pl.pallas_call(
@@ -289,6 +321,7 @@
         in_specs=[vmem, vmem],
         out_specs=(vmem, pl.BlockSpec(memory_space=pltpu.SMEM)),
         name="finish",
+        compiler_params=pltpu.CompilerParams(vmem_limit_bytes=8 << 20),
     )(part, source)
 
 

time: 86.2 us -> 81.1 us (0.941)
  Pallas kernels: 16.7 us -> 12.8 us
  blocking collectives: 27.8 us -> 26.8 us
    ppermute x5, waiting for transfers between devices: 15.1 us -> 11 us  [from_z(): return lax.ppermute(array, 'z', [(z, (z - u) % NZ) for z in range(NZ)])]
    all_to_all x1, waiting for transfers between devices: 5.94 us -> 9.7 us  [local(): shared = lax.all_to_all(shared, PLANE, 0, 0, tiled=True)]
    pallas_call x1, Pallas kernels: 6.79 us -> 3.61 us  [local(): pl.pallas_call(absorb, out_shape=shape(f32, NZ, 1, LONG), in_specs=[vmem]...]
    pallas_call x2 -> x3, Pallas kernels: 6.73 us -> 8.4 us  [the longest x1 3.03 us: local(): pl.pallas_call(prepare, out_shape=shape(bf16, BUNDLE, CELLS), in_specs=[v...]
    pallas_call x1, Pallas kernels: 1.47 us -> 0.05 us  [local(): pl.pallas_call(gather_z, out_shape=shape(f32, NQ * NF, 1, LONG), in_specs...]
    unnamed x8 -> x10, local copies, waits for them, and re-layouts: 1.47 us -> 2.43 us
    pallas_call x1, Pallas kernels: 1.68 us -> 0.76 us  [local(): pl.pallas_call(finish, out_shape=(shape(f32, 1, CELLS), shape(f32, 1)), i...]
  transfers between devices with their start and end apart: 6 -> 6, of which waited for: 6 -> 6; matrix products, arithmetic and copies ran while one was open for 1% -> 0% of each run, Pallas kernels for 3% -> 7%
where the time goes in v9:
time: 81.1 us; the launch traced here: 80.8 us
  blocking collectives  26.8 us (33%)
  waiting for transfers between devices  20.7 us (26%)
  starting transfers between devices  17.3 us (21%)
  Pallas kernels  12.8 us (16%)
  local copies, waits for them, and re-layouts  2.47 us (3%)
    all_to_all x1, blocking collectives, local(): part = lax.all_to_all(part, PLANE + FREQ, 0, 0, tiled=True)  15.2 us
    ppermute x5, starting transfers between devices, from_z(): return lax.ppermute(array, 'z', [(z, (z - u) % NZ) for z in range(NZ)])  12.2 us
    all_to_all x1, blocking collectives, local(): part = lax.all_to_all(part, 'z', 0, 0, tiled=True)  11.6 us
    ppermute x5, waiting for transfers between devices, from_z(): return lax.ppermute(array, 'z', [(z, (z - u) % NZ) for z in range(NZ)])  11 us
    all_to_all x1, waiting for transfers between devices, local(): shared = lax.all_to_all(shared, PLANE, 0, 0, tiled=True)  9.7 us
    all_to_all x1, starting transfers between devices, local(): shared = lax.all_to_all(shared, PLANE, 0, 0, tiled=True)  5.12 us
    pallas_call x1, Pallas kernels, local(): pl.pallas_call(absorb, out_shape=shape(f32, NZ, 1, LONG), in_specs=[vmem]...  3.61 us
    pallas_call x1, Pallas kernels, local(): pl.pallas_call(prepare, out_shape=shape(bf16, BUNDLE, CELLS), in_specs=[v...  3.03 us
  transfers between devices with their start and end apart: 6, of which 6 were waited for; matrix products, arithmetic and copies ran while one was open for 0% of the time, Pallas kernels for 7%

profile of v9, /device:TPU:1, one launch (start us, length us, event | category | flops | bytes accessed | tf_op | source)
XLA Modules:
  0.0 80.8 jit_solution(2827394175553741091)
XLA Ops:
  0.6 2.4 %pack_line.1 = (bf16[200,1024]{1,0:T(8,128)(2,1)}, bf16[168,1024]{1,0:T(8,128)(2,1)}, bf16[64,512]{1,0:T(8,128)(2,1)}, f32[64,128]{1,0:T(8,128)}) custom-call(bf16[2,64,1024]{2,1,0:T(8,128)(2,1)} %bitcast.2, s32[64,4096]{1,0:T(8,128)} %mask.3, bf16[2,64]{1,0:T(2,128)(2,1)} %bitcast.5), custom_call_target="tpu_custom_call" | custom-call | tf_op jit(solution)/shard_map/pack_line/pallas_call | solution.py:259
  3.0 6.4 %collective-permute-start = (bf16[200,1024]{1,0:T(8,128)(2,1)}, bf16[200,1024]{1,0:T(8,128)(2,1)S(1)}, u32[]{:S(2)}, u32[]{:S(2)}) collective-permute-start(bf16[200,1024]{1,0:T(8,128)(2,1)} %get-tuple-element.7), channel_id=1, source_target_pairs={{0,224},{32,0},{64,32},{96,64},{128,96},{160,128},{192,160},{224,1... | collective-permute-start | bytes 1228808 | tf_op jit(solution)/shard_map/ppermute | solution.py:253
  9.4 0.0 collective-permute-start.3
  9.4 3.0 %pack_plane.1 = bf16[8,152,1024]{2,1,0:T(8,128)(2,1)} custom-call(bf16[2,64,1024]{2,1,0:T(8,128)(2,1)} %bitcast.3, s32[64,4096]{1,0:T(8,128)} %mask.3, f32[64,128]{1,0:T(8,128)} %get-tuple-element.6.own_spec), custom_call_target="tpu_custom_call" | custom-call | tf_op jit(solution)/shard_map/pack_plane/pallas_call | solution.py:271
  12.4 5.1 %all-to-all-start = ((bf16[8,152,1024]{2,1,0:T(8,128)(2,1)}), bf16[8,152,1024]{2,1,0:T(8,128)(2,1)S(1)}, u32[]{:S(2)}, u32[]{:S(2)}) async-start(bf16[8,152,1024]{2,1,0:T(8,128)(2,1)} %pack_plane.1), calls=%async_computation | async-start | bytes 4980736 | tf_op jit(solution)/shard_map/all_to_all | solution.py:280
  17.5 0.4 collective-permute-done.one
  17.9 0.0 copy-start.2
  17.9 3.4 %collective-permute-start.1 = (bf16[168,1024]{1,0:T(8,128)(2,1)S(1)}, bf16[168,1024]{1,0:T(8,128)(2,1)S(1)}, u32[]{:S(2)}, u32[]{:S(2)}) collective-permute-start(bf16[168,1024]{1,0:T(8,128)(2,1)S(1)} %slice.8), channel_id=1, source_target_pairs={{0,224},{32,0},{64,32},{96,64},{128,96},{160,128},{192,160},{224,1... | collective-permute-start | bytes 1032200 | tf_op jit(solution)/shard_map/ppermute | solution.py:253
  21.3 4.8 %collective-permute-done.3 = bf16[168,1024]{1,0:T(8,128)(2,1)} collective-permute-done((bf16[168,1024]{1,0:T(8,128)(2,1)}, bf16[168,1024]{1,0:T(8,128)(2,1)}, u32[]{:S(2)}, u32[]{:S(2)}) %collective-permute-start.3) | collective-permute-done | bytes 344096 | tf_op jit(solution)/shard_map/ppermute | solution.py:253
  26.1 0.0 collective-permute-start.4
  26.1 1.0 %collective-permute-done.1.two = bf16[168,1024]{1,0:T(8,128)(2,1)S(1)} collective-permute-done((bf16[168,1024]{1,0:T(8,128)(2,1)S(1)}, bf16[168,1024]{1,0:T(8,128)(2,1)S(1)}, u32[]{:S(2)}, u32[]{:S(2)}) %collective-permute-start.1) | collective-permute-done | bytes 344096 | tf_op jit(solution)/shard_map/ppermute | solution.py:253
  27.1 0.0 copy-start.3
  27.1 2.4 %collective-permute-start.2 = (bf16[136,1024]{1,0:T(8,128)(2,1)S(1)}, bf16[136,1024]{1,0:T(8,128)(2,1)S(1)}, u32[]{:S(2)}, u32[]{:S(2)}) collective-permute-start(bf16[136,1024]{1,0:T(8,128)(2,1)S(1)} %slice.9), channel_id=1, source_target_pairs={{0,192},{32,224},{64,0},{96,32},{128,64},{160,96},{192,128},{224,1... | collective-permute-start | bytes 835592 | tf_op jit(solution)/shard_map/ppermute | solution.py:253
  29.5 4.4 %collective-permute-done.4.three = bf16[168,1024]{1,0:T(8,128)(2,1)S(1)} collective-permute-done((bf16[168,1024]{1,0:T(8,128)(2,1)}, bf16[168,1024]{1,0:T(8,128)(2,1)S(1)}, u32[]{:S(2)}, u32[]{:S(2)}) %collective-permute-start.4) | collective-permute-done | bytes 344096 | tf_op jit(solution)/shard_map/ppermute | solution.py:253
  34.0 0.0 copy-done.3
  34.0 0.0 copy-start.4
  34.0 0.7 copy-done.4
  34.7 0.0 copy-done.2
  34.7 0.0 copy-start.1
  34.7 3.0 %prepare.1.bundle = bf16[1184,1024]{1,0:T(8,128)(2,1)} custom-call(f32[1,1024]{1,0:T(1,128)} %source.5, bf16[2,64,1024]{2,1,0:T(8,128)(2,1)} %bitcast.4, bf16[64,512]{1,0:T(8,128)(2,1)} %get-tuple-element.8.own_mask, f32[64,128]{1,0:T(8,128)} %get-tuple-element.6.own_spec, bf16[200,1024]{1,0:T(8,128)(2,1)} %copy-done.2, bf16[168,1024]{1,0:T(8,128)(2,1)} %copy-done.3, ...), custom_call_target="tpu_custom_call" | custom-call | flops 16499999744 | tf_op jit(solution)/shard_map/prepare/pallas_call | solution.py:283
  37.7 0.4 collective-permute-done.2.four
  38.2 9.7 %all-to-all-done.shared = bf16[8,152,1024]{2,1,0:T(8,128)(2,1)S(1)} async-done(((bf16[8,152,1024]{2,1,0:T(8,128)(2,1)}), bf16[8,152,1024]{2,1,0:T(8,128)(2,1)S(1)}, u32[]{:S(2)}, u32[]{:S(2)}) %all-to-all-start) | async-done | bytes 2490400 | tf_op jit(solution)/shard_map/all_to_all | solution.py:280
  47.9 0.0 copy-done.1
  47.9 0.0 copy-start
  47.9 1.7 %copy-done = bf16[1184,1024]{1,0:T(8,128)(2,1)S(1)} copy-done((bf16[1184,1024]{1,0:T(8,128)(2,1)S(1)}, bf16[1184,1024]{1,0:T(8,128)(2,1)}, u32[]{:S(2)}) %copy-start) | copy-done | bytes 2424856
  49.6 3.6 %absorb.1 = f32[8,1,1152]{2,1,0:T(1,128)S(1)} custom-call(bf16[8,152,1024]{2,1,0:T(8,128)(2,1)S(1)} %all-to-all-done.shared, f32[1,1024]{1,0:T(1,128)S(1)} %copy-done.1, bf16[136,1024]{1,0:T(8,128)(2,1)S(1)} %collective-permute-done.2.four, bf16[1184,1024]{1,0:T(8,128)(2,1)S(1)} %copy-done), custom_call_target="tpu_custom_call" | custom-call | tf_op jit(solution)/shard_map/absorb/pallas_call | solution.py:293
  53.2 11.6 %all_to_all.15.parts = f32[8,1,1152]{2,1,0:T(1,128)S(1)} all-to-all(f32[8,1,1152]{2,1,0:T(1,128)S(1)} %absorb.1), channel_id=1, replica_groups=mesh['z'=8,'xl'=2,'y'=4,'xh'=2,'core'=2] {'z'}, dimensions={0} | all-to-all | bytes 73728 | tf_op jit(solution)/shard_map/all_to_all | solution.py:308
  64.8 15.2 %all_to_all.16.parts = f32[32,1,1152]{2,1,0:T(1,128)S(1)} all-to-all(f32[32,1,1152]{2,1,0:T(1,128)S(1)} %gather_z.1), channel_id=1, replica_groups=mesh['z'=8,'xl'=2,'y'=4,'xh'=2,'core'=2] {'xl','y','xh','core'}, dimensions={0} | all-to-all | bytes 294912 | tf_op jit(solution)/shard_map/all_to_all | solution.py:317
  80.0 0.8 finish.1
  (3 shorter events, 0.1 us)
Async XLA Ops:
  3.0 14.9 %collective-permute-start = (bf16[200,1024]{1,0:T(8,128)(2,1)}, bf16[200,1024]{1,0:T(8,128)(2,1)S(1)}, u32[]{:S(2)}, u32[]{:S(2)}) collective-permute-start(bf16[200,1024]{1,0:T(8,128)(2,1)} %get-tuple-element.7), channel_id=1, source_target_pairs={{0,224},{32,0},{64,32},{96,64},{128,96},{160,128},{192,160},{224,1... | collective-permute-start | bytes 1228808 | tf_op jit(solution)/shard_map/ppermute | solution.py:253
  9.4 16.7 %collective-permute-start.3 = (bf16[168,1024]{1,0:T(8,128)(2,1)}, bf16[168,1024]{1,0:T(8,128)(2,1)}, u32[]{:S(2)}, u32[]{:S(2)}) collective-permute-start(bf16[168,1024]{1,0:T(8,128)(2,1)} %get-tuple-element.9), channel_id=1, source_target_pairs={{0,64},{32,96},{64,128},{96,160},{128,192},{160,224},{192,0},{224,... | collective-permute-start | bytes 1032200 | tf_op jit(solution)/shard_map/ppermute | solution.py:253
  12.4 35.5 %all-to-all-start = ((bf16[8,152,1024]{2,1,0:T(8,128)(2,1)}), bf16[8,152,1024]{2,1,0:T(8,128)(2,1)S(1)}, u32[]{:S(2)}, u32[]{:S(2)}) async-start(bf16[8,152,1024]{2,1,0:T(8,128)(2,1)} %pack_plane.1), calls=%async_computation | async-start | bytes 4980736 | tf_op jit(solution)/shard_map/all_to_all | solution.py:280
  17.9 16.8 %copy-start.2 = (bf16[200,1024]{1,0:T(8,128)(2,1)}, bf16[200,1024]{1,0:T(8,128)(2,1)S(1)}, u32[]{:S(2)}) copy-start(bf16[200,1024]{1,0:T(8,128)(2,1)S(1)} %collective-permute-done.one) | copy-start | bytes 1228804
  17.9 9.2 %collective-permute-start.1 = (bf16[168,1024]{1,0:T(8,128)(2,1)S(1)}, bf16[168,1024]{1,0:T(8,128)(2,1)S(1)}, u32[]{:S(2)}, u32[]{:S(2)}) collective-permute-start(bf16[168,1024]{1,0:T(8,128)(2,1)S(1)} %slice.8), channel_id=1, source_target_pairs={{0,224},{32,0},{64,32},{96,64},{128,96},{160,128},{192,160},{224,1... | collective-permute-start | bytes 1032200 | tf_op jit(solution)/shard_map/ppermute | solution.py:253
  26.1 7.9 %collective-permute-start.4 = (bf16[168,1024]{1,0:T(8,128)(2,1)}, bf16[168,1024]{1,0:T(8,128)(2,1)S(1)}, u32[]{:S(2)}, u32[]{:S(2)}) collective-permute-start(bf16[168,1024]{1,0:T(8,128)(2,1)} %collective-permute-done.3), channel_id=1, source_target_pairs={{0,32},{32,64},{64,96},{96,128},{128,160},{160,192},{192,224},{224... | collective-permute-start | bytes 1032200 | tf_op jit(solution)/shard_map/ppermute | solution.py:253
  27.1 6.9 %copy-start.3 = (bf16[168,1024]{1,0:T(8,128)(2,1)}, bf16[168,1024]{1,0:T(8,128)(2,1)S(1)}, u32[]{:S(2)}) copy-start(bf16[168,1024]{1,0:T(8,128)(2,1)S(1)} %collective-permute-done.1.two) | copy-start | bytes 1032196
  27.1 11.0 %collective-permute-start.2 = (bf16[136,1024]{1,0:T(8,128)(2,1)S(1)}, bf16[136,1024]{1,0:T(8,128)(2,1)S(1)}, u32[]{:S(2)}, u32[]{:S(2)}) collective-permute-start(bf16[136,1024]{1,0:T(8,128)(2,1)S(1)} %slice.9), channel_id=1, source_target_pairs={{0,192},{32,224},{64,0},{96,32},{128,64},{160,96},{192,128},{224,1... | collective-permute-start | bytes 835592 | tf_op jit(solution)/shard_map/ppermute | solution.py:253
  34.0 0.7 copy-start.4
  34.7 13.2 %copy-start.1 = (f32[1,1024]{1,0:T(1,128)S(1)}, f32[1,1024]{1,0:T(1,128)}, u32[]{:S(2)}) copy-start(f32[1,1024]{1,0:T(1,128)} %source.5) | copy-start | bytes 12292
  47.9 1.7 %copy-start = (bf16[1184,1024]{1,0:T(8,128)(2,1)S(1)}, bf16[1184,1024]{1,0:T(8,128)(2,1)}, u32[]{:S(2)}) copy-start(bf16[1184,1024]{1,0:T(8,128)(2,1)} %prepare.1.bundle) | copy-start | bytes 7274500

commit v10 on v9

--- a/solution.py
+++ b/solution.py
@@ -70,7 +70,7 @@
         ref[:, 128 * g : 128 * (g + 1)] = spectra[8 * g : 8 * (g + 1)]
 
 
-def pack_line(green, mask, spec_row, near, far, own_mask, own_spec):
+def pack(green, mask, spec_row, near, far, shared, own_mask, own_spec):
     z = lax.axis_index("z")
     row = spec_row[...]
     col = nt(identity(ROWS), row)
@@ -87,11 +87,6 @@
     for u, ref, at in ((1, near, NEXT), (2, near, MASK), (-3, far, MASK)):
         put_mask(ref.at[at : at + 32], window(mask, z - u).astype(bf16))
     own_mask[...] = window(mask, z).astype(bf16)
-
-
-def pack_plane(green, mask, own_spec, shared):
-    z = lax.axis_index("z")
-    spectra = own_spec[...].astype(bf16)
     wide = [window(mask, z + u) for u in OFFSETS]
     for q in range(NQ):
         shared[q, 0:64, :] = green[0]
@@ -104,25 +99,24 @@
             shared[q, 128:144, 256 * g : 256 * (g + 1)] = part[16 * g : 16 * (g + 1)]
 
 
-MOST = 4 * ROWS
+MOST = 3 * ROWS
 WT_RE, WT_IM, NEAR_RE, NEAR_IM, COUNT = (MOST * i for i in range(5))
 SPECTRA = COUNT + MOST // 2
 BUNDLE = SPECTRA + MOST // 8
 
 
-def prepare(source, green, own_mask, own_spec, one, two, three, bundle):
+def prepare(source, green, own_mask, own_spec, one, two, bundle):
     scale = source[...]
     real, imag = slice(REAL, REAL + ROWS), slice(IMAG, IMAG + ROWS)
     us = [own_spec[...]]
     held = [(green[0], green[1])]
-    for ref in (one, two, three):
+    for ref in (one, two):
         us.append(take_spectra(ref, SPEC))
         held.append((ref[real, :], ref[imag, :]))
     masks = [
         own_mask[...].astype(f32),
         take_mask(one, NEXT),
         take_mask(two, MASK),
-        take_mask(three, MASK),
     ]
     for k, (re, im) in enumerate(held):
         at = ROWS * k
@@ -135,26 +129,29 @@
         bundle[COUNT : COUNT + MOST // 2, WIDE * h : WIDE * (h + 1)] = counts[
             MOST // 2 * h : MOST // 2 * (h + 1)
         ]
-    spectra = jnp.concatenate(us, axis=0).astype(bf16)
+    spectra = jnp.concatenate(us, axis=0)
     for h in range(8):
         bundle[SPECTRA : SPECTRA + MOST // 8, 128 * h : 128 * (h + 1)] = spectra[
             MOST // 8 * h : MOST // 8 * (h + 1)
-        ]
-
-
-def absorb(shared, source, four, bundle, out, far_re, far_im, far_spec, back, wt):
+        ].astype(bf16)
+
+
+def absorb(shared, source, three, four, bundle, out, far_re, far_im, far_spec, back, wt):
     real, imag = slice(REAL, REAL + ROWS), slice(IMAG, IMAG + ROWS)
     tall = 5 * ROWS
     scale = source[...]
     for at, near, part in ((0, WT_RE, real), (tall, WT_IM, imag)):
         wt[at : at + MOST, :] = bundle[near : near + MOST, :]
-        wt[at + MOST : at + tall, :] = (scale * four[part, :].astype(f32)).astype(bf16)
+        for k, ref in ((3, three), (4, four)):
+            wt[at + ROWS * k : at + ROWS * (k + 1), :] = (
+                scale * ref[part, :].astype(f32)
+            ).astype(bf16)
     spec = jnp.concatenate(
         [
             bundle[SPECTRA : SPECTRA + MOST // 8, 128 * h : 128 * (h + 1)].astype(f32)
             for h in range(8)
         ]
-        + [take_spectra(four, SPEC)],
+        + [take_spectra(three, SPEC), take_spectra(four, SPEC)],
         axis=0,
     )
     u_re, u_im = spec[:, 0:1], spec[:, 1:2]
@@ -162,7 +159,8 @@
         [
             bundle[COUNT : COUNT + MOST // 2, WIDE * h : WIDE * (h + 1)].astype(f32)
             for h in range(2)
-        ],
+        ]
+        + [take_mask(three, MASK)],
         axis=0,
     )
     for q in range(NQ):
@@ -201,7 +199,7 @@
     by_re = nn(resid, g_re)
     by_im = nn(resid, g_im)
     held = []
-    for k in range(4):
+    for k in range(3):
         at = ROWS * k
         held.append(
             (
@@ -209,7 +207,8 @@
                 bundle[NEAR_IM + at : NEAR_IM + at + ROWS, :],
             )
         )
-    held.append((four[real, :], four[imag, :]))
+    for ref in (three, four):
+        held.append((ref[real, :], ref[imag, :]))
     total = jnp.zeros((ROWS, CELLS), f32)
     for k, (re, im) in enumerate(held):
         rows = slice(ROWS * k, ROWS * (k + 1))
@@ -256,25 +255,19 @@
 def local(spectra, green, source, pair_mask):
     g = green[0]
     vmem = pl.BlockSpec(memory_space=pltpu.VMEM)
-    near, far, own_mask, own_spec = pl.pallas_call(
-        pack_line,
+    near, far, shared, own_mask, own_spec = pl.pallas_call(
+        pack,
         out_shape=[
             shape(bf16, FULL, CELLS),
             shape(bf16, NEXT, CELLS),
+            shape(bf16, NQ, SHARED, CELLS),
             shape(bf16, ROWS, WIDE),
             shape(f32, ROWS, 128),
         ],
         in_specs=[vmem] * 3,
-        out_specs=[vmem] * 4,
-        name="pack_line",
+        out_specs=[vmem] * 5,
+        name="pack",
     )(g, pair_mask, spectra[0])
-    shared = pl.pallas_call(
-        pack_plane,
-        out_shape=shape(bf16, NQ, SHARED, CELLS),
-        in_specs=[vmem] * 3,
-        out_specs=vmem,
-        name="pack_plane",
-    )(g, pair_mask, own_spec)
     three = from_z(from_z(far, -2), -1)
     one = from_z(near, 1)
     shared = lax.all_to_all(shared, PLANE, 0, 0, tiled=True)
@@ -283,17 +276,17 @@
     ready = pl.pallas_call(
         prepare,
         out_shape=shape(bf16, BUNDLE, CELLS),
-        in_specs=[vmem] * 7,
+        in_specs=[vmem] * 6,
         out_specs=vmem,
         cost_estimate=pl.CostEstimate(
             flops=PREPARE, transcendentals=0, bytes_accessed=0
         ),
         name="prepare",
-    )(source, g, own_mask, own_spec, one, two, three)
+    )(source, g, own_mask, own_spec, one, two)
     part = pl.pallas_call(
         absorb,
         out_shape=shape(f32, NZ, 1, LONG),
-        in_specs=[vmem] * 4,
+        in_specs=[vmem] * 5,
         out_specs=vmem,
         scratch_shapes=[
             pltpu.VMEM((WIDE, CELLS), bf16),
@@ -304,7 +297,7 @@
         ],
         name="absorb",
         compiler_params=pltpu.CompilerParams(vmem_limit_bytes=40 << 20),
-    )(shared, source, four, ready)
+    )(shared, source, three, four, ready)
     part = lax.all_to_all(part, "z", 0, 0, tiled=True)
     part = pl.pallas_call(
         gather_z,

time: 81.1 us -> 83.5 us (1.030)
  Pallas kernels: 12.8 us -> 10.4 us
  blocking collectives: 26.8 us -> 29 us
  waiting for transfers between devices: 20.7 us -> 22.2 us
  starting transfers between devices: 17.3 us -> 18.6 us
    ppermute x5, waiting for transfers between devices: 11 us -> 22.2 us  [from_z(): return lax.ppermute(array, 'z', [(z, (z - u) % NZ) for z in range(NZ)])]
    all_to_all x1, waiting for transfers between devices: 9.7 us -> 0.01 us  [local(): shared = lax.all_to_all(shared, PLANE, 0, 0, tiled=True)]
    pallas_call x2 -> x1, Pallas kernels: 5.36 us -> 3.31 us  [local(): pl.pallas_call(pack, out_shape=[shape(bf16, FULL, CELLS), shape(bf16, NEX...]
    all_to_all x1, blocking collectives: 15.2 us -> 16.4 us  [local(): part = lax.all_to_all(part, PLANE + FREQ, 0, 0, tiled=True)]
    ppermute x5, starting transfers between devices: 12.2 us -> 13.3 us  [from_z(): return lax.ppermute(array, 'z', [(z, (z - u) % NZ) for z in range(NZ)])]
    all_to_all x1, blocking collectives: 11.6 us -> 12.5 us  [local(): part = lax.all_to_all(part, 'z', 0, 0, tiled=True)]
    unnamed x10, local copies, waits for them, and re-layouts: 2.43 us -> 1.51 us
  transfers between devices with their start and end apart: 6 -> 6, of which waited for: 6 -> 4; matrix products, arithmetic and copies ran while one was open for 0% -> 1% of each run, Pallas kernels for 7% -> 3%
where the time goes in v10:
time: 83.5 us; the launch traced here: 83.1 us
  blocking collectives  29 us (35%)
  waiting for transfers between devices  22.2 us (27%)
  starting transfers between devices  18.6 us (22%)
  Pallas kernels  10.4 us (12%)
  local copies, waits for them, and re-layouts  2.31 us (3%)
    ppermute x5, waiting for transfers between devices, from_z(): return lax.ppermute(array, 'z', [(z, (z - u) % NZ) for z in range(NZ)])  22.2 us
    all_to_all x1, blocking collectives, local(): part = lax.all_to_all(part, PLANE + FREQ, 0, 0, tiled=True)  16.4 us
    ppermute x5, starting transfers between devices, from_z(): return lax.ppermute(array, 'z', [(z, (z - u) % NZ) for z in range(NZ)])  13.3 us
    all_to_all x1, blocking collectives, local(): part = lax.all_to_all(part, 'z', 0, 0, tiled=True)  12.5 us
    all_to_all x1, starting transfers between devices, local(): shared = lax.all_to_all(shared, PLANE, 0, 0, tiled=True)  5.25 us
    pallas_call x1, Pallas kernels, local(): pl.pallas_call(absorb, out_shape=shape(f32, NZ, 1, LONG), in_specs=[vmem]...  3.61 us
    pallas_call x1, Pallas kernels, local(): pl.pallas_call(pack, out_shape=[shape(bf16, FULL, CELLS), shape(bf16, NEX...  3.31 us
    pallas_call x1, Pallas kernels, local(): pl.pallas_call(prepare, out_shape=shape(bf16, BUNDLE, CELLS), in_specs=[v...  2.67 us
  transfers between devices with their start and end apart: 6, of which 4 were waited for; matrix products, arithmetic and copies ran while one was open for 1% of the time, Pallas kernels for 3%

profile of v10, /device:TPU:1, one launch (start us, length us, event | category | flops | bytes accessed | tf_op | source)
XLA Modules:
  0.0 83.1 jit_solution(11636620587874889375)
XLA Ops:
  0.6 3.3 %pack.1 = (bf16[200,1024]{1,0:T(8,128)(2,1)}, bf16[168,1024]{1,0:T(8,128)(2,1)}, bf16[8,152,1024]{2,1,0:T(8,128)(2,1)}, bf16[64,512]{1,0:T(8,128)(2,1)}, f32[64,128]{1,0:T(8,128)}) custom-call(bf16[2,64,1024]{2,1,0:T(8,128)(2,1)} %bitcast.2, s32[64,4096]{1,0:T(8,128)} %mask.1, bf16[2,64]{1,0:T(2,128)(2,1)} %bitcast.4), custom_call_target="tpu_custom_call" | custom-call | tf_op jit(solution)/shard_map/pack/pallas_call | solution.py:258
  3.9 6.4 %collective-permute-start.2 = (bf16[200,1024]{1,0:T(8,128)(2,1)}, bf16[200,1024]{1,0:T(8,128)(2,1)S(1)}, u32[]{:S(2)}, u32[]{:S(2)}) collective-permute-start(bf16[200,1024]{1,0:T(8,128)(2,1)} %get-tuple-element.9), channel_id=1, source_target_pairs={{0,224},{32,0},{64,32},{96,64},{128,96},{160,128},{192,160},{224,1... | collective-permute-start | bytes 1228808 | tf_op jit(solution)/shard_map/ppermute | solution.py:252
  10.3 0.0 copy-start.4
  10.3 5.2 %all-to-all-start = ((bf16[8,152,1024]{2,1,0:T(8,128)(2,1)}), bf16[8,152,1024]{2,1,0:T(8,128)(2,1)S(1)}, u32[]{:S(2)}, u32[]{:S(2)}) async-start(bf16[8,152,1024]{2,1,0:T(8,128)(2,1)} %get-tuple-element.7), calls=%async_computation | async-start | bytes 4980736 | tf_op jit(solution)/shard_map/all_to_all | solution.py:273
  15.6 0.0 copy-done.4
  15.6 0.1 collective-permute-start
  15.7 3.1 %collective-permute-done.2.one = bf16[200,1024]{1,0:T(8,128)(2,1)S(1)} collective-permute-done((bf16[200,1024]{1,0:T(8,128)(2,1)}, bf16[200,1024]{1,0:T(8,128)(2,1)S(1)}, u32[]{:S(2)}, u32[]{:S(2)}) %collective-permute-start.2) | collective-permute-done | bytes 409632 | tf_op jit(solution)/shard_map/ppermute | solution.py:252
  18.8 0.0 copy-start.2
  18.8 3.4 %collective-permute-start.3 = (bf16[168,1024]{1,0:T(8,128)(2,1)S(1)}, bf16[168,1024]{1,0:T(8,128)(2,1)S(1)}, u32[]{:S(2)}, u32[]{:S(2)}) collective-permute-start(bf16[168,1024]{1,0:T(8,128)(2,1)S(1)} %slice.8), channel_id=1, source_target_pairs={{0,224},{32,0},{64,32},{96,64},{128,96},{160,128},{192,160},{224,1... | collective-permute-start | bytes 1032200 | tf_op jit(solution)/shard_map/ppermute | solution.py:252
  22.2 9.8 %collective-permute-done = bf16[168,1024]{1,0:T(8,128)(2,1)} collective-permute-done((bf16[168,1024]{1,0:T(8,128)(2,1)S(1)}, bf16[168,1024]{1,0:T(8,128)(2,1)}, u32[]{:S(2)}, u32[]{:S(2)}) %collective-permute-start) | collective-permute-done | bytes 344096 | tf_op jit(solution)/shard_map/ppermute | solution.py:252
  32.0 0.0 collective-permute-start.1
  32.0 0.0 collective-permute-done.3.two
  32.0 0.0 copy-start.3
  32.0 0.8 slice.9
  32.8 3.5 %collective-permute-start.4 = (bf16[136,1024]{1,0:T(8,128)(2,1)}, bf16[136,1024]{1,0:T(8,128)(2,1)S(1)}, u32[]{:S(2)}, u32[]{:S(2)}) collective-permute-start(bf16[136,1024]{1,0:T(8,128)(2,1)} %slice.9), channel_id=1, source_target_pairs={{0,192},{32,224},{64,0},{96,32},{128,64},{160,96},{192,128},{224,1... | collective-permute-start | bytes 835592 | tf_op jit(solution)/shard_map/ppermute | solution.py:252
  36.2 0.0 copy-done.3
  36.2 0.0 copy-done.2
  36.2 0.0 copy-start.1
  36.2 2.7 %prepare.1.bundle = bf16[888,1024]{1,0:T(8,128)(2,1)} custom-call(f32[1,1024]{1,0:T(1,128)} %source.5, bf16[2,64,1024]{2,1,0:T(8,128)(2,1)} %bitcast.3, bf16[64,512]{1,0:T(8,128)(2,1)} %get-tuple-element.10.own_mask, f32[64,128]{1,0:T(8,128)} %get-tuple-element.11.own_spec, bf16[200,1024]{1,0:T(8,128)(2,1)} %copy-done.2, bf16[168,1024]{1,0:T(8,128)(2,1)} %copy-done.3), custom_call_target="tpu_custom_call" | custom-call | flops 16499999744 | tf_op jit(solution)/shard_map/prepare/pallas_call | solution.py:276
  38.9 0.9 %collective-permute-done.1.three = bf16[168,1024]{1,0:T(8,128)(2,1)S(1)} collective-permute-done((bf16[168,1024]{1,0:T(8,128)(2,1)}, bf16[168,1024]{1,0:T(8,128)(2,1)S(1)}, u32[]{:S(2)}, u32[]{:S(2)}) %collective-permute-start.1) | collective-permute-done | bytes 344096 | tf_op jit(solution)/shard_map/ppermute | solution.py:252
  39.8 8.5 %collective-permute-done.4.four = bf16[136,1024]{1,0:T(8,128)(2,1)S(1)} collective-permute-done((bf16[136,1024]{1,0:T(8,128)(2,1)}, bf16[136,1024]{1,0:T(8,128)(2,1)S(1)}, u32[]{:S(2)}, u32[]{:S(2)}) %collective-permute-start.4) | collective-permute-done | bytes 278560 | tf_op jit(solution)/shard_map/ppermute | solution.py:252
  48.3 0.0 all-to-all-done.shared
  48.3 0.0 copy-done.1
  48.3 0.0 copy-start
  48.3 1.5 %copy-done = bf16[888,1024]{1,0:T(8,128)(2,1)S(1)} copy-done((bf16[888,1024]{1,0:T(8,128)(2,1)S(1)}, bf16[888,1024]{1,0:T(8,128)(2,1)}, u32[]{:S(2)}) %copy-start) | copy-done | bytes 1818648
  49.8 3.6 %absorb.1 = f32[8,1,1152]{2,1,0:T(1,128)S(1)} custom-call(bf16[8,152,1024]{2,1,0:T(8,128)(2,1)S(1)} %all-to-all-done.shared, f32[1,1024]{1,0:T(1,128)S(1)} %copy-done.1, bf16[168,1024]{1,0:T(8,128)(2,1)S(1)} %collective-permute-done.1.three, bf16[136,1024]{1,0:T(8,128)(2,1)S(1)} %collective-permute-done.4.four, bf16[888,1024]{1,0:T(8,128)(2,1)S(1)} %copy-done), custom_call_target="tpu_custom_call" | custom-call | tf_op jit(solution)/shard_map/absorb/pallas_call | solution.py:286
  53.4 12.5 %all_to_all.15.parts = f32[8,1,1152]{2,1,0:T(1,128)S(1)} all-to-all(f32[8,1,1152]{2,1,0:T(1,128)S(1)} %absorb.1), channel_id=1, replica_groups=mesh['z'=8,'xl'=2,'y'=4,'xh'=2,'core'=2] {'z'}, dimensions={0} | all-to-all | bytes 73728 | tf_op jit(solution)/shard_map/all_to_all | solution.py:301
  65.9 16.4 %all_to_all.16.parts = f32[32,1,1152]{2,1,0:T(1,128)S(1)} all-to-all(f32[32,1,1152]{2,1,0:T(1,128)S(1)} %gather_z.1), channel_id=1, replica_groups=mesh['z'=8,'xl'=2,'y'=4,'xh'=2,'core'=2] {'xl','y','xh','core'}, dimensions={0} | all-to-all | bytes 294912 | tf_op jit(solution)/shard_map/all_to_all | solution.py:310
  82.4 0.8 finish.1
  (2 shorter events, 0.1 us)
Async XLA Ops:
  3.9 14.9 %collective-permute-start.2 = (bf16[200,1024]{1,0:T(8,128)(2,1)}, bf16[200,1024]{1,0:T(8,128)(2,1)S(1)}, u32[]{:S(2)}, u32[]{:S(2)}) collective-permute-start(bf16[200,1024]{1,0:T(8,128)(2,1)} %get-tuple-element.9), channel_id=1, source_target_pairs={{0,224},{32,0},{64,32},{96,64},{128,96},{160,128},{192,160},{224,1... | collective-permute-start | bytes 1228808 | tf_op jit(solution)/shard_map/ppermute | solution.py:252
  10.3 5.3 %copy-start.4 = (bf16[168,1024]{1,0:T(8,128)(2,1)S(1)}, bf16[168,1024]{1,0:T(8,128)(2,1)}, u32[]{:S(2)}) copy-start(bf16[168,1024]{1,0:T(8,128)(2,1)} %get-tuple-element.8) | copy-start | bytes 1032196
  10.3 37.9 %all-to-all-start = ((bf16[8,152,1024]{2,1,0:T(8,128)(2,1)}), bf16[8,152,1024]{2,1,0:T(8,128)(2,1)S(1)}, u32[]{:S(2)}, u32[]{:S(2)}) async-start(bf16[8,152,1024]{2,1,0:T(8,128)(2,1)} %get-tuple-element.7), calls=%async_computation | async-start | bytes 4980736 | tf_op jit(solution)/shard_map/all_to_all | solution.py:273
  15.6 16.4 %collective-permute-start = (bf16[168,1024]{1,0:T(8,128)(2,1)S(1)}, bf16[168,1024]{1,0:T(8,128)(2,1)}, u32[]{:S(2)}, u32[]{:S(2)}) collective-permute-start(bf16[168,1024]{1,0:T(8,128)(2,1)S(1)} %copy-done.4), channel_id=1, source_target_pairs={{0,64},{32,96},{64,128},{96,160},{128,192},{160,224},{192,0},{224,... | collective-permute-start | bytes 1032200 | tf_op jit(solution)/shard_map/ppermute | solution.py:252
  18.8 17.4 %copy-start.2 = (bf16[200,1024]{1,0:T(8,128)(2,1)}, bf16[200,1024]{1,0:T(8,128)(2,1)S(1)}, u32[]{:S(2)}) copy-start(bf16[200,1024]{1,0:T(8,128)(2,1)S(1)} %collective-permute-done.2.one) | copy-start | bytes 1228804
  18.8 13.2 %collective-permute-start.3 = (bf16[168,1024]{1,0:T(8,128)(2,1)S(1)}, bf16[168,1024]{1,0:T(8,128)(2,1)S(1)}, u32[]{:S(2)}, u32[]{:S(2)}) collective-permute-start(bf16[168,1024]{1,0:T(8,128)(2,1)S(1)} %slice.8), channel_id=1, source_target_pairs={{0,224},{32,0},{64,32},{96,64},{128,96},{160,128},{192,160},{224,1... | collective-permute-start | bytes 1032200 | tf_op jit(solution)/shard_map/ppermute | solution.py:252
  32.0 7.8 %collective-permute-start.1 = (bf16[168,1024]{1,0:T(8,128)(2,1)}, bf16[168,1024]{1,0:T(8,128)(2,1)S(1)}, u32[]{:S(2)}, u32[]{:S(2)}) collective-permute-start(bf16[168,1024]{1,0:T(8,128)(2,1)} %collective-permute-done), channel_id=1, source_target_pairs={{0,32},{32,64},{64,96},{96,128},{128,160},{160,192},{192,224},{224... | collective-permute-start | bytes 1032200 | tf_op jit(solution)/shard_map/ppermute | solution.py:252
  32.0 4.2 %copy-start.3 = (bf16[168,1024]{1,0:T(8,128)(2,1)}, bf16[168,1024]{1,0:T(8,128)(2,1)S(1)}, u32[]{:S(2)}) copy-start(bf16[168,1024]{1,0:T(8,128)(2,1)S(1)} %collective-permute-done.3.two) | copy-start | bytes 1032196
  32.8 15.5 %collective-permute-start.4 = (bf16[136,1024]{1,0:T(8,128)(2,1)}, bf16[136,1024]{1,0:T(8,128)(2,1)S(1)}, u32[]{:S(2)}, u32[]{:S(2)}) collective-permute-start(bf16[136,1024]{1,0:T(8,128)(2,1)} %slice.9), channel_id=1, source_target_pairs={{0,192},{32,224},{64,0},{96,32},{128,64},{160,96},{192,128},{224,1... | collective-permute-start | bytes 835592 | tf_op jit(solution)/shard_map/ppermute | solution.py:252
  36.2 12.0 %copy-start.1 = (f32[1,1024]{1,0:T(1,128)S(1)}, f32[1,1024]{1,0:T(1,128)}, u32[]{:S(2)}) copy-start(f32[1,1024]{1,0:T(1,128)} %source.5) | copy-start | bytes 12292
  48.3 1.5 %copy-start = (bf16[888,1024]{1,0:T(8,128)(2,1)S(1)}, bf16[888,1024]{1,0:T(8,128)(2,1)}, u32[]{:S(2)}) copy-start(bf16[888,1024]{1,0:T(8,128)(2,1)} %prepare.1.bundle) | copy-start | bytes 5455876

commit v11 on v10

--- a/solution.py
+++ b/solution.py
@@ -39,7 +39,7 @@
 
 
 SPEC, IMAG, REAL, MASK, NEXT, FULL = 0, 8, 72, 136, 168, 200
-PREPARE = 16_500_000_000
+PREPARE = 17_500_000_000
 
 
 def window(mask, at):
@@ -268,7 +268,7 @@
         out_specs=[vmem] * 5,
         name="pack",
     )(g, pair_mask, spectra[0])
-    three = from_z(from_z(far, -2), -1)
+    three = from_z(from_z(far, -1), -2)
     one = from_z(near, 1)
     shared = lax.all_to_all(shared, PLANE, 0, 0, tiled=True)
     two = from_z(one[:NEXT], 1)

time: 83.5 us -> 78.8 us (0.944)
  blocking collectives: 29 us -> 26.6 us
  starting transfers between devices: 18.6 us -> 17.3 us
  waiting for transfers between devices: 22.2 us -> 21.2 us
    ppermute x5, waiting for transfers between devices: 22.2 us -> 18.7 us  [from_z(): return lax.ppermute(array, 'z', [(z, (z - u) % NZ) for z in range(NZ)])]
    all_to_all x1, blocking collectives: 12.5 us -> 9.62 us  [local(): part = lax.all_to_all(part, 'z', 0, 0, tiled=True)]
    all_to_all x1, waiting for transfers between devices: 0.01 us -> 2.45 us  [local(): shared = lax.all_to_all(shared, PLANE, 0, 0, tiled=True)]
    ppermute x5, starting transfers between devices: 13.3 us -> 12.1 us  [from_z(): return lax.ppermute(array, 'z', [(z, (z - u) % NZ) for z in range(NZ)])]
  transfers between devices with their start and end apart: 6 -> 6, of which waited for: 4 -> 5; matrix products, arithmetic and copies ran while one was open for 1% -> 1% of each run, Pallas kernels for 3% -> 3%
where the time goes in v11:
time: 78.8 us; the launch traced here: 78.5 us
  blocking collectives  26.6 us (34%)
  waiting for transfers between devices  21.2 us (27%)
  starting transfers between devices  17.3 us (22%)
  Pallas kernels  10.4 us (13%)
  local copies, waits for them, and re-layouts  2.31 us (3%)
    ppermute x5, waiting for transfers between devices, from_z(): return lax.ppermute(array, 'z', [(z, (z - u) % NZ) for z in range(NZ)])  18.7 us
    all_to_all x1, blocking collectives, local(): part = lax.all_to_all(part, PLANE + FREQ, 0, 0, tiled=True)  17 us
    ppermute x5, starting transfers between devices, from_z(): return lax.ppermute(array, 'z', [(z, (z - u) % NZ) for z in range(NZ)])  12.1 us
    all_to_all x1, blocking collectives, local(): part = lax.all_to_all(part, 'z', 0, 0, tiled=True)  9.62 us
    all_to_all x1, starting transfers between devices, local(): shared = lax.all_to_all(shared, PLANE, 0, 0, tiled=True)  5.25 us
    pallas_call x1, Pallas kernels, local(): pl.pallas_call(absorb, out_shape=shape(f32, NZ, 1, LONG), in_specs=[vmem]...  3.61 us
    pallas_call x1, Pallas kernels, local(): pl.pallas_call(pack, out_shape=[shape(bf16, FULL, CELLS), shape(bf16, NEX...  3.31 us
    pallas_call x1, Pallas kernels, local(): pl.pallas_call(prepare, out_shape=shape(bf16, BUNDLE, CELLS), in_specs=[v...  2.67 us
  transfers between devices with their start and end apart: 6, of which 5 were waited for; matrix products, arithmetic and copies ran while one was open for 1% of the time, Pallas kernels for 3%

profile of v11, /device:TPU:1, one launch (start us, length us, event | category | flops | bytes accessed | tf_op | source)
XLA Modules:
  0.0 78.5 jit_solution(17042704144236752042)
XLA Ops:
  0.6 3.3 %pack.1 = (bf16[200,1024]{1,0:T(8,128)(2,1)}, bf16[168,1024]{1,0:T(8,128)(2,1)}, bf16[8,152,1024]{2,1,0:T(8,128)(2,1)}, bf16[64,512]{1,0:T(8,128)(2,1)}, f32[64,128]{1,0:T(8,128)}) custom-call(bf16[2,64,1024]{2,1,0:T(8,128)(2,1)} %bitcast.2, s32[64,4096]{1,0:T(8,128)} %mask.1, bf16[2,64]{1,0:T(2,128)(2,1)} %bitcast.4), custom_call_target="tpu_custom_call" | custom-call | tf_op jit(solution)/shard_map/pack/pallas_call | solution.py:258
  3.9 6.4 %collective-permute-start.2 = (bf16[200,1024]{1,0:T(8,128)(2,1)}, bf16[200,1024]{1,0:T(8,128)(2,1)S(1)}, u32[]{:S(2)}, u32[]{:S(2)}) collective-permute-start(bf16[200,1024]{1,0:T(8,128)(2,1)} %get-tuple-element.9), channel_id=1, source_target_pairs={{0,224},{32,0},{64,32},{96,64},{128,96},{160,128},{192,160},{224,1... | collective-permute-start | bytes 1228808 | tf_op jit(solution)/shard_map/ppermute | solution.py:252
  10.3 0.0 copy-start.4
  10.3 5.2 %all-to-all-start = ((bf16[8,152,1024]{2,1,0:T(8,128)(2,1)}), bf16[8,152,1024]{2,1,0:T(8,128)(2,1)S(1)}, u32[]{:S(2)}, u32[]{:S(2)}) async-start(bf16[8,152,1024]{2,1,0:T(8,128)(2,1)} %get-tuple-element.7), calls=%async_computation | async-start | bytes 4980736 | tf_op jit(solution)/shard_map/all_to_all | solution.py:273
  15.6 0.0 copy-done.4
  15.6 0.1 collective-permute-start
  15.7 3.1 %collective-permute-done.2.one = bf16[200,1024]{1,0:T(8,128)(2,1)S(1)} collective-permute-done((bf16[200,1024]{1,0:T(8,128)(2,1)}, bf16[200,1024]{1,0:T(8,128)(2,1)S(1)}, u32[]{:S(2)}, u32[]{:S(2)}) %collective-permute-start.2) | collective-permute-done | bytes 409632 | tf_op jit(solution)/shard_map/ppermute | solution.py:252
  18.8 0.0 copy-start.2
  18.8 3.4 %collective-permute-start.3 = (bf16[168,1024]{1,0:T(8,128)(2,1)S(1)}, bf16[168,1024]{1,0:T(8,128)(2,1)S(1)}, u32[]{:S(2)}, u32[]{:S(2)}) collective-permute-start(bf16[168,1024]{1,0:T(8,128)(2,1)S(1)} %slice.8), channel_id=1, source_target_pairs={{0,224},{32,0},{64,32},{96,64},{128,96},{160,128},{192,160},{224,1... | collective-permute-start | bytes 1032200 | tf_op jit(solution)/shard_map/ppermute | solution.py:252
  22.2 3.1 %collective-permute-done = bf16[168,1024]{1,0:T(8,128)(2,1)} collective-permute-done((bf16[168,1024]{1,0:T(8,128)(2,1)S(1)}, bf16[168,1024]{1,0:T(8,128)(2,1)}, u32[]{:S(2)}, u32[]{:S(2)}) %collective-permute-start) | collective-permute-done | bytes 344096 | tf_op jit(solution)/shard_map/ppermute | solution.py:252
  25.3 0.0 collective-permute-start.1
  25.3 2.7 %collective-permute-done.3.two = bf16[168,1024]{1,0:T(8,128)(2,1)S(1)} collective-permute-done((bf16[168,1024]{1,0:T(8,128)(2,1)S(1)}, bf16[168,1024]{1,0:T(8,128)(2,1)S(1)}, u32[]{:S(2)}, u32[]{:S(2)}) %collective-permute-start.3) | collective-permute-done | bytes 344096 | tf_op jit(solution)/shard_map/ppermute | solution.py:252
  28.0 0.0 copy-start.3
  28.0 0.8 slice.9
  28.8 2.2 %collective-permute-start.4 = (bf16[136,1024]{1,0:T(8,128)(2,1)}, bf16[136,1024]{1,0:T(8,128)(2,1)S(1)}, u32[]{:S(2)}, u32[]{:S(2)}) collective-permute-start(bf16[136,1024]{1,0:T(8,128)(2,1)} %slice.9), channel_id=1, source_target_pairs={{0,192},{32,224},{64,0},{96,32},{128,64},{160,96},{192,128},{224,1... | collective-permute-start | bytes 835592 | tf_op jit(solution)/shard_map/ppermute | solution.py:252
  31.0 0.0 copy-done.3
  31.0 0.0 copy-done.2
  31.0 0.0 copy-start.1
  31.0 2.7 %prepare.1.bundle = bf16[888,1024]{1,0:T(8,128)(2,1)} custom-call(f32[1,1024]{1,0:T(1,128)} %source.5, bf16[2,64,1024]{2,1,0:T(8,128)(2,1)} %bitcast.3, bf16[64,512]{1,0:T(8,128)(2,1)} %get-tuple-element.10.own_mask, f32[64,128]{1,0:T(8,128)} %get-tuple-element.11.own_spec, bf16[200,1024]{1,0:T(8,128)(2,1)} %copy-done.2, bf16[168,1024]{1,0:T(8,128)(2,1)} %copy-done.3), custom_call_target="tpu_custom_call" | custom-call | flops 17500000256 | tf_op jit(solution)/shard_map/prepare/pallas_call | solution.py:276
  33.7 9.8 %collective-permute-done.1.three = bf16[168,1024]{1,0:T(8,128)(2,1)S(1)} collective-permute-done((bf16[168,1024]{1,0:T(8,128)(2,1)}, bf16[168,1024]{1,0:T(8,128)(2,1)S(1)}, u32[]{:S(2)}, u32[]{:S(2)}) %collective-permute-start.1) | collective-permute-done | bytes 344096 | tf_op jit(solution)/shard_map/ppermute | solution.py:252
  43.5 0.0 collective-permute-done.4.four
  43.5 2.5 %all-to-all-done.shared = bf16[8,152,1024]{2,1,0:T(8,128)(2,1)S(1)} async-done(((bf16[8,152,1024]{2,1,0:T(8,128)(2,1)}), bf16[8,152,1024]{2,1,0:T(8,128)(2,1)S(1)}, u32[]{:S(2)}, u32[]{:S(2)}) %all-to-all-start) | async-done | bytes 2490400 | tf_op jit(solution)/shard_map/all_to_all | solution.py:273
  45.9 0.0 copy-done.1
  45.9 0.0 copy-start
  45.9 1.5 %copy-done = bf16[888,1024]{1,0:T(8,128)(2,1)S(1)} copy-done((bf16[888,1024]{1,0:T(8,128)(2,1)S(1)}, bf16[888,1024]{1,0:T(8,128)(2,1)}, u32[]{:S(2)}) %copy-start) | copy-done | bytes 1818648
  47.4 3.6 %absorb.1 = f32[8,1,1152]{2,1,0:T(1,128)S(1)} custom-call(bf16[8,152,1024]{2,1,0:T(8,128)(2,1)S(1)} %all-to-all-done.shared, f32[1,1024]{1,0:T(1,128)S(1)} %copy-done.1, bf16[168,1024]{1,0:T(8,128)(2,1)S(1)} %collective-permute-done.1.three, bf16[136,1024]{1,0:T(8,128)(2,1)S(1)} %collective-permute-done.4.four, bf16[888,1024]{1,0:T(8,128)(2,1)S(1)} %copy-done), custom_call_target="tpu_custom_call" | custom-call | tf_op jit(solution)/shard_map/absorb/pallas_call | solution.py:286
  51.1 9.6 %all_to_all.15.parts = f32[8,1,1152]{2,1,0:T(1,128)S(1)} all-to-all(f32[8,1,1152]{2,1,0:T(1,128)S(1)} %absorb.1), channel_id=1, replica_groups=mesh['z'=8,'xl'=2,'y'=4,'xh'=2,'core'=2] {'z'}, dimensions={0} | all-to-all | bytes 73728 | tf_op jit(solution)/shard_map/all_to_all | solution.py:301
  60.7 17.0 %all_to_all.16.parts = f32[32,1,1152]{2,1,0:T(1,128)S(1)} all-to-all(f32[32,1,1152]{2,1,0:T(1,128)S(1)} %gather_z.1), channel_id=1, replica_groups=mesh['z'=8,'xl'=2,'y'=4,'xh'=2,'core'=2] {'xl','y','xh','core'}, dimensions={0} | all-to-all | bytes 294912 | tf_op jit(solution)/shard_map/all_to_all | solution.py:310
  77.7 0.8 finish.1
  (2 shorter events, 0.1 us)
Async XLA Ops:
  3.9 14.9 %collective-permute-start.2 = (bf16[200,1024]{1,0:T(8,128)(2,1)}, bf16[200,1024]{1,0:T(8,128)(2,1)S(1)}, u32[]{:S(2)}, u32[]{:S(2)}) collective-permute-start(bf16[200,1024]{1,0:T(8,128)(2,1)} %get-tuple-element.9), channel_id=1, source_target_pairs={{0,224},{32,0},{64,32},{96,64},{128,96},{160,128},{192,160},{224,1... | collective-permute-start | bytes 1228808 | tf_op jit(solution)/shard_map/ppermute | solution.py:252
  10.3 5.3 %copy-start.4 = (bf16[168,1024]{1,0:T(8,128)(2,1)S(1)}, bf16[168,1024]{1,0:T(8,128)(2,1)}, u32[]{:S(2)}) copy-start(bf16[168,1024]{1,0:T(8,128)(2,1)} %get-tuple-element.8) | copy-start | bytes 1032196
  10.3 35.6 %all-to-all-start = ((bf16[8,152,1024]{2,1,0:T(8,128)(2,1)}), bf16[8,152,1024]{2,1,0:T(8,128)(2,1)S(1)}, u32[]{:S(2)}, u32[]{:S(2)}) async-start(bf16[8,152,1024]{2,1,0:T(8,128)(2,1)} %get-tuple-element.7), calls=%async_computation | async-start | bytes 4980736 | tf_op jit(solution)/shard_map/all_to_all | solution.py:273
  15.6 9.7 %collective-permute-start = (bf16[168,1024]{1,0:T(8,128)(2,1)S(1)}, bf16[168,1024]{1,0:T(8,128)(2,1)}, u32[]{:S(2)}, u32[]{:S(2)}) collective-permute-start(bf16[168,1024]{1,0:T(8,128)(2,1)S(1)} %copy-done.4), channel_id=1, source_target_pairs={{0,32},{32,64},{64,96},{96,128},{128,160},{160,192},{192,224},{224... | collective-permute-start | bytes 1032200 | tf_op jit(solution)/shard_map/ppermute | solution.py:252
  18.8 12.2 %copy-start.2 = (bf16[200,1024]{1,0:T(8,128)(2,1)}, bf16[200,1024]{1,0:T(8,128)(2,1)S(1)}, u32[]{:S(2)}) copy-start(bf16[200,1024]{1,0:T(8,128)(2,1)S(1)} %collective-permute-done.2.one) | copy-start | bytes 1228804
  18.8 9.2 %collective-permute-start.3 = (bf16[168,1024]{1,0:T(8,128)(2,1)S(1)}, bf16[168,1024]{1,0:T(8,128)(2,1)S(1)}, u32[]{:S(2)}, u32[]{:S(2)}) collective-permute-start(bf16[168,1024]{1,0:T(8,128)(2,1)S(1)} %slice.8), channel_id=1, source_target_pairs={{0,224},{32,0},{64,32},{96,64},{128,96},{160,128},{192,160},{224,1... | collective-permute-start | bytes 1032200 | tf_op jit(solution)/shard_map/ppermute | solution.py:252
  25.3 18.2 %collective-permute-start.1 = (bf16[168,1024]{1,0:T(8,128)(2,1)}, bf16[168,1024]{1,0:T(8,128)(2,1)S(1)}, u32[]{:S(2)}, u32[]{:S(2)}) collective-permute-start(bf16[168,1024]{1,0:T(8,128)(2,1)} %collective-permute-done), channel_id=1, source_target_pairs={{0,64},{32,96},{64,128},{96,160},{128,192},{160,224},{192,0},{224,... | collective-permute-start | bytes 1032200 | tf_op jit(solution)/shard_map/ppermute | solution.py:252
  28.0 3.0 %copy-start.3 = (bf16[168,1024]{1,0:T(8,128)(2,1)}, bf16[168,1024]{1,0:T(8,128)(2,1)S(1)}, u32[]{:S(2)}) copy-start(bf16[168,1024]{1,0:T(8,128)(2,1)S(1)} %collective-permute-done.3.two) | copy-start | bytes 1032196
  28.8 14.7 %collective-permute-start.4 = (bf16[136,1024]{1,0:T(8,128)(2,1)}, bf16[136,1024]{1,0:T(8,128)(2,1)S(1)}, u32[]{:S(2)}, u32[]{:S(2)}) collective-permute-start(bf16[136,1024]{1,0:T(8,128)(2,1)} %slice.9), channel_id=1, source_target_pairs={{0,192},{32,224},{64,0},{96,32},{128,64},{160,96},{192,128},{224,1... | collective-permute-start | bytes 835592 | tf_op jit(solution)/shard_map/ppermute | solution.py:252
  31.0 14.9 %copy-start.1 = (f32[1,1024]{1,0:T(1,128)S(1)}, f32[1,1024]{1,0:T(1,128)}, u32[]{:S(2)}) copy-start(f32[1,1024]{1,0:T(1,128)} %source.5) | copy-start | bytes 12292
  45.9 1.5 %copy-start = (bf16[888,1024]{1,0:T(8,128)(2,1)S(1)}, bf16[888,1024]{1,0:T(8,128)(2,1)}, u32[]{:S(2)}) copy-start(bf16[888,1024]{1,0:T(8,128)(2,1)} %prepare.1.bundle) | copy-start | bytes 5455876

commit v12 on v11

--- a/solution.py
+++ b/solution.py
@@ -100,30 +100,19 @@
 
 
 MOST = 3 * ROWS
-WT_RE, WT_IM, NEAR_RE, NEAR_IM, COUNT = (MOST * i for i in range(5))
+NEAR_RE, NEAR_IM, COUNT = 0, 2 * ROWS, 4 * ROWS
 SPECTRA = COUNT + MOST // 2
 BUNDLE = SPECTRA + MOST // 8
 
 
-def prepare(source, green, own_mask, own_spec, one, two, bundle):
-    scale = source[...]
-    real, imag = slice(REAL, REAL + ROWS), slice(IMAG, IMAG + ROWS)
+def prepare(own_mask, own_spec, one, two, bundle):
     us = [own_spec[...]]
-    held = [(green[0], green[1])]
-    for ref in (one, two):
+    for k, ref in enumerate((one, two)):
         us.append(take_spectra(ref, SPEC))
-        held.append((ref[real, :], ref[imag, :]))
-    masks = [
-        own_mask[...].astype(f32),
-        take_mask(one, NEXT),
-        take_mask(two, MASK),
-    ]
-    for k, (re, im) in enumerate(held):
         at = ROWS * k
-        bundle[NEAR_RE + at : NEAR_RE + at + ROWS, :] = re
-        bundle[NEAR_IM + at : NEAR_IM + at + ROWS, :] = im
-        bundle[WT_RE + at : WT_RE + at + ROWS, :] = (scale * re.astype(f32)).astype(bf16)
-        bundle[WT_IM + at : WT_IM + at + ROWS, :] = (scale * im.astype(f32)).astype(bf16)
+        bundle[NEAR_RE + at : NEAR_RE + at + ROWS, :] = ref[REAL : REAL + ROWS, :]
+        bundle[NEAR_IM + at : NEAR_IM + at + ROWS, :] = ref[IMAG : IMAG + ROWS, :]
+    masks = [own_mask[...].astype(f32), take_mask(one, NEXT), take_mask(two, MASK)]
     counts = jnp.concatenate(masks, axis=0).astype(bf16)
     for h in range(2):
         bundle[COUNT : COUNT + MOST // 2, WIDE * h : WIDE * (h + 1)] = counts[
@@ -136,16 +125,20 @@
         ].astype(bf16)
 
 
-def absorb(shared, source, three, four, bundle, out, far_re, far_im, far_spec, back, wt):
+def absorb(shared, source, green, three, four, bundle, out, far_re, far_im, far_spec, back, wt):
     real, imag = slice(REAL, REAL + ROWS), slice(IMAG, IMAG + ROWS)
     tall = 5 * ROWS
     scale = source[...]
-    for at, near, part in ((0, WT_RE, real), (tall, WT_IM, imag)):
-        wt[at : at + MOST, :] = bundle[near : near + MOST, :]
-        for k, ref in ((3, three), (4, four)):
-            wt[at + ROWS * k : at + ROWS * (k + 1), :] = (
-                scale * ref[part, :].astype(f32)
-            ).astype(bf16)
+    held = [(green[0], green[1])]
+    for k in range(2):
+        re, im = NEAR_RE + ROWS * k, NEAR_IM + ROWS * k
+        held.append((bundle[re : re + ROWS, :], bundle[im : im + ROWS, :]))
+    for ref in (three, four):
+        held.append((ref[real, :], ref[imag, :]))
+    for k, (re, im) in enumerate(held):
+        at = ROWS * k
+        wt[at : at + ROWS, :] = (scale * re.astype(f32)).astype(bf16)
+        wt[tall + at : tall + at + ROWS, :] = (scale * im.astype(f32)).astype(bf16)
     spec = jnp.concatenate(
         [
             bundle[SPECTRA : SPECTRA + MOST // 8, 128 * h : 128 * (h + 1)].astype(f32)
@@ -198,17 +191,6 @@
     )
     by_re = nn(resid, g_re)
     by_im = nn(resid, g_im)
-    held = []
-    for k in range(3):
-        at = ROWS * k
-        held.append(
-            (
-                bundle[NEAR_RE + at : NEAR_RE + at + ROWS, :],
-                bundle[NEAR_IM + at : NEAR_IM + at + ROWS, :],
-            )
-        )
-    for ref in (three, four):
-        held.append((ref[real, :], ref[imag, :]))
     total = jnp.zeros((ROWS, CELLS), f32)
     for k, (re, im) in enumerate(held):
         rows = slice(ROWS * k, ROWS * (k + 1))
@@ -276,17 +258,17 @@
     ready = pl.pallas_call(
         prepare,
         out_shape=shape(bf16, BUNDLE, CELLS),
-        in_specs=[vmem] * 6,
+        in_specs=[vmem] * 4,
         out_specs=vmem,
         cost_estimate=pl.CostEstimate(
             flops=PREPARE, transcendentals=0, bytes_accessed=0
         ),
         name="prepare",
-    )(source, g, own_mask, own_spec, one, two)
+    )(own_mask, own_spec, one, two)
     part = pl.pallas_call(
         absorb,
         out_shape=shape(f32, NZ, 1, LONG),
-        in_specs=[vmem] * 5,
+        in_specs=[vmem] * 6,
         out_specs=vmem,
         scratch_shapes=[
             pltpu.VMEM((WIDE, CELLS), bf16),
@@ -297,7 +279,7 @@
         ],
         name="absorb",
         compiler_params=pltpu.CompilerParams(vmem_limit_bytes=40 << 20),
-    )(shared, source, three, four, ready)
+    )(shared, source, g, three, four, ready)
     part = lax.all_to_all(part, "z", 0, 0, tiled=True)
     part = pl.pallas_call(
         gather_z,

time: 78.8 us -> 78.3 us (level)
  no operation moved by 1% of the time
where the time goes in v12:
time: 78.3 us; the launch traced here: 78 us
  blocking collectives  26.6 us (34%)
  waiting for transfers between devices  21.7 us (28%)
  starting transfers between devices  17.3 us (22%)
  Pallas kernels  9.79 us (13%)
  local copies, waits for them, and re-layouts  1.94 us (2%)
    ppermute x5, waiting for transfers between devices, from_z(): return lax.ppermute(array, 'z', [(z, (z - u) % NZ) for z in range(NZ)])  19.3 us
    all_to_all x1, blocking collectives, local(): part = lax.all_to_all(part, PLANE + FREQ, 0, 0, tiled=True)  17 us
    ppermute x5, starting transfers between devices, from_z(): return lax.ppermute(array, 'z', [(z, (z - u) % NZ) for z in range(NZ)])  12.1 us
    all_to_all x1, blocking collectives, local(): part = lax.all_to_all(part, 'z', 0, 0, tiled=True)  9.61 us
    all_to_all x1, starting transfers between devices, local(): shared = lax.all_to_all(shared, PLANE, 0, 0, tiled=True)  5.25 us
    pallas_call x1, Pallas kernels, local(): pl.pallas_call(absorb, out_shape=shape(f32, NZ, 1, LONG), in_specs=[vmem]...  3.54 us
    pallas_call x1, Pallas kernels, local(): pl.pallas_call(pack, out_shape=[shape(bf16, FULL, CELLS), shape(bf16, NEX...  3.32 us
    all_to_all x1, waiting for transfers between devices, local(): shared = lax.all_to_all(shared, PLANE, 0, 0, tiled=True)  2.45 us
  transfers between devices with their start and end apart: 6, of which 5 were waited for; matrix products, arithmetic and copies ran while one was open for 1% of the time, Pallas kernels for 3%

profile of v12, /device:TPU:1, one launch (start us, length us, event | category | flops | bytes accessed | tf_op | source)
XLA Modules:
  0.0 78.0 jit_solution(9837564364442559218)
XLA Ops:
  0.6 3.3 %pack.1 = (bf16[200,1024]{1,0:T(8,128)(2,1)}, bf16[168,1024]{1,0:T(8,128)(2,1)}, bf16[8,152,1024]{2,1,0:T(8,128)(2,1)}, bf16[64,512]{1,0:T(8,128)(2,1)}, f32[64,128]{1,0:T(8,128)}) custom-call(bf16[2,64,1024]{2,1,0:T(8,128)(2,1)} %bitcast.2, s32[64,4096]{1,0:T(8,128)} %mask.1, bf16[2,64]{1,0:T(2,128)(2,1)} %bitcast.4), custom_call_target="tpu_custom_call" | custom-call | tf_op jit(solution)/shard_map/pack/pallas_call | solution.py:240
  4.0 6.4 %collective-permute-start.2 = (bf16[200,1024]{1,0:T(8,128)(2,1)}, bf16[200,1024]{1,0:T(8,128)(2,1)S(1)}, u32[]{:S(2)}, u32[]{:S(2)}) collective-permute-start(bf16[200,1024]{1,0:T(8,128)(2,1)} %get-tuple-element.9), channel_id=1, source_target_pairs={{0,224},{32,0},{64,32},{96,64},{128,96},{160,128},{192,160},{224,1... | collective-permute-start | bytes 1228808 | tf_op jit(solution)/shard_map/ppermute | solution.py:234
  10.4 0.0 copy-start.5
  10.4 5.2 %all-to-all-start = ((bf16[8,152,1024]{2,1,0:T(8,128)(2,1)}), bf16[8,152,1024]{2,1,0:T(8,128)(2,1)S(1)}, u32[]{:S(2)}, u32[]{:S(2)}) async-start(bf16[8,152,1024]{2,1,0:T(8,128)(2,1)} %get-tuple-element.7), calls=%async_computation | async-start | bytes 4980736 | tf_op jit(solution)/shard_map/all_to_all | solution.py:255
  15.6 0.0 copy-done.5
  15.6 0.1 collective-permute-start
  15.7 3.1 %collective-permute-done.2.one = bf16[200,1024]{1,0:T(8,128)(2,1)S(1)} collective-permute-done((bf16[200,1024]{1,0:T(8,128)(2,1)}, bf16[200,1024]{1,0:T(8,128)(2,1)S(1)}, u32[]{:S(2)}, u32[]{:S(2)}) %collective-permute-start.2) | collective-permute-done | bytes 409632 | tf_op jit(solution)/shard_map/ppermute | solution.py:234
  18.8 0.0 copy-start.3
  18.8 3.4 %collective-permute-start.3 = (bf16[168,1024]{1,0:T(8,128)(2,1)S(1)}, bf16[168,1024]{1,0:T(8,128)(2,1)S(1)}, u32[]{:S(2)}, u32[]{:S(2)}) collective-permute-start(bf16[168,1024]{1,0:T(8,128)(2,1)S(1)} %slice.8), channel_id=1, source_target_pairs={{0,224},{32,0},{64,32},{96,64},{128,96},{160,128},{192,160},{224,1... | collective-permute-start | bytes 1032200 | tf_op jit(solution)/shard_map/ppermute | solution.py:234
  22.2 0.0 copy-done.3
  22.2 3.1 %collective-permute-done = bf16[168,1024]{1,0:T(8,128)(2,1)} collective-permute-done((bf16[168,1024]{1,0:T(8,128)(2,1)S(1)}, bf16[168,1024]{1,0:T(8,128)(2,1)}, u32[]{:S(2)}, u32[]{:S(2)}) %collective-permute-start) | collective-permute-done | bytes 344096 | tf_op jit(solution)/shard_map/ppermute | solution.py:234
  25.3 0.0 collective-permute-start.1
  25.3 2.7 %collective-permute-done.3.two = bf16[168,1024]{1,0:T(8,128)(2,1)S(1)} collective-permute-done((bf16[168,1024]{1,0:T(8,128)(2,1)S(1)}, bf16[168,1024]{1,0:T(8,128)(2,1)S(1)}, u32[]{:S(2)}, u32[]{:S(2)}) %collective-permute-start.3) | collective-permute-done | bytes 344096 | tf_op jit(solution)/shard_map/ppermute | solution.py:234
  28.0 0.0 copy-start.4
  28.0 0.8 slice.9
  28.8 2.2 %collective-permute-start.4 = (bf16[136,1024]{1,0:T(8,128)(2,1)}, bf16[136,1024]{1,0:T(8,128)(2,1)S(1)}, u32[]{:S(2)}, u32[]{:S(2)}) collective-permute-start(bf16[136,1024]{1,0:T(8,128)(2,1)} %slice.9), channel_id=1, source_target_pairs={{0,192},{32,224},{64,0},{96,32},{128,64},{160,96},{192,128},{224,1... | collective-permute-start | bytes 835592 | tf_op jit(solution)/shard_map/ppermute | solution.py:234
  31.0 0.0 copy-done.4
  31.0 0.0 copy-start
  31.0 0.0 copy-start.2
  31.0 2.1 %prepare.1.bundle = bf16[376,1024]{1,0:T(8,128)(2,1)} custom-call(bf16[64,512]{1,0:T(8,128)(2,1)} %get-tuple-element.10.own_mask, f32[64,128]{1,0:T(8,128)} %get-tuple-element.11.own_spec, bf16[200,1024]{1,0:T(8,128)(2,1)} %copy-done.3, bf16[168,1024]{1,0:T(8,128)(2,1)} %copy-done.4), custom_call_target="tpu_custom_call" | custom-call | flops 17500000256 | tf_op jit(solution)/shard_map/prepare/pallas_call | solution.py:258
  33.1 10.4 %collective-permute-done.1.three = bf16[168,1024]{1,0:T(8,128)(2,1)S(1)} collective-permute-done((bf16[168,1024]{1,0:T(8,128)(2,1)}, bf16[168,1024]{1,0:T(8,128)(2,1)S(1)}, u32[]{:S(2)}, u32[]{:S(2)}) %collective-permute-start.1) | collective-permute-done | bytes 344096 | tf_op jit(solution)/shard_map/ppermute | solution.py:234
  43.5 0.0 collective-permute-done.4.four
  43.5 2.5 %all-to-all-done.shared = bf16[8,152,1024]{2,1,0:T(8,128)(2,1)S(1)} async-done(((bf16[8,152,1024]{2,1,0:T(8,128)(2,1)}), bf16[8,152,1024]{2,1,0:T(8,128)(2,1)S(1)}, u32[]{:S(2)}, u32[]{:S(2)}) %all-to-all-start) | async-done | bytes 2490400 | tf_op jit(solution)/shard_map/all_to_all | solution.py:255
  46.0 0.0 copy-done
  46.0 0.0 copy-done.2
  46.0 0.0 copy-start.1
  46.0 1.1 %copy-done.1 = bf16[376,1024]{1,0:T(8,128)(2,1)S(1)} copy-done((bf16[376,1024]{1,0:T(8,128)(2,1)S(1)}, bf16[376,1024]{1,0:T(8,128)(2,1)}, u32[]{:S(2)}) %copy-start.1) | copy-done | bytes 770072
  47.1 3.5 %absorb.1 = f32[8,1,1152]{2,1,0:T(1,128)S(1)} custom-call(bf16[8,152,1024]{2,1,0:T(8,128)(2,1)S(1)} %all-to-all-done.shared, f32[1,1024]{1,0:T(1,128)S(1)} %copy-done.2, bf16[2,64,1024]{2,1,0:T(8,128)(2,1)S(1)} %bitcast.3, bf16[168,1024]{1,0:T(8,128)(2,1)S(1)} %collective-permute-done.1.three, bf16[136,1024]{1,0:T(8,128)(2,1)S(1)} %collective-permute-done.4.four, ...), custom_call_target="tpu_custom_call" | custom-call | tf_op jit(solution)/shard_map/absorb/pallas_call | solution.py:268
  50.6 9.6 %all_to_all.15.parts = f32[8,1,1152]{2,1,0:T(1,128)S(1)} all-to-all(f32[8,1,1152]{2,1,0:T(1,128)S(1)} %absorb.1), channel_id=1, replica_groups=mesh['z'=8,'xl'=2,'y'=4,'xh'=2,'core'=2] {'z'}, dimensions={0} | all-to-all | bytes 73728 | tf_op jit(solution)/shard_map/all_to_all | solution.py:283
  60.3 17.0 %all_to_all.16.parts = f32[32,1,1152]{2,1,0:T(1,128)S(1)} all-to-all(f32[32,1,1152]{2,1,0:T(1,128)S(1)} %gather_z.1), channel_id=1, replica_groups=mesh['z'=8,'xl'=2,'y'=4,'xh'=2,'core'=2] {'xl','y','xh','core'}, dimensions={0} | all-to-all | bytes 294912 | tf_op jit(solution)/shard_map/all_to_all | solution.py:292
  77.3 0.8 finish.1
  (2 shorter events, 0.1 us)
Async XLA Ops:
  4.0 14.9 %collective-permute-start.2 = (bf16[200,1024]{1,0:T(8,128)(2,1)}, bf16[200,1024]{1,0:T(8,128)(2,1)S(1)}, u32[]{:S(2)}, u32[]{:S(2)}) collective-permute-start(bf16[200,1024]{1,0:T(8,128)(2,1)} %get-tuple-element.9), channel_id=1, source_target_pairs={{0,224},{32,0},{64,32},{96,64},{128,96},{160,128},{192,160},{224,1... | collective-permute-start | bytes 1228808 | tf_op jit(solution)/shard_map/ppermute | solution.py:234
  10.4 5.3 %copy-start.5 = (bf16[168,1024]{1,0:T(8,128)(2,1)S(1)}, bf16[168,1024]{1,0:T(8,128)(2,1)}, u32[]{:S(2)}) copy-start(bf16[168,1024]{1,0:T(8,128)(2,1)} %get-tuple-element.8) | copy-start | bytes 1032196
  10.4 35.6 %all-to-all-start = ((bf16[8,152,1024]{2,1,0:T(8,128)(2,1)}), bf16[8,152,1024]{2,1,0:T(8,128)(2,1)S(1)}, u32[]{:S(2)}, u32[]{:S(2)}) async-start(bf16[8,152,1024]{2,1,0:T(8,128)(2,1)} %get-tuple-element.7), calls=%async_computation | async-start | bytes 4980736 | tf_op jit(solution)/shard_map/all_to_all | solution.py:255
  15.6 9.7 %collective-permute-start = (bf16[168,1024]{1,0:T(8,128)(2,1)S(1)}, bf16[168,1024]{1,0:T(8,128)(2,1)}, u32[]{:S(2)}, u32[]{:S(2)}) collective-permute-start(bf16[168,1024]{1,0:T(8,128)(2,1)S(1)} %copy-done.5), channel_id=1, source_target_pairs={{0,32},{32,64},{64,96},{96,128},{128,160},{160,192},{192,224},{224... | collective-permute-start | bytes 1032200 | tf_op jit(solution)/shard_map/ppermute | solution.py:234
  18.8 3.4 %copy-start.3 = (bf16[200,1024]{1,0:T(8,128)(2,1)}, bf16[200,1024]{1,0:T(8,128)(2,1)S(1)}, u32[]{:S(2)}) copy-start(bf16[200,1024]{1,0:T(8,128)(2,1)S(1)} %collective-permute-done.2.one) | copy-start | bytes 1228804
  18.8 9.2 %collective-permute-start.3 = (bf16[168,1024]{1,0:T(8,128)(2,1)S(1)}, bf16[168,1024]{1,0:T(8,128)(2,1)S(1)}, u32[]{:S(2)}, u32[]{:S(2)}) collective-permute-start(bf16[168,1024]{1,0:T(8,128)(2,1)S(1)} %slice.8), channel_id=1, source_target_pairs={{0,224},{32,0},{64,32},{96,64},{128,96},{160,128},{192,160},{224,1... | collective-permute-start | bytes 1032200 | tf_op jit(solution)/shard_map/ppermute | solution.py:234
  25.3 18.2 %collective-permute-start.1 = (bf16[168,1024]{1,0:T(8,128)(2,1)}, bf16[168,1024]{1,0:T(8,128)(2,1)S(1)}, u32[]{:S(2)}, u32[]{:S(2)}) collective-permute-start(bf16[168,1024]{1,0:T(8,128)(2,1)} %collective-permute-done), channel_id=1, source_target_pairs={{0,64},{32,96},{64,128},{96,160},{128,192},{160,224},{192,0},{224,... | collective-permute-start | bytes 1032200 | tf_op jit(solution)/shard_map/ppermute | solution.py:234
  28.0 3.0 %copy-start.4 = (bf16[168,1024]{1,0:T(8,128)(2,1)}, bf16[168,1024]{1,0:T(8,128)(2,1)S(1)}, u32[]{:S(2)}) copy-start(bf16[168,1024]{1,0:T(8,128)(2,1)S(1)} %collective-permute-done.3.two) | copy-start | bytes 1032196
  28.8 14.7 %collective-permute-start.4 = (bf16[136,1024]{1,0:T(8,128)(2,1)}, bf16[136,1024]{1,0:T(8,128)(2,1)S(1)}, u32[]{:S(2)}, u32[]{:S(2)}) collective-permute-start(bf16[136,1024]{1,0:T(8,128)(2,1)} %slice.9), channel_id=1, source_target_pairs={{0,192},{32,224},{64,0},{96,32},{128,64},{160,96},{192,128},{224,1... | collective-permute-start | bytes 835592 | tf_op jit(solution)/shard_map/ppermute | solution.py:234
  31.0 15.0 %copy-start = (bf16[1,2,64,1024]{3,2,1,0:T(8,128)(2,1)S(1)}, bf16[1,2,64,1024]{3,2,1,0:T(8,128)(2,1)}, u32[]{:S(2)}) copy-start(bf16[1,2,64,1024]{3,2,1,0:T(8,128)(2,1)} %param.5) | copy-start | bytes 786436
  31.0 15.0 %copy-start.2 = (f32[1,1024]{1,0:T(1,128)S(1)}, f32[1,1024]{1,0:T(1,128)}, u32[]{:S(2)}) copy-start(f32[1,1024]{1,0:T(1,128)} %source.3) | copy-start | bytes 12292
  46.0 1.1 %copy-start.1 = (bf16[376,1024]{1,0:T(8,128)(2,1)S(1)}, bf16[376,1024]{1,0:T(8,128)(2,1)}, u32[]{:S(2)}) copy-start(bf16[376,1024]{1,0:T(8,128)(2,1)} %prepare.1.bundle) | copy-start | bytes 2310148

commit v13 on v12

--- a/solution.py
+++ b/solution.py
@@ -200,11 +200,11 @@
             + im.astype(f32) * (by_im[rows] + by_re[more])
         )
     total = -jnp.sum(total, axis=0, keepdims=True)
-    out[:, :, 0:CELLS] = jnp.broadcast_to(total[None], (NZ, 1, CELLS))
-    out[:, :, CELLS:LONG] = jnp.broadcast_to(mis[None], (NZ, 1, 128))
-
-
-def gather_z(parts, out):
+    out[:, :, 0:CELLS] = jnp.broadcast_to(total[None], (NZ * NY, 1, CELLS))
+    out[:, :, CELLS:LONG] = jnp.broadcast_to(mis[None], (NZ * NY, 1, 128))
+
+
+def gather_zy(parts, out):
     out[...] = jnp.broadcast_to(
         jnp.sum(parts[...], axis=0, keepdims=True), out.shape
     )
@@ -216,8 +216,8 @@
     own = jnp.zeros((1, LONG), f32)
     for f in range(NF):
         here = parts[f]
-        for q in range(1, NQ):
-            here = here + parts[q * NF + f]
+        for x in range(1, NX):
+            here = here + parts[x * NF + f]
         squares = squares + here[:, 0:CELLS] * here[:, 0:CELLS]
         own = jnp.where(mine == f, here, own)
     rms = jnp.sqrt(jnp.sum(squares, keepdims=True) / (NF * CELLS) + 1e-06)
@@ -267,7 +267,7 @@
     )(own_mask, own_spec, one, two)
     part = pl.pallas_call(
         absorb,
-        out_shape=shape(f32, NZ, 1, LONG),
+        out_shape=shape(f32, NZ * NY, 1, LONG),
         in_specs=[vmem] * 6,
         out_specs=vmem,
         scratch_shapes=[
@@ -280,16 +280,16 @@
         name="absorb",
         compiler_params=pltpu.CompilerParams(vmem_limit_bytes=40 << 20),
     )(shared, source, g, three, four, ready)
-    part = lax.all_to_all(part, "z", 0, 0, tiled=True)
+    part = lax.all_to_all(part, ("z", "y"), 0, 0, tiled=True)
     part = pl.pallas_call(
-        gather_z,
-        out_shape=shape(f32, NQ * NF, 1, LONG),
+        gather_zy,
+        out_shape=shape(f32, NX * NF, 1, LONG),
         in_specs=[vmem],
         out_specs=vmem,
-        name="gather_z",
+        name="gather_zy",
         compiler_params=pltpu.CompilerParams(vmem_limit_bytes=8 << 20),
     )(part)
-    part = lax.all_to_all(part, PLANE + FREQ, 0, 0, tiled=True)
+    part = lax.all_to_all(part, ("xl",) + FREQ, 0, 0, tiled=True)
     return pl.pallas_call(
         finish,
         out_shape=(shape(f32, 1, CELLS), shape(f32, 1)),

time: 78.3 us -> 78.3 us (level)
  no operation moved by 1% of the time
where the time goes in v13:
time: 78.3 us; the launch traced here: 77.9 us
  blocking collectives  26.5 us (34%)
  waiting for transfers between devices  21.7 us (28%)
  starting transfers between devices  17.3 us (22%)
  Pallas kernels  9.83 us (13%)
  local copies, waits for them, and re-layouts  1.94 us (2%)
    ppermute x5, waiting for transfers between devices, from_z(): return lax.ppermute(array, 'z', [(z, (z - u) % NZ) for z in range(NZ)])  19.3 us
    all_to_all x1, blocking collectives, local(): part = lax.all_to_all(part, ('z', 'y'), 0, 0, tiled=True)  14.6 us
    ppermute x5, starting transfers between devices, from_z(): return lax.ppermute(array, 'z', [(z, (z - u) % NZ) for z in range(NZ)])  12.1 us
    all_to_all x1, blocking collectives, local(): part = lax.all_to_all(part, ('xl',) + FREQ, 0, 0, tiled=True)  11.9 us
    all_to_all x1, starting transfers between devices, local(): shared = lax.all_to_all(shared, PLANE, 0, 0, tiled=True)  5.25 us
    pallas_call x1, Pallas kernels, local(): pl.pallas_call(absorb, out_shape=shape(f32, NZ * NY, 1, LONG), in_specs=[...  3.52 us
    pallas_call x1, Pallas kernels, local(): pl.pallas_call(pack, out_shape=[shape(bf16, FULL, CELLS), shape(bf16, NEX...  3.32 us
    all_to_all x1, waiting for transfers between devices, local(): shared = lax.all_to_all(shared, PLANE, 0, 0, tiled=True)  2.45 us
  transfers between devices with their start and end apart: 6, of which 5 were waited for; matrix products, arithmetic and copies ran while one was open for 1% of the time, Pallas kernels for 3%

profile of v13, /device:TPU:1, one launch (start us, length us, event | category | flops | bytes accessed | tf_op | source)
XLA Modules:
  0.0 77.9 jit_solution(14476987325448815092)
XLA Ops:
  0.6 3.3 %pack.1 = (bf16[200,1024]{1,0:T(8,128)(2,1)}, bf16[168,1024]{1,0:T(8,128)(2,1)}, bf16[8,152,1024]{2,1,0:T(8,128)(2,1)}, bf16[64,512]{1,0:T(8,128)(2,1)}, f32[64,128]{1,0:T(8,128)}) custom-call(bf16[2,64,1024]{2,1,0:T(8,128)(2,1)} %bitcast.2, s32[64,4096]{1,0:T(8,128)} %mask.1, bf16[2,64]{1,0:T(2,128)(2,1)} %bitcast.4), custom_call_target="tpu_custom_call" | custom-call | tf_op jit(solution)/shard_map/pack/pallas_call | solution.py:240
  4.0 6.4 %collective-permute-start.2 = (bf16[200,1024]{1,0:T(8,128)(2,1)}, bf16[200,1024]{1,0:T(8,128)(2,1)S(1)}, u32[]{:S(2)}, u32[]{:S(2)}) collective-permute-start(bf16[200,1024]{1,0:T(8,128)(2,1)} %get-tuple-element.9), channel_id=1, source_target_pairs={{0,224},{32,0},{64,32},{96,64},{128,96},{160,128},{192,160},{224,1... | collective-permute-start | bytes 1228808 | tf_op jit(solution)/shard_map/ppermute | solution.py:234
  10.4 0.0 copy-start.5
  10.4 5.2 %all-to-all-start = ((bf16[8,152,1024]{2,1,0:T(8,128)(2,1)}), bf16[8,152,1024]{2,1,0:T(8,128)(2,1)S(1)}, u32[]{:S(2)}, u32[]{:S(2)}) async-start(bf16[8,152,1024]{2,1,0:T(8,128)(2,1)} %get-tuple-element.7), calls=%async_computation | async-start | bytes 4980736 | tf_op jit(solution)/shard_map/all_to_all | solution.py:255
  15.6 0.0 copy-done.5
  15.6 0.1 collective-permute-start
  15.7 3.1 %collective-permute-done.2.one = bf16[200,1024]{1,0:T(8,128)(2,1)S(1)} collective-permute-done((bf16[200,1024]{1,0:T(8,128)(2,1)}, bf16[200,1024]{1,0:T(8,128)(2,1)S(1)}, u32[]{:S(2)}, u32[]{:S(2)}) %collective-permute-start.2) | collective-permute-done | bytes 409632 | tf_op jit(solution)/shard_map/ppermute | solution.py:234
  18.8 0.0 copy-start.3
  18.8 3.4 %collective-permute-start.3 = (bf16[168,1024]{1,0:T(8,128)(2,1)S(1)}, bf16[168,1024]{1,0:T(8,128)(2,1)S(1)}, u32[]{:S(2)}, u32[]{:S(2)}) collective-permute-start(bf16[168,1024]{1,0:T(8,128)(2,1)S(1)} %slice.8), channel_id=1, source_target_pairs={{0,224},{32,0},{64,32},{96,64},{128,96},{160,128},{192,160},{224,1... | collective-permute-start | bytes 1032200 | tf_op jit(solution)/shard_map/ppermute | solution.py:234
  22.2 0.0 copy-done.3
  22.2 3.1 %collective-permute-done = bf16[168,1024]{1,0:T(8,128)(2,1)} collective-permute-done((bf16[168,1024]{1,0:T(8,128)(2,1)S(1)}, bf16[168,1024]{1,0:T(8,128)(2,1)}, u32[]{:S(2)}, u32[]{:S(2)}) %collective-permute-start) | collective-permute-done | bytes 344096 | tf_op jit(solution)/shard_map/ppermute | solution.py:234
  25.3 0.0 collective-permute-start.1
  25.3 2.7 %collective-permute-done.3.two = bf16[168,1024]{1,0:T(8,128)(2,1)S(1)} collective-permute-done((bf16[168,1024]{1,0:T(8,128)(2,1)S(1)}, bf16[168,1024]{1,0:T(8,128)(2,1)S(1)}, u32[]{:S(2)}, u32[]{:S(2)}) %collective-permute-start.3) | collective-permute-done | bytes 344096 | tf_op jit(solution)/shard_map/ppermute | solution.py:234
  28.0 0.0 copy-start.4
  28.0 0.8 slice.9
  28.8 2.2 %collective-permute-start.4 = (bf16[136,1024]{1,0:T(8,128)(2,1)}, bf16[136,1024]{1,0:T(8,128)(2,1)S(1)}, u32[]{:S(2)}, u32[]{:S(2)}) collective-permute-start(bf16[136,1024]{1,0:T(8,128)(2,1)} %slice.9), channel_id=1, source_target_pairs={{0,192},{32,224},{64,0},{96,32},{128,64},{160,96},{192,128},{224,1... | collective-permute-start | bytes 835592 | tf_op jit(solution)/shard_map/ppermute | solution.py:234
  31.0 0.0 copy-done.4
  31.0 0.0 copy-start
  31.0 0.0 copy-start.2
  31.0 2.1 %prepare.1.bundle = bf16[376,1024]{1,0:T(8,128)(2,1)} custom-call(bf16[64,512]{1,0:T(8,128)(2,1)} %get-tuple-element.10.own_mask, f32[64,128]{1,0:T(8,128)} %get-tuple-element.11.own_spec, bf16[200,1024]{1,0:T(8,128)(2,1)} %copy-done.3, bf16[168,1024]{1,0:T(8,128)(2,1)} %copy-done.4), custom_call_target="tpu_custom_call" | custom-call | flops 17500000256 | tf_op jit(solution)/shard_map/prepare/pallas_call | solution.py:258
  33.1 10.4 %collective-permute-done.1.three = bf16[168,1024]{1,0:T(8,128)(2,1)S(1)} collective-permute-done((bf16[168,1024]{1,0:T(8,128)(2,1)}, bf16[168,1024]{1,0:T(8,128)(2,1)S(1)}, u32[]{:S(2)}, u32[]{:S(2)}) %collective-permute-start.1) | collective-permute-done | bytes 344096 | tf_op jit(solution)/shard_map/ppermute | solution.py:234
  43.5 0.0 collective-permute-done.4.four
  43.5 2.5 %all-to-all-done.shared = bf16[8,152,1024]{2,1,0:T(8,128)(2,1)S(1)} async-done(((bf16[8,152,1024]{2,1,0:T(8,128)(2,1)}), bf16[8,152,1024]{2,1,0:T(8,128)(2,1)S(1)}, u32[]{:S(2)}, u32[]{:S(2)}) %all-to-all-start) | async-done | bytes 2490400 | tf_op jit(solution)/shard_map/all_to_all | solution.py:255
  46.0 0.0 copy-done
  46.0 0.0 copy-done.2
  46.0 0.0 copy-start.1
  46.0 1.1 %copy-done.1 = bf16[376,1024]{1,0:T(8,128)(2,1)S(1)} copy-done((bf16[376,1024]{1,0:T(8,128)(2,1)S(1)}, bf16[376,1024]{1,0:T(8,128)(2,1)}, u32[]{:S(2)}) %copy-start.1) | copy-done | bytes 770072
  47.1 3.5 %absorb.1 = f32[32,1,1152]{2,1,0:T(1,128)S(1)} custom-call(bf16[8,152,1024]{2,1,0:T(8,128)(2,1)S(1)} %all-to-all-done.shared, f32[1,1024]{1,0:T(1,128)S(1)} %copy-done.2, bf16[2,64,1024]{2,1,0:T(8,128)(2,1)S(1)} %bitcast.3, bf16[168,1024]{1,0:T(8,128)(2,1)S(1)} %collective-permute-done.1.three, bf16[136,1024]{1,0:T(8,128)(2,1)S(1)} %collective-permute-done.4.four, ...), custom_call_target="tpu_custom_call" | custom-call | tf_op jit(solution)/shard_map/absorb/pallas_call | solution.py:268
  50.6 14.6 %all_to_all.15.parts = f32[32,1,1152]{2,1,0:T(1,128)S(1)} all-to-all(f32[32,1,1152]{2,1,0:T(1,128)S(1)} %absorb.1), channel_id=1, replica_groups=mesh['z'=8,'xl'=2,'y'=4,'xh'=2,'core'=2] {'z','y'}, dimensions={0} | all-to-all | bytes 294912 | tf_op jit(solution)/shard_map/all_to_all | solution.py:283
  65.2 0.1 gather_zy.1
  65.3 11.9 %all_to_all.16.parts = f32[8,1,1152]{2,1,0:T(1,128)S(1)} all-to-all(f32[8,1,1152]{2,1,0:T(1,128)S(1)} %gather_zy.1), channel_id=1, replica_groups=mesh['z'=8,'xl'=2,'y'=4,'xh'=2,'core'=2] {'xl','xh','core'}, dimensions={0} | all-to-all | bytes 73728 | tf_op jit(solution)/shard_map/all_to_all | solution.py:292
  77.2 0.8 finish.1
  (1 shorter events, 0.0 us)
Async XLA Ops:
  4.0 14.9 %collective-permute-start.2 = (bf16[200,1024]{1,0:T(8,128)(2,1)}, bf16[200,1024]{1,0:T(8,128)(2,1)S(1)}, u32[]{:S(2)}, u32[]{:S(2)}) collective-permute-start(bf16[200,1024]{1,0:T(8,128)(2,1)} %get-tuple-element.9), channel_id=1, source_target_pairs={{0,224},{32,0},{64,32},{96,64},{128,96},{160,128},{192,160},{224,1... | collective-permute-start | bytes 1228808 | tf_op jit(solution)/shard_map/ppermute | solution.py:234
  10.4 5.3 %copy-start.5 = (bf16[168,1024]{1,0:T(8,128)(2,1)S(1)}, bf16[168,1024]{1,0:T(8,128)(2,1)}, u32[]{:S(2)}) copy-start(bf16[168,1024]{1,0:T(8,128)(2,1)} %get-tuple-element.8) | copy-start | bytes 1032196
  10.4 35.6 %all-to-all-start = ((bf16[8,152,1024]{2,1,0:T(8,128)(2,1)}), bf16[8,152,1024]{2,1,0:T(8,128)(2,1)S(1)}, u32[]{:S(2)}, u32[]{:S(2)}) async-start(bf16[8,152,1024]{2,1,0:T(8,128)(2,1)} %get-tuple-element.7), calls=%async_computation | async-start | bytes 4980736 | tf_op jit(solution)/shard_map/all_to_all | solution.py:255
  15.6 9.7 %collective-permute-start = (bf16[168,1024]{1,0:T(8,128)(2,1)S(1)}, bf16[168,1024]{1,0:T(8,128)(2,1)}, u32[]{:S(2)}, u32[]{:S(2)}) collective-permute-start(bf16[168,1024]{1,0:T(8,128)(2,1)S(1)} %copy-done.5), channel_id=1, source_target_pairs={{0,32},{32,64},{64,96},{96,128},{128,160},{160,192},{192,224},{224... | collective-permute-start | bytes 1032200 | tf_op jit(solution)/shard_map/ppermute | solution.py:234
  18.8 3.4 %copy-start.3 = (bf16[200,1024]{1,0:T(8,128)(2,1)}, bf16[200,1024]{1,0:T(8,128)(2,1)S(1)}, u32[]{:S(2)}) copy-start(bf16[200,1024]{1,0:T(8,128)(2,1)S(1)} %collective-permute-done.2.one) | copy-start | bytes 1228804
  18.8 9.2 %collective-permute-start.3 = (bf16[168,1024]{1,0:T(8,128)(2,1)S(1)}, bf16[168,1024]{1,0:T(8,128)(2,1)S(1)}, u32[]{:S(2)}, u32[]{:S(2)}) collective-permute-start(bf16[168,1024]{1,0:T(8,128)(2,1)S(1)} %slice.8), channel_id=1, source_target_pairs={{0,224},{32,0},{64,32},{96,64},{128,96},{160,128},{192,160},{224,1... | collective-permute-start | bytes 1032200 | tf_op jit(solution)/shard_map/ppermute | solution.py:234
  25.3 18.2 %collective-permute-start.1 = (bf16[168,1024]{1,0:T(8,128)(2,1)}, bf16[168,1024]{1,0:T(8,128)(2,1)S(1)}, u32[]{:S(2)}, u32[]{:S(2)}) collective-permute-start(bf16[168,1024]{1,0:T(8,128)(2,1)} %collective-permute-done), channel_id=1, source_target_pairs={{0,64},{32,96},{64,128},{96,160},{128,192},{160,224},{192,0},{224,... | collective-permute-start | bytes 1032200 | tf_op jit(solution)/shard_map/ppermute | solution.py:234
  28.0 3.0 %copy-start.4 = (bf16[168,1024]{1,0:T(8,128)(2,1)}, bf16[168,1024]{1,0:T(8,128)(2,1)S(1)}, u32[]{:S(2)}) copy-start(bf16[168,1024]{1,0:T(8,128)(2,1)S(1)} %collective-permute-done.3.two) | copy-start | bytes 1032196
  28.8 14.7 %collective-permute-start.4 = (bf16[136,1024]{1,0:T(8,128)(2,1)}, bf16[136,1024]{1,0:T(8,128)(2,1)S(1)}, u32[]{:S(2)}, u32[]{:S(2)}) collective-permute-start(bf16[136,1024]{1,0:T(8,128)(2,1)} %slice.9), channel_id=1, source_target_pairs={{0,192},{32,224},{64,0},{96,32},{128,64},{160,96},{192,128},{224,1... | collective-permute-start | bytes 835592 | tf_op jit(solution)/shard_map/ppermute | solution.py:234
  31.0 15.0 %copy-start = (bf16[1,2,64,1024]{3,2,1,0:T(8,128)(2,1)S(1)}, bf16[1,2,64,1024]{3,2,1,0:T(8,128)(2,1)}, u32[]{:S(2)}) copy-start(bf16[1,2,64,1024]{3,2,1,0:T(8,128)(2,1)} %param.5) | copy-start | bytes 786436
  31.0 15.0 %copy-start.2 = (f32[1,1024]{1,0:T(1,128)S(1)}, f32[1,1024]{1,0:T(1,128)}, u32[]{:S(2)}) copy-start(f32[1,1024]{1,0:T(1,128)} %source.3) | copy-start | bytes 12292
  46.0 1.1 %copy-start.1 = (bf16[376,1024]{1,0:T(8,128)(2,1)S(1)}, bf16[376,1024]{1,0:T(8,128)(2,1)}, u32[]{:S(2)}) copy-start(bf16[376,1024]{1,0:T(8,128)(2,1)} %prepare.1.bundle) | copy-start | bytes 2310148

commit v14 on v12

--- a/solution.py
+++ b/solution.py
@@ -14,8 +14,8 @@
 PLANE = ("xl", "y")
 FREQ = ("xh", "core")
 STA = ("z",) + PLANE
-OFFSETS = (1, 2, -3, 4)
-SHARED = 152
+OFFSETS = (1, 2, -3)
+SHARED = 144
 LONG = CELLS + 128
 f32, bf16 = jnp.float32, jnp.bfloat16
 
@@ -70,7 +70,7 @@
         ref[:, 128 * g : 128 * (g + 1)] = spectra[8 * g : 8 * (g + 1)]
 
 
-def pack(green, mask, spec_row, near, far, shared, own_mask, own_spec):
+def pack(green, mask, spec_row, near, far, last, shared, own_mask, own_spec):
     z = lax.axis_index("z")
     row = spec_row[...]
     col = nt(identity(ROWS), row)
@@ -86,14 +86,15 @@
         put_spectra(ref.at[SPEC : SPEC + 8], spectra)
     for u, ref, at in ((1, near, NEXT), (2, near, MASK), (-3, far, MASK)):
         put_mask(ref.at[at : at + 32], window(mask, z - u).astype(bf16))
+    put_mask(last, window(mask, z - 4).astype(bf16))
     own_mask[...] = window(mask, z).astype(bf16)
     wide = [window(mask, z + u) for u in OFFSETS]
+    rows = own_spec[:, 64:128]
     for q in range(NQ):
         shared[q, 0:64, :] = green[0]
         shared[q, 64:128, :] = green[1]
-        put_spectra(shared.at[q, 144:152], spectra)
         part = jnp.concatenate(
-            [w[:, ROWS * q : ROWS * (q + 1)] for w in wide], axis=1
+            [w[:, ROWS * q : ROWS * (q + 1)] for w in wide] + [rows], axis=1
         ).astype(bf16)
         for g in range(4):
             shared[q, 128:144, 256 * g : 256 * (g + 1)] = part[16 * g : 16 * (g + 1)]
@@ -125,7 +126,7 @@
         ].astype(bf16)
 
 
-def absorb(shared, source, green, three, four, bundle, out, far_re, far_im, far_spec, back, wt):
+def absorb(shared, source, green, three, four, last, bundle, out, far_re, far_im, far_spec, back, wt):
     real, imag = slice(REAL, REAL + ROWS), slice(IMAG, IMAG + ROWS)
     tall = 5 * ROWS
     scale = source[...]
@@ -165,13 +166,13 @@
             back[ROWS * q + 16 * g : ROWS * q + 16 * (g + 1), :] = ref[
                 128:144, 256 * g : 256 * (g + 1)
             ]
-        far_spec[0:2, rows] = ref[144:152, 0:128].astype(f32)[0:2, 64:128]
+        far_spec[0:2, rows] = ref[128:144, 128:256].astype(f32)[0:2, 64:128]
     behind = nt(identity(4 * ROWS), back[...])
     counts = jnp.concatenate(
         [
             weight[0:ROWS],
             weight[ROWS : 4 * ROWS] + behind[0 : 3 * ROWS],
-            behind[3 * ROWS : 4 * ROWS],
+            take_mask(last, 0),
         ],
         axis=0,
     )
@@ -237,17 +238,18 @@
 def local(spectra, green, source, pair_mask):
     g = green[0]
     vmem = pl.BlockSpec(memory_space=pltpu.VMEM)
-    near, far, shared, own_mask, own_spec = pl.pallas_call(
+    near, far, last, shared, own_mask, own_spec = pl.pallas_call(
         pack,
         out_shape=[
             shape(bf16, FULL, CELLS),
             shape(bf16, NEXT, CELLS),
+            shape(bf16, 32, CELLS),
             shape(bf16, NQ, SHARED, CELLS),
             shape(bf16, ROWS, WIDE),
             shape(f32, ROWS, 128),
         ],
         in_specs=[vmem] * 3,
-        out_specs=[vmem] * 5,
+        out_specs=[vmem] * 6,
         name="pack",
     )(g, pair_mask, spectra[0])
     three = from_z(from_z(far, -1), -2)
@@ -255,6 +257,7 @@
     shared = lax.all_to_all(shared, PLANE, 0, 0, tiled=True)
     two = from_z(one[:NEXT], 1)
     four = from_z(two[:MASK], 2)
+    last = from_z(last, 4)
     ready = pl.pallas_call(
         prepare,
         out_shape=shape(bf16, BUNDLE, CELLS),
@@ -268,7 +271,7 @@
     part = pl.pallas_call(
         absorb,
         out_shape=shape(f32, NZ, 1, LONG),
-        in_specs=[vmem] * 6,
+        in_specs=[vmem] * 7,
         out_specs=vmem,
         scratch_shapes=[
             pltpu.VMEM((WIDE, CELLS), bf16),
@@ -279,7 +282,7 @@
         ],
         name="absorb",
         compiler_params=pltpu.CompilerParams(vmem_limit_bytes=40 << 20),
-    )(shared, source, g, three, four, ready)
+    )(shared, source, g, three, four, last, ready)
     part = lax.all_to_all(part, "z", 0, 0, tiled=True)
     part = pl.pallas_call(
         gather_z,

time: 78.3 us -> 79.3 us (1.013)
  blocking collectives: 26.6 us -> 29 us
  waiting for transfers between devices: 21.7 us -> 20 us
    all_to_all x1, waiting for transfers between devices: 2.45 us -> 0.26 us  [local(): shared = lax.all_to_all(shared, PLANE, 0, 0, tiled=True)]
    all_to_all x1, blocking collectives: 9.61 us -> 10.9 us  [local(): part = lax.all_to_all(part, 'z', 0, 0, tiled=True)]
    all_to_all x1, blocking collectives: 17 us -> 18.1 us  [local(): part = lax.all_to_all(part, PLANE + FREQ, 0, 0, tiled=True)]
    ppermute x5 -> x6, waiting for transfers between devices: 19.3 us -> 19.8 us  [from_z(): return lax.ppermute(array, 'z', [(z, (z - u) % NZ) for z in range(NZ)])]
    ppermute x5 -> x6, starting transfers between devices: 12.1 us -> 12.3 us  [from_z(): return lax.ppermute(array, 'z', [(z, (z - u) % NZ) for z in range(NZ)])]
  transfers between devices with their start and end apart: 6 -> 7, of which waited for: 5 -> 5; matrix products, arithmetic and copies ran while one was open for 1% -> 1% of each run, Pallas kernels for 3% -> 3%
where the time goes in v14:
time: 79.3 us; the launch traced here: 79 us
  blocking collectives  29 us (37%)
  waiting for transfers between devices  20 us (25%)
  starting transfers between devices  17.6 us (22%)
  Pallas kernels  9.79 us (12%)
  local copies, waits for them, and re-layouts  1.94 us (2%)
    ppermute x6, waiting for transfers between devices, from_z(): return lax.ppermute(array, 'z', [(z, (z - u) % NZ) for z in range(NZ)])  19.8 us
    all_to_all x1, blocking collectives, local(): part = lax.all_to_all(part, PLANE + FREQ, 0, 0, tiled=True)  18.1 us
    ppermute x6, starting transfers between devices, from_z(): return lax.ppermute(array, 'z', [(z, (z - u) % NZ) for z in range(NZ)])  12.3 us
    all_to_all x1, blocking collectives, local(): part = lax.all_to_all(part, 'z', 0, 0, tiled=True)  10.9 us
    all_to_all x1, starting transfers between devices, local(): shared = lax.all_to_all(shared, PLANE, 0, 0, tiled=True)  5.25 us
    pallas_call x1, Pallas kernels, local(): pl.pallas_call(absorb, out_shape=shape(f32, NZ, 1, LONG), in_specs=[vmem]...  3.54 us
    pallas_call x1, Pallas kernels, local(): pl.pallas_call(pack, out_shape=[shape(bf16, FULL, CELLS), shape(bf16, NEX...  3.31 us
    pallas_call x1, Pallas kernels, local(): pl.pallas_call(prepare, out_shape=shape(bf16, BUNDLE, CELLS), in_specs=[v...  2.14 us
  transfers between devices with their start and end apart: 7, of which 5 were waited for; matrix products, arithmetic and copies ran while one was open for 1% of the time, Pallas kernels for 3%

profile of v14, /device:TPU:1, one launch (start us, length us, event | category | flops | bytes accessed | tf_op | source)
XLA Modules:
  0.0 79.0 jit_solution(17772480821841149824)
XLA Ops:
  0.6 3.3 %pack.1 = (bf16[200,1024]{1,0:T(8,128)(2,1)}, bf16[168,1024]{1,0:T(8,128)(2,1)}, bf16[32,1024]{1,0:T(8,128)(2,1)}, bf16[8,144,1024]{2,1,0:T(8,128)(2,1)}, bf16[64,512]{1,0:T(8,128)(2,1)}, /*index=5*/f32[64,128]{1,0:T(8,128)}) custom-call(bf16[2,64,1024]{2,1,0:T(8,128)(2,1)} %bitcast.2, s32[64,4096]{1,0:T(8,128)} %mask.1, bf16[2,64]{1,0:T(2,128)(2,1)} %bitcast.4), custom_call_target="tpu_custom_call" | custom-call | tf_op jit(solution)/shard_map/pack/pallas_call | solution.py:241
  3.9 6.4 %collective-permute-start.2 = (bf16[200,1024]{1,0:T(8,128)(2,1)}, bf16[200,1024]{1,0:T(8,128)(2,1)S(1)}, u32[]{:S(2)}, u32[]{:S(2)}) collective-permute-start(bf16[200,1024]{1,0:T(8,128)(2,1)} %get-tuple-element.10), channel_id=1, source_target_pairs={{0,224},{32,0},{64,32},{96,64},{128,96},{160,128},{192,160},{224,1... | collective-permute-start | bytes 1228808 | tf_op jit(solution)/shard_map/ppermute | solution.py:235
  10.3 0.0 copy-start.5
  10.3 0.0 copy-start.6
  10.3 5.2 %all-to-all-start = ((bf16[8,144,1024]{2,1,0:T(8,128)(2,1)}), bf16[8,144,1024]{2,1,0:T(8,128)(2,1)S(1)}, u32[]{:S(2)}, u32[]{:S(2)}) async-start(bf16[8,144,1024]{2,1,0:T(8,128)(2,1)} %get-tuple-element.8), calls=%async_computation | async-start | bytes 4718592 | tf_op jit(solution)/shard_map/all_to_all | solution.py:257
  15.6 0.0 copy-done.5
  15.6 0.1 collective-permute-start
  15.7 3.1 %collective-permute-done.2.one = bf16[200,1024]{1,0:T(8,128)(2,1)S(1)} collective-permute-done((bf16[200,1024]{1,0:T(8,128)(2,1)}, bf16[200,1024]{1,0:T(8,128)(2,1)S(1)}, u32[]{:S(2)}, u32[]{:S(2)}) %collective-permute-start.2) | collective-permute-done | bytes 409632 | tf_op jit(solution)/shard_map/ppermute | solution.py:235
  18.8 0.0 copy-start.3
  18.8 3.4 %collective-permute-start.3 = (bf16[168,1024]{1,0:T(8,128)(2,1)S(1)}, bf16[168,1024]{1,0:T(8,128)(2,1)S(1)}, u32[]{:S(2)}, u32[]{:S(2)}) collective-permute-start(bf16[168,1024]{1,0:T(8,128)(2,1)S(1)} %slice.8), channel_id=1, source_target_pairs={{0,224},{32,0},{64,32},{96,64},{128,96},{160,128},{192,160},{224,1... | collective-permute-start | bytes 1032200 | tf_op jit(solution)/shard_map/ppermute | solution.py:235
  22.2 0.0 copy-done.3
  22.2 0.0 copy-done.6
  22.2 1.5 %collective-permute-start.5 = (bf16[32,1024]{1,0:T(8,128)(2,1)S(1)}, bf16[32,1024]{1,0:T(8,128)(2,1)S(1)}, u32[]{:S(2)}, u32[]{:S(2)}) collective-permute-start(bf16[32,1024]{1,0:T(8,128)(2,1)S(1)} %copy-done.6), channel_id=1, source_target_pairs={{0,128},{32,160},{64,192},{96,224},{128,0},{160,32},{192,64},{224,... | collective-permute-start | bytes 196616 | tf_op jit(solution)/shard_map/ppermute | solution.py:235
  23.7 2.3 %collective-permute-done = bf16[168,1024]{1,0:T(8,128)(2,1)} collective-permute-done((bf16[168,1024]{1,0:T(8,128)(2,1)S(1)}, bf16[168,1024]{1,0:T(8,128)(2,1)}, u32[]{:S(2)}, u32[]{:S(2)}) %collective-permute-start) | collective-permute-done | bytes 344096 | tf_op jit(solution)/shard_map/ppermute | solution.py:235
  26.0 0.0 collective-permute-start.1
  26.0 3.3 %collective-permute-done.3.two = bf16[168,1024]{1,0:T(8,128)(2,1)S(1)} collective-permute-done((bf16[168,1024]{1,0:T(8,128)(2,1)S(1)}, bf16[168,1024]{1,0:T(8,128)(2,1)S(1)}, u32[]{:S(2)}, u32[]{:S(2)}) %collective-permute-start.3) | collective-permute-done | bytes 344096 | tf_op jit(solution)/shard_map/ppermute | solution.py:235
  29.3 0.0 copy-start.4
  29.3 0.8 slice.9
  30.0 0.9 %collective-permute-start.4 = (bf16[136,1024]{1,0:T(8,128)(2,1)}, bf16[136,1024]{1,0:T(8,128)(2,1)S(1)}, u32[]{:S(2)}, u32[]{:S(2)}) collective-permute-start(bf16[136,1024]{1,0:T(8,128)(2,1)} %slice.9), channel_id=1, source_target_pairs={{0,192},{32,224},{64,0},{96,32},{128,64},{160,96},{192,128},{224,1... | collective-permute-start | bytes 835592 | tf_op jit(solution)/shard_map/ppermute | solution.py:235
  31.0 0.0 copy-done.4
  31.0 0.0 copy-start
  31.0 0.0 copy-start.2
  31.0 2.1 %prepare.1.bundle = bf16[376,1024]{1,0:T(8,128)(2,1)} custom-call(bf16[64,512]{1,0:T(8,128)(2,1)} %get-tuple-element.12.own_mask, f32[64,128]{1,0:T(8,128)} %get-tuple-element.13.own_spec, bf16[200,1024]{1,0:T(8,128)(2,1)} %copy-done.3, bf16[168,1024]{1,0:T(8,128)(2,1)} %copy-done.4), custom_call_target="tpu_custom_call" | custom-call | flops 17500000256 | tf_op jit(solution)/shard_map/prepare/pallas_call | solution.py:261
  33.1 0.0 collective-permute-done.5.last
  33.1 11.1 %collective-permute-done.1.three = bf16[168,1024]{1,0:T(8,128)(2,1)S(1)} collective-permute-done((bf16[168,1024]{1,0:T(8,128)(2,1)}, bf16[168,1024]{1,0:T(8,128)(2,1)S(1)}, u32[]{:S(2)}, u32[]{:S(2)}) %collective-permute-start.1) | collective-permute-done | bytes 344096 | tf_op jit(solution)/shard_map/ppermute | solution.py:235
  44.3 0.0 collective-permute-done.4.four
  44.3 0.3 all-to-all-done.shared
  44.5 0.0 copy-done
  44.5 0.0 copy-done.2
  44.5 0.0 copy-start.1
  44.5 1.1 %copy-done.1 = bf16[376,1024]{1,0:T(8,128)(2,1)S(1)} copy-done((bf16[376,1024]{1,0:T(8,128)(2,1)S(1)}, bf16[376,1024]{1,0:T(8,128)(2,1)}, u32[]{:S(2)}) %copy-start.1) | copy-done | bytes 770072
  45.7 3.5 %absorb.1 = f32[8,1,1152]{2,1,0:T(1,128)S(1)} custom-call(bf16[8,144,1024]{2,1,0:T(8,128)(2,1)S(1)} %all-to-all-done.shared, f32[1,1024]{1,0:T(1,128)S(1)} %copy-done.2, bf16[2,64,1024]{2,1,0:T(8,128)(2,1)S(1)} %bitcast.3, bf16[168,1024]{1,0:T(8,128)(2,1)S(1)} %collective-permute-done.1.three, bf16[136,1024]{1,0:T(8,128)(2,1)S(1)} %collective-permute-done.4.four, ...), custom_call_target="tpu_custom_call" | custom-call | tf_op jit(solution)/shard_map/absorb/pallas_call | solution.py:271
  49.2 10.9 %all_to_all.15.parts = f32[8,1,1152]{2,1,0:T(1,128)S(1)} all-to-all(f32[8,1,1152]{2,1,0:T(1,128)S(1)} %absorb.1), channel_id=1, replica_groups=mesh['z'=8,'xl'=2,'y'=4,'xh'=2,'core'=2] {'z'}, dimensions={0} | all-to-all | bytes 73728 | tf_op jit(solution)/shard_map/all_to_all | solution.py:286
  60.2 18.1 %all_to_all.16.parts = f32[32,1,1152]{2,1,0:T(1,128)S(1)} all-to-all(f32[32,1,1152]{2,1,0:T(1,128)S(1)} %gather_z.1), channel_id=1, replica_groups=mesh['z'=8,'xl'=2,'y'=4,'xh'=2,'core'=2] {'xl','y','xh','core'}, dimensions={0} | all-to-all | bytes 294912 | tf_op jit(solution)/shard_map/all_to_all | solution.py:295
  78.3 0.8 finish.1
  (2 shorter events, 0.1 us)
Async XLA Ops:
  3.9 14.9 %collective-permute-start.2 = (bf16[200,1024]{1,0:T(8,128)(2,1)}, bf16[200,1024]{1,0:T(8,128)(2,1)S(1)}, u32[]{:S(2)}, u32[]{:S(2)}) collective-permute-start(bf16[200,1024]{1,0:T(8,128)(2,1)} %get-tuple-element.10), channel_id=1, source_target_pairs={{0,224},{32,0},{64,32},{96,64},{128,96},{160,128},{192,160},{224,1... | collective-permute-start | bytes 1228808 | tf_op jit(solution)/shard_map/ppermute | solution.py:235
  10.3 5.3 %copy-start.5 = (bf16[168,1024]{1,0:T(8,128)(2,1)S(1)}, bf16[168,1024]{1,0:T(8,128)(2,1)}, u32[]{:S(2)}) copy-start(bf16[168,1024]{1,0:T(8,128)(2,1)} %get-tuple-element.9) | copy-start | bytes 1032196
  10.3 11.9 %copy-start.6 = (bf16[32,1024]{1,0:T(8,128)(2,1)S(1)}, bf16[32,1024]{1,0:T(8,128)(2,1)}, u32[]{:S(2)}) copy-start(bf16[32,1024]{1,0:T(8,128)(2,1)} %get-tuple-element.11) | copy-start | bytes 196612
  10.3 34.2 %all-to-all-start = ((bf16[8,144,1024]{2,1,0:T(8,128)(2,1)}), bf16[8,144,1024]{2,1,0:T(8,128)(2,1)S(1)}, u32[]{:S(2)}, u32[]{:S(2)}) async-start(bf16[8,144,1024]{2,1,0:T(8,128)(2,1)} %get-tuple-element.8), calls=%async_computation | async-start | bytes 4718592 | tf_op jit(solution)/shard_map/all_to_all | solution.py:257
  15.6 10.4 %collective-permute-start = (bf16[168,1024]{1,0:T(8,128)(2,1)S(1)}, bf16[168,1024]{1,0:T(8,128)(2,1)}, u32[]{:S(2)}, u32[]{:S(2)}) collective-permute-start(bf16[168,1024]{1,0:T(8,128)(2,1)S(1)} %copy-done.5), channel_id=1, source_target_pairs={{0,32},{32,64},{64,96},{96,128},{128,160},{160,192},{192,224},{224... | collective-permute-start | bytes 1032200 | tf_op jit(solution)/shard_map/ppermute | solution.py:235
  18.8 3.4 %copy-start.3 = (bf16[200,1024]{1,0:T(8,128)(2,1)}, bf16[200,1024]{1,0:T(8,128)(2,1)S(1)}, u32[]{:S(2)}) copy-start(bf16[200,1024]{1,0:T(8,128)(2,1)S(1)} %collective-permute-done.2.one) | copy-start | bytes 1228804
  18.8 10.5 %collective-permute-start.3 = (bf16[168,1024]{1,0:T(8,128)(2,1)S(1)}, bf16[168,1024]{1,0:T(8,128)(2,1)S(1)}, u32[]{:S(2)}, u32[]{:S(2)}) collective-permute-start(bf16[168,1024]{1,0:T(8,128)(2,1)S(1)} %slice.8), channel_id=1, source_target_pairs={{0,224},{32,0},{64,32},{96,64},{128,96},{160,128},{192,160},{224,1... | collective-permute-start | bytes 1032200 | tf_op jit(solution)/shard_map/ppermute | solution.py:235
  22.2 10.9 %collective-permute-start.5 = (bf16[32,1024]{1,0:T(8,128)(2,1)S(1)}, bf16[32,1024]{1,0:T(8,128)(2,1)S(1)}, u32[]{:S(2)}, u32[]{:S(2)}) collective-permute-start(bf16[32,1024]{1,0:T(8,128)(2,1)S(1)} %copy-done.6), channel_id=1, source_target_pairs={{0,128},{32,160},{64,192},{96,224},{128,0},{160,32},{192,64},{224,... | collective-permute-start | bytes 196616 | tf_op jit(solution)/shard_map/ppermute | solution.py:235
  26.0 18.3 %collective-permute-start.1 = (bf16[168,1024]{1,0:T(8,128)(2,1)}, bf16[168,1024]{1,0:T(8,128)(2,1)S(1)}, u32[]{:S(2)}, u32[]{:S(2)}) collective-permute-start(bf16[168,1024]{1,0:T(8,128)(2,1)} %collective-permute-done), channel_id=1, source_target_pairs={{0,64},{32,96},{64,128},{96,160},{128,192},{160,224},{192,0},{224,... | collective-permute-start | bytes 1032200 | tf_op jit(solution)/shard_map/ppermute | solution.py:235
  29.3 1.7 %copy-start.4 = (bf16[168,1024]{1,0:T(8,128)(2,1)}, bf16[168,1024]{1,0:T(8,128)(2,1)S(1)}, u32[]{:S(2)}) copy-start(bf16[168,1024]{1,0:T(8,128)(2,1)S(1)} %collective-permute-done.3.two) | copy-start | bytes 1032196
  30.0 14.2 %collective-permute-start.4 = (bf16[136,1024]{1,0:T(8,128)(2,1)}, bf16[136,1024]{1,0:T(8,128)(2,1)S(1)}, u32[]{:S(2)}, u32[]{:S(2)}) collective-permute-start(bf16[136,1024]{1,0:T(8,128)(2,1)} %slice.9), channel_id=1, source_target_pairs={{0,192},{32,224},{64,0},{96,32},{128,64},{160,96},{192,128},{224,1... | collective-permute-start | bytes 835592 | tf_op jit(solution)/shard_map/ppermute | solution.py:235
  31.0 13.6 %copy-start = (bf16[1,2,64,1024]{3,2,1,0:T(8,128)(2,1)S(1)}, bf16[1,2,64,1024]{3,2,1,0:T(8,128)(2,1)}, u32[]{:S(2)}) copy-start(bf16[1,2,64,1024]{3,2,1,0:T(8,128)(2,1)} %param.5) | copy-start | bytes 786436
  31.0 13.6 %copy-start.2 = (f32[1,1024]{1,0:T(1,128)S(1)}, f32[1,1024]{1,0:T(1,128)}, u32[]{:S(2)}) copy-start(f32[1,1024]{1,0:T(1,128)} %source.3) | copy-start | bytes 12292
  44.5 1.1 %copy-start.1 = (bf16[376,1024]{1,0:T(8,128)(2,1)S(1)}, bf16[376,1024]{1,0:T(8,128)(2,1)}, u32[]{:S(2)}) copy-start(bf16[376,1024]{1,0:T(8,128)(2,1)} %prepare.1.bundle) | copy-start | bytes 2310148

commit v15 on v13

--- a/solution.py
+++ b/solution.py
@@ -200,11 +200,11 @@
             + im.astype(f32) * (by_im[rows] + by_re[more])
         )
     total = -jnp.sum(total, axis=0, keepdims=True)
-    out[:, :, 0:CELLS] = jnp.broadcast_to(total[None], (NZ * NY, 1, CELLS))
-    out[:, :, CELLS:LONG] = jnp.broadcast_to(mis[None], (NZ * NY, 1, 128))
-
-
-def gather_zy(parts, out):
+    out[:, :, 0:CELLS] = jnp.broadcast_to(total[None], (NZ * NX, 1, CELLS))
+    out[:, :, CELLS:LONG] = jnp.broadcast_to(mis[None], (NZ * NX, 1, 128))
+
+
+def gather_zx(parts, out):
     out[...] = jnp.broadcast_to(
         jnp.sum(parts[...], axis=0, keepdims=True), out.shape
     )
@@ -216,8 +216,8 @@
     own = jnp.zeros((1, LONG), f32)
     for f in range(NF):
         here = parts[f]
-        for x in range(1, NX):
-            here = here + parts[x * NF + f]
+        for y in range(1, NY):
+            here = here + parts[y * NF + f]
         squares = squares + here[:, 0:CELLS] * here[:, 0:CELLS]
         own = jnp.where(mine == f, here, own)
     rms = jnp.sqrt(jnp.sum(squares, keepdims=True) / (NF * CELLS) + 1e-06)
@@ -267,7 +267,7 @@
     )(own_mask, own_spec, one, two)
     part = pl.pallas_call(
         absorb,
-        out_shape=shape(f32, NZ * NY, 1, LONG),
+        out_shape=shape(f32, NZ * NX, 1, LONG),
         in_specs=[vmem] * 6,
         out_specs=vmem,
         scratch_shapes=[
@@ -280,16 +280,16 @@
         name="absorb",
         compiler_params=pltpu.CompilerParams(vmem_limit_bytes=40 << 20),
     )(shared, source, g, three, four, ready)
-    part = lax.all_to_all(part, ("z", "y"), 0, 0, tiled=True)
+    part = lax.all_to_all(part, ("z", "xl"), 0, 0, tiled=True)
     part = pl.pallas_call(
-        gather_zy,
-        out_shape=shape(f32, NX * NF, 1, LONG),
+        gather_zx,
+        out_shape=shape(f32, NY * NF, 1, LONG),
         in_specs=[vmem],
         out_specs=vmem,
-        name="gather_zy",
+        name="gather_zx",
         compiler_params=pltpu.CompilerParams(vmem_limit_bytes=8 << 20),
     )(part)
-    part = lax.all_to_all(part, ("xl",) + FREQ, 0, 0, tiled=True)
+    part = lax.all_to_all(part, ("y",) + FREQ, 0, 0, tiled=True)
     return pl.pallas_call(
         finish,
         out_shape=(shape(f32, 1, CELLS), shape(f32, 1)),

time: 78.3 us -> 79.7 us (1.018)
  blocking collectives: 26.5 us -> 27.9 us
    all_to_all x2, blocking collectives: 26.5 us -> 27.9 us  [the longest x1 16.2 us: local(): part = lax.all_to_all(part, ('y',) + FREQ, 0, 0, tiled=True)]
where the time goes in v15:
time: 79.7 us; the launch traced here: 79.4 us
  blocking collectives  27.9 us (35%)
  waiting for transfers between devices  21.7 us (27%)
  starting transfers between devices  17.3 us (22%)
  Pallas kernels  9.79 us (12%)
  local copies, waits for them, and re-layouts  1.94 us (2%)
    ppermute x5, waiting for transfers between devices, from_z(): return lax.ppermute(array, 'z', [(z, (z - u) % NZ) for z in range(NZ)])  19.3 us
    all_to_all x1, blocking collectives, local(): part = lax.all_to_all(part, ('y',) + FREQ, 0, 0, tiled=True)  16.2 us
    ppermute x5, starting transfers between devices, from_z(): return lax.ppermute(array, 'z', [(z, (z - u) % NZ) for z in range(NZ)])  12.1 us
    all_to_all x1, blocking collectives, local(): part = lax.all_to_all(part, ('z', 'xl'), 0, 0, tiled=True)  11.7 us
    all_to_all x1, starting transfers between devices, local(): shared = lax.all_to_all(shared, PLANE, 0, 0, tiled=True)  5.25 us
    pallas_call x1, Pallas kernels, local(): pl.pallas_call(absorb, out_shape=shape(f32, NZ * NX, 1, LONG), in_specs=[...  3.53 us
    pallas_call x1, Pallas kernels, local(): pl.pallas_call(pack, out_shape=[shape(bf16, FULL, CELLS), shape(bf16, NEX...  3.32 us
    all_to_all x1, waiting for transfers between devices, local(): shared = lax.all_to_all(shared, PLANE, 0, 0, tiled=True)  2.45 us
  transfers between devices with their start and end apart: 6, of which 5 were waited for; matrix products, arithmetic and copies ran while one was open for 1% of the time, Pallas kernels for 3%

profile of v15, /device:TPU:1, one launch (start us, length us, event | category | flops | bytes accessed | tf_op | source)
XLA Modules:
  0.0 79.4 jit_solution(3148447538259150509)
XLA Ops:
  0.6 3.3 %pack.1 = (bf16[200,1024]{1,0:T(8,128)(2,1)}, bf16[168,1024]{1,0:T(8,128)(2,1)}, bf16[8,152,1024]{2,1,0:T(8,128)(2,1)}, bf16[64,512]{1,0:T(8,128)(2,1)}, f32[64,128]{1,0:T(8,128)}) custom-call(bf16[2,64,1024]{2,1,0:T(8,128)(2,1)} %bitcast.2, s32[64,4096]{1,0:T(8,128)} %mask.1, bf16[2,64]{1,0:T(2,128)(2,1)} %bitcast.4), custom_call_target="tpu_custom_call" | custom-call | tf_op jit(solution)/shard_map/pack/pallas_call | solution.py:240
  4.0 6.4 %collective-permute-start.2 = (bf16[200,1024]{1,0:T(8,128)(2,1)}, bf16[200,1024]{1,0:T(8,128)(2,1)S(1)}, u32[]{:S(2)}, u32[]{:S(2)}) collective-permute-start(bf16[200,1024]{1,0:T(8,128)(2,1)} %get-tuple-element.9), channel_id=1, source_target_pairs={{0,224},{32,0},{64,32},{96,64},{128,96},{160,128},{192,160},{224,1... | collective-permute-start | bytes 1228808 | tf_op jit(solution)/shard_map/ppermute | solution.py:234
  10.4 0.0 copy-start.5
  10.4 5.2 %all-to-all-start = ((bf16[8,152,1024]{2,1,0:T(8,128)(2,1)}), bf16[8,152,1024]{2,1,0:T(8,128)(2,1)S(1)}, u32[]{:S(2)}, u32[]{:S(2)}) async-start(bf16[8,152,1024]{2,1,0:T(8,128)(2,1)} %get-tuple-element.7), calls=%async_computation | async-start | bytes 4980736 | tf_op jit(solution)/shard_map/all_to_all | solution.py:255
  15.6 0.0 copy-done.5
  15.6 0.1 collective-permute-start
  15.7 3.1 %collective-permute-done.2.one = bf16[200,1024]{1,0:T(8,128)(2,1)S(1)} collective-permute-done((bf16[200,1024]{1,0:T(8,128)(2,1)}, bf16[200,1024]{1,0:T(8,128)(2,1)S(1)}, u32[]{:S(2)}, u32[]{:S(2)}) %collective-permute-start.2) | collective-permute-done | bytes 409632 | tf_op jit(solution)/shard_map/ppermute | solution.py:234
  18.8 0.0 copy-start.3
  18.8 3.4 %collective-permute-start.3 = (bf16[168,1024]{1,0:T(8,128)(2,1)S(1)}, bf16[168,1024]{1,0:T(8,128)(2,1)S(1)}, u32[]{:S(2)}, u32[]{:S(2)}) collective-permute-start(bf16[168,1024]{1,0:T(8,128)(2,1)S(1)} %slice.8), channel_id=1, source_target_pairs={{0,224},{32,0},{64,32},{96,64},{128,96},{160,128},{192,160},{224,1... | collective-permute-start | bytes 1032200 | tf_op jit(solution)/shard_map/ppermute | solution.py:234
  22.2 0.0 copy-done.3
  22.2 3.1 %collective-permute-done = bf16[168,1024]{1,0:T(8,128)(2,1)} collective-permute-done((bf16[168,1024]{1,0:T(8,128)(2,1)S(1)}, bf16[168,1024]{1,0:T(8,128)(2,1)}, u32[]{:S(2)}, u32[]{:S(2)}) %collective-permute-start) | collective-permute-done | bytes 344096 | tf_op jit(solution)/shard_map/ppermute | solution.py:234
  25.3 0.0 collective-permute-start.1
  25.3 2.7 %collective-permute-done.3.two = bf16[168,1024]{1,0:T(8,128)(2,1)S(1)} collective-permute-done((bf16[168,1024]{1,0:T(8,128)(2,1)S(1)}, bf16[168,1024]{1,0:T(8,128)(2,1)S(1)}, u32[]{:S(2)}, u32[]{:S(2)}) %collective-permute-start.3) | collective-permute-done | bytes 344096 | tf_op jit(solution)/shard_map/ppermute | solution.py:234
  28.0 0.0 copy-start.4
  28.0 0.8 slice.9
  28.8 2.2 %collective-permute-start.4 = (bf16[136,1024]{1,0:T(8,128)(2,1)}, bf16[136,1024]{1,0:T(8,128)(2,1)S(1)}, u32[]{:S(2)}, u32[]{:S(2)}) collective-permute-start(bf16[136,1024]{1,0:T(8,128)(2,1)} %slice.9), channel_id=1, source_target_pairs={{0,192},{32,224},{64,0},{96,32},{128,64},{160,96},{192,128},{224,1... | collective-permute-start | bytes 835592 | tf_op jit(solution)/shard_map/ppermute | solution.py:234
  31.0 0.0 copy-done.4
  31.0 0.0 copy-start
  31.0 0.0 copy-start.2
  31.0 2.1 %prepare.1.bundle = bf16[376,1024]{1,0:T(8,128)(2,1)} custom-call(bf16[64,512]{1,0:T(8,128)(2,1)} %get-tuple-element.10.own_mask, f32[64,128]{1,0:T(8,128)} %get-tuple-element.11.own_spec, bf16[200,1024]{1,0:T(8,128)(2,1)} %copy-done.3, bf16[168,1024]{1,0:T(8,128)(2,1)} %copy-done.4), custom_call_target="tpu_custom_call" | custom-call | flops 17500000256 | tf_op jit(solution)/shard_map/prepare/pallas_call | solution.py:258
  33.1 10.4 %collective-permute-done.1.three = bf16[168,1024]{1,0:T(8,128)(2,1)S(1)} collective-permute-done((bf16[168,1024]{1,0:T(8,128)(2,1)}, bf16[168,1024]{1,0:T(8,128)(2,1)S(1)}, u32[]{:S(2)}, u32[]{:S(2)}) %collective-permute-start.1) | collective-permute-done | bytes 344096 | tf_op jit(solution)/shard_map/ppermute | solution.py:234
  43.5 0.0 collective-permute-done.4.four
  43.5 2.5 %all-to-all-done.shared = bf16[8,152,1024]{2,1,0:T(8,128)(2,1)S(1)} async-done(((bf16[8,152,1024]{2,1,0:T(8,128)(2,1)}), bf16[8,152,1024]{2,1,0:T(8,128)(2,1)S(1)}, u32[]{:S(2)}, u32[]{:S(2)}) %all-to-all-start) | async-done | bytes 2490400 | tf_op jit(solution)/shard_map/all_to_all | solution.py:255
  46.0 0.0 copy-done
  46.0 0.0 copy-done.2
  46.0 0.0 copy-start.1
  46.0 1.1 %copy-done.1 = bf16[376,1024]{1,0:T(8,128)(2,1)S(1)} copy-done((bf16[376,1024]{1,0:T(8,128)(2,1)S(1)}, bf16[376,1024]{1,0:T(8,128)(2,1)}, u32[]{:S(2)}) %copy-start.1) | copy-done | bytes 770072
  47.1 3.5 %absorb.1 = f32[16,1,1152]{2,1,0:T(1,128)S(1)} custom-call(bf16[8,152,1024]{2,1,0:T(8,128)(2,1)S(1)} %all-to-all-done.shared, f32[1,1024]{1,0:T(1,128)S(1)} %copy-done.2, bf16[2,64,1024]{2,1,0:T(8,128)(2,1)S(1)} %bitcast.3, bf16[168,1024]{1,0:T(8,128)(2,1)S(1)} %collective-permute-done.1.three, bf16[136,1024]{1,0:T(8,128)(2,1)S(1)} %collective-permute-done.4.four, ...), custom_call_target="tpu_custom_call" | custom-call | tf_op jit(solution)/shard_map/absorb/pallas_call | solution.py:268
  50.6 11.7 %all_to_all.15.parts = f32[16,1,1152]{2,1,0:T(1,128)S(1)} all-to-all(f32[16,1,1152]{2,1,0:T(1,128)S(1)} %absorb.1), channel_id=1, replica_groups=mesh['z'=8,'xl'=2,'y'=4,'xh'=2,'core'=2] {'z','xl'}, dimensions={0} | all-to-all | bytes 147456 | tf_op jit(solution)/shard_map/all_to_all | solution.py:283
  62.3 0.1 gather_zx.1
  62.4 16.2 %all_to_all.16.parts = f32[16,1,1152]{2,1,0:T(1,128)S(1)} all-to-all(f32[16,1,1152]{2,1,0:T(1,128)S(1)} %gather_zx.1), channel_id=1, replica_groups=mesh['z'=8,'xl'=2,'y'=4,'xh'=2,'core'=2] {'y','xh','core'}, dimensions={0} | all-to-all | bytes 147456 | tf_op jit(solution)/shard_map/all_to_all | solution.py:292
  78.6 0.8 finish.1
  (1 shorter events, 0.0 us)
Async XLA Ops:
  4.0 14.9 %collective-permute-start.2 = (bf16[200,1024]{1,0:T(8,128)(2,1)}, bf16[200,1024]{1,0:T(8,128)(2,1)S(1)}, u32[]{:S(2)}, u32[]{:S(2)}) collective-permute-start(bf16[200,1024]{1,0:T(8,128)(2,1)} %get-tuple-element.9), channel_id=1, source_target_pairs={{0,224},{32,0},{64,32},{96,64},{128,96},{160,128},{192,160},{224,1... | collective-permute-start | bytes 1228808 | tf_op jit(solution)/shard_map/ppermute | solution.py:234
  10.4 5.3 %copy-start.5 = (bf16[168,1024]{1,0:T(8,128)(2,1)S(1)}, bf16[168,1024]{1,0:T(8,128)(2,1)}, u32[]{:S(2)}) copy-start(bf16[168,1024]{1,0:T(8,128)(2,1)} %get-tuple-element.8) | copy-start | bytes 1032196
  10.4 35.6 %all-to-all-start = ((bf16[8,152,1024]{2,1,0:T(8,128)(2,1)}), bf16[8,152,1024]{2,1,0:T(8,128)(2,1)S(1)}, u32[]{:S(2)}, u32[]{:S(2)}) async-start(bf16[8,152,1024]{2,1,0:T(8,128)(2,1)} %get-tuple-element.7), calls=%async_computation | async-start | bytes 4980736 | tf_op jit(solution)/shard_map/all_to_all | solution.py:255
  15.6 9.7 %collective-permute-start = (bf16[168,1024]{1,0:T(8,128)(2,1)S(1)}, bf16[168,1024]{1,0:T(8,128)(2,1)}, u32[]{:S(2)}, u32[]{:S(2)}) collective-permute-start(bf16[168,1024]{1,0:T(8,128)(2,1)S(1)} %copy-done.5), channel_id=1, source_target_pairs={{0,32},{32,64},{64,96},{96,128},{128,160},{160,192},{192,224},{224... | collective-permute-start | bytes 1032200 | tf_op jit(solution)/shard_map/ppermute | solution.py:234
  18.8 3.4 %copy-start.3 = (bf16[200,1024]{1,0:T(8,128)(2,1)}, bf16[200,1024]{1,0:T(8,128)(2,1)S(1)}, u32[]{:S(2)}) copy-start(bf16[200,1024]{1,0:T(8,128)(2,1)S(1)} %collective-permute-done.2.one) | copy-start | bytes 1228804
  18.8 9.2 %collective-permute-start.3 = (bf16[168,1024]{1,0:T(8,128)(2,1)S(1)}, bf16[168,1024]{1,0:T(8,128)(2,1)S(1)}, u32[]{:S(2)}, u32[]{:S(2)}) collective-permute-start(bf16[168,1024]{1,0:T(8,128)(2,1)S(1)} %slice.8), channel_id=1, source_target_pairs={{0,224},{32,0},{64,32},{96,64},{128,96},{160,128},{192,160},{224,1... | collective-permute-start | bytes 1032200 | tf_op jit(solution)/shard_map/ppermute | solution.py:234
  25.3 18.2 %collective-permute-start.1 = (bf16[168,1024]{1,0:T(8,128)(2,1)}, bf16[168,1024]{1,0:T(8,128)(2,1)S(1)}, u32[]{:S(2)}, u32[]{:S(2)}) collective-permute-start(bf16[168,1024]{1,0:T(8,128)(2,1)} %collective-permute-done), channel_id=1, source_target_pairs={{0,64},{32,96},{64,128},{96,160},{128,192},{160,224},{192,0},{224,... | collective-permute-start | bytes 1032200 | tf_op jit(solution)/shard_map/ppermute | solution.py:234
  28.0 3.0 %copy-start.4 = (bf16[168,1024]{1,0:T(8,128)(2,1)}, bf16[168,1024]{1,0:T(8,128)(2,1)S(1)}, u32[]{:S(2)}) copy-start(bf16[168,1024]{1,0:T(8,128)(2,1)S(1)} %collective-permute-done.3.two) | copy-start | bytes 1032196
  28.8 14.7 %collective-permute-start.4 = (bf16[136,1024]{1,0:T(8,128)(2,1)}, bf16[136,1024]{1,0:T(8,128)(2,1)S(1)}, u32[]{:S(2)}, u32[]{:S(2)}) collective-permute-start(bf16[136,1024]{1,0:T(8,128)(2,1)} %slice.9), channel_id=1, source_target_pairs={{0,192},{32,224},{64,0},{96,32},{128,64},{160,96},{192,128},{224,1... | collective-permute-start | bytes 835592 | tf_op jit(solution)/shard_map/ppermute | solution.py:234
  31.0 15.0 %copy-start = (bf16[1,2,64,1024]{3,2,1,0:T(8,128)(2,1)S(1)}, bf16[1,2,64,1024]{3,2,1,0:T(8,128)(2,1)}, u32[]{:S(2)}) copy-start(bf16[1,2,64,1024]{3,2,1,0:T(8,128)(2,1)} %param.5) | copy-start | bytes 786436
  31.0 15.0 %copy-start.2 = (f32[1,1024]{1,0:T(1,128)S(1)}, f32[1,1024]{1,0:T(1,128)}, u32[]{:S(2)}) copy-start(f32[1,1024]{1,0:T(1,128)} %source.3) | copy-start | bytes 12292
  46.0 1.1 %copy-start.1 = (bf16[376,1024]{1,0:T(8,128)(2,1)S(1)}, bf16[376,1024]{1,0:T(8,128)(2,1)}, u32[]{:S(2)}) copy-start(bf16[376,1024]{1,0:T(8,128)(2,1)} %prepare.1.bundle) | copy-start | bytes 2310148

commit v16 on v12

--- a/solution.py
+++ b/solution.py
@@ -39,7 +39,7 @@
 
 
 SPEC, IMAG, REAL, MASK, NEXT, FULL = 0, 8, 72, 136, 168, 200
-PREPARE = 17_500_000_000
+PREPARE = 10_000_000_000
 
 
 def window(mask, at):

time: 78.3 us -> 81.9 us (1.046)
  blocking collectives: 26.6 us -> 30.1 us
    all_to_all x1, blocking collectives: 9.61 us -> 13.1 us  [local(): part = lax.all_to_all(part, 'z', 0, 0, tiled=True)]
    all_to_all x1, waiting for transfers between devices: 2.45 us -> 0.01 us  [local(): shared = lax.all_to_all(shared, PLANE, 0, 0, tiled=True)]
    ppermute x5, waiting for transfers between devices: 19.3 us -> 21.7 us  [from_z(): return lax.ppermute(array, 'z', [(z, (z - u) % NZ) for z in range(NZ)])]
    all_to_all x1, starting transfers between devices: 5.25 us -> 6.08 us  [local(): shared = lax.all_to_all(shared, PLANE, 0, 0, tiled=True)]
  transfers between devices with their start and end apart: 6 -> 6, of which waited for: 5 -> 3; matrix products, arithmetic and copies ran while one was open for 1% -> 1% of each run, Pallas kernels for 3% -> 3%
where the time goes in v16:
time: 81.9 us; the launch traced here: 81.6 us
  blocking collectives  30.1 us (37%)
  waiting for transfers between devices  21.7 us (26%)
  starting transfers between devices  17.4 us (21%)
  Pallas kernels  9.81 us (12%)
  local copies, waits for them, and re-layouts  1.94 us (2%)
    ppermute x5, waiting for transfers between devices, from_z(): return lax.ppermute(array, 'z', [(z, (z - u) % NZ) for z in range(NZ)])  21.7 us
    all_to_all x1, blocking collectives, local(): part = lax.all_to_all(part, PLANE + FREQ, 0, 0, tiled=True)  16.9 us
    all_to_all x1, blocking collectives, local(): part = lax.all_to_all(part, 'z', 0, 0, tiled=True)  13.1 us
    ppermute x5, starting transfers between devices, from_z(): return lax.ppermute(array, 'z', [(z, (z - u) % NZ) for z in range(NZ)])  11.3 us
    all_to_all x1, starting transfers between devices, local(): shared = lax.all_to_all(shared, PLANE, 0, 0, tiled=True)  6.08 us
    pallas_call x1, Pallas kernels, local(): pl.pallas_call(absorb, out_shape=shape(f32, NZ, 1, LONG), in_specs=[vmem]...  3.53 us
    pallas_call x1, Pallas kernels, local(): pl.pallas_call(pack, out_shape=[shape(bf16, FULL, CELLS), shape(bf16, NEX...  3.33 us
    pallas_call x1, Pallas kernels, local(): pl.pallas_call(prepare, out_shape=shape(bf16, BUNDLE, CELLS), in_specs=[v...  2.13 us
  transfers between devices with their start and end apart: 6, of which 3 were waited for; matrix products, arithmetic and copies ran while one was open for 1% of the time, Pallas kernels for 3%

profile of v16, /device:TPU:1, one launch (start us, length us, event | category | flops | bytes accessed | tf_op | source)
XLA Modules:
  0.0 81.6 jit_solution(12991829203868154494)
XLA Ops:
  0.6 3.3 %pack.1 = (bf16[200,1024]{1,0:T(8,128)(2,1)}, bf16[168,1024]{1,0:T(8,128)(2,1)}, bf16[8,152,1024]{2,1,0:T(8,128)(2,1)}, bf16[64,512]{1,0:T(8,128)(2,1)}, f32[64,128]{1,0:T(8,128)}) custom-call(bf16[2,64,1024]{2,1,0:T(8,128)(2,1)} %bitcast.2, s32[64,4096]{1,0:T(8,128)} %mask.1, bf16[2,64]{1,0:T(2,128)(2,1)} %bitcast.4), custom_call_target="tpu_custom_call" | custom-call | tf_op jit(solution)/shard_map/pack/pallas_call | solution.py:240
  4.0 0.0 copy-start.5
  4.0 0.0 copy-start.6
  4.0 6.1 %all-to-all-start = ((bf16[8,152,1024]{2,1,0:T(8,128)(2,1)}), bf16[8,152,1024]{2,1,0:T(8,128)(2,1)S(1)}, u32[]{:S(2)}, u32[]{:S(2)}) async-start(bf16[8,152,1024]{2,1,0:T(8,128)(2,1)} %get-tuple-element.7), calls=%async_computation | async-start | bytes 4980736 | tf_op jit(solution)/shard_map/all_to_all | solution.py:255
  10.0 0.0 copy-done.5
  10.1 5.7 %collective-permute-start.2 = (bf16[200,1024]{1,0:T(8,128)(2,1)S(1)}, bf16[200,1024]{1,0:T(8,128)(2,1)S(1)}, u32[]{:S(2)}, u32[]{:S(2)}) collective-permute-start(bf16[200,1024]{1,0:T(8,128)(2,1)S(1)} %copy-done.5), channel_id=1, source_target_pairs={{0,224},{32,0},{64,32},{96,64},{128,96},{160,128},{192,160},{224,1... | collective-permute-start | bytes 1228808 | tf_op jit(solution)/shard_map/ppermute | solution.py:234
  15.7 0.0 copy-done.6
  15.7 0.0 collective-permute-start
  15.7 7.8 %collective-permute-done.2.one = bf16[200,1024]{1,0:T(8,128)(2,1)S(1)} collective-permute-done((bf16[200,1024]{1,0:T(8,128)(2,1)S(1)}, bf16[200,1024]{1,0:T(8,128)(2,1)S(1)}, u32[]{:S(2)}, u32[]{:S(2)}) %collective-permute-start.2) | collective-permute-done | bytes 409632 | tf_op jit(solution)/shard_map/ppermute | solution.py:234
  23.5 0.0 copy-start.3
  23.6 3.5 %collective-permute-start.3 = (bf16[168,1024]{1,0:T(8,128)(2,1)S(1)}, bf16[168,1024]{1,0:T(8,128)(2,1)S(1)}, u32[]{:S(2)}, u32[]{:S(2)}) collective-permute-start(bf16[168,1024]{1,0:T(8,128)(2,1)S(1)} %slice.8), channel_id=1, source_target_pairs={{0,224},{32,0},{64,32},{96,64},{128,96},{160,128},{192,160},{224,1... | collective-permute-start | bytes 1032200 | tf_op jit(solution)/shard_map/ppermute | solution.py:234
  27.0 0.0 collective-permute-done
  27.0 0.0 collective-permute-start.1
  27.0 5.5 %collective-permute-done.3.two = bf16[168,1024]{1,0:T(8,128)(2,1)S(1)} collective-permute-done((bf16[168,1024]{1,0:T(8,128)(2,1)S(1)}, bf16[168,1024]{1,0:T(8,128)(2,1)S(1)}, u32[]{:S(2)}, u32[]{:S(2)}) %collective-permute-start.3) | collective-permute-done | bytes 344096 | tf_op jit(solution)/shard_map/ppermute | solution.py:234
  32.5 0.0 copy-start.4
  32.5 0.8 slice.9
  33.3 2.2 %collective-permute-start.4 = (bf16[136,1024]{1,0:T(8,128)(2,1)}, bf16[136,1024]{1,0:T(8,128)(2,1)S(1)}, u32[]{:S(2)}, u32[]{:S(2)}) collective-permute-start(bf16[136,1024]{1,0:T(8,128)(2,1)} %slice.9), channel_id=1, source_target_pairs={{0,192},{32,224},{64,0},{96,32},{128,64},{160,96},{192,128},{224,1... | collective-permute-start | bytes 835592 | tf_op jit(solution)/shard_map/ppermute | solution.py:234
  35.5 0.0 copy-done.3
  35.5 0.0 copy-done.4
  35.5 0.0 copy-start
  35.5 0.0 copy-start.2
  35.5 2.1 %prepare.1.bundle = bf16[376,1024]{1,0:T(8,128)(2,1)} custom-call(bf16[64,512]{1,0:T(8,128)(2,1)} %get-tuple-element.10.own_mask, f32[64,128]{1,0:T(8,128)} %get-tuple-element.11.own_spec, bf16[200,1024]{1,0:T(8,128)(2,1)} %copy-done.3, bf16[168,1024]{1,0:T(8,128)(2,1)} %copy-done.4), custom_call_target="tpu_custom_call" | custom-call | flops 10000000000 | tf_op jit(solution)/shard_map/prepare/pallas_call | solution.py:258
  37.7 8.4 %collective-permute-done.1.three = bf16[168,1024]{1,0:T(8,128)(2,1)S(1)} collective-permute-done((bf16[168,1024]{1,0:T(8,128)(2,1)}, bf16[168,1024]{1,0:T(8,128)(2,1)S(1)}, u32[]{:S(2)}, u32[]{:S(2)}) %collective-permute-start.1) | collective-permute-done | bytes 344096 | tf_op jit(solution)/shard_map/ppermute | solution.py:234
  46.0 0.0 collective-permute-done.4.four
  46.0 0.0 all-to-all-done.shared
  46.0 0.0 copy-done
  46.0 0.0 copy-done.2
  46.1 0.0 copy-start.1
  46.1 1.1 %copy-done.1 = bf16[376,1024]{1,0:T(8,128)(2,1)S(1)} copy-done((bf16[376,1024]{1,0:T(8,128)(2,1)S(1)}, bf16[376,1024]{1,0:T(8,128)(2,1)}, u32[]{:S(2)}) %copy-start.1) | copy-done | bytes 770072
  47.2 3.5 %absorb.1 = f32[8,1,1152]{2,1,0:T(1,128)S(1)} custom-call(bf16[8,152,1024]{2,1,0:T(8,128)(2,1)S(1)} %all-to-all-done.shared, f32[1,1024]{1,0:T(1,128)S(1)} %copy-done.2, bf16[2,64,1024]{2,1,0:T(8,128)(2,1)S(1)} %bitcast.3, bf16[168,1024]{1,0:T(8,128)(2,1)S(1)} %collective-permute-done.1.three, bf16[136,1024]{1,0:T(8,128)(2,1)S(1)} %collective-permute-done.4.four, ...), custom_call_target="tpu_custom_call" | custom-call | tf_op jit(solution)/shard_map/absorb/pallas_call | solution.py:268
  50.7 13.1 %all_to_all.15.parts = f32[8,1,1152]{2,1,0:T(1,128)S(1)} all-to-all(f32[8,1,1152]{2,1,0:T(1,128)S(1)} %absorb.1), channel_id=1, replica_groups=mesh['z'=8,'xl'=2,'y'=4,'xh'=2,'core'=2] {'z'}, dimensions={0} | all-to-all | bytes 73728 | tf_op jit(solution)/shard_map/all_to_all | solution.py:283
  63.9 16.9 %all_to_all.16.parts = f32[32,1,1152]{2,1,0:T(1,128)S(1)} all-to-all(f32[32,1,1152]{2,1,0:T(1,128)S(1)} %gather_z.1), channel_id=1, replica_groups=mesh['z'=8,'xl'=2,'y'=4,'xh'=2,'core'=2] {'xl','y','xh','core'}, dimensions={0} | all-to-all | bytes 294912 | tf_op jit(solution)/shard_map/all_to_all | solution.py:292
  80.8 0.8 finish.1
  (2 shorter events, 0.1 us)
Async XLA Ops:
  4.0 6.1 %copy-start.5 = (bf16[200,1024]{1,0:T(8,128)(2,1)S(1)}, bf16[200,1024]{1,0:T(8,128)(2,1)}, u32[]{:S(2)}) copy-start(bf16[200,1024]{1,0:T(8,128)(2,1)} %get-tuple-element.9) | copy-start | bytes 1228804
  4.0 11.7 %copy-start.6 = (bf16[168,1024]{1,0:T(8,128)(2,1)S(1)}, bf16[168,1024]{1,0:T(8,128)(2,1)}, u32[]{:S(2)}) copy-start(bf16[168,1024]{1,0:T(8,128)(2,1)} %get-tuple-element.8) | copy-start | bytes 1032196
  4.0 42.1 %all-to-all-start = ((bf16[8,152,1024]{2,1,0:T(8,128)(2,1)}), bf16[8,152,1024]{2,1,0:T(8,128)(2,1)S(1)}, u32[]{:S(2)}, u32[]{:S(2)}) async-start(bf16[8,152,1024]{2,1,0:T(8,128)(2,1)} %get-tuple-element.7), calls=%async_computation | async-start | bytes 4980736 | tf_op jit(solution)/shard_map/all_to_all | solution.py:255
  10.1 13.5 %collective-permute-start.2 = (bf16[200,1024]{1,0:T(8,128)(2,1)S(1)}, bf16[200,1024]{1,0:T(8,128)(2,1)S(1)}, u32[]{:S(2)}, u32[]{:S(2)}) collective-permute-start(bf16[200,1024]{1,0:T(8,128)(2,1)S(1)} %copy-done.5), channel_id=1, source_target_pairs={{0,224},{32,0},{64,32},{96,64},{128,96},{160,128},{192,160},{224,1... | collective-permute-start | bytes 1228808 | tf_op jit(solution)/shard_map/ppermute | solution.py:234
  15.7 11.3 %collective-permute-start = (bf16[168,1024]{1,0:T(8,128)(2,1)S(1)}, bf16[168,1024]{1,0:T(8,128)(2,1)}, u32[]{:S(2)}, u32[]{:S(2)}) collective-permute-start(bf16[168,1024]{1,0:T(8,128)(2,1)S(1)} %copy-done.6), channel_id=1, source_target_pairs={{0,32},{32,64},{64,96},{96,128},{128,160},{160,192},{192,224},{224... | collective-permute-start | bytes 1032200 | tf_op jit(solution)/shard_map/ppermute | solution.py:234
  23.5 12.0 %copy-start.3 = (bf16[200,1024]{1,0:T(8,128)(2,1)}, bf16[200,1024]{1,0:T(8,128)(2,1)S(1)}, u32[]{:S(2)}) copy-start(bf16[200,1024]{1,0:T(8,128)(2,1)S(1)} %collective-permute-done.2.one) | copy-start | bytes 1228804
  23.6 9.0 %collective-permute-start.3 = (bf16[168,1024]{1,0:T(8,128)(2,1)S(1)}, bf16[168,1024]{1,0:T(8,128)(2,1)S(1)}, u32[]{:S(2)}, u32[]{:S(2)}) collective-permute-start(bf16[168,1024]{1,0:T(8,128)(2,1)S(1)} %slice.8), channel_id=1, source_target_pairs={{0,224},{32,0},{64,32},{96,64},{128,96},{160,128},{192,160},{224,1... | collective-permute-start | bytes 1032200 | tf_op jit(solution)/shard_map/ppermute | solution.py:234
  27.0 19.0 %collective-permute-start.1 = (bf16[168,1024]{1,0:T(8,128)(2,1)}, bf16[168,1024]{1,0:T(8,128)(2,1)S(1)}, u32[]{:S(2)}, u32[]{:S(2)}) collective-permute-start(bf16[168,1024]{1,0:T(8,128)(2,1)} %collective-permute-done), channel_id=1, source_target_pairs={{0,64},{32,96},{64,128},{96,160},{128,192},{160,224},{192,0},{224,... | collective-permute-start | bytes 1032200 | tf_op jit(solution)/shard_map/ppermute | solution.py:234
  32.5 3.0 %copy-start.4 = (bf16[168,1024]{1,0:T(8,128)(2,1)}, bf16[168,1024]{1,0:T(8,128)(2,1)S(1)}, u32[]{:S(2)}) copy-start(bf16[168,1024]{1,0:T(8,128)(2,1)S(1)} %collective-permute-done.3.two) | copy-start | bytes 1032196
  33.3 12.7 %collective-permute-start.4 = (bf16[136,1024]{1,0:T(8,128)(2,1)}, bf16[136,1024]{1,0:T(8,128)(2,1)S(1)}, u32[]{:S(2)}, u32[]{:S(2)}) collective-permute-start(bf16[136,1024]{1,0:T(8,128)(2,1)} %slice.9), channel_id=1, source_target_pairs={{0,192},{32,224},{64,0},{96,32},{128,64},{160,96},{192,128},{224,1... | collective-permute-start | bytes 835592 | tf_op jit(solution)/shard_map/ppermute | solution.py:234
  35.5 10.5 %copy-start = (bf16[1,2,64,1024]{3,2,1,0:T(8,128)(2,1)S(1)}, bf16[1,2,64,1024]{3,2,1,0:T(8,128)(2,1)}, u32[]{:S(2)}) copy-start(bf16[1,2,64,1024]{3,2,1,0:T(8,128)(2,1)} %param.5) | copy-start | bytes 786436
  35.5 10.5 %copy-start.2 = (f32[1,1024]{1,0:T(1,128)S(1)}, f32[1,1024]{1,0:T(1,128)}, u32[]{:S(2)}) copy-start(f32[1,1024]{1,0:T(1,128)} %source.3) | copy-start | bytes 12292
  46.1 1.1 %copy-start.1 = (bf16[376,1024]{1,0:T(8,128)(2,1)S(1)}, bf16[376,1024]{1,0:T(8,128)(2,1)}, u32[]{:S(2)}) copy-start(bf16[376,1024]{1,0:T(8,128)(2,1)} %prepare.1.bundle) | copy-start | bytes 2310148
